TPU v7x, 32 devices: a whole 2x2x4 slice. The times are simulated.
32 devices in a mesh: outer: 8 (over z, core), inner: 4 (over y, x).
Axes of the slice: x: 2, y: 2, z: 4, core: 2. Of those that a mesh axis runs over, the one named last changes fastest.
Arguments:
- queries: bfloat16 [2048, 4096], P(('outer', 'inner')), may hold values from -6 to 6
- keys: bfloat16 [2048, 4096], P(('outer', 'inner')), may hold values from -6 to 6
- values: bfloat16 [2048, 4096], P(('outer', 'inner')), may hold values from -6 to 6
- lengths: int32 [16], replicated, may hold values from 1 to 32, 128 in all
- norm_gain: float32 [4096], replicated, may hold values from 0.5 to 1.5
Outputs:
- attended: bfloat16 [2048, 4096], P(('outer', 'inner'))
Inputs may be any that keep to these rules, and one draw needn't show every extreme that they name: The lengths sum to 128; one document is exactly 32 units long.
All inputs are finite; a program needn't handle non-finite values.
Results may differ from a plain program's by a relative error of at most 0.0049.
Values sent between devices are 32-bit elements; how exact they have to be, the bound alone decides.
No kernel may reach another device: no remote copies, remote signals or barrier semaphores. Data moves between devices by JAX's collectives and lax.ppermute only.
A program may use at most 64 MiB of HBM per device.

v0:
```python
import jax
import jax.numpy as jnp
from jax import lax
from jax.sharding import PartitionSpec as P

HEAD_DIM = 128
BLOCK = 16


EPSILON = 1e-05


def carried_in(shard, axis, combine, identity):
    devices, index = (lax.axis_size(axis), lax.axis_index(axis))
    everything = jax.tree.map(lambda part: lax.all_gather(part, axis), shard)
    start = jax.tree.map(
        lambda part, zero: jnp.broadcast_to(jnp.asarray(zero, part.dtype), part.shape),
        shard,
        identity,
    )

    def lap(k, before):
        reached = k < index
        new = combine(before, jax.tree.map(lambda part: part[k], everything))
        return jax.tree.map(lambda a, b: jnp.where(reached, a, b), new, before)

    return lax.fori_loop(0, devices, lap, start)


def join_states(earlier, later):
    return (jnp.maximum(earlier[0], later[0]), later[1] + (1.0 - later[0]) * earlier[1])


def doc_ids(tok_rows, doc_starts):
    return jnp.sum((tok_rows[:, None] >= doc_starts[None, :]).astype(jnp.int32), axis=1) - 1


def body(queries, keys, values, lengths, norm_gain):
    tok_count = queries.shape[0]
    head_count = queries.shape[1] // HEAD_DIM
    state_rows = head_count * HEAD_DIM
    inner_count = lax.axis_size("inner")
    share_rows = state_rows // inner_count
    inner_place = lax.axis_index("inner")
    outer_place = lax.axis_index("outer")
    device_place = outer_place * inner_count + inner_place
    first_row = device_place * tok_count
    tok_rows = first_row + jnp.arange(tok_count, dtype=jnp.int32)
    doc_starts = BLOCK * (jnp.cumsum(lengths) - lengths)
    docs = doc_ids(tok_rows, doc_starts)
    first_doc = docs[0]
    final_doc = docs[-1]
    opens_block = jnp.any(doc_starts == first_row).astype(jnp.float32)
    group_places = outer_place * inner_count + jnp.arange(inner_count, dtype=jnp.int32)
    group_first = group_places * tok_count
    block_flags = jnp.any(
        (doc_starts[None, :] >= group_first[:, None])
        & (doc_starts[None, :] < group_first[:, None] + tok_count),
        axis=1,
    ).astype(jnp.float32)
    query_heads = queries.reshape(tok_count, head_count, HEAD_DIM)
    key_heads = keys.reshape(tok_count, head_count, HEAD_DIM)
    value_heads = values.reshape(tok_count, head_count, HEAD_DIM)
    final_keys = jnp.where((docs == final_doc)[:, None, None], key_heads, jnp.zeros_like(key_heads))
    local_state = jnp.einsum(
        "thd,the->hde", final_keys, value_heads, preferred_element_type=jnp.float32
    )
    shares = lax.all_to_all(
        local_state.reshape(1, state_rows, HEAD_DIM),
        "inner",
        split_axis=1,
        concat_axis=0,
        tiled=True,
    )
    scores = jnp.einsum("thd,shd->hts", query_heads, key_heads, preferred_element_type=jnp.float32)
    allowed = (tok_rows[:, None] >= tok_rows[None, :]) & (docs[:, None] == docs[None, :])
    weights = jnp.where(allowed[None], scores, 0.0).astype(jnp.bfloat16)
    intra = jnp.einsum("hts,she->the", weights, value_heads, preferred_element_type=jnp.float32)

    def walk(carried, item):
        return (join_states(carried, item), carried)

    share_zero = (jnp.float32(0.0), jnp.zeros((share_rows, HEAD_DIM), jnp.float32))
    group_total, earlier_in_group = lax.scan(walk, share_zero, (block_flags, shares))
    outer_prefix = carried_in(group_total, "outer", join_states, share_zero)
    combined = (
        earlier_in_group[1] + (1.0 - earlier_in_group[0])[:, None, None] * outer_prefix[1][None]
    )
    returned = lax.all_to_all(combined, "inner", split_axis=0, concat_axis=1, tiled=True)
    prefix_state = returned.reshape(head_count, HEAD_DIM, HEAD_DIM)
    carry_in = (1.0 - opens_block) * prefix_state
    held = carry_in.astype(jnp.bfloat16)
    inter = jnp.einsum("thd,hde->the", query_heads, held, preferred_element_type=jnp.float32)
    inter = jnp.where((docs == first_doc)[:, None, None], inter, 0.0)
    mixed = intra + inter
    scale = lax.rsqrt(jnp.mean(mixed * mixed, axis=-1, keepdims=True) + EPSILON)
    gain_heads = norm_gain.reshape(head_count, HEAD_DIM)
    attended = (mixed * scale * gain_heads[None]).astype(jnp.bfloat16)
    return attended.reshape(tok_count, head_count * HEAD_DIM)


def solution(mesh):
    placed = (
        P(("outer", "inner"), None),
        P(("outer", "inner"), None),
        P(("outer", "inner"), None),
        P(),
        P(),
    )
    return jax.shard_map(
        body, mesh=mesh, in_specs=placed, out_specs=P(("outer", "inner"), None), check_vma=False
    )
```

profile of v0, /device:TPU:0, one launch (start us, length us, event | category | flops | bytes accessed | tf_op | source)
XLA Modules:
  0.0 167.0 jit_solution(1256728201418256629)
XLA Ops:
  6.5 0.0 copy-start
  6.5 0.8 copy.26
  7.4 0.1 reduce
  7.5 1.4 compare_reduce_fusion
  8.9 0.1 convert_reduce_fusion
  9.0 0.6 fusion.27
  9.6 1.3 broadcast_compare_fusion.1
  10.9 0.0 copy-done
  10.9 2.9 %fusion.5 = f32[32,128,128]{2,1,0:T(8,128)} fusion(pred[64]{0:T(512)(128)(4,1)S(1)} %get-tuple-element.213, bf16[64,4096]{1,0:T(8,128)(2,1)S(1)} %copy-done, bf16[64,4096]{1,0:T(8,128)(2,1)} %param.10), kind=kOutput, calls=%fused_computation.16 | convolution fusion | flops 67371008 | bytes 3145792 | tf_op jit(solution)/shard_map/thd,the->hde/dot_general | solution.py:65
  13.8 5.2 %all-to-all-start = ((f32[1,4096,128]{2,0,1:T(1,128)}), f32[1,4096,128]{2,0,1:T(1,128)S(1)}, u32[]{:S(2)}, u32[]{:S(2)}) async-start(f32[1,4096,128]{2,0,1:T(1,128)} %bitcast.90), calls=%async_computation | async-start | bytes 4194304 | tf_op jit(solution)/shard_map/all_to_all | solution.py:68
  19.0 0.0 all-gather.3.cloned.1.call-start
  19.0 0.2 and_reduce_fusion
  19.2 24.6 %all-to-all-done = f32[1,4096,128]{2,0,1:T(1,128)S(1)} async-done(((f32[1,4096,128]{2,0,1:T(1,128)}), f32[1,4096,128]{2,0,1:T(1,128)S(1)}, u32[]{:S(2)}, u32[]{:S(2)}) %all-to-all-start) | async-done | bytes 2097184 | tf_op jit(solution)/shard_map/all_to_all | solution.py:68
  43.8 12.1 %while.31 = (s32[]{:T(128)}, f32[]{:T(128)}, f32[1024,128]{1,0:T(8,128)S(1)}, f32[4]{0:T(128)S(1)}, f32[4,1024,128]{2,1,0:T(8,128)}, /*index=5*/f32[4]{0:T(128)S...) while((s32[]{:T(128)}, f32[]{:T(128)}, f32[1024,128]{1,0:T(8,128)S(1)}, ...), condition=%wide.region_5.6_spmd.clone, body=%wide.region_4.5_spmd.clone.sunk | while | flops 524293 | bytes 2622128 | solution.py:84
  43.8 0.8 bitcast_dynamic-update-slice_fusion.2
  44.7 0.6 dynamic_slice.33
  46.0 0.1 bitcast_add_fusion.3
  46.7 0.1 dynamic_update_slice.14
  46.8 0.8 bitcast_dynamic-update-slice_fusion.2
  47.7 0.6 dynamic_slice.33
  49.0 0.1 bitcast_add_fusion.3
  49.8 0.1 dynamic_update_slice.14
  49.9 0.8 bitcast_dynamic-update-slice_fusion.2
  50.7 0.6 dynamic_slice.33
  52.0 0.1 bitcast_add_fusion.3
  52.8 0.1 dynamic_update_slice.14
  52.9 0.8 bitcast_dynamic-update-slice_fusion.2
  53.7 0.6 dynamic_slice.33
  55.0 0.1 bitcast_add_fusion.3
  55.8 0.1 dynamic_update_slice.14
  55.9 0.8 copy-done.1
  56.7 0.0 all-gather.3.cloned.1.call-update
  56.7 0.0 copy-done.7
  56.8 0.7 dynamic-slice
  57.4 0.8 dynamic-update-slice
  58.2 16.4 %all-reduce = f32[8]{0:T(128)S(1)} all-reduce(f32[8]{0:T(128)S(1)} %dynamic-update-slice), channel_id=1, replica_groups=mesh['outer'=8,'inner'=4] {'outer'}, use_global_device_ids=true, to_apply=%add | all-reduce | flops 8 | bytes 64
  74.6 29.9 %all-gather.3.cloned.1.call-done = f32[8192,128]{1,0:T(8,128)} async-done(((f32[1024,128]{1,0:T(8,128)}), f32[8192,128]{1,0:T(8,128)}) %all-gather.3.cloned.1.call-update) | async-done | bytes 4194320 | tf_op jit(solution)/shard_map/all_gather | solution.py:15
  104.5 21.9 %while.32 = (s32[]{:T(128)}, f32[1024,128]{1,0:T(8,128)S(1)}, s32[]{:T(128)}, f32[8,1024,128]{2,1,0:T(8,128)}, f32[8]{0:T(128)S(1)}, /*index=5*/s32[]{:T(128)}, f32[1]{0:T(128)}, s32[]{:T(128)}) while((s32[]{:T(128)}, f32[1024,128]{1,0:T(8,128)S(1)}, s32[]{:T(128)}, f32[8,1024,128]{2,1,0:T(8,128)}, f32[8]{0:T(128)S(1)}, ...), condition=%wide.region_7.8_spmd.clone, body=%wide.region_6.7_spmd.clone.sunk | while | flops 524293 | bytes 1573001 | solution.py:27
  104.5 0.6 dynamic_slice.35
  105.8 1.5 fusion.37
  107.3 0.6 dynamic_slice.35
  108.5 1.5 fusion.37
  110.0 0.6 dynamic_slice.35
  111.2 1.5 fusion.37
  112.7 0.6 dynamic_slice.35
  114.0 1.5 fusion.37
  115.5 0.6 dynamic_slice.35
  116.7 1.5 fusion.37
  118.2 0.6 dynamic_slice.35
  119.5 1.5 fusion.37
  120.9 0.6 dynamic_slice.35
  122.2 1.5 fusion.37
  123.7 0.6 dynamic_slice.35
  124.9 1.5 fusion.37
  126.4 1.6 multiply_add_fusion
  128.0 4.0 %all-to-all-start.1 = ((f32[4,1024,128]{2,1,0:T(8,128)}), f32[4,1024,128]{2,1,0:T(8,128)S(1)}, u32[]{:S(2)}, u32[]{:S(2)}) async-start(f32[4,1024,128]{2,1,0:T(8,128)} %multiply_add_fusion), calls=%async_computation.1 | async-start | bytes 4194304 | tf_op jit(solution)/shard_map/all_to_all | solution.py:89
  132.6 0.1 compare_and_fusion
  132.7 2.6 %convolution_bitcast_fusion = f32[64,32,128]{2,0,1:T(8,128)} fusion(pred[64,64]{1,0:T(8,128)(4,1)S(1)} %compare_and_fusion, bf16[64,4096]{1,0:T(8,128)(2,1)S(1)} %copy-done, bf16[64,4096]{1,0:T(8,128)(2,1)S(1)} %copy-done.4, bf16[64,4096]{1,0:T(8,128)(2,1)} %param.9), kind=kOutput, calls=%fused_computation.10 | convolution fusion | flops 67371008 | bytes 2625536 | tf_op jit(solution)/shard_map/hts,she->the/dot_general | solution.py:78
  135.3 22.0 %all-to-all-done.1 = f32[4,1024,128]{2,1,0:T(8,128)S(1)} async-done(((f32[4,1024,128]{2,1,0:T(8,128)}), f32[4,1024,128]{2,1,0:T(8,128)S(1)}, u32[]{:S(2)}, u32[]{:S(2)}) %all-to-all-start.1) | async-done | bytes 2097184 | tf_op jit(solution)/shard_map/all_to_all | solution.py:89
  157.3 0.2 multiply_convert_fusion
  157.4 0.0 copy-start.6
  157.5 1.0 copy-done.3
  158.5 0.5 multiply_reduce_fusion
  159.0 1.1 copy_bitcast_fusion
  (22 shorter events, 0.1 us)
Async XLA Ops:
  6.5 4.3 %copy-start = (bf16[64,4096]{1,0:T(8,128)(2,1)S(1)}, bf16[64,4096]{1,0:T(8,128)(2,1)}, u32[]{:S(2)}) copy-start(bf16[64,4096]{1,0:T(8,128)(2,1)} %param.11) | copy-start | bytes 1572868
  13.8 30.0 %all-to-all-start = ((f32[1,4096,128]{2,0,1:T(1,128)}), f32[1,4096,128]{2,0,1:T(1,128)S(1)}, u32[]{:S(2)}, u32[]{:S(2)}) async-start(f32[1,4096,128]{2,0,1:T(1,128)} %bitcast.90), calls=%async_computation | async-start | bytes 4194304 | tf_op jit(solution)/shard_map/all_to_all | solution.py:68
  19.0 85.6 %all-gather.3.cloned.1.call-start = ((), (), s32[]{:S(2)}) async-start(), calls=%async_computation.2 | async-start | bytes 4718592 | tf_op jit(solution)/shard_map/all_gather | solution.py:15
  43.8 12.9 %copy-start.7 = (u32[32]{0:T(128)S(1)}, u32[32]{0:T(128)}, u32[]{:S(2)}) copy-start(u32[32]{0:T(128)} %constant.84) | copy-start | bytes 388
  55.9 0.8 copy-start.1
  55.9 70.5 %copy-start.2 = (f32[4,1024,128]{2,1,0:T(8,128)S(1)}, f32[4,1024,128]{2,1,0:T(8,128)}, u32[]{:S(2)}) copy-start(f32[4,1024,128]{2,1,0:T(8,128)} %get-tuple-element.139) | copy-start | bytes 6291460
  128.0 4.7 %copy-start.4 = (bf16[64,4096]{1,0:T(8,128)(2,1)S(1)}, bf16[64,4096]{1,0:T(8,128)(2,1)}, u32[]{:S(2)}) copy-start(bf16[64,4096]{1,0:T(8,128)(2,1)} %param.10) | copy-start | bytes 1572868
  128.0 29.3 %all-to-all-start.1 = ((f32[4,1024,128]{2,1,0:T(8,128)}), f32[4,1024,128]{2,1,0:T(8,128)S(1)}, u32[]{:S(2)}, u32[]{:S(2)}) async-start(f32[4,1024,128]{2,1,0:T(8,128)} %multiply_add_fusion), calls=%async_computation.1 | async-start | bytes 4194304 | tf_op jit(solution)/shard_map/all_to_all | solution.py:89
  135.3 22.2 %copy-start.5 = (bf16[64,4096]{1,0:T(8,128)(2,1)S(1)}, bf16[64,4096]{1,0:T(8,128)(2,1)}, u32[]{:S(2)}) copy-start(bf16[64,4096]{1,0:T(8,128)(2,1)} %param.9) | copy-start | bytes 1572868
  157.3 1.2 copy-start.3
  157.4 1.6 copy-start.6
Sparse Core Ops, SparseCore 0:
  56.8 47.6 all-gather.2
where the time goes:
time: 168 us; the launch traced here: 167 us
  waiting for transfers between devices  76.5 us (46%)
  other arithmetic  21.8 us (13%)
  blocking collectives  16.4 us (10%)
  between operations  14.2 us (8%)
  local copies, waits for them, and re-layouts  12.4 us (7%)
  loops' own time  10.5 us (6%)
  starting transfers between devices  9.12 us (5%)
  matrix products  6.03 us (4%)
    all_gather x1, waiting for transfers between devices, carried_in(): everything = jax.tree.map(lambda part: lax.all_gather(part, axis), shard)  29.9 us
    all_to_all x1, waiting for transfers between devices, body(): lax.all_to_all(local_state.reshape(1, state_rows, HEAD_DIM), 'inner', spl...  24.6 us
    all_to_all x1, waiting for transfers between devices, body(): lax.all_to_all(combined, 'inner', split_axis=0, concat_axis=1, tiled=True)  22 us
    unnamed x1, blocking collectives  16.4 us
    select_n x8, other arithmetic, lap(): return jax.tree.map(lambda a, b: jnp.where(reached, a, b), new, before)  11.8 us
    another operation x1, loops' own time, carried_in(): return lax.fori_loop(0, devices, lap, start)  5.38 us
    all_to_all x1, starting transfers between devices, body(): lax.all_to_all(local_state.reshape(1, state_rows, HEAD_DIM), 'inner', spl...  5.17 us
    another operation x1, loops' own time, body(): lax.scan(walk, share_zero, (block_flags, shares))  5.11 us
  transfers between devices with their start and end apart: 3, of which 3 were waited for; matrix products, arithmetic and copies ran while one was open for 3% of the time, Pallas kernels for 0%

commit v1 on v0

v1 whole, which is shorter than its diff:
```python
import functools

import jax
import jax.numpy as jnp
from jax import lax
from jax.experimental import pallas as pl
from jax.experimental.pallas import tpu as pltpu
from jax.sharding import PartitionSpec as P

HEAD_DIM = 128
BLOCK = 16
CORES = 2
SHARE = 4
EPSILON = 1e-05


def spread(members, width, place, *refs):
    count = len(refs) - members
    sources, outs = refs[:count], refs[count:]
    me = place[0]
    for d in range(members):
        column = pl.multiple_of((me ^ d) * width, width)
        for i, source in enumerate(sources):
            part = source[:, pl.ds(column, width)].astype(jnp.float32)
            if count == 1:
                outs[d][...] = part
            else:
                outs[d][i] = part


def doc_table(lengths, starts, docs):
    total = jnp.int32(0)
    for i in range(docs):
        starts[i] = total
        total = total + lengths[i] * BLOCK


def start_of(starts, docs, token):
    found = jnp.int32(0)
    for i in range(docs):
        found = jnp.where(starts[i] <= token, starts[i], found)
    return found


def gather_states(members, heads, docs, rows, place, lengths, *refs):
    parts = refs[:members]
    key_out, value_out, carry_out, total_out, starts, first_of = refs[members:]
    me, base = place[0], place[1]
    doc_table(lengths, starts, docs)
    for j in range(members + 1):
        first_of[j] = start_of(starts, docs, base + j * rows)
    for d in range(members):
        j = me ^ d
        key_out[j] = parts[d][0].astype(jnp.bfloat16)
        value_out[j] = parts[d][1].astype(jnp.bfloat16)
    row = lax.broadcasted_iota(jnp.int32, (rows, heads * HEAD_DIM), 0)
    state = [jnp.zeros((HEAD_DIM, HEAD_DIM), jnp.float32) for _ in range(heads)]
    for j in range(members):
        begin = base + j * rows
        since = first_of[j + 1]
        keys = key_out[j].astype(jnp.float32)
        keys = jnp.where(row + begin >= since, keys, 0.0).astype(jnp.bfloat16)
        values = value_out[j]
        keep = jnp.where(since <= begin, 1.0, 0.0).astype(jnp.float32)
        for h in range(heads):
            span = slice(h * HEAD_DIM, (h + 1) * HEAD_DIM)
            carry_out[j, h] = state[h]
            own = lax.dot_general(
                keys[:, span], values[:, span], (((0,), (0,)), ((), ())), preferred_element_type=jnp.float32
            )
            state[h] = keep * state[h] + own
    for h in range(heads):
        total_out[h] = state[h]


def attend(members, heads, docs, rows, place, lengths, *refs):
    query_parts = refs[:members]
    keys, values, carry, earlier, gain = refs[members : members + 5]
    outs = refs[members + 5 : 2 * members + 5]
    starts = refs[2 * members + 5]
    me, base = place[0], place[1]
    doc_table(lengths, starts, docs)
    row = lax.broadcasted_iota(jnp.int32, (rows, HEAD_DIM), 0)
    lane = lax.broadcasted_iota(jnp.int32, (rows, rows), 1)
    for d in range(members):
        j = me ^ d
        begin = base + j * rows
        token = row + begin
        since = jnp.zeros((rows, HEAD_DIM), jnp.int32)
        for i in range(docs):
            since = jnp.where(starts[i] <= token, starts[i], since)
        local = since - begin
        continued = local <= 0
        allowed = (lane <= row[:, :rows]) & (lane >= local[:, :rows])
        from_earlier = jnp.where(start_of(starts, docs, begin) < base, 1.0, 0.0).astype(jnp.float32)
        for h in range(heads):
            span = slice(h * HEAD_DIM, (h + 1) * HEAD_DIM)
            query = query_parts[d][:, span].astype(jnp.bfloat16)
            scores = lax.dot_general(
                query, keys[j, :, span], (((1,), (1,)), ((), ())), preferred_element_type=jnp.float32
            )
            weights = jnp.where(allowed, scores, 0.0).astype(jnp.bfloat16)
            mixed = jnp.dot(weights, values[j, :, span], preferred_element_type=jnp.float32)
            held = (carry[j, h] + from_earlier * earlier[h]).astype(jnp.bfloat16)
            inter = jnp.dot(query, held, preferred_element_type=jnp.float32)
            mixed = mixed + jnp.where(continued, inter, 0.0)
            scale = lax.rsqrt(jnp.mean(mixed * mixed, axis=-1, keepdims=True) + EPSILON)
            outs[d][:, span] = mixed * scale * gain[:, pl.ds(pl.multiple_of(me * heads * HEAD_DIM, HEAD_DIM) + h * HEAD_DIM, HEAD_DIM)]


def place_rows(members, width, place, *refs):
    out = refs[members]
    me = place[0]
    for d in range(members):
        column = pl.multiple_of((me ^ d) * width, width)
        out[:, pl.ds(column, width)] = refs[d][...].astype(jnp.bfloat16)


def body(queries, keys, values, lengths, norm_gain):
    rows, columns = queries.shape
    head_count = columns // HEAD_DIM
    docs = lengths.shape[0]
    inner_count = lax.axis_size("inner")
    devices = lax.axis_size("outer") * inner_count
    members = CORES * inner_count
    planes = devices // members
    heads = head_count // members
    width = heads * HEAD_DIM
    reach = -(-(devices // SHARE) // members)
    everyone = ("outer", "inner")
    index = lax.axis_index("outer") * inner_count + lax.axis_index("inner")
    me = index % members
    base = (index - me) * rows
    place = jnp.stack([me, base]).astype(jnp.int32)
    smem = pl.BlockSpec(memory_space=pltpu.SMEM)
    vmem = pl.BlockSpec(memory_space=pltpu.VMEM)
    params = pltpu.CompilerParams(vmem_limit_bytes=48 * 1024 * 1024)
    f32 = jnp.float32

    def exchange(parts):
        got = [parts[0]]
        for d in range(1, members):
            pairs = [(g, g - g % members + (g % members ^ d)) for g in range(devices)]
            got.append(lax.ppermute(parts[d], everyone, pairs))
        return got

    pair_parts = pl.pallas_call(
        functools.partial(spread, members, width),
        out_shape=[jax.ShapeDtypeStruct((2, rows, width), f32)] * members,
        in_specs=[smem, vmem, vmem],
        out_specs=[vmem] * members,
        compiler_params=params,
        name="spread_kv",
    )(place, keys, values)
    pair_got = exchange(pair_parts)
    query_parts = pl.pallas_call(
        functools.partial(spread, members, width),
        out_shape=[jax.ShapeDtypeStruct((rows, width), f32)] * members,
        in_specs=[smem, vmem],
        out_specs=[vmem] * members,
        compiler_params=params,
        name="spread_q",
    )(place, queries)
    query_got = exchange(query_parts)
    key_blocks, value_blocks, carry, total = pl.pallas_call(
        functools.partial(gather_states, members, heads, docs, rows),
        out_shape=[
            jax.ShapeDtypeStruct((members, rows, width), jnp.bfloat16),
            jax.ShapeDtypeStruct((members, rows, width), jnp.bfloat16),
            jax.ShapeDtypeStruct((members, heads, HEAD_DIM, HEAD_DIM), f32),
            jax.ShapeDtypeStruct((heads, HEAD_DIM, HEAD_DIM), f32),
        ],
        in_specs=[smem, smem] + [vmem] * members,
        out_specs=[vmem] * 4,
        scratch_shapes=[pltpu.SMEM((docs,), jnp.int32), pltpu.SMEM((members + 1,), jnp.int32)],
        compiler_params=params,
        name="gather_states",
    )(place, lengths, *pair_got)
    up = [(g, g + members) for g in range(devices - members)]
    moving = lax.ppermute(total, everyone, up)
    earlier = moving
    if reach > 1:
        starts = BLOCK * (jnp.cumsum(lengths) - lengths)
        opens = jnp.max(jnp.where(starts <= base, starts, 0))
        for k in range(2, min(reach, planes - 1) + 1):
            moving = lax.ppermute(moving, everyone, up)
            earlier = earlier + jnp.where(opens < base - (k - 1) * members * rows, moving, 0.0)
    mixed_parts = pl.pallas_call(
        functools.partial(attend, members, heads, docs, rows),
        out_shape=[jax.ShapeDtypeStruct((rows, width), f32)] * members,
        in_specs=[smem, smem] + [vmem] * (members + 5),
        out_specs=[vmem] * members,
        scratch_shapes=[pltpu.SMEM((docs,), jnp.int32)],
        compiler_params=params,
        name="attend",
    )(place, lengths, *query_got, key_blocks, value_blocks, carry, earlier, norm_gain.reshape(1, columns))
    mixed_got = exchange(mixed_parts)
    return pl.pallas_call(
        functools.partial(place_rows, members, width),
        out_shape=jax.ShapeDtypeStruct((rows, columns), jnp.bfloat16),
        in_specs=[smem] + [vmem] * members,
        out_specs=vmem,
        compiler_params=params,
        name="place_rows",
    )(place, *mixed_got)


def solution(mesh):
    placed = (
        P(("outer", "inner"), None),
        P(("outer", "inner"), None),
        P(("outer", "inner"), None),
        P(),
        P(),
    )
    return jax.shard_map(
        body, mesh=mesh, in_specs=placed, out_specs=P(("outer", "inner"), None), check_vma=False
    )
```

time: 168 us -> 66.3 us (0.39)
  waiting for transfers between devices: 76.5 us -> 28.5 us
  other arithmetic: 21.8 us -> 0.07 us
  starting transfers between devices: 9.12 us -> 26.6 us
  blocking collectives: 16.4 us -> 0 us
  between operations: 14.2 us -> 0.08 us
  loops' own time: 10.5 us -> 0 us
  local copies, waits for them, and re-layouts: 12.4 us -> 3.78 us
  Pallas kernels: 0 us -> 7.09 us
  matrix products: 6.03 us -> 0 us
    all_to_all x2 -> x0, waiting for transfers between devices: 46.6 us -> none  [the longest x1 24.6 us: body(): lax.all_to_all(local_state.reshape(1, state_rows, HEAD_DIM), 'inner', spl...]
    all_gather x1 -> x0, waiting for transfers between devices: 29.9 us -> none  [carried_in(): everything = jax.tree.map(lambda part: lax.all_gather(part, axis), shard)]
    ppermute x0 -> x22, waiting for transfers between devices: none -> 28.5 us  [the longest x21 28.5 us: exchange(): got.append(lax.ppermute(parts[d], everyone, pairs))]
    ppermute x0 -> x22, starting transfers between devices: none -> 26.6 us  [the longest x21 23.1 us: exchange(): got.append(lax.ppermute(parts[d], everyone, pairs))]
    unnamed x1 -> x0, blocking collectives: 16.4 us -> none
    select_n x8 -> x0, other arithmetic: 11.8 us -> none  [lap(): return jax.tree.map(lambda a, b: jnp.where(reached, a, b), new, before)]
    another operation x2 -> x0, loops' own time: 10.5 us -> none  [the longest x1 5.38 us: carried_in(): return lax.fori_loop(0, devices, lap, start)]
    all_to_all x2 -> x0, starting transfers between devices: 9.12 us -> none  [the longest x1 5.17 us: body(): lax.all_to_all(local_state.reshape(1, state_rows, HEAD_DIM), 'inner', spl...]
  transfers between devices with their start and end apart: 3 -> 22, of which waited for: 3 -> 11; matrix products, arithmetic and copies ran while one was open for 3% -> 0% of each run, Pallas kernels for 0% -> 3%
where the time goes in v1:
time: 66.3 us; the launch traced here: 66.1 us
  waiting for transfers between devices  28.5 us (43%)
  starting transfers between devices  26.6 us (40%)
  Pallas kernels  7.09 us (11%)
  local copies, waits for them, and re-layouts  3.78 us (6%)
    ppermute x21, waiting for transfers between devices, exchange(): got.append(lax.ppermute(parts[d], everyone, pairs))  28.5 us
    ppermute x21, starting transfers between devices, exchange(): got.append(lax.ppermute(parts[d], everyone, pairs))  23.1 us
    unnamed x10, local copies, waits for them, and re-layouts  3.78 us
    ppermute x1, starting transfers between devices, body(): moving = lax.ppermute(total, everyone, up)  3.5 us
    pallas_call x1, Pallas kernels, body(): pl.pallas_call(functools.partial(attend, members, heads, docs, rows), out...  3.28 us
    pallas_call x1, Pallas kernels, body(): pl.pallas_call(functools.partial(place_rows, members, width), out_shape=j...  1.39 us
  transfers between devices with their start and end apart: 22, of which 11 were waited for; matrix products, arithmetic and copies ran while one was open for 0% of the time, Pallas kernels for 3%

profile of v1, /device:TPU:0, one launch (start us, length us, event | category | flops | bytes accessed | tf_op | source)
XLA Modules:
  0.0 66.1 jit_solution(18040659164406822705)
XLA Ops:
  0.0 0.0 copy-start.3
  0.0 0.1 pad_add_fusion.place
  0.1 0.0 copy-start.1
  0.1 1.0 %copy-done.1 = bf16[64,4096]{1,0:T(8,128)(2,1)S(1)} copy-done((bf16[64,4096]{1,0:T(8,128)(2,1)S(1)}, bf16[64,4096]{1,0:T(8,128)(2,1)}, u32[]{:S(2)}) %copy-start.1) | copy-done | bytes 524312
  1.1 0.0 copy-start.2
  1.1 1.0 %copy-done.2 = bf16[64,4096]{1,0:T(8,128)(2,1)S(1)} copy-done((bf16[64,4096]{1,0:T(8,128)(2,1)S(1)}, bf16[64,4096]{1,0:T(8,128)(2,1)}, u32[]{:S(2)}) %copy-start.2) | copy-done | bytes 524312
  2.2 0.7 %spread_kv.1 = (f32[2,64,512]{2,1,0:T(8,128)S(1)}, f32[2,64,512]{2,1,0:T(8,128)S(1)}, f32[2,64,512]{2,1,0:T(8,128)S(1)}, f32[2,64,512]{2,1,0:T(8,128)S(1)}, f32[...) custom-call(s32[2]{0:T(128)S(1)} %pad_add_fusion.place, ...), custom_call_target="tpu_custom_call" | custom-call | tf_op jit(solution)/shard_map/spread_kv/pallas_call | solution.py:147
  2.9 0.5 collective-permute-start.10
  3.4 2.6 %collective-permute-start.11 = (f32[2,64,512]{2,1,0:T(8,128)S(1)}, f32[2,64,512]{2,1,0:T(8,128)S(1)}, u32[]{:S(2)}, u32[]{:S(2)}) collective-permute-start(f32[2,64,512]{2,1,0:T(8,128)S(1)} %get-tuple-element.46), channel_id=1, source_target_pairs={{0,5},{1,4},{2,7},{3,6},{4,1},{5,0},{6,3},{7,2},{8,13},{9,12},{10,... | collective-permute-start | bytes 786440 | tf_op jit(solution)/shard_map/ppermute | solution.py:144
  6.0 1.2 %collective-permute-start.12 = (f32[2,64,512]{2,1,0:T(8,128)S(1)}, f32[2,64,512]{2,1,0:T(8,128)S(1)}, u32[]{:S(2)}, u32[]{:S(2)}) collective-permute-start(f32[2,64,512]{2,1,0:T(8,128)S(1)} %get-tuple-element.47), channel_id=1, source_target_pairs={{0,6},{1,7},{2,4},{3,5},{4,2},{5,3},{6,0},{7,1},{8,14},{9,15},{10,... | collective-permute-start | bytes 786440 | tf_op jit(solution)/shard_map/ppermute | solution.py:144
  7.2 0.0 collective-permute-start.13
  7.2 2.0 %collective-permute-start.7 = (f32[2,64,512]{2,1,0:T(8,128)S(1)}, f32[2,64,512]{2,1,0:T(8,128)S(1)}, u32[]{:S(2)}, u32[]{:S(2)}) collective-permute-start(f32[2,64,512]{2,1,0:T(8,128)S(1)} %get-tuple-element.42), channel_id=1, source_target_pairs={{0,1},{1,0},{2,3},{3,2},{4,5},{5,4},{6,7},{7,6},{8,9},{9,8},{10,11... | collective-permute-start | bytes 786440 | tf_op jit(solution)/shard_map/ppermute | solution.py:144
  9.2 0.0 collective-permute-done.10.refs_4_
  9.2 1.5 %collective-permute-start.8 = (f32[2,64,512]{2,1,0:T(8,128)S(1)}, f32[2,64,512]{2,1,0:T(8,128)S(1)}, u32[]{:S(2)}, u32[]{:S(2)}) collective-permute-start(f32[2,64,512]{2,1,0:T(8,128)S(1)} %get-tuple-element.43), channel_id=1, source_target_pairs={{0,2},{1,3},{2,0},{3,1},{4,6},{5,7},{6,4},{7,5},{8,10},{9,11},{10,... | collective-permute-start | bytes 786440 | tf_op jit(solution)/shard_map/ppermute | solution.py:144
  10.7 1.9 %collective-permute-done.11.refs_5_ = f32[2,64,512]{2,1,0:T(8,128)S(1)} collective-permute-done((f32[2,64,512]{2,1,0:T(8,128)S(1)}, f32[2,64,512]{2,1,0:T(8,128)S(1)}, u32[]{:S(2)}, u32[]{:S(2)}) %collective-permute-start.11) | collective-permute-done | bytes 262176 | tf_op jit(solution)/shard_map/ppermute | solution.py:144
  12.6 2.3 %collective-permute-start.9 = (f32[2,64,512]{2,1,0:T(8,128)S(1)}, f32[2,64,512]{2,1,0:T(8,128)S(1)}, u32[]{:S(2)}, u32[]{:S(2)}) collective-permute-start(f32[2,64,512]{2,1,0:T(8,128)S(1)} %get-tuple-element.44), channel_id=1, source_target_pairs={{0,3},{1,2},{2,1},{3,0},{4,7},{5,6},{6,5},{7,4},{8,11},{9,10},{10,... | collective-permute-start | bytes 786440 | tf_op jit(solution)/shard_map/ppermute | solution.py:144
  14.9 0.0 copy-start
  14.9 1.0 %copy-done = bf16[64,4096]{1,0:T(8,128)(2,1)S(1)} copy-done((bf16[64,4096]{1,0:T(8,128)(2,1)S(1)}, bf16[64,4096]{1,0:T(8,128)(2,1)}, u32[]{:S(2)}) %copy-start) | copy-done | bytes 524312
  16.0 0.6 spread_q.1
  16.6 3.1 %collective-permute-done.12.refs_6_ = f32[2,64,512]{2,1,0:T(8,128)S(1)} collective-permute-done((f32[2,64,512]{2,1,0:T(8,128)S(1)}, f32[2,64,512]{2,1,0:T(8,128)S(1)}, u32[]{:S(2)}, u32[]{:S(2)}) %collective-permute-start.12) | collective-permute-done | bytes 262176 | tf_op jit(solution)/shard_map/ppermute | solution.py:144
  19.7 0.1 collective-permute-start
  19.8 0.0 collective-permute-done.13.refs_7_
  19.8 2.0 %collective-permute-start.1 = (f32[64,512]{1,0:T(8,128)S(1)}, f32[64,512]{1,0:T(8,128)S(1)}, u32[]{:S(2)}, u32[]{:S(2)}) collective-permute-start(f32[64,512]{1,0:T(8,128)S(1)} %get-tuple-element.35), channel_id=1, source_target_pairs={{0,2},{1,3},{2,0},{3,1},{4,6},{5,7},{6,4},{7,5},{8,10},{9,11},{10,... | collective-permute-start | bytes 393224 | tf_op jit(solution)/shard_map/ppermute | solution.py:144
  21.8 2.6 %collective-permute-done.7.refs_1_ = f32[2,64,512]{2,1,0:T(8,128)S(1)} collective-permute-done((f32[2,64,512]{2,1,0:T(8,128)S(1)}, f32[2,64,512]{2,1,0:T(8,128)S(1)}, u32[]{:S(2)}, u32[]{:S(2)}) %collective-permute-start.7) | collective-permute-done | bytes 262176 | tf_op jit(solution)/shard_map/ppermute | solution.py:144
  24.4 3.0 %collective-permute-start.2 = (f32[64,512]{1,0:T(8,128)S(1)}, f32[64,512]{1,0:T(8,128)S(1)}, u32[]{:S(2)}, u32[]{:S(2)}) collective-permute-start(f32[64,512]{1,0:T(8,128)S(1)} %get-tuple-element.36), channel_id=1, source_target_pairs={{0,3},{1,2},{2,1},{3,0},{4,7},{5,6},{6,5},{7,4},{8,11},{9,10},{10,... | collective-permute-start | bytes 393224 | tf_op jit(solution)/shard_map/ppermute | solution.py:144
  27.3 4.3 %collective-permute-done.8.refs_2_ = f32[2,64,512]{2,1,0:T(8,128)S(1)} collective-permute-done((f32[2,64,512]{2,1,0:T(8,128)S(1)}, f32[2,64,512]{2,1,0:T(8,128)S(1)}, u32[]{:S(2)}, u32[]{:S(2)}) %collective-permute-start.8) | collective-permute-done | bytes 262176 | tf_op jit(solution)/shard_map/ppermute | solution.py:144
  31.7 0.0 collective-permute-done.9.refs_3_
  31.7 0.0 copy-start.4
  31.7 0.7 copy-done.4
  32.3 1.1 %gather_states.1 = (bf16[8,64,512]{2,1,0:T(8,128)(2,1)S(1)}, bf16[8,64,512]{2,1,0:T(8,128)(2,1)S(1)}, f32[8,4,128,128]{3,2,1,0:T(8,128)S(1)}, f32[4,128,128]{2,1,0:T(8,128)S(1)}) custom-call(s32[2]{0:T(128)S(1)} %pad_add_fusion.place, s32[16]{0:T(128)S(1)} %copy-done.4, f32[2,64,512]{2,1,0:T(8,128)S(1)} %get-tuple-element.41.refs_0_, ...), custom_call_target="tpu_custom_call" | custom-call | tf_op jit(solution)/shard_map/gather_states/pallas_call | solution.py:165
  33.5 3.5 %collective-permute-start.14 = (f32[4,128,128]{2,1,0:T(8,128)S(1)}, f32[4,128,128]{2,1,0:T(8,128)S(1)}, u32[]{:S(2)}, u32[]{:S(2)}) collective-permute-start(f32[4,128,128]{2,1,0:T(8,128)S(1)} %get-tuple-element.52), channel_id=1, source_target_pairs={{0,8},{1,9},{2,10},{3,11},{4,12},{5,13},{6,14},{7,15},{8,16},{9,17... | collective-permute-start | bytes 786440 | tf_op jit(solution)/shard_map/ppermute | solution.py:180
  37.0 0.1 collective-permute-start.3
  37.1 0.0 collective-permute-done.refs_1_
  37.1 1.4 %collective-permute-start.4 = (f32[64,512]{1,0:T(8,128)S(1)}, f32[64,512]{1,0:T(8,128)S(1)}, u32[]{:S(2)}, u32[]{:S(2)}) collective-permute-start(f32[64,512]{1,0:T(8,128)S(1)} %get-tuple-element.38), channel_id=1, source_target_pairs={{0,5},{1,4},{2,7},{3,6},{4,1},{5,0},{6,3},{7,2},{8,13},{9,12},{10,... | collective-permute-start | bytes 393224 | tf_op jit(solution)/shard_map/ppermute | solution.py:144
  38.5 0.0 collective-permute-done.1.refs_2_
  38.5 0.4 collective-permute-start.5
  38.9 0.0 collective-permute-done.2.refs_3_
  38.9 1.5 %collective-permute-start.6 = (f32[64,512]{1,0:T(8,128)S(1)}, f32[64,512]{1,0:T(8,128)S(1)}, u32[]{:S(2)}, u32[]{:S(2)}) collective-permute-start(f32[64,512]{1,0:T(8,128)S(1)} %get-tuple-element.40), channel_id=1, source_target_pairs={{0,7},{1,6},{2,5},{3,4},{4,3},{5,2},{6,1},{7,0},{8,15},{9,14},{10,... | collective-permute-start | bytes 393224 | tf_op jit(solution)/shard_map/ppermute | solution.py:144
  40.4 0.0 collective-permute-done.3.refs_4_
  40.4 2.0 %collective-permute-done.4.refs_5_ = f32[64,512]{1,0:T(8,128)S(1)} collective-permute-done((f32[64,512]{1,0:T(8,128)S(1)}, f32[64,512]{1,0:T(8,128)S(1)}, u32[]{:S(2)}, u32[]{:S(2)}) %collective-permute-start.4) | collective-permute-done | bytes 131104 | tf_op jit(solution)/shard_map/ppermute | solution.py:144
  42.4 4.5 %collective-permute-done.5.refs_6_ = f32[64,512]{1,0:T(8,128)S(1)} collective-permute-done((f32[64,512]{1,0:T(8,128)S(1)}, f32[64,512]{1,0:T(8,128)S(1)}, u32[]{:S(2)}, u32[]{:S(2)}) %collective-permute-start.5) | collective-permute-done | bytes 131104 | tf_op jit(solution)/shard_map/ppermute | solution.py:144
  46.9 0.0 collective-permute-done.6.refs_7_
  46.9 0.0 collective-permute-done.14.refs_11_
  46.9 0.0 copy-done.3
  46.9 3.3 %attend.1 = (f32[64,512]{1,0:T(8,128)S(1)}, f32[64,512]{1,0:T(8,128)S(1)}, f32[64,512]{1,0:T(8,128)S(1)}, f32[64,512]{1,0:T(8,128)S(1)}, f32[64,512]{1,0:T(8,128...) custom-call(s32[2]{0:T(128)S(1)} %pad_add_fusion.place, s32[16]{0:T(128)S(1)} %copy-done.4, ...), custom_call_target="tpu_custom_call" | custom-call | tf_op jit(solution)/shard_map/attend/pallas_call | solution.py:188
  50.1 0.8 %collective-permute-start.15 = (f32[64,512]{1,0:T(8,128)S(1)}, f32[64,512]{1,0:T(8,128)S(1)}, u32[]{:S(2)}, u32[]{:S(2)}) collective-permute-start(f32[64,512]{1,0:T(8,128)S(1)} %get-tuple-element.54), channel_id=1, source_target_pairs={{0,1},{1,0},{2,3},{3,2},{4,5},{5,4},{6,7},{7,6},{8,9},{9,8},{10,11... | collective-permute-start | bytes 393224 | tf_op jit(solution)/shard_map/ppermute | solution.py:144
  50.9 1.5 %collective-permute-start.16 = (f32[64,512]{1,0:T(8,128)S(1)}, f32[64,512]{1,0:T(8,128)S(1)}, u32[]{:S(2)}, u32[]{:S(2)}) collective-permute-start(f32[64,512]{1,0:T(8,128)S(1)} %get-tuple-element.55), channel_id=1, source_target_pairs={{0,2},{1,3},{2,0},{3,1},{4,6},{5,7},{6,4},{7,5},{8,10},{9,11},{10,... | collective-permute-start | bytes 393224 | tf_op jit(solution)/shard_map/ppermute | solution.py:144
  52.4 1.3 %collective-permute-start.17 = (f32[64,512]{1,0:T(8,128)S(1)}, f32[64,512]{1,0:T(8,128)S(1)}, u32[]{:S(2)}, u32[]{:S(2)}) collective-permute-start(f32[64,512]{1,0:T(8,128)S(1)} %get-tuple-element.56), channel_id=1, source_target_pairs={{0,3},{1,2},{2,1},{3,0},{4,7},{5,6},{6,5},{7,4},{8,11},{9,10},{10,... | collective-permute-start | bytes 393224 | tf_op jit(solution)/shard_map/ppermute | solution.py:144
  53.7 0.0 collective-permute-start.18
  53.7 0.8 %collective-permute-start.19 = (f32[64,512]{1,0:T(8,128)S(1)}, f32[64,512]{1,0:T(8,128)S(1)}, u32[]{:S(2)}, u32[]{:S(2)}) collective-permute-start(f32[64,512]{1,0:T(8,128)S(1)} %get-tuple-element.58), channel_id=1, source_target_pairs={{0,5},{1,4},{2,7},{3,6},{4,1},{5,0},{6,3},{7,2},{8,13},{9,12},{10,... | collective-permute-start | bytes 393224 | tf_op jit(solution)/shard_map/ppermute | solution.py:144
  54.5 2.0 %collective-permute-done.15.refs_1_ = f32[64,512]{1,0:T(8,128)S(1)} collective-permute-done((f32[64,512]{1,0:T(8,128)S(1)}, f32[64,512]{1,0:T(8,128)S(1)}, u32[]{:S(2)}, u32[]{:S(2)}) %collective-permute-start.15) | collective-permute-done | bytes 131104 | tf_op jit(solution)/shard_map/ppermute | solution.py:144
  56.6 0.0 collective-permute-start.20
  56.6 1.6 %collective-permute-done.16.refs_2_ = f32[64,512]{1,0:T(8,128)S(1)} collective-permute-done((f32[64,512]{1,0:T(8,128)S(1)}, f32[64,512]{1,0:T(8,128)S(1)}, u32[]{:S(2)}, u32[]{:S(2)}) %collective-permute-start.16) | collective-permute-done | bytes 131104 | tf_op jit(solution)/shard_map/ppermute | solution.py:144
  58.1 0.1 collective-permute-start.21
  58.2 1.6 %collective-permute-done.17.refs_3_ = f32[64,512]{1,0:T(8,128)S(1)} collective-permute-done((f32[64,512]{1,0:T(8,128)S(1)}, f32[64,512]{1,0:T(8,128)S(1)}, u32[]{:S(2)}, u32[]{:S(2)}) %collective-permute-start.17) | collective-permute-done | bytes 131104 | tf_op jit(solution)/shard_map/ppermute | solution.py:144
  59.8 0.0 collective-permute-done.18.refs_4_
  59.8 0.7 %collective-permute-done.19.refs_5_ = f32[64,512]{1,0:T(8,128)S(1)} collective-permute-done((f32[64,512]{1,0:T(8,128)S(1)}, f32[64,512]{1,0:T(8,128)S(1)}, u32[]{:S(2)}, u32[]{:S(2)}) %collective-permute-start.19) | collective-permute-done | bytes 131104 | tf_op jit(solution)/shard_map/ppermute | solution.py:144
  60.5 4.2 %collective-permute-done.20.refs_6_ = f32[64,512]{1,0:T(8,128)S(1)} collective-permute-done((f32[64,512]{1,0:T(8,128)S(1)}, f32[64,512]{1,0:T(8,128)S(1)}, u32[]{:S(2)}, u32[]{:S(2)}) %collective-permute-start.20) | collective-permute-done | bytes 131104 | tf_op jit(solution)/shard_map/ppermute | solution.py:144
  64.7 0.0 collective-permute-done.21.refs_7_
  64.7 1.4 %place_rows.1 = bf16[64,4096]{1,0:T(8,128)(2,1)} custom-call(s32[2]{0:T(128)S(1)} %pad_add_fusion.place, f32[64,512]{1,0:T(8,128)S(1)} %get-tuple-element.53.refs_0_, f32[64,512]{1,0:T(8,128)S(1)} %collective-permute-done.15.refs_1_, f32[64,512]{1,0:T(8,128)S(1)} %collective-permute-done.16.refs_2_, f32[64,512]{1,0:T(8,128)S(1)} %collective-permute-done.17.refs_3_, ...), custom_call_target="tpu_custom_call" | custom-call | tf_op jit(solution)/shard_map/place_rows/pallas_call | solution.py:198
Async XLA Ops:
  0.0 46.9 %copy-start.3 = (f32[4096]{0:T(1024)S(1)}, f32[4096]{0:T(1024)}, u32[]{:S(2)}) copy-start(f32[4096]{0:T(1024)} %param.9) | copy-start | bytes 49156
  0.1 1.0 %copy-start.1 = (bf16[64,4096]{1,0:T(8,128)(2,1)S(1)}, bf16[64,4096]{1,0:T(8,128)(2,1)}, u32[]{:S(2)}) copy-start(bf16[64,4096]{1,0:T(8,128)(2,1)} %refs_0_.3) | copy-start | bytes 1572868
  1.1 1.0 %copy-start.2 = (bf16[64,4096]{1,0:T(8,128)(2,1)S(1)}, bf16[64,4096]{1,0:T(8,128)(2,1)}, u32[]{:S(2)}) copy-start(bf16[64,4096]{1,0:T(8,128)(2,1)} %refs_1_.1) | copy-start | bytes 1572868
  2.9 6.3 %collective-permute-start.10 = (f32[2,64,512]{2,1,0:T(8,128)S(1)}, f32[2,64,512]{2,1,0:T(8,128)S(1)}, u32[]{:S(2)}, u32[]{:S(2)}) collective-permute-start(f32[2,64,512]{2,1,0:T(8,128)S(1)} %get-tuple-element.45), channel_id=1, source_target_pairs={{0,4},{1,5},{2,6},{3,7},{4,0},{5,1},{6,2},{7,3},{8,12},{9,13},{10,... | collective-permute-start | bytes 786440 | tf_op jit(solution)/shard_map/ppermute | solution.py:144
  3.4 9.3 %collective-permute-start.11 = (f32[2,64,512]{2,1,0:T(8,128)S(1)}, f32[2,64,512]{2,1,0:T(8,128)S(1)}, u32[]{:S(2)}, u32[]{:S(2)}) collective-permute-start(f32[2,64,512]{2,1,0:T(8,128)S(1)} %get-tuple-element.46), channel_id=1, source_target_pairs={{0,5},{1,4},{2,7},{3,6},{4,1},{5,0},{6,3},{7,2},{8,13},{9,12},{10,... | collective-permute-start | bytes 786440 | tf_op jit(solution)/shard_map/ppermute | solution.py:144
  6.0 13.7 %collective-permute-start.12 = (f32[2,64,512]{2,1,0:T(8,128)S(1)}, f32[2,64,512]{2,1,0:T(8,128)S(1)}, u32[]{:S(2)}, u32[]{:S(2)}) collective-permute-start(f32[2,64,512]{2,1,0:T(8,128)S(1)} %get-tuple-element.47), channel_id=1, source_target_pairs={{0,6},{1,7},{2,4},{3,5},{4,2},{5,3},{6,0},{7,1},{8,14},{9,15},{10,... | collective-permute-start | bytes 786440 | tf_op jit(solution)/shard_map/ppermute | solution.py:144
  7.2 12.6 %collective-permute-start.13 = (f32[2,64,512]{2,1,0:T(8,128)S(1)}, f32[2,64,512]{2,1,0:T(8,128)S(1)}, u32[]{:S(2)}, u32[]{:S(2)}) collective-permute-start(f32[2,64,512]{2,1,0:T(8,128)S(1)} %get-tuple-element.48), channel_id=1, source_target_pairs={{0,7},{1,6},{2,5},{3,4},{4,3},{5,2},{6,1},{7,0},{8,15},{9,14},{10,... | collective-permute-start | bytes 786440 | tf_op jit(solution)/shard_map/ppermute | solution.py:144
  7.2 17.2 %collective-permute-start.7 = (f32[2,64,512]{2,1,0:T(8,128)S(1)}, f32[2,64,512]{2,1,0:T(8,128)S(1)}, u32[]{:S(2)}, u32[]{:S(2)}) collective-permute-start(f32[2,64,512]{2,1,0:T(8,128)S(1)} %get-tuple-element.42), channel_id=1, source_target_pairs={{0,1},{1,0},{2,3},{3,2},{4,5},{5,4},{6,7},{7,6},{8,9},{9,8},{10,11... | collective-permute-start | bytes 786440 | tf_op jit(solution)/shard_map/ppermute | solution.py:144
  9.2 22.5 %collective-permute-start.8 = (f32[2,64,512]{2,1,0:T(8,128)S(1)}, f32[2,64,512]{2,1,0:T(8,128)S(1)}, u32[]{:S(2)}, u32[]{:S(2)}) collective-permute-start(f32[2,64,512]{2,1,0:T(8,128)S(1)} %get-tuple-element.43), channel_id=1, source_target_pairs={{0,2},{1,3},{2,0},{3,1},{4,6},{5,7},{6,4},{7,5},{8,10},{9,11},{10,... | collective-permute-start | bytes 786440 | tf_op jit(solution)/shard_map/ppermute | solution.py:144
  12.6 19.1 %collective-permute-start.9 = (f32[2,64,512]{2,1,0:T(8,128)S(1)}, f32[2,64,512]{2,1,0:T(8,128)S(1)}, u32[]{:S(2)}, u32[]{:S(2)}) collective-permute-start(f32[2,64,512]{2,1,0:T(8,128)S(1)} %get-tuple-element.44), channel_id=1, source_target_pairs={{0,3},{1,2},{2,1},{3,0},{4,7},{5,6},{6,5},{7,4},{8,11},{9,10},{10,... | collective-permute-start | bytes 786440 | tf_op jit(solution)/shard_map/ppermute | solution.py:144
  14.9 1.0 %copy-start = (bf16[64,4096]{1,0:T(8,128)(2,1)S(1)}, bf16[64,4096]{1,0:T(8,128)(2,1)}, u32[]{:S(2)}) copy-start(bf16[64,4096]{1,0:T(8,128)(2,1)} %refs_0_.2) | copy-start | bytes 1572868
  19.7 17.4 %collective-permute-start = (f32[64,512]{1,0:T(8,128)S(1)}, f32[64,512]{1,0:T(8,128)S(1)}, u32[]{:S(2)}, u32[]{:S(2)}) collective-permute-start(f32[64,512]{1,0:T(8,128)S(1)} %get-tuple-element.34), channel_id=1, source_target_pairs={{0,1},{1,0},{2,3},{3,2},{4,5},{5,4},{6,7},{7,6},{8,9},{9,8},{10,11... | collective-permute-start | bytes 393224 | tf_op jit(solution)/shard_map/ppermute | solution.py:144
  19.8 18.7 %collective-permute-start.1 = (f32[64,512]{1,0:T(8,128)S(1)}, f32[64,512]{1,0:T(8,128)S(1)}, u32[]{:S(2)}, u32[]{:S(2)}) collective-permute-start(f32[64,512]{1,0:T(8,128)S(1)} %get-tuple-element.35), channel_id=1, source_target_pairs={{0,2},{1,3},{2,0},{3,1},{4,6},{5,7},{6,4},{7,5},{8,10},{9,11},{10,... | collective-permute-start | bytes 393224 | tf_op jit(solution)/shard_map/ppermute | solution.py:144
  24.4 14.6 %collective-permute-start.2 = (f32[64,512]{1,0:T(8,128)S(1)}, f32[64,512]{1,0:T(8,128)S(1)}, u32[]{:S(2)}, u32[]{:S(2)}) collective-permute-start(f32[64,512]{1,0:T(8,128)S(1)} %get-tuple-element.36), channel_id=1, source_target_pairs={{0,3},{1,2},{2,1},{3,0},{4,7},{5,6},{6,5},{7,4},{8,11},{9,10},{10,... | collective-permute-start | bytes 393224 | tf_op jit(solution)/shard_map/ppermute | solution.py:144
  31.7 0.7 copy-start.4
  33.5 13.4 %collective-permute-start.14 = (f32[4,128,128]{2,1,0:T(8,128)S(1)}, f32[4,128,128]{2,1,0:T(8,128)S(1)}, u32[]{:S(2)}, u32[]{:S(2)}) collective-permute-start(f32[4,128,128]{2,1,0:T(8,128)S(1)} %get-tuple-element.52), channel_id=1, source_target_pairs={{0,8},{1,9},{2,10},{3,11},{4,12},{5,13},{6,14},{7,15},{8,16},{9,17... | collective-permute-start | bytes 786440 | tf_op jit(solution)/shard_map/ppermute | solution.py:180
  37.0 3.4 %collective-permute-start.3 = (f32[64,512]{1,0:T(8,128)S(1)}, f32[64,512]{1,0:T(8,128)S(1)}, u32[]{:S(2)}, u32[]{:S(2)}) collective-permute-start(f32[64,512]{1,0:T(8,128)S(1)} %get-tuple-element.37), channel_id=1, source_target_pairs={{0,4},{1,5},{2,6},{3,7},{4,0},{5,1},{6,2},{7,3},{8,12},{9,13},{10,... | collective-permute-start | bytes 393224 | tf_op jit(solution)/shard_map/ppermute | solution.py:144
  37.1 5.3 %collective-permute-start.4 = (f32[64,512]{1,0:T(8,128)S(1)}, f32[64,512]{1,0:T(8,128)S(1)}, u32[]{:S(2)}, u32[]{:S(2)}) collective-permute-start(f32[64,512]{1,0:T(8,128)S(1)} %get-tuple-element.38), channel_id=1, source_target_pairs={{0,5},{1,4},{2,7},{3,6},{4,1},{5,0},{6,3},{7,2},{8,13},{9,12},{10,... | collective-permute-start | bytes 393224 | tf_op jit(solution)/shard_map/ppermute | solution.py:144
  38.5 8.4 %collective-permute-start.5 = (f32[64,512]{1,0:T(8,128)S(1)}, f32[64,512]{1,0:T(8,128)S(1)}, u32[]{:S(2)}, u32[]{:S(2)}) collective-permute-start(f32[64,512]{1,0:T(8,128)S(1)} %get-tuple-element.39), channel_id=1, source_target_pairs={{0,6},{1,7},{2,4},{3,5},{4,2},{5,3},{6,0},{7,1},{8,14},{9,15},{10,... | collective-permute-start | bytes 393224 | tf_op jit(solution)/shard_map/ppermute | solution.py:144
  38.9 7.9 %collective-permute-start.6 = (f32[64,512]{1,0:T(8,128)S(1)}, f32[64,512]{1,0:T(8,128)S(1)}, u32[]{:S(2)}, u32[]{:S(2)}) collective-permute-start(f32[64,512]{1,0:T(8,128)S(1)} %get-tuple-element.40), channel_id=1, source_target_pairs={{0,7},{1,6},{2,5},{3,4},{4,3},{5,2},{6,1},{7,0},{8,15},{9,14},{10,... | collective-permute-start | bytes 393224 | tf_op jit(solution)/shard_map/ppermute | solution.py:144
  50.1 6.4 %collective-permute-start.15 = (f32[64,512]{1,0:T(8,128)S(1)}, f32[64,512]{1,0:T(8,128)S(1)}, u32[]{:S(2)}, u32[]{:S(2)}) collective-permute-start(f32[64,512]{1,0:T(8,128)S(1)} %get-tuple-element.54), channel_id=1, source_target_pairs={{0,1},{1,0},{2,3},{3,2},{4,5},{5,4},{6,7},{7,6},{8,9},{9,8},{10,11... | collective-permute-start | bytes 393224 | tf_op jit(solution)/shard_map/ppermute | solution.py:144
  50.9 7.2 %collective-permute-start.16 = (f32[64,512]{1,0:T(8,128)S(1)}, f32[64,512]{1,0:T(8,128)S(1)}, u32[]{:S(2)}, u32[]{:S(2)}) collective-permute-start(f32[64,512]{1,0:T(8,128)S(1)} %get-tuple-element.55), channel_id=1, source_target_pairs={{0,2},{1,3},{2,0},{3,1},{4,6},{5,7},{6,4},{7,5},{8,10},{9,11},{10,... | collective-permute-start | bytes 393224 | tf_op jit(solution)/shard_map/ppermute | solution.py:144
  52.4 7.4 %collective-permute-start.17 = (f32[64,512]{1,0:T(8,128)S(1)}, f32[64,512]{1,0:T(8,128)S(1)}, u32[]{:S(2)}, u32[]{:S(2)}) collective-permute-start(f32[64,512]{1,0:T(8,128)S(1)} %get-tuple-element.56), channel_id=1, source_target_pairs={{0,3},{1,2},{2,1},{3,0},{4,7},{5,6},{6,5},{7,4},{8,11},{9,10},{10,... | collective-permute-start | bytes 393224 | tf_op jit(solution)/shard_map/ppermute | solution.py:144
  53.7 6.1 %collective-permute-start.18 = (f32[64,512]{1,0:T(8,128)S(1)}, f32[64,512]{1,0:T(8,128)S(1)}, u32[]{:S(2)}, u32[]{:S(2)}) collective-permute-start(f32[64,512]{1,0:T(8,128)S(1)} %get-tuple-element.57), channel_id=1, source_target_pairs={{0,4},{1,5},{2,6},{3,7},{4,0},{5,1},{6,2},{7,3},{8,12},{9,13},{10,... | collective-permute-start | bytes 393224 | tf_op jit(solution)/shard_map/ppermute | solution.py:144
  53.7 6.8 %collective-permute-start.19 = (f32[64,512]{1,0:T(8,128)S(1)}, f32[64,512]{1,0:T(8,128)S(1)}, u32[]{:S(2)}, u32[]{:S(2)}) collective-permute-start(f32[64,512]{1,0:T(8,128)S(1)} %get-tuple-element.58), channel_id=1, source_target_pairs={{0,5},{1,4},{2,7},{3,6},{4,1},{5,0},{6,3},{7,2},{8,13},{9,12},{10,... | collective-permute-start | bytes 393224 | tf_op jit(solution)/shard_map/ppermute | solution.py:144
  56.6 8.1 %collective-permute-start.20 = (f32[64,512]{1,0:T(8,128)S(1)}, f32[64,512]{1,0:T(8,128)S(1)}, u32[]{:S(2)}, u32[]{:S(2)}) collective-permute-start(f32[64,512]{1,0:T(8,128)S(1)} %get-tuple-element.59), channel_id=1, source_target_pairs={{0,6},{1,7},{2,4},{3,5},{4,2},{5,3},{6,0},{7,1},{8,14},{9,15},{10,... | collective-permute-start | bytes 393224 | tf_op jit(solution)/shard_map/ppermute | solution.py:144
  58.1 6.6 %collective-permute-start.21 = (f32[64,512]{1,0:T(8,128)S(1)}, f32[64,512]{1,0:T(8,128)S(1)}, u32[]{:S(2)}, u32[]{:S(2)}) collective-permute-start(f32[64,512]{1,0:T(8,128)S(1)} %get-tuple-element.60), channel_id=1, source_target_pairs={{0,7},{1,6},{2,5},{3,4},{4,3},{5,2},{6,1},{7,0},{8,15},{9,14},{10,... | collective-permute-start | bytes 393224 | tf_op jit(solution)/shard_map/ppermute | solution.py:144

commit v2 on v0

v2 whole, which is shorter than its diff:
```python
import functools

import jax
import jax.numpy as jnp
from jax import lax
from jax.experimental import pallas as pl
from jax.experimental.pallas import tpu as pltpu
from jax.sharding import PartitionSpec as P

HEAD_DIM = 128
BLOCK = 16
CORES = 2
SHARE = 4
EPSILON = 1e-05
SMEM = pl.BlockSpec(memory_space=pltpu.SMEM)
VMEM = pl.BlockSpec(memory_space=pltpu.VMEM)
ANY = pl.BlockSpec(memory_space=pl.ANY)


def columns_of(member, width):
    return pl.ds(pl.multiple_of(member * width, width), width)


def heads_of(heads):
    return [slice(h * HEAD_DIM, (h + 1) * HEAD_DIM) for h in range(heads)]


def start_of(lengths, docs, token):
    begin = jnp.int32(0)
    found = jnp.int32(0)
    after = jnp.int32(jnp.iinfo(jnp.int32).max)
    for i in range(docs):
        found = jnp.where(begin <= token, begin, found)
        after = jnp.where(begin > token, jnp.minimum(begin, after), after)
        begin = begin + lengths[i] * BLOCK
    return found, after


def spread_pairs(members, width, place, keys, values, *refs):
    outs = refs[:members]
    key_buffer, value_buffer, sems = refs[members:]
    me = place[0]

    def copies(d):
        span = columns_of(me ^ d, width)
        return [
            pltpu.make_async_copy(keys.at[:, span], key_buffer.at[d], sems.at[0, d]),
            pltpu.make_async_copy(values.at[:, span], value_buffer.at[d], sems.at[1, d]),
        ]

    order = list(reversed(range(members)))
    for d in order:
        for copy in copies(d):
            copy.start()
    for d in order:
        for copy in copies(d):
            copy.wait()
        outs[d][0] = key_buffer[d].astype(jnp.float32)
        outs[d][1] = value_buffer[d].astype(jnp.float32)


def pick_other(members, width, place, queries, out):
    half = members // CORES
    side = 1 - place[0] // half
    out[...] = queries[:, columns_of(side, half * width)].astype(jnp.float32)


def spread_queries(members, width, gates, place, queries, swapped, *refs):
    half = members // CORES
    outs = refs[gates:]
    me = place[0]
    for e in range(half):
        outs[e][0] = queries[:, columns_of(me ^ e, width)].astype(jnp.float32)
        outs[e][1] = swapped[:, columns_of((me ^ e) % half, width)]


def gather_states(members, heads, docs, rows, place, lengths, *refs):
    parts = refs[:members]
    carry_out, total_out, key_blocks, value_blocks = refs[members + 1 :]
    me, base = place[0], place[1]
    row = lax.broadcasted_iota(jnp.int32, (rows, heads * HEAD_DIM), 0)
    for d in range(members):
        j = me ^ d
        since, _ = start_of(lengths, docs, base + (j + 1) * rows)
        key_blocks[j] = jnp.where(row >= since - base - j * rows, parts[d][0], 0.0).astype(jnp.bfloat16)
        value_blocks[j] = parts[d][1].astype(jnp.bfloat16)
    state = [jnp.zeros((HEAD_DIM, HEAD_DIM), jnp.float32) for _ in range(heads)]
    for j in range(members):
        since, _ = start_of(lengths, docs, base + (j + 1) * rows)
        keep = jnp.where(since <= base + j * rows, 1.0, 0.0).astype(jnp.float32)
        for h, span in enumerate(heads_of(heads)):
            carry_out[j, h] = state[h]
            own = lax.dot_general(
                key_blocks[j, :, span],
                value_blocks[j, :, span],
                (((0,), (0,)), ((), ())),
                preferred_element_type=jnp.float32,
            )
            state[h] = keep * state[h] + own
    for h in range(heads):
        total_out[h] = state[h]


def inside(head_count, docs, rows, place, lengths, queries, keys, values, out):
    begin = place[2]
    row = lax.broadcasted_iota(jnp.int32, (rows, rows), 0)
    lane = lax.broadcasted_iota(jnp.int32, (rows, rows), 1)
    since = jnp.zeros((rows, rows), jnp.int32)
    start = -begin
    for i in range(docs):
        since = jnp.where(start <= row, start, since)
        start = start + lengths[i] * BLOCK
    allowed = (lane <= row) & (lane >= since)
    for span in heads_of(head_count):
        scores = lax.dot_general(
            queries[:, span], keys[:, span], (((1,), (1,)), ((), ())), preferred_element_type=jnp.float32
        )
        weights = jnp.where(allowed, scores, 0.0).astype(jnp.bfloat16)
        out[:, span] = jnp.dot(weights, values[:, span], preferred_element_type=jnp.float32)


def reach_back(members, heads, docs, rows, place, lengths, *refs):
    half = members // CORES
    query_parts = refs[:half]
    carry, earlier = refs[half : half + 2]
    outs = refs[half + 2 :]
    me, base = place[0], place[1]
    for e in range(half):
        for side in range(CORES):
            d = e ^ (side * half)
            j = me ^ d
            first, _ = start_of(lengths, docs, base + j * rows)
            before = jnp.where(first < base, 1.0, 0.0).astype(jnp.float32)
            for h, span in enumerate(heads_of(heads)):
                held = (carry[j, h] + before * earlier[h]).astype(jnp.bfloat16)
                query = query_parts[e][side, :, span].astype(jnp.bfloat16)
                outs[d][:, span] = jnp.dot(query, held, preferred_element_type=jnp.float32)


def finish(chosen, heads, docs, rows, place, lengths, own, gain, *refs):
    count = len(chosen)
    parts, out = refs[:count], refs[-3]
    buffer, sems = refs[-2:]
    width = heads * HEAD_DIM
    me, begin = place[0], place[2]
    row = lax.broadcasted_iota(jnp.int32, (rows, HEAD_DIM), 0)
    _, after = start_of(lengths, docs, begin)
    continued = row < after - begin
    copies = []
    for i, d in enumerate(chosen):
        columns = columns_of(me ^ d, width)
        inner = own[:, columns]
        scales = gain[:, columns]
        for span in heads_of(heads):
            mixed = inner[:, span] + jnp.where(continued, parts[i][:, span], 0.0)
            scale = lax.rsqrt(jnp.mean(mixed * mixed, axis=-1, keepdims=True) + EPSILON)
            buffer[i, :, span] = (mixed * scale * scales[:, span]).astype(jnp.bfloat16)
        copy = pltpu.make_async_copy(buffer.at[i], out.at[:, columns], sems.at[i])
        copy.start()
        copies.append(copy)
    for copy in copies:
        copy.wait()


def body(queries, keys, values, lengths, norm_gain):
    rows, columns = queries.shape
    head_count = columns // HEAD_DIM
    docs = lengths.shape[0]
    inner_count = lax.axis_size("inner")
    devices = lax.axis_size("outer") * inner_count
    members = CORES * inner_count
    half = inner_count
    planes = devices // members
    heads = head_count // members
    width = heads * HEAD_DIM
    reach = -(-(devices // SHARE) // members)
    everyone = ("outer", "inner")
    index = lax.axis_index("outer") * inner_count + lax.axis_index("inner")
    me = index % members
    base = (index - me) * rows
    place = jnp.stack([me, base, index * rows]).astype(jnp.int32)
    f32, bf16 = jnp.float32, jnp.bfloat16
    params = pltpu.CompilerParams(vmem_limit_bytes=48 * 1024 * 1024)

    def call(kernel, name, out_shape, in_specs, out_specs, scratch=(), flops=0, moved=0, aliases=None):
        return pl.pallas_call(
            kernel,
            out_shape=out_shape,
            in_specs=in_specs,
            out_specs=out_specs,
            scratch_shapes=scratch,
            compiler_params=params,
            cost_estimate=pl.CostEstimate(flops=flops, bytes_accessed=moved, transcendentals=0),
            input_output_aliases=aliases or {},
            name=name,
        )

    def shape(*sizes, dtype=f32):
        return jax.ShapeDtypeStruct(sizes, dtype)

    def swap(part, d):
        pairs = [(g, g - g % members + (g % members ^ d)) for g in range(devices)]
        return lax.ppermute(part, everyone, pairs)

    block_bytes = rows * columns * 4
    pair_parts = call(
        functools.partial(spread_pairs, members, width),
        "spread_pairs",
        [shape(2, rows, width)] * members,
        [SMEM, ANY, ANY],
        [VMEM] * members,
        [
            pltpu.VMEM((members, rows, width), bf16),
            pltpu.VMEM((members, rows, width), bf16),
            pltpu.SemaphoreType.DMA((2, members)),
        ],
        moved=3 * block_bytes,
    )(place, keys, values)
    pair_got = [pair_parts[0]] + [swap(pair_parts[d], d) for d in range(1, members)]

    other = call(
        functools.partial(pick_other, members, width),
        "pick_other",
        shape(rows, half * width),
        [SMEM, VMEM],
        VMEM,
        moved=block_bytes,
    )(place, queries)
    swapped = swap(other, half)
    gates = pair_got[half:]
    query_parts = call(
        functools.partial(spread_queries, members, width, len(gates)),
        "spread_queries",
        [shape(CORES, rows, width)] * half,
        [SMEM, VMEM, VMEM] + [ANY] * len(gates),
        [VMEM] * half,
        moved=2 * block_bytes,
    )(place, queries, swapped, *gates)
    query_got = [query_parts[0]] + [swap(query_parts[e], e) for e in range(1, half)]

    own = call(
        functools.partial(inside, head_count, docs, rows),
        "inside",
        shape(rows, columns),
        [SMEM, SMEM, VMEM, VMEM, VMEM],
        VMEM,
        flops=4 * rows * rows * columns,
        moved=3 * block_bytes,
    )(place, lengths, queries, keys, values)

    carry, total = call(
        functools.partial(gather_states, members, heads, docs, rows),
        "gather_states",
        [shape(members, heads, HEAD_DIM, HEAD_DIM), shape(heads, HEAD_DIM, HEAD_DIM)],
        [SMEM, SMEM] + [VMEM] * members + [ANY],
        [VMEM] * 2,
        [pltpu.VMEM((members, rows, width), bf16)] * 2,
        flops=2 * rows * HEAD_DIM * columns,
        moved=4 * block_bytes,
    )(place, lengths, *pair_got, query_parts[0])
    up = [(g, g + members) for g in range(devices - members)]
    moving = lax.ppermute(total, everyone, up)
    earlier = moving
    if reach > 1:
        starts = BLOCK * (jnp.cumsum(lengths) - lengths)
        opens = jnp.max(jnp.where(starts <= base, starts, 0))
        for k in range(2, min(reach, planes - 1) + 1):
            moving = lax.ppermute(moving, everyone, up)
            earlier = earlier + jnp.where(opens < base - (k - 1) * members * rows, moving, 0.0)
    crossed = call(
        functools.partial(reach_back, members, heads, docs, rows),
        "reach_back",
        [shape(rows, width)] * members,
        [SMEM, SMEM] + [VMEM] * (half + 2),
        [VMEM] * members,
        flops=2 * rows * HEAD_DIM * columns,
        moved=4 * block_bytes,
    )(place, lengths, *query_got, carry, earlier)
    crossed_got = [crossed[0]] + [swap(crossed[d], d) for d in range(1, members)]

    gain = norm_gain.reshape(1, columns)
    first = [0] + list(range(half, members))
    last = list(range(1, half))
    out = None
    for chosen in (first, last):
        more = [] if out is None else [out]
        out = call(
            functools.partial(finish, chosen, heads, docs, rows),
            "finish",
            shape(rows, columns, dtype=bf16),
            [SMEM, SMEM, VMEM, VMEM] + [VMEM] * len(chosen) + [ANY] * len(more),
            ANY,
            [pltpu.VMEM((len(chosen), rows, width), bf16), pltpu.SemaphoreType.DMA((len(chosen),))],
            moved=2 * block_bytes,
            aliases={4 + len(chosen): 0} if more else None,
        )(place, lengths, own, gain, *[crossed_got[d] for d in chosen], *more)
    return out


def solution(mesh):
    placed = (
        P(("outer", "inner"), None),
        P(("outer", "inner"), None),
        P(("outer", "inner"), None),
        P(),
        P(),
    )
    return jax.shard_map(
        body, mesh=mesh, in_specs=placed, out_specs=P(("outer", "inner"), None), check_vma=False
    )
```

time: 168 us -> 73.6 us (0.44)
  waiting for transfers between devices: 76.5 us -> 32.9 us
  other arithmetic: 21.8 us -> 0.08 us
  blocking collectives: 16.4 us -> 0 us
  starting transfers between devices: 9.12 us -> 24.6 us
  between operations: 14.2 us -> 0.15 us
  Pallas kernels: 0 us -> 12.4 us
  loops' own time: 10.5 us -> 0 us
  local copies, waits for them, and re-layouts: 12.4 us -> 3.15 us
  matrix products: 6.03 us -> 0 us
    all_to_all x2 -> x0, waiting for transfers between devices: 46.6 us -> none  [the longest x1 24.6 us: body(): lax.all_to_all(local_state.reshape(1, state_rows, HEAD_DIM), 'inner', spl...]
    ppermute x0 -> x19, waiting for transfers between devices: none -> 32.9 us  [the longest x18 31 us: swap(): return lax.ppermute(part, everyone, pairs)]
    all_gather x1 -> x0, waiting for transfers between devices: 29.9 us -> none  [carried_in(): everything = jax.tree.map(lambda part: lax.all_gather(part, axis), shard)]
    ppermute x0 -> x19, starting transfers between devices: none -> 24.6 us  [the longest x18 21 us: swap(): return lax.ppermute(part, everyone, pairs)]
    unnamed x1 -> x0, blocking collectives: 16.4 us -> none
    pallas_call x0 -> x8, Pallas kernels: none -> 12.4 us  [the longest x1 4.93 us: body(): call(functools.partial(inside, head_count, docs, rows), 'inside', shape(r...]
    select_n x8 -> x0, other arithmetic: 11.8 us -> none  [lap(): return jax.tree.map(lambda a, b: jnp.where(reached, a, b), new, before)]
    another operation x2 -> x0, loops' own time: 10.5 us -> none  [the longest x1 5.38 us: carried_in(): return lax.fori_loop(0, devices, lap, start)]
  transfers between devices with their start and end apart: 3 -> 19, of which waited for: 3 -> 9; matrix products, arithmetic and copies ran while one was open for 3% -> 0% of each run, Pallas kernels for 0% -> 10%
where the time goes in v2:
time: 73.6 us; the launch traced here: 73.3 us
  waiting for transfers between devices  32.9 us (45%)
  starting transfers between devices  24.6 us (33%)
  Pallas kernels  12.4 us (17%)
  local copies, waits for them, and re-layouts  3.15 us (4%)
    ppermute x18, waiting for transfers between devices, swap(): return lax.ppermute(part, everyone, pairs)  31 us
    ppermute x18, starting transfers between devices, swap(): return lax.ppermute(part, everyone, pairs)  21 us
    pallas_call x1, Pallas kernels, body(): call(functools.partial(inside, head_count, docs, rows), 'inside', shape(r...  4.93 us
    ppermute x1, starting transfers between devices, body(): moving = lax.ppermute(total, everyone, up)  3.62 us
    unnamed x16, local copies, waits for them, and re-layouts  3.15 us
    pallas_call x2, Pallas kernels, body(): call(functools.partial(finish, chosen, heads, docs, rows), 'finish', shap...  2.96 us
    ppermute x1, waiting for transfers between devices, body(): moving = lax.ppermute(total, everyone, up)  1.97 us
  transfers between devices with their start and end apart: 19, of which 9 were waited for; matrix products, arithmetic and copies ran while one was open for 0% of the time, Pallas kernels for 10%

profile of v2, /device:TPU:0, one launch (start us, length us, event | category | flops | bytes accessed | tf_op | source)
XLA Modules:
  0.0 73.3 jit_solution(15334820521377368277)
XLA Ops:
  0.0 0.1 pad_add_fusion.place
  0.1 0.0 copy-start.2
  0.1 1.0 %copy-done.2 = bf16[64,4096]{1,0:T(8,128)(2,1)S(1)} copy-done((bf16[64,4096]{1,0:T(8,128)(2,1)S(1)}, bf16[64,4096]{1,0:T(8,128)(2,1)}, u32[]{:S(2)}) %copy-start.2) | copy-done | bytes 524312
  1.1 0.0 copy-start.4
  1.1 1.0 %copy-done.4 = bf16[64,4096]{1,0:T(8,128)(2,1)S(1)} copy-done((bf16[64,4096]{1,0:T(8,128)(2,1)S(1)}, bf16[64,4096]{1,0:T(8,128)(2,1)}, u32[]{:S(2)}) %copy-start.4) | copy-done | bytes 524312
  2.2 0.0 copy-start.7
  2.2 1.1 %spread_pairs.1 = (f32[2,64,512]{2,1,0:T(8,128)S(1)}, f32[2,64,512]{2,1,0:T(8,128)S(1)}, f32[2,64,512]{2,1,0:T(8,128)S(1)}, f32[2,64,512]{2,1,0:T(8,128)S(1)}, f...) custom-call(s32[3]{0:T(128)S(1)} %pad_add_fusion.place, ...), custom_call_target="tpu_custom_call" | custom-call | bytes 3145728 | tf_op jit(solution)/shard_map/spread_pairs/pallas_call | solution.py:206
  3.2 0.5 collective-permute-start.1
  3.8 2.6 %collective-permute-start.2 = (f32[2,64,512]{2,1,0:T(8,128)S(1)}, f32[2,64,512]{2,1,0:T(8,128)S(1)}, u32[]{:S(2)}, u32[]{:S(2)}) collective-permute-start(f32[2,64,512]{2,1,0:T(8,128)S(1)} %get-tuple-element.28), channel_id=1, source_target_pairs={{0,5},{1,4},{2,7},{3,6},{4,1},{5,0},{6,3},{7,2},{8,13},{9,12},{10,... | collective-permute-start | bytes 786440 | tf_op jit(solution)/shard_map/ppermute | solution.py:203
  6.4 0.0 copy-start
  6.4 1.0 %copy-done = bf16[64,4096]{1,0:T(8,128)(2,1)S(1)} copy-done((bf16[64,4096]{1,0:T(8,128)(2,1)S(1)}, bf16[64,4096]{1,0:T(8,128)(2,1)}, u32[]{:S(2)}) %copy-start) | copy-done | bytes 524312
  7.4 0.6 pick_other.1
  8.0 0.1 collective-permute-start
  8.1 1.6 %collective-permute-start.3 = (f32[2,64,512]{2,1,0:T(8,128)S(1)}, f32[2,64,512]{2,1,0:T(8,128)S(1)}, u32[]{:S(2)}, u32[]{:S(2)}) collective-permute-start(f32[2,64,512]{2,1,0:T(8,128)S(1)} %get-tuple-element.29), channel_id=1, source_target_pairs={{0,6},{1,7},{2,4},{3,5},{4,2},{5,3},{6,0},{7,1},{8,14},{9,15},{10,... | collective-permute-start | bytes 786440 | tf_op jit(solution)/shard_map/ppermute | solution.py:203
  9.7 0.0 collective-permute-start.4
  9.7 0.0 collective-permute-done.1.refs_0_.refs_4_
  9.7 2.6 %collective-permute-start.10 = (f32[2,64,512]{2,1,0:T(8,128)S(1)}, f32[2,64,512]{2,1,0:T(8,128)S(1)}, u32[]{:S(2)}, u32[]{:S(2)}) collective-permute-start(f32[2,64,512]{2,1,0:T(8,128)S(1)} %get-tuple-element.38), channel_id=1, source_target_pairs={{0,3},{1,2},{2,1},{3,0},{4,7},{5,6},{6,5},{7,4},{8,11},{9,10},{10,... | collective-permute-start | bytes 786440 | tf_op jit(solution)/shard_map/ppermute | solution.py:203
  12.3 0.7 collective-permute-done.2.refs_1_.refs_5_
  13.0 1.3 %collective-permute-start.8 = (f32[2,64,512]{2,1,0:T(8,128)S(1)}, f32[2,64,512]{2,1,0:T(8,128)S(1)}, u32[]{:S(2)}, u32[]{:S(2)}) collective-permute-start(f32[2,64,512]{2,1,0:T(8,128)S(1)} %get-tuple-element.36), channel_id=1, source_target_pairs={{0,1},{1,0},{2,3},{3,2},{4,5},{5,4},{6,7},{7,6},{8,9},{9,8},{10,11... | collective-permute-start | bytes 786440 | tf_op jit(solution)/shard_map/ppermute | solution.py:203
  14.4 13.1 %collective-permute-done.3.refs_2_.refs_6_ = f32[2,64,512]{2,1,0:T(8,128)S(1)} collective-permute-done((f32[2,64,512]{2,1,0:T(8,128)S(1)}, f32[2,64,512]{2,1,0:T(8,128)S(1)}, u32[]{:S(2)}, u32[]{:S(2)}) %collective-permute-start.3) | collective-permute-done | bytes 262176 | tf_op jit(solution)/shard_map/ppermute | solution.py:203
  27.4 1.5 %collective-permute-start.9 = (f32[2,64,512]{2,1,0:T(8,128)S(1)}, f32[2,64,512]{2,1,0:T(8,128)S(1)}, u32[]{:S(2)}, u32[]{:S(2)}) collective-permute-start(f32[2,64,512]{2,1,0:T(8,128)S(1)} %get-tuple-element.37), channel_id=1, source_target_pairs={{0,2},{1,3},{2,0},{3,1},{4,6},{5,7},{6,4},{7,5},{8,10},{9,11},{10,... | collective-permute-start | bytes 786440 | tf_op jit(solution)/shard_map/ppermute | solution.py:203
  28.9 0.0 collective-permute-done.4.refs_3_.refs_7_
  28.9 0.0 collective-permute-done.swapped
  28.9 0.6 spread_queries.1
  29.6 0.0 collective-permute-done.10.refs_3_
  29.6 0.5 collective-permute-done.8.refs_1_
  30.1 6.2 %collective-permute-done.9.refs_2_ = f32[2,64,512]{2,1,0:T(8,128)S(1)} collective-permute-done((f32[2,64,512]{2,1,0:T(8,128)S(1)}, f32[2,64,512]{2,1,0:T(8,128)S(1)}, u32[]{:S(2)}, u32[]{:S(2)}) %collective-permute-start.9) | collective-permute-done | bytes 262176 | tf_op jit(solution)/shard_map/ppermute | solution.py:203
  36.3 0.0 copy-done.7
  36.3 1.2 %gather_states.1 = (f32[8,4,128,128]{3,2,1,0:T(8,128)S(1)}, f32[4,128,128]{2,1,0:T(8,128)S(1)}) custom-call(s32[3]{0:T(128)S(1)} %pad_add_fusion.place, s32[16]{0:T(128)S(1)} %copy-done.7, f32[2,64,512]{2,1,0:T(8,128)S(1)} %get-tuple-element.35.refs_0_, f32[2,64,512]{2,1,0:T(8,128)S(1)} %collective-permute-done.8.refs_1_, ...), custom_call_target="tpu_custom_call" | custom-call | flops 67108864 | bytes 4194304 | tf_op jit(solution)/shard_map/gather_states/pallas_call | solution.py:251
  37.6 0.0 copy-start.1
  37.6 0.0 copy-start.3
  37.6 0.0 copy-start.5
  37.6 3.6 %collective-permute-start.11 = (f32[4,128,128]{2,1,0:T(8,128)S(1)}, f32[4,128,128]{2,1,0:T(8,128)S(1)}, u32[]{:S(2)}, u32[]{:S(2)}) collective-permute-start(f32[4,128,128]{2,1,0:T(8,128)S(1)} %get-tuple-element.40), channel_id=1, source_target_pairs={{0,8},{1,9},{2,10},{3,11},{4,12},{5,13},{6,14},{7,15},{8,16},{9,17... | collective-permute-start | bytes 786440 | tf_op jit(solution)/shard_map/ppermute | solution.py:262
  41.2 0.6 collective-permute-start.5
  41.8 1.5 %collective-permute-start.6 = (f32[2,64,512]{2,1,0:T(8,128)S(1)}, f32[2,64,512]{2,1,0:T(8,128)S(1)}, u32[]{:S(2)}, u32[]{:S(2)}) collective-permute-start(f32[2,64,512]{2,1,0:T(8,128)S(1)} %get-tuple-element.33), channel_id=1, source_target_pairs={{0,2},{1,3},{2,0},{3,1},{4,6},{5,7},{6,4},{7,5},{8,10},{9,11},{10,... | collective-permute-start | bytes 786440 | tf_op jit(solution)/shard_map/ppermute | solution.py:203
  43.3 1.4 %collective-permute-start.7 = (f32[2,64,512]{2,1,0:T(8,128)S(1)}, f32[2,64,512]{2,1,0:T(8,128)S(1)}, u32[]{:S(2)}, u32[]{:S(2)}) collective-permute-start(f32[2,64,512]{2,1,0:T(8,128)S(1)} %get-tuple-element.34), channel_id=1, source_target_pairs={{0,3},{1,2},{2,1},{3,0},{4,7},{5,6},{6,5},{7,4},{8,11},{9,10},{10,... | collective-permute-start | bytes 786440 | tf_op jit(solution)/shard_map/ppermute | solution.py:203
  44.8 2.0 %collective-permute-done.11.refs_5_ = f32[4,128,128]{2,1,0:T(8,128)S(1)} collective-permute-done((f32[4,128,128]{2,1,0:T(8,128)S(1)}, f32[4,128,128]{2,1,0:T(8,128)S(1)}, u32[]{:S(2)}, u32[]{:S(2)}) %collective-permute-start.11) | collective-permute-done | bytes 262176 | tf_op jit(solution)/shard_map/ppermute | solution.py:262
  46.7 3.8 %collective-permute-done.5.refs_1_ = f32[2,64,512]{2,1,0:T(8,128)S(1)} collective-permute-done((f32[2,64,512]{2,1,0:T(8,128)S(1)}, f32[2,64,512]{2,1,0:T(8,128)S(1)}, u32[]{:S(2)}, u32[]{:S(2)}) %collective-permute-start.5) | collective-permute-done | bytes 262176 | tf_op jit(solution)/shard_map/ppermute | solution.py:203
  50.5 3.5 %collective-permute-done.6.refs_2_ = f32[2,64,512]{2,1,0:T(8,128)S(1)} collective-permute-done((f32[2,64,512]{2,1,0:T(8,128)S(1)}, f32[2,64,512]{2,1,0:T(8,128)S(1)}, u32[]{:S(2)}, u32[]{:S(2)}) %collective-permute-start.6) | collective-permute-done | bytes 262176 | tf_op jit(solution)/shard_map/ppermute | solution.py:203
  54.0 1.6 %collective-permute-done.7.refs_3_ = f32[2,64,512]{2,1,0:T(8,128)S(1)} collective-permute-done((f32[2,64,512]{2,1,0:T(8,128)S(1)}, f32[2,64,512]{2,1,0:T(8,128)S(1)}, u32[]{:S(2)}, u32[]{:S(2)}) %collective-permute-start.7) | collective-permute-done | bytes 262176 | tf_op jit(solution)/shard_map/ppermute | solution.py:203
  55.6 1.0 %reach_back.1 = (f32[64,512]{1,0:T(8,128)S(1)}, f32[64,512]{1,0:T(8,128)S(1)}, f32[64,512]{1,0:T(8,128)S(1)}, f32[64,512]{1,0:T(8,128)S(1)}, f32[64,512]{1,0:T(8...) custom-call(s32[3]{0:T(128)S(1)} %pad_add_fusion.place, s32[16]{0:T(128)S(1)} %copy-done.7, ...), custom_call_target="tpu_custom_call" | custom-call | flops 67108864 | bytes 4194304 | tf_op jit(solution)/shard_map/reach_back/pallas_call | solution.py:270
  56.6 0.0 copy-start.6
  56.7 0.1 collective-permute-start.15
  56.7 0.9 %collective-permute-start.16 = (f32[64,512]{1,0:T(8,128)S(1)}, f32[64,512]{1,0:T(8,128)S(1)}, u32[]{:S(2)}, u32[]{:S(2)}) collective-permute-start(f32[64,512]{1,0:T(8,128)S(1)} %get-tuple-element.46), channel_id=1, source_target_pairs={{0,5},{1,4},{2,7},{3,6},{4,1},{5,0},{6,3},{7,2},{8,13},{9,12},{10,... | collective-permute-start | bytes 393224 | tf_op jit(solution)/shard_map/ppermute | solution.py:203
  57.6 1.2 %collective-permute-start.17 = (f32[64,512]{1,0:T(8,128)S(1)}, f32[64,512]{1,0:T(8,128)S(1)}, u32[]{:S(2)}, u32[]{:S(2)}) collective-permute-start(f32[64,512]{1,0:T(8,128)S(1)} %get-tuple-element.47), channel_id=1, source_target_pairs={{0,6},{1,7},{2,4},{3,5},{4,2},{5,3},{6,0},{7,1},{8,14},{9,15},{10,... | collective-permute-start | bytes 393224 | tf_op jit(solution)/shard_map/ppermute | solution.py:203
  58.8 1.2 %collective-permute-start.18 = (f32[64,512]{1,0:T(8,128)S(1)}, f32[64,512]{1,0:T(8,128)S(1)}, u32[]{:S(2)}, u32[]{:S(2)}) collective-permute-start(f32[64,512]{1,0:T(8,128)S(1)} %get-tuple-element.48), channel_id=1, source_target_pairs={{0,7},{1,6},{2,5},{3,4},{4,3},{5,2},{6,1},{7,0},{8,15},{9,14},{10,... | collective-permute-start | bytes 393224 | tf_op jit(solution)/shard_map/ppermute | solution.py:203
  60.1 0.8 %collective-permute-start.12 = (f32[64,512]{1,0:T(8,128)S(1)}, f32[64,512]{1,0:T(8,128)S(1)}, u32[]{:S(2)}, u32[]{:S(2)}) collective-permute-start(f32[64,512]{1,0:T(8,128)S(1)} %get-tuple-element.41), channel_id=1, source_target_pairs={{0,1},{1,0},{2,3},{3,2},{4,5},{5,4},{6,7},{7,6},{8,9},{9,8},{10,11... | collective-permute-start | bytes 393224 | tf_op jit(solution)/shard_map/ppermute | solution.py:203
  60.9 0.0 collective-permute-done.15.refs_1_
  60.9 1.5 %collective-permute-start.13 = (f32[64,512]{1,0:T(8,128)S(1)}, f32[64,512]{1,0:T(8,128)S(1)}, u32[]{:S(2)}, u32[]{:S(2)}) collective-permute-start(f32[64,512]{1,0:T(8,128)S(1)} %get-tuple-element.42), channel_id=1, source_target_pairs={{0,2},{1,3},{2,0},{3,1},{4,6},{5,7},{6,4},{7,5},{8,10},{9,11},{10,... | collective-permute-start | bytes 393224 | tf_op jit(solution)/shard_map/ppermute | solution.py:203
  62.4 0.0 collective-permute-done.16.refs_2_
  62.4 1.4 %collective-permute-start.14 = (f32[64,512]{1,0:T(8,128)S(1)}, f32[64,512]{1,0:T(8,128)S(1)}, u32[]{:S(2)}, u32[]{:S(2)}) collective-permute-start(f32[64,512]{1,0:T(8,128)S(1)} %get-tuple-element.43), channel_id=1, source_target_pairs={{0,3},{1,2},{2,1},{3,0},{4,7},{5,6},{6,5},{7,4},{8,11},{9,10},{10,... | collective-permute-start | bytes 393224 | tf_op jit(solution)/shard_map/ppermute | solution.py:203
  63.8 0.0 copy-done.1
  63.8 0.0 copy-done.3
  63.8 0.0 copy-done.5
  63.8 4.9 %inside.1.own = f32[64,4096]{1,0:T(8,128)S(1)} custom-call(s32[3]{0:T(128)S(1)} %pad_add_fusion.place, s32[16]{0:T(128)S(1)} %copy-done.7, bf16[64,4096]{1,0:T(8,128)(2,1)S(1)} %copy-done.1, bf16[64,4096]{1,0:T(8,128)(2,1)S(1)} %copy-done.3, bf16[64,4096]{1,0:T(8,128)(2,1)S(1)} %copy-done.5), custom_call_target="tpu_custom_call" | custom-call | flops 67108864 | bytes 3145728 | tf_op jit(solution)/shard_map/inside/pallas_call | solution.py:241
  68.7 0.0 collective-permute-done.17.refs_3_
  68.7 0.0 collective-permute-done.18.refs_4_
  68.7 0.0 copy-done.6
  68.7 1.5 %finish.2.refs_3_ = bf16[64,4096]{1,0:T(8,128)(2,1)} custom-call(s32[3]{0:T(128)S(1)} %pad_add_fusion.place, s32[16]{0:T(128)S(1)} %copy-done.7, f32[64,4096]{1,0:T(8,128)S(1)} %inside.1.own, f32[1,4096]{1,0:T(1,128)S(1)} %bitcast.4, f32[64,512]{1,0:T(8,128)S(1)} %get-tuple-element.44.refs_0_, f32[64,512]{1,0:T(8,128)S(1)} %collective-permute-done.15.refs_1_, ...), custom_call_target="tpu_custom_call" | custom-call | bytes 2097152 | tf_op jit(solution)/shard_map/finish/pallas_call | solution.py:287
  70.3 0.0 collective-permute-done.12.refs_0_
  70.3 1.6 %collective-permute-done.13.refs_1_ = f32[64,512]{1,0:T(8,128)S(1)} collective-permute-done((f32[64,512]{1,0:T(8,128)S(1)}, f32[64,512]{1,0:T(8,128)S(1)}, u32[]{:S(2)}, u32[]{:S(2)}) %collective-permute-start.13) | collective-permute-done | bytes 131104 | tf_op jit(solution)/shard_map/ppermute | solution.py:203
  71.9 0.0 collective-permute-done.14.refs_2_
  71.9 1.4 %finish.3 = bf16[64,4096]{1,0:T(8,128)(2,1)} custom-call(s32[3]{0:T(128)S(1)} %pad_add_fusion.place, s32[16]{0:T(128)S(1)} %copy-done.7, f32[64,4096]{1,0:T(8,128)S(1)} %inside.1.own, f32[1,4096]{1,0:T(1,128)S(1)} %bitcast.5, f32[64,512]{1,0:T(8,128)S(1)} %collective-permute-done.12.refs_0_, ...), custom_call_target="tpu_custom_call", output_to_operand_aliasing={{}: (7, {})} | custom-call | bytes 2097152 | tf_op jit(solution)/shard_map/finish/pallas_call | solution.py:287
Async XLA Ops:
  0.1 1.0 %copy-start.2 = (bf16[64,4096]{1,0:T(8,128)(2,1)S(1)}, bf16[64,4096]{1,0:T(8,128)(2,1)}, u32[]{:S(2)}) copy-start(bf16[64,4096]{1,0:T(8,128)(2,1)} %keys.3) | copy-start | bytes 1572868
  1.1 1.0 %copy-start.4 = (bf16[64,4096]{1,0:T(8,128)(2,1)S(1)}, bf16[64,4096]{1,0:T(8,128)(2,1)}, u32[]{:S(2)}) copy-start(bf16[64,4096]{1,0:T(8,128)(2,1)} %values.3) | copy-start | bytes 1572868
  2.2 34.2 %copy-start.7 = (s32[16]{0:T(128)S(1)}, s32[16]{0:T(128)}, u32[]{:S(2)}) copy-start(s32[16]{0:T(128)} %lengths.9) | copy-start | bytes 196
  3.2 6.5 %collective-permute-start.1 = (f32[2,64,512]{2,1,0:T(8,128)S(1)}, f32[2,64,512]{2,1,0:T(8,128)S(1)}, u32[]{:S(2)}, u32[]{:S(2)}) collective-permute-start(f32[2,64,512]{2,1,0:T(8,128)S(1)} %get-tuple-element.27), channel_id=1, source_target_pairs={{0,4},{1,5},{2,6},{3,7},{4,0},{5,1},{6,2},{7,3},{8,12},{9,13},{10,... | collective-permute-start | bytes 786440 | tf_op jit(solution)/shard_map/ppermute | solution.py:203
  3.8 9.3 %collective-permute-start.2 = (f32[2,64,512]{2,1,0:T(8,128)S(1)}, f32[2,64,512]{2,1,0:T(8,128)S(1)}, u32[]{:S(2)}, u32[]{:S(2)}) collective-permute-start(f32[2,64,512]{2,1,0:T(8,128)S(1)} %get-tuple-element.28), channel_id=1, source_target_pairs={{0,5},{1,4},{2,7},{3,6},{4,1},{5,0},{6,3},{7,2},{8,13},{9,12},{10,... | collective-permute-start | bytes 786440 | tf_op jit(solution)/shard_map/ppermute | solution.py:203
  6.4 1.0 %copy-start = (bf16[64,4096]{1,0:T(8,128)(2,1)S(1)}, bf16[64,4096]{1,0:T(8,128)(2,1)}, u32[]{:S(2)}) copy-start(bf16[64,4096]{1,0:T(8,128)(2,1)} %queries.5) | copy-start | bytes 1572868
  8.0 20.9 %collective-permute-start = (f32[64,2048]{1,0:T(8,128)S(1)}, f32[64,2048]{1,0:T(8,128)S(1)}, u32[]{:S(2)}, u32[]{:S(2)}) collective-permute-start(f32[64,2048]{1,0:T(8,128)S(1)} %pick_other.1), channel_id=1, source_target_pairs={{0,4},{1,5},{2,6},{3,7},{4,0},{5,1},{6,2},{7,3},{8,12},{9,13},{10,... | collective-permute-start | bytes 1572872 | tf_op jit(solution)/shard_map/ppermute | solution.py:203
  8.1 19.3 %collective-permute-start.3 = (f32[2,64,512]{2,1,0:T(8,128)S(1)}, f32[2,64,512]{2,1,0:T(8,128)S(1)}, u32[]{:S(2)}, u32[]{:S(2)}) collective-permute-start(f32[2,64,512]{2,1,0:T(8,128)S(1)} %get-tuple-element.29), channel_id=1, source_target_pairs={{0,6},{1,7},{2,4},{3,5},{4,2},{5,3},{6,0},{7,1},{8,14},{9,15},{10,... | collective-permute-start | bytes 786440 | tf_op jit(solution)/shard_map/ppermute | solution.py:203
  9.7 19.2 %collective-permute-start.4 = (f32[2,64,512]{2,1,0:T(8,128)S(1)}, f32[2,64,512]{2,1,0:T(8,128)S(1)}, u32[]{:S(2)}, u32[]{:S(2)}) collective-permute-start(f32[2,64,512]{2,1,0:T(8,128)S(1)} %get-tuple-element.30), channel_id=1, source_target_pairs={{0,7},{1,6},{2,5},{3,4},{4,3},{5,2},{6,1},{7,0},{8,15},{9,14},{10,... | collective-permute-start | bytes 786440 | tf_op jit(solution)/shard_map/ppermute | solution.py:203
  9.7 19.8 %collective-permute-start.10 = (f32[2,64,512]{2,1,0:T(8,128)S(1)}, f32[2,64,512]{2,1,0:T(8,128)S(1)}, u32[]{:S(2)}, u32[]{:S(2)}) collective-permute-start(f32[2,64,512]{2,1,0:T(8,128)S(1)} %get-tuple-element.38), channel_id=1, source_target_pairs={{0,3},{1,2},{2,1},{3,0},{4,7},{5,6},{6,5},{7,4},{8,11},{9,10},{10,... | collective-permute-start | bytes 786440 | tf_op jit(solution)/shard_map/ppermute | solution.py:203
  13.0 17.1 %collective-permute-start.8 = (f32[2,64,512]{2,1,0:T(8,128)S(1)}, f32[2,64,512]{2,1,0:T(8,128)S(1)}, u32[]{:S(2)}, u32[]{:S(2)}) collective-permute-start(f32[2,64,512]{2,1,0:T(8,128)S(1)} %get-tuple-element.36), channel_id=1, source_target_pairs={{0,1},{1,0},{2,3},{3,2},{4,5},{5,4},{6,7},{7,6},{8,9},{9,8},{10,11... | collective-permute-start | bytes 786440 | tf_op jit(solution)/shard_map/ppermute | solution.py:203
  27.4 8.9 %collective-permute-start.9 = (f32[2,64,512]{2,1,0:T(8,128)S(1)}, f32[2,64,512]{2,1,0:T(8,128)S(1)}, u32[]{:S(2)}, u32[]{:S(2)}) collective-permute-start(f32[2,64,512]{2,1,0:T(8,128)S(1)} %get-tuple-element.37), channel_id=1, source_target_pairs={{0,2},{1,3},{2,0},{3,1},{4,6},{5,7},{6,4},{7,5},{8,10},{9,11},{10,... | collective-permute-start | bytes 786440 | tf_op jit(solution)/shard_map/ppermute | solution.py:203
  37.6 26.2 %copy-start.1 = (bf16[64,4096]{1,0:T(8,128)(2,1)S(1)}, bf16[64,4096]{1,0:T(8,128)(2,1)}, u32[]{:S(2)}) copy-start(bf16[64,4096]{1,0:T(8,128)(2,1)} %queries.5) | copy-start | bytes 1572868
  37.6 26.2 %copy-start.3 = (bf16[64,4096]{1,0:T(8,128)(2,1)S(1)}, bf16[64,4096]{1,0:T(8,128)(2,1)}, u32[]{:S(2)}) copy-start(bf16[64,4096]{1,0:T(8,128)(2,1)} %keys.3) | copy-start | bytes 1572868
  37.6 26.2 %copy-start.5 = (bf16[64,4096]{1,0:T(8,128)(2,1)S(1)}, bf16[64,4096]{1,0:T(8,128)(2,1)}, u32[]{:S(2)}) copy-start(bf16[64,4096]{1,0:T(8,128)(2,1)} %values.3) | copy-start | bytes 1572868
  37.6 9.2 %collective-permute-start.11 = (f32[4,128,128]{2,1,0:T(8,128)S(1)}, f32[4,128,128]{2,1,0:T(8,128)S(1)}, u32[]{:S(2)}, u32[]{:S(2)}) collective-permute-start(f32[4,128,128]{2,1,0:T(8,128)S(1)} %get-tuple-element.40), channel_id=1, source_target_pairs={{0,8},{1,9},{2,10},{3,11},{4,12},{5,13},{6,14},{7,15},{8,16},{9,17... | collective-permute-start | bytes 786440 | tf_op jit(solution)/shard_map/ppermute | solution.py:262
  41.2 9.3 %collective-permute-start.5 = (f32[2,64,512]{2,1,0:T(8,128)S(1)}, f32[2,64,512]{2,1,0:T(8,128)S(1)}, u32[]{:S(2)}, u32[]{:S(2)}) collective-permute-start(f32[2,64,512]{2,1,0:T(8,128)S(1)} %get-tuple-element.32), channel_id=1, source_target_pairs={{0,1},{1,0},{2,3},{3,2},{4,5},{5,4},{6,7},{7,6},{8,9},{9,8},{10,11... | collective-permute-start | bytes 786440 | tf_op jit(solution)/shard_map/ppermute | solution.py:203
  41.8 12.2 %collective-permute-start.6 = (f32[2,64,512]{2,1,0:T(8,128)S(1)}, f32[2,64,512]{2,1,0:T(8,128)S(1)}, u32[]{:S(2)}, u32[]{:S(2)}) collective-permute-start(f32[2,64,512]{2,1,0:T(8,128)S(1)} %get-tuple-element.33), channel_id=1, source_target_pairs={{0,2},{1,3},{2,0},{3,1},{4,6},{5,7},{6,4},{7,5},{8,10},{9,11},{10,... | collective-permute-start | bytes 786440 | tf_op jit(solution)/shard_map/ppermute | solution.py:203
  43.3 12.3 %collective-permute-start.7 = (f32[2,64,512]{2,1,0:T(8,128)S(1)}, f32[2,64,512]{2,1,0:T(8,128)S(1)}, u32[]{:S(2)}, u32[]{:S(2)}) collective-permute-start(f32[2,64,512]{2,1,0:T(8,128)S(1)} %get-tuple-element.34), channel_id=1, source_target_pairs={{0,3},{1,2},{2,1},{3,0},{4,7},{5,6},{6,5},{7,4},{8,11},{9,10},{10,... | collective-permute-start | bytes 786440 | tf_op jit(solution)/shard_map/ppermute | solution.py:203
  56.6 12.1 %copy-start.6 = (f32[4096]{0:T(1024)S(1)}, f32[4096]{0:T(1024)}, u32[]{:S(2)}) copy-start(f32[4096]{0:T(1024)} %param.9) | copy-start | bytes 49156
  56.7 4.2 %collective-permute-start.15 = (f32[64,512]{1,0:T(8,128)S(1)}, f32[64,512]{1,0:T(8,128)S(1)}, u32[]{:S(2)}, u32[]{:S(2)}) collective-permute-start(f32[64,512]{1,0:T(8,128)S(1)} %get-tuple-element.45), channel_id=1, source_target_pairs={{0,4},{1,5},{2,6},{3,7},{4,0},{5,1},{6,2},{7,3},{8,12},{9,13},{10,... | collective-permute-start | bytes 393224 | tf_op jit(solution)/shard_map/ppermute | solution.py:203
  56.7 5.6 %collective-permute-start.16 = (f32[64,512]{1,0:T(8,128)S(1)}, f32[64,512]{1,0:T(8,128)S(1)}, u32[]{:S(2)}, u32[]{:S(2)}) collective-permute-start(f32[64,512]{1,0:T(8,128)S(1)} %get-tuple-element.46), channel_id=1, source_target_pairs={{0,5},{1,4},{2,7},{3,6},{4,1},{5,0},{6,3},{7,2},{8,13},{9,12},{10,... | collective-permute-start | bytes 393224 | tf_op jit(solution)/shard_map/ppermute | solution.py:203
  57.6 11.1 %collective-permute-start.17 = (f32[64,512]{1,0:T(8,128)S(1)}, f32[64,512]{1,0:T(8,128)S(1)}, u32[]{:S(2)}, u32[]{:S(2)}) collective-permute-start(f32[64,512]{1,0:T(8,128)S(1)} %get-tuple-element.47), channel_id=1, source_target_pairs={{0,6},{1,7},{2,4},{3,5},{4,2},{5,3},{6,0},{7,1},{8,14},{9,15},{10,... | collective-permute-start | bytes 393224 | tf_op jit(solution)/shard_map/ppermute | solution.py:203
  58.8 9.9 %collective-permute-start.18 = (f32[64,512]{1,0:T(8,128)S(1)}, f32[64,512]{1,0:T(8,128)S(1)}, u32[]{:S(2)}, u32[]{:S(2)}) collective-permute-start(f32[64,512]{1,0:T(8,128)S(1)} %get-tuple-element.48), channel_id=1, source_target_pairs={{0,7},{1,6},{2,5},{3,4},{4,3},{5,2},{6,1},{7,0},{8,15},{9,14},{10,... | collective-permute-start | bytes 393224 | tf_op jit(solution)/shard_map/ppermute | solution.py:203
  60.1 10.2 %collective-permute-start.12 = (f32[64,512]{1,0:T(8,128)S(1)}, f32[64,512]{1,0:T(8,128)S(1)}, u32[]{:S(2)}, u32[]{:S(2)}) collective-permute-start(f32[64,512]{1,0:T(8,128)S(1)} %get-tuple-element.41), channel_id=1, source_target_pairs={{0,1},{1,0},{2,3},{3,2},{4,5},{5,4},{6,7},{7,6},{8,9},{9,8},{10,11... | collective-permute-start | bytes 393224 | tf_op jit(solution)/shard_map/ppermute | solution.py:203
  60.9 11.0 %collective-permute-start.13 = (f32[64,512]{1,0:T(8,128)S(1)}, f32[64,512]{1,0:T(8,128)S(1)}, u32[]{:S(2)}, u32[]{:S(2)}) collective-permute-start(f32[64,512]{1,0:T(8,128)S(1)} %get-tuple-element.42), channel_id=1, source_target_pairs={{0,2},{1,3},{2,0},{3,1},{4,6},{5,7},{6,4},{7,5},{8,10},{9,11},{10,... | collective-permute-start | bytes 393224 | tf_op jit(solution)/shard_map/ppermute | solution.py:203
  62.4 9.5 %collective-permute-start.14 = (f32[64,512]{1,0:T(8,128)S(1)}, f32[64,512]{1,0:T(8,128)S(1)}, u32[]{:S(2)}, u32[]{:S(2)}) collective-permute-start(f32[64,512]{1,0:T(8,128)S(1)} %get-tuple-element.43), channel_id=1, source_target_pairs={{0,3},{1,2},{2,1},{3,0},{4,7},{5,6},{6,5},{7,4},{8,11},{9,10},{10,... | collective-permute-start | bytes 393224 | tf_op jit(solution)/shard_map/ppermute | solution.py:203

commit v3 on v2

--- a/solution.py
+++ b/solution.py
@@ -15,6 +15,7 @@
 SMEM = pl.BlockSpec(memory_space=pltpu.SMEM)
 VMEM = pl.BlockSpec(memory_space=pltpu.VMEM)
 ANY = pl.BlockSpec(memory_space=pl.ANY)
+HBM = pl.BlockSpec(memory_space=pltpu.HBM)
 
 
 def columns_of(member, width):
@@ -36,45 +37,48 @@
     return found, after
 
 
-def spread_pairs(members, width, place, keys, values, *refs):
-    outs = refs[:members]
-    key_buffer, value_buffer, sems = refs[members:]
+def spread(members, width, place, queries, keys, values, *refs):
+    half = members // CORES
+    near, cross = refs[:half], refs[half]
+    buffers, sems = refs[half + 1 : half + 4], refs[half + 4]
     me = place[0]
 
     def copies(d):
         span = columns_of(me ^ d, width)
+        sources = (keys, values) if d < half else (keys, values, queries)
         return [
-            pltpu.make_async_copy(keys.at[:, span], key_buffer.at[d], sems.at[0, d]),
-            pltpu.make_async_copy(values.at[:, span], value_buffer.at[d], sems.at[1, d]),
+            pltpu.make_async_copy(source.at[:, span], buffers[i].at[d], sems.at[i, d])
+            for i, source in enumerate(sources)
         ]
 
-    order = list(reversed(range(members)))
-    for d in order:
+    for d in range(members):
         for copy in copies(d):
             copy.start()
-    for d in order:
-        for copy in copies(d):
+    for d in range(members):
+        for i, copy in enumerate(copies(d)):
             copy.wait()
-        outs[d][0] = key_buffer[d].astype(jnp.float32)
-        outs[d][1] = value_buffer[d].astype(jnp.float32)
-
-
-def pick_other(members, width, place, queries, out):
-    half = members // CORES
-    side = 1 - place[0] // half
-    out[...] = queries[:, columns_of(side, half * width)].astype(jnp.float32)
-
-
-def spread_queries(members, width, gates, place, queries, swapped, *refs):
-    half = members // CORES
+            part = buffers[i][d].astype(jnp.float32)
+            if d < half:
+                near[d][i] = part
+            else:
+                cross[d - half, i] = part
+
+
+def forward(half, swapped, *outs):
+    for e in range(1, half):
+        outs[e - 1][...] = swapped[e, 0:2]
+
+
+def join_queries(half, width, gates, place, queries, swapped, *refs):
     outs = refs[gates:]
     me = place[0]
     for e in range(half):
         outs[e][0] = queries[:, columns_of(me ^ e, width)].astype(jnp.float32)
-        outs[e][1] = swapped[:, columns_of((me ^ e) % half, width)]
+        outs[e][1] = swapped[e, 2]
 
 
 def gather_states(members, heads, docs, rows, place, lengths, *refs):
+    half = members // CORES
     parts = refs[:members]
     carry_out, total_out, key_blocks, value_blocks = refs[members + 1 :]
     me, base = place[0], place[1]
@@ -82,8 +86,9 @@
     for d in range(members):
         j = me ^ d
         since, _ = start_of(lengths, docs, base + (j + 1) * rows)
-        key_blocks[j] = jnp.where(row >= since - base - j * rows, parts[d][0], 0.0).astype(jnp.bfloat16)
-        value_blocks[j] = parts[d][1].astype(jnp.bfloat16)
+        key, value = (parts[d][0, 0], parts[d][0, 1]) if d == half else (parts[d][0], parts[d][1])
+        key_blocks[j] = jnp.where(row >= since - base - j * rows, key, 0.0).astype(jnp.bfloat16)
+        value_blocks[j] = value.astype(jnp.bfloat16)
     state = [jnp.zeros((HEAD_DIM, HEAD_DIM), jnp.float32) for _ in range(heads)]
     for j in range(members):
         since, _ = start_of(lengths, docs, base + (j + 1) * rows)
@@ -123,7 +128,7 @@
     half = members // CORES
     query_parts = refs[:half]
     carry, earlier = refs[half : half + 2]
-    outs = refs[half + 2 :]
+    outs = refs[half + 3 :]
     me, base = place[0], place[1]
     for e in range(half):
         for side in range(CORES):
@@ -203,34 +208,30 @@
         return lax.ppermute(part, everyone, pairs)
 
     block_bytes = rows * columns * 4
-    pair_parts = call(
-        functools.partial(spread_pairs, members, width),
-        "spread_pairs",
-        [shape(2, rows, width)] * members,
-        [SMEM, ANY, ANY],
-        [VMEM] * members,
-        [
-            pltpu.VMEM((members, rows, width), bf16),
-            pltpu.VMEM((members, rows, width), bf16),
-            pltpu.SemaphoreType.DMA((2, members)),
-        ],
-        moved=3 * block_bytes,
-    )(place, keys, values)
-    pair_got = [pair_parts[0]] + [swap(pair_parts[d], d) for d in range(1, members)]
-
-    other = call(
-        functools.partial(pick_other, members, width),
-        "pick_other",
-        shape(rows, half * width),
-        [SMEM, VMEM],
-        VMEM,
-        moved=block_bytes,
-    )(place, queries)
-    swapped = swap(other, half)
-    gates = pair_got[half:]
+    parts = call(
+        functools.partial(spread, members, width),
+        "spread",
+        [shape(2, rows, width)] * half + [shape(half, 3, rows, width)],
+        [SMEM, HBM, HBM, HBM],
+        [VMEM] * (half + 1),
+        [pltpu.VMEM((members, rows, width), bf16)] * 3 + [pltpu.SemaphoreType.DMA((3, members))],
+        moved=4 * block_bytes,
+    )(place, queries, keys, values)
+    near_got = [parts[0]] + [swap(parts[e], e) for e in range(1, half)]
+    swapped = swap(parts[half], half)
+    far_parts = call(
+        functools.partial(forward, half),
+        "forward",
+        [shape(2, rows, width)] * (half - 1),
+        [VMEM],
+        [VMEM] * (half - 1),
+        moved=2 * block_bytes,
+    )(swapped)
+    far_got = [swapped] + [swap(part, e + 1) for e, part in enumerate(far_parts)]
+    gates = near_got[1:]
     query_parts = call(
-        functools.partial(spread_queries, members, width, len(gates)),
-        "spread_queries",
+        functools.partial(join_queries, half, width, len(gates)),
+        "join_queries",
         [shape(CORES, rows, width)] * half,
         [SMEM, VMEM, VMEM] + [ANY] * len(gates),
         [VMEM] * half,
@@ -257,7 +258,7 @@
         [pltpu.VMEM((members, rows, width), bf16)] * 2,
         flops=2 * rows * HEAD_DIM * columns,
         moved=4 * block_bytes,
-    )(place, lengths, *pair_got, query_parts[0])
+    )(place, lengths, *near_got, *far_got, query_parts[0])
     up = [(g, g + members) for g in range(devices - members)]
     moving = lax.ppermute(total, everyone, up)
     earlier = moving
@@ -271,11 +272,11 @@
         functools.partial(reach_back, members, heads, docs, rows),
         "reach_back",
         [shape(rows, width)] * members,
-        [SMEM, SMEM] + [VMEM] * (half + 2),
+        [SMEM, SMEM] + [VMEM] * (half + 2) + [ANY],
         [VMEM] * members,
         flops=2 * rows * HEAD_DIM * columns,
         moved=4 * block_bytes,
-    )(place, lengths, *query_got, carry, earlier)
+    )(place, lengths, *query_got, carry, earlier, own)
     crossed_got = [crossed[0]] + [swap(crossed[d], d) for d in range(1, members)]
 
     gain = norm_gain.reshape(1, columns)

time: 73.6 us -> 62.5 us (0.85)
  waiting for transfers between devices: 32.9 us -> 20.2 us
  starting transfers between devices: 24.6 us -> 26.6 us
    ppermute x18 -> x17, waiting for transfers between devices: 31 us -> 20.2 us  [swap(): return lax.ppermute(part, everyone, pairs)]
    ppermute x18 -> x17, starting transfers between devices: 21 us -> 23.1 us  [swap(): return lax.ppermute(part, everyone, pairs)]
    ppermute x1, waiting for transfers between devices: 1.97 us -> 0.01 us  [body(): moving = lax.ppermute(total, everyone, up)]
    unnamed x16 -> x14, local copies, waits for them, and re-layouts: 3.15 us -> 3.14 us
  transfers between devices with their start and end apart: 19 -> 18, of which waited for: 9 -> 8; matrix products, arithmetic and copies ran while one was open for 0% -> 0% of each run, Pallas kernels for 10% -> 13%
where the time goes in v3:
time: 62.5 us; the launch traced here: 62.2 us
  starting transfers between devices  26.6 us (43%)
  waiting for transfers between devices  20.2 us (32%)
  Pallas kernels  12.1 us (19%)
  local copies, waits for them, and re-layouts  3.14 us (5%)
    ppermute x17, starting transfers between devices, swap(): return lax.ppermute(part, everyone, pairs)  23.1 us
    ppermute x17, waiting for transfers between devices, swap(): return lax.ppermute(part, everyone, pairs)  20.2 us
    pallas_call x1, Pallas kernels, body(): call(functools.partial(inside, head_count, docs, rows), 'inside', shape(r...  4.93 us
    ppermute x1, starting transfers between devices, body(): moving = lax.ppermute(total, everyone, up)  3.5 us
    unnamed x14, local copies, waits for them, and re-layouts  3.14 us
    pallas_call x2, Pallas kernels, body(): call(functools.partial(finish, chosen, heads, docs, rows), 'finish', shap...  2.95 us
  transfers between devices with their start and end apart: 18, of which 8 were waited for; matrix products, arithmetic and copies ran while one was open for 0% of the time, Pallas kernels for 13%

profile of v3, /device:TPU:0, one launch (start us, length us, event | category | flops | bytes accessed | tf_op | source)
XLA Modules:
  0.0 62.2 jit_solution(17114716550285871850)
XLA Ops:
  0.0 0.1 pad_add_fusion.place
  0.1 0.0 copy-start
  0.1 1.0 %copy-done = bf16[64,4096]{1,0:T(8,128)(2,1)S(1)} copy-done((bf16[64,4096]{1,0:T(8,128)(2,1)S(1)}, bf16[64,4096]{1,0:T(8,128)(2,1)}, u32[]{:S(2)}) %copy-start) | copy-done | bytes 524312
  1.1 0.0 copy-start.2
  1.1 1.0 %copy-done.2 = bf16[64,4096]{1,0:T(8,128)(2,1)S(1)} copy-done((bf16[64,4096]{1,0:T(8,128)(2,1)S(1)}, bf16[64,4096]{1,0:T(8,128)(2,1)}, u32[]{:S(2)}) %copy-start.2) | copy-done | bytes 524312
  2.2 0.0 copy-start.3
  2.2 1.0 %copy-done.3 = bf16[64,4096]{1,0:T(8,128)(2,1)S(1)} copy-done((bf16[64,4096]{1,0:T(8,128)(2,1)S(1)}, bf16[64,4096]{1,0:T(8,128)(2,1)}, u32[]{:S(2)}) %copy-start.3) | copy-done | bytes 524312
  3.2 1.2 %spread.1 = (f32[2,64,512]{2,1,0:T(8,128)S(1)}, f32[2,64,512]{2,1,0:T(8,128)S(1)}, f32[2,64,512]{2,1,0:T(8,128)S(1)}, f32[2,64,512]{2,1,0:T(8,128)S(1)}, f32[4,3,64,512]{3,2,1,0:T(8,128)S(1)}) custom-call(s32[3]{0:T(128)S(1)} %pad_add_fusion.place, bf16[64,4096]{1,0:T(8,128)(2,1)S(1)} %copy-done, bf16[64,4096]{1,0:T(8,128)(2,1)S(1)} %copy-done.2, ...), custom_call_target="tpu_custom_call" | custom-call | bytes 4194304 | tf_op jit(solution)/shard_map/spread/pallas_call | solution.py:211
  4.4 0.5 collective-permute-start
  5.0 2.6 %collective-permute-start.1 = (f32[2,64,512]{2,1,0:T(8,128)S(1)}, f32[2,64,512]{2,1,0:T(8,128)S(1)}, u32[]{:S(2)}, u32[]{:S(2)}) collective-permute-start(f32[2,64,512]{2,1,0:T(8,128)S(1)} %get-tuple-element.28), channel_id=1, source_target_pairs={{0,1},{1,0},{2,3},{3,2},{4,5},{5,4},{6,7},{7,6},{8,9},{9,8},{10,11... | collective-permute-start | bytes 786440 | tf_op jit(solution)/shard_map/ppermute | solution.py:208
  7.5 1.5 %collective-permute-start.2 = (f32[2,64,512]{2,1,0:T(8,128)S(1)}, f32[2,64,512]{2,1,0:T(8,128)S(1)}, u32[]{:S(2)}, u32[]{:S(2)}) collective-permute-start(f32[2,64,512]{2,1,0:T(8,128)S(1)} %get-tuple-element.29), channel_id=1, source_target_pairs={{0,2},{1,3},{2,0},{3,1},{4,6},{5,7},{6,4},{7,5},{8,10},{9,11},{10,... | collective-permute-start | bytes 786440 | tf_op jit(solution)/shard_map/ppermute | solution.py:208
  9.0 0.0 collective-permute-start.3
  9.1 0.0 collective-permute-done.swapped.refs_4_
  9.1 0.1 forward.1
  9.1 0.0 copy-start.6
  9.1 2.0 %collective-permute-start.7 = (f32[2,64,512]{2,1,0:T(8,128)S(1)}, f32[2,64,512]{2,1,0:T(8,128)S(1)}, u32[]{:S(2)}, u32[]{:S(2)}) collective-permute-start(f32[2,64,512]{2,1,0:T(8,128)S(1)} %get-tuple-element.36), channel_id=1, source_target_pairs={{0,1},{1,0},{2,3},{3,2},{4,5},{5,4},{6,7},{7,6},{8,9},{9,8},{10,11... | collective-permute-start | bytes 786440 | tf_op jit(solution)/shard_map/ppermute | solution.py:208
  11.2 1.5 %collective-permute-start.8 = (f32[2,64,512]{2,1,0:T(8,128)S(1)}, f32[2,64,512]{2,1,0:T(8,128)S(1)}, u32[]{:S(2)}, u32[]{:S(2)}) collective-permute-start(f32[2,64,512]{2,1,0:T(8,128)S(1)} %get-tuple-element.37), channel_id=1, source_target_pairs={{0,2},{1,3},{2,0},{3,1},{4,6},{5,7},{6,4},{7,5},{8,10},{9,11},{10,... | collective-permute-start | bytes 786440 | tf_op jit(solution)/shard_map/ppermute | solution.py:208
  12.7 2.0 %collective-permute-done.1.refs_0_.refs_1_ = f32[2,64,512]{2,1,0:T(8,128)S(1)} collective-permute-done((f32[2,64,512]{2,1,0:T(8,128)S(1)}, f32[2,64,512]{2,1,0:T(8,128)S(1)}, u32[]{:S(2)}, u32[]{:S(2)}) %collective-permute-start.1) | collective-permute-done | bytes 262176 | tf_op jit(solution)/shard_map/ppermute | solution.py:208
  14.7 2.9 %collective-permute-start.9 = (f32[2,64,512]{2,1,0:T(8,128)S(1)}, f32[2,64,512]{2,1,0:T(8,128)S(1)}, u32[]{:S(2)}, u32[]{:S(2)}) collective-permute-start(f32[2,64,512]{2,1,0:T(8,128)S(1)} %get-tuple-element.38), channel_id=1, source_target_pairs={{0,3},{1,2},{2,1},{3,0},{4,7},{5,6},{6,5},{7,4},{8,11},{9,10},{10,... | collective-permute-start | bytes 786440 | tf_op jit(solution)/shard_map/ppermute | solution.py:208
  17.6 4.7 %collective-permute-done.2.refs_1_.refs_2_ = f32[2,64,512]{2,1,0:T(8,128)S(1)} collective-permute-done((f32[2,64,512]{2,1,0:T(8,128)S(1)}, f32[2,64,512]{2,1,0:T(8,128)S(1)}, u32[]{:S(2)}, u32[]{:S(2)}) %collective-permute-start.2) | collective-permute-done | bytes 262176 | tf_op jit(solution)/shard_map/ppermute | solution.py:208
  22.3 0.0 collective-permute-done.3.refs_2_.refs_3_
  22.3 0.6 join_queries.1
  22.9 1.0 %collective-permute-start.4 = (f32[2,64,512]{2,1,0:T(8,128)S(1)}, f32[2,64,512]{2,1,0:T(8,128)S(1)}, u32[]{:S(2)}, u32[]{:S(2)}) collective-permute-start(f32[2,64,512]{2,1,0:T(8,128)S(1)} %get-tuple-element.32), channel_id=1, source_target_pairs={{0,1},{1,0},{2,3},{3,2},{4,5},{5,4},{6,7},{7,6},{8,9},{9,8},{10,11... | collective-permute-start | bytes 786440 | tf_op jit(solution)/shard_map/ppermute | solution.py:208
  23.9 1.1 %collective-permute-start.5 = (f32[2,64,512]{2,1,0:T(8,128)S(1)}, f32[2,64,512]{2,1,0:T(8,128)S(1)}, u32[]{:S(2)}, u32[]{:S(2)}) collective-permute-start(f32[2,64,512]{2,1,0:T(8,128)S(1)} %get-tuple-element.33), channel_id=1, source_target_pairs={{0,2},{1,3},{2,0},{3,1},{4,6},{5,7},{6,4},{7,5},{8,10},{9,11},{10,... | collective-permute-start | bytes 786440 | tf_op jit(solution)/shard_map/ppermute | solution.py:208
  25.0 0.9 %collective-permute-done.7.refs_5_ = f32[2,64,512]{2,1,0:T(8,128)S(1)} collective-permute-done((f32[2,64,512]{2,1,0:T(8,128)S(1)}, f32[2,64,512]{2,1,0:T(8,128)S(1)}, u32[]{:S(2)}, u32[]{:S(2)}) %collective-permute-start.7) | collective-permute-done | bytes 262176 | tf_op jit(solution)/shard_map/ppermute | solution.py:208
  26.0 2.9 %collective-permute-start.6 = (f32[2,64,512]{2,1,0:T(8,128)S(1)}, f32[2,64,512]{2,1,0:T(8,128)S(1)}, u32[]{:S(2)}, u32[]{:S(2)}) collective-permute-start(f32[2,64,512]{2,1,0:T(8,128)S(1)} %get-tuple-element.34), channel_id=1, source_target_pairs={{0,3},{1,2},{2,1},{3,0},{4,7},{5,6},{6,5},{7,4},{8,11},{9,10},{10,... | collective-permute-start | bytes 786440 | tf_op jit(solution)/shard_map/ppermute | solution.py:208
  28.9 4.7 %collective-permute-done.8.refs_6_ = f32[2,64,512]{2,1,0:T(8,128)S(1)} collective-permute-done((f32[2,64,512]{2,1,0:T(8,128)S(1)}, f32[2,64,512]{2,1,0:T(8,128)S(1)}, u32[]{:S(2)}, u32[]{:S(2)}) %collective-permute-start.8) | collective-permute-done | bytes 262176 | tf_op jit(solution)/shard_map/ppermute | solution.py:208
  33.5 0.0 collective-permute-done.9.refs_7_
  33.5 0.0 copy-done.6
  33.5 0.0 copy-start.1
  33.5 0.0 copy-start.4
  33.6 1.2 %gather_states.1 = (f32[8,4,128,128]{3,2,1,0:T(8,128)S(1)}, f32[4,128,128]{2,1,0:T(8,128)S(1)}) custom-call(s32[3]{0:T(128)S(1)} %pad_add_fusion.place, s32[16]{0:T(128)S(1)} %copy-done.6, f32[2,64,512]{2,1,0:T(8,128)S(1)} %get-tuple-element.35.refs_0_, f32[2,64,512]{2,1,0:T(8,128)S(1)} %collective-permute-done.1.refs_0_.refs_1_, ...), custom_call_target="tpu_custom_call" | custom-call | flops 67108864 | bytes 4194304 | tf_op jit(solution)/shard_map/gather_states/pallas_call | solution.py:252
  34.8 3.5 %collective-permute-start.10 = (f32[4,128,128]{2,1,0:T(8,128)S(1)}, f32[4,128,128]{2,1,0:T(8,128)S(1)}, u32[]{:S(2)}, u32[]{:S(2)}) collective-permute-start(f32[4,128,128]{2,1,0:T(8,128)S(1)} %get-tuple-element.40), channel_id=1, source_target_pairs={{0,8},{1,9},{2,10},{3,11},{4,12},{5,13},{6,14},{7,15},{8,16},{9,17... | collective-permute-start | bytes 786440 | tf_op jit(solution)/shard_map/ppermute | solution.py:263
  38.3 0.0 copy-done.1
  38.3 0.0 copy-done.4
  38.3 4.9 %inside.1.refs_6_.own = f32[64,4096]{1,0:T(8,128)S(1)} custom-call(s32[3]{0:T(128)S(1)} %pad_add_fusion.place, s32[16]{0:T(128)S(1)} %copy-done.6, bf16[64,4096]{1,0:T(8,128)(2,1)S(1)} %copy-done.1, bf16[64,4096]{1,0:T(8,128)(2,1)S(1)} %copy-done.2, bf16[64,4096]{1,0:T(8,128)(2,1)S(1)} %copy-done.4), custom_call_target="tpu_custom_call" | custom-call | flops 67108864 | bytes 3145728 | tf_op jit(solution)/shard_map/inside/pallas_call | solution.py:242
  43.2 0.0 collective-permute-done.4.refs_1_
  43.3 0.7 %collective-permute-done.5.refs_2_ = f32[2,64,512]{2,1,0:T(8,128)S(1)} collective-permute-done((f32[2,64,512]{2,1,0:T(8,128)S(1)}, f32[2,64,512]{2,1,0:T(8,128)S(1)}, u32[]{:S(2)}, u32[]{:S(2)}) %collective-permute-start.5) | collective-permute-done | bytes 262176 | tf_op jit(solution)/shard_map/ppermute | solution.py:208
  44.0 0.0 collective-permute-done.6.refs_3_
  44.0 0.0 collective-permute-done.10.refs_5_
  44.0 0.0 copy-start.5
  44.0 1.1 %reach_back.1 = (f32[64,512]{1,0:T(8,128)S(1)}, f32[64,512]{1,0:T(8,128)S(1)}, f32[64,512]{1,0:T(8,128)S(1)}, f32[64,512]{1,0:T(8,128)S(1)}, f32[64,512]{1,0:T(8...) custom-call(s32[3]{0:T(128)S(1)} %pad_add_fusion.place, s32[16]{0:T(128)S(1)} %copy-done.6, ...), custom_call_target="tpu_custom_call" | custom-call | flops 67108864 | bytes 4194304 | tf_op jit(solution)/shard_map/reach_back/pallas_call | solution.py:271
  45.1 0.1 collective-permute-start.14
  45.2 1.4 %collective-permute-start.15 = (f32[64,512]{1,0:T(8,128)S(1)}, f32[64,512]{1,0:T(8,128)S(1)}, u32[]{:S(2)}, u32[]{:S(2)}) collective-permute-start(f32[64,512]{1,0:T(8,128)S(1)} %get-tuple-element.46), channel_id=1, source_target_pairs={{0,5},{1,4},{2,7},{3,6},{4,1},{5,0},{6,3},{7,2},{8,13},{9,12},{10,... | collective-permute-start | bytes 393224 | tf_op jit(solution)/shard_map/ppermute | solution.py:208
  46.6 0.4 collective-permute-start.16
  47.0 1.5 %collective-permute-start.17 = (f32[64,512]{1,0:T(8,128)S(1)}, f32[64,512]{1,0:T(8,128)S(1)}, u32[]{:S(2)}, u32[]{:S(2)}) collective-permute-start(f32[64,512]{1,0:T(8,128)S(1)} %get-tuple-element.48), channel_id=1, source_target_pairs={{0,7},{1,6},{2,5},{3,4},{4,3},{5,2},{6,1},{7,0},{8,15},{9,14},{10,... | collective-permute-start | bytes 393224 | tf_op jit(solution)/shard_map/ppermute | solution.py:208
  48.5 1.3 %collective-permute-start.11 = (f32[64,512]{1,0:T(8,128)S(1)}, f32[64,512]{1,0:T(8,128)S(1)}, u32[]{:S(2)}, u32[]{:S(2)}) collective-permute-start(f32[64,512]{1,0:T(8,128)S(1)} %get-tuple-element.41), channel_id=1, source_target_pairs={{0,1},{1,0},{2,3},{3,2},{4,5},{5,4},{6,7},{7,6},{8,9},{9,8},{10,11... | collective-permute-start | bytes 393224 | tf_op jit(solution)/shard_map/ppermute | solution.py:208
  49.8 0.0 collective-permute-done.14.refs_1_
  49.8 0.7 %collective-permute-start.12 = (f32[64,512]{1,0:T(8,128)S(1)}, f32[64,512]{1,0:T(8,128)S(1)}, u32[]{:S(2)}, u32[]{:S(2)}) collective-permute-start(f32[64,512]{1,0:T(8,128)S(1)} %get-tuple-element.42), channel_id=1, source_target_pairs={{0,2},{1,3},{2,0},{3,1},{4,6},{5,7},{6,4},{7,5},{8,10},{9,11},{10,... | collective-permute-start | bytes 393224 | tf_op jit(solution)/shard_map/ppermute | solution.py:208
  50.5 0.0 collective-permute-done.15.refs_2_
  50.5 1.5 %collective-permute-start.13 = (f32[64,512]{1,0:T(8,128)S(1)}, f32[64,512]{1,0:T(8,128)S(1)}, u32[]{:S(2)}, u32[]{:S(2)}) collective-permute-start(f32[64,512]{1,0:T(8,128)S(1)} %get-tuple-element.43), channel_id=1, source_target_pairs={{0,3},{1,2},{2,1},{3,0},{4,7},{5,6},{6,5},{7,4},{8,11},{9,10},{10,... | collective-permute-start | bytes 393224 | tf_op jit(solution)/shard_map/ppermute | solution.py:208
  52.1 2.4 %collective-permute-done.16.refs_3_ = f32[64,512]{1,0:T(8,128)S(1)} collective-permute-done((f32[64,512]{1,0:T(8,128)S(1)}, f32[64,512]{1,0:T(8,128)S(1)}, u32[]{:S(2)}, u32[]{:S(2)}) %collective-permute-start.16) | collective-permute-done | bytes 131104 | tf_op jit(solution)/shard_map/ppermute | solution.py:208
  54.5 0.0 collective-permute-done.17.refs_4_
  54.5 0.0 copy-done.5
  54.5 1.5 %finish.2.refs_3_ = bf16[64,4096]{1,0:T(8,128)(2,1)} custom-call(s32[3]{0:T(128)S(1)} %pad_add_fusion.place, s32[16]{0:T(128)S(1)} %copy-done.6, f32[64,4096]{1,0:T(8,128)S(1)} %inside.1.refs_6_.own, f32[1,4096]{1,0:T(1,128)S(1)} %bitcast.4, f32[64,512]{1,0:T(8,128)S(1)} %get-tuple-element.44.refs_0_, f32[64,512]{1,0:T(8,128)S(1)} %collective-permute-done.14.refs_1_, ...), custom_call_target="tpu_custom_call" | custom-call | bytes 2097152 | tf_op jit(solution)/shard_map/finish/pallas_call | solution.py:288
  56.0 1.0 %collective-permute-done.11.refs_0_ = f32[64,512]{1,0:T(8,128)S(1)} collective-permute-done((f32[64,512]{1,0:T(8,128)S(1)}, f32[64,512]{1,0:T(8,128)S(1)}, u32[]{:S(2)}, u32[]{:S(2)}) %collective-permute-start.11) | collective-permute-done | bytes 131104 | tf_op jit(solution)/shard_map/ppermute | solution.py:208
  57.0 3.8 %collective-permute-done.12.refs_1_ = f32[64,512]{1,0:T(8,128)S(1)} collective-permute-done((f32[64,512]{1,0:T(8,128)S(1)}, f32[64,512]{1,0:T(8,128)S(1)}, u32[]{:S(2)}, u32[]{:S(2)}) %collective-permute-start.12) | collective-permute-done | bytes 131104 | tf_op jit(solution)/shard_map/ppermute | solution.py:208
  60.8 0.0 collective-permute-done.13.refs_2_
  60.8 1.4 %finish.3 = bf16[64,4096]{1,0:T(8,128)(2,1)} custom-call(s32[3]{0:T(128)S(1)} %pad_add_fusion.place, s32[16]{0:T(128)S(1)} %copy-done.6, f32[64,4096]{1,0:T(8,128)S(1)} %inside.1.refs_6_.own, f32[1,4096]{1,0:T(1,128)S(1)} %bitcast.5, f32[64,512]{1,0:T(8,128)S(1)} %collective-permute-done.11.refs_0_, ...), custom_call_target="tpu_custom_call", output_to_operand_aliasing={{}: (7, {})} | custom-call | bytes 2097152 | tf_op jit(solution)/shard_map/finish/pallas_call | solution.py:288
Async XLA Ops:
  0.1 1.0 %copy-start = (bf16[64,4096]{1,0:T(8,128)(2,1)S(1)}, bf16[64,4096]{1,0:T(8,128)(2,1)}, u32[]{:S(2)}) copy-start(bf16[64,4096]{1,0:T(8,128)(2,1)} %queries.5) | copy-start | bytes 1572868
  1.1 1.0 %copy-start.2 = (bf16[64,4096]{1,0:T(8,128)(2,1)S(1)}, bf16[64,4096]{1,0:T(8,128)(2,1)}, u32[]{:S(2)}) copy-start(bf16[64,4096]{1,0:T(8,128)(2,1)} %keys.3) | copy-start | bytes 1572868
  2.2 1.0 %copy-start.3 = (bf16[64,4096]{1,0:T(8,128)(2,1)S(1)}, bf16[64,4096]{1,0:T(8,128)(2,1)}, u32[]{:S(2)}) copy-start(bf16[64,4096]{1,0:T(8,128)(2,1)} %values.3) | copy-start | bytes 1572868
  4.4 4.6 %collective-permute-start = (f32[4,3,64,512]{3,2,1,0:T(8,128)S(1)}, f32[4,3,64,512]{3,2,1,0:T(8,128)S(1)}, u32[]{:S(2)}, u32[]{:S(2)}) collective-permute-start(f32[4,3,64,512]{3,2,1,0:T(8,128)S(1)} %get-tuple-element.27), channel_id=1, source_target_pairs={{0,4},{1,5},{2,6},{3,7},{4,0},{5,1},{6,2},{7,3},{8,12},{9,13},{10,... | collective-permute-start | bytes 4718600 | tf_op jit(solution)/shard_map/ppermute | solution.py:208
  5.0 9.7 %collective-permute-start.1 = (f32[2,64,512]{2,1,0:T(8,128)S(1)}, f32[2,64,512]{2,1,0:T(8,128)S(1)}, u32[]{:S(2)}, u32[]{:S(2)}) collective-permute-start(f32[2,64,512]{2,1,0:T(8,128)S(1)} %get-tuple-element.28), channel_id=1, source_target_pairs={{0,1},{1,0},{2,3},{3,2},{4,5},{5,4},{6,7},{7,6},{8,9},{9,8},{10,11... | collective-permute-start | bytes 786440 | tf_op jit(solution)/shard_map/ppermute | solution.py:208
  7.5 14.8 %collective-permute-start.2 = (f32[2,64,512]{2,1,0:T(8,128)S(1)}, f32[2,64,512]{2,1,0:T(8,128)S(1)}, u32[]{:S(2)}, u32[]{:S(2)}) collective-permute-start(f32[2,64,512]{2,1,0:T(8,128)S(1)} %get-tuple-element.29), channel_id=1, source_target_pairs={{0,2},{1,3},{2,0},{3,1},{4,6},{5,7},{6,4},{7,5},{8,10},{9,11},{10,... | collective-permute-start | bytes 786440 | tf_op jit(solution)/shard_map/ppermute | solution.py:208
  9.0 13.3 %collective-permute-start.3 = (f32[2,64,512]{2,1,0:T(8,128)S(1)}, f32[2,64,512]{2,1,0:T(8,128)S(1)}, u32[]{:S(2)}, u32[]{:S(2)}) collective-permute-start(f32[2,64,512]{2,1,0:T(8,128)S(1)} %get-tuple-element.30), channel_id=1, source_target_pairs={{0,3},{1,2},{2,1},{3,0},{4,7},{5,6},{6,5},{7,4},{8,11},{9,10},{10,... | collective-permute-start | bytes 786440 | tf_op jit(solution)/shard_map/ppermute | solution.py:208
  9.1 24.4 %copy-start.6 = (s32[16]{0:T(128)S(1)}, s32[16]{0:T(128)}, u32[]{:S(2)}) copy-start(s32[16]{0:T(128)} %lengths.9) | copy-start | bytes 196
  9.1 16.8 %collective-permute-start.7 = (f32[2,64,512]{2,1,0:T(8,128)S(1)}, f32[2,64,512]{2,1,0:T(8,128)S(1)}, u32[]{:S(2)}, u32[]{:S(2)}) collective-permute-start(f32[2,64,512]{2,1,0:T(8,128)S(1)} %get-tuple-element.36), channel_id=1, source_target_pairs={{0,1},{1,0},{2,3},{3,2},{4,5},{5,4},{6,7},{7,6},{8,9},{9,8},{10,11... | collective-permute-start | bytes 786440 | tf_op jit(solution)/shard_map/ppermute | solution.py:208
  11.2 22.4 %collective-permute-start.8 = (f32[2,64,512]{2,1,0:T(8,128)S(1)}, f32[2,64,512]{2,1,0:T(8,128)S(1)}, u32[]{:S(2)}, u32[]{:S(2)}) collective-permute-start(f32[2,64,512]{2,1,0:T(8,128)S(1)} %get-tuple-element.37), channel_id=1, source_target_pairs={{0,2},{1,3},{2,0},{3,1},{4,6},{5,7},{6,4},{7,5},{8,10},{9,11},{10,... | collective-permute-start | bytes 786440 | tf_op jit(solution)/shard_map/ppermute | solution.py:208
  14.7 18.8 %collective-permute-start.9 = (f32[2,64,512]{2,1,0:T(8,128)S(1)}, f32[2,64,512]{2,1,0:T(8,128)S(1)}, u32[]{:S(2)}, u32[]{:S(2)}) collective-permute-start(f32[2,64,512]{2,1,0:T(8,128)S(1)} %get-tuple-element.38), channel_id=1, source_target_pairs={{0,3},{1,2},{2,1},{3,0},{4,7},{5,6},{6,5},{7,4},{8,11},{9,10},{10,... | collective-permute-start | bytes 786440 | tf_op jit(solution)/shard_map/ppermute | solution.py:208
  22.9 20.3 %collective-permute-start.4 = (f32[2,64,512]{2,1,0:T(8,128)S(1)}, f32[2,64,512]{2,1,0:T(8,128)S(1)}, u32[]{:S(2)}, u32[]{:S(2)}) collective-permute-start(f32[2,64,512]{2,1,0:T(8,128)S(1)} %get-tuple-element.32), channel_id=1, source_target_pairs={{0,1},{1,0},{2,3},{3,2},{4,5},{5,4},{6,7},{7,6},{8,9},{9,8},{10,11... | collective-permute-start | bytes 786440 | tf_op jit(solution)/shard_map/ppermute | solution.py:208
  23.9 20.1 %collective-permute-start.5 = (f32[2,64,512]{2,1,0:T(8,128)S(1)}, f32[2,64,512]{2,1,0:T(8,128)S(1)}, u32[]{:S(2)}, u32[]{:S(2)}) collective-permute-start(f32[2,64,512]{2,1,0:T(8,128)S(1)} %get-tuple-element.33), channel_id=1, source_target_pairs={{0,2},{1,3},{2,0},{3,1},{4,6},{5,7},{6,4},{7,5},{8,10},{9,11},{10,... | collective-permute-start | bytes 786440 | tf_op jit(solution)/shard_map/ppermute | solution.py:208
  26.0 18.0 %collective-permute-start.6 = (f32[2,64,512]{2,1,0:T(8,128)S(1)}, f32[2,64,512]{2,1,0:T(8,128)S(1)}, u32[]{:S(2)}, u32[]{:S(2)}) collective-permute-start(f32[2,64,512]{2,1,0:T(8,128)S(1)} %get-tuple-element.34), channel_id=1, source_target_pairs={{0,3},{1,2},{2,1},{3,0},{4,7},{5,6},{6,5},{7,4},{8,11},{9,10},{10,... | collective-permute-start | bytes 786440 | tf_op jit(solution)/shard_map/ppermute | solution.py:208
  33.5 4.8 %copy-start.1 = (bf16[64,4096]{1,0:T(8,128)(2,1)S(1)}, bf16[64,4096]{1,0:T(8,128)(2,1)}, u32[]{:S(2)}) copy-start(bf16[64,4096]{1,0:T(8,128)(2,1)} %queries.5) | copy-start | bytes 1572868
  33.5 4.8 %copy-start.4 = (bf16[64,4096]{1,0:T(8,128)(2,1)S(1)}, bf16[64,4096]{1,0:T(8,128)(2,1)}, u32[]{:S(2)}) copy-start(bf16[64,4096]{1,0:T(8,128)(2,1)} %values.3) | copy-start | bytes 1572868
  34.8 9.2 %collective-permute-start.10 = (f32[4,128,128]{2,1,0:T(8,128)S(1)}, f32[4,128,128]{2,1,0:T(8,128)S(1)}, u32[]{:S(2)}, u32[]{:S(2)}) collective-permute-start(f32[4,128,128]{2,1,0:T(8,128)S(1)} %get-tuple-element.40), channel_id=1, source_target_pairs={{0,8},{1,9},{2,10},{3,11},{4,12},{5,13},{6,14},{7,15},{8,16},{9,17... | collective-permute-start | bytes 786440 | tf_op jit(solution)/shard_map/ppermute | solution.py:263
  44.0 10.5 %copy-start.5 = (f32[4096]{0:T(1024)S(1)}, f32[4096]{0:T(1024)}, u32[]{:S(2)}) copy-start(f32[4096]{0:T(1024)} %param.9) | copy-start | bytes 49156
  45.1 4.7 %collective-permute-start.14 = (f32[64,512]{1,0:T(8,128)S(1)}, f32[64,512]{1,0:T(8,128)S(1)}, u32[]{:S(2)}, u32[]{:S(2)}) collective-permute-start(f32[64,512]{1,0:T(8,128)S(1)} %get-tuple-element.45), channel_id=1, source_target_pairs={{0,4},{1,5},{2,6},{3,7},{4,0},{5,1},{6,2},{7,3},{8,12},{9,13},{10,... | collective-permute-start | bytes 393224 | tf_op jit(solution)/shard_map/ppermute | solution.py:208
  45.2 5.4 %collective-permute-start.15 = (f32[64,512]{1,0:T(8,128)S(1)}, f32[64,512]{1,0:T(8,128)S(1)}, u32[]{:S(2)}, u32[]{:S(2)}) collective-permute-start(f32[64,512]{1,0:T(8,128)S(1)} %get-tuple-element.46), channel_id=1, source_target_pairs={{0,5},{1,4},{2,7},{3,6},{4,1},{5,0},{6,3},{7,2},{8,13},{9,12},{10,... | collective-permute-start | bytes 393224 | tf_op jit(solution)/shard_map/ppermute | solution.py:208
  46.6 7.9 %collective-permute-start.16 = (f32[64,512]{1,0:T(8,128)S(1)}, f32[64,512]{1,0:T(8,128)S(1)}, u32[]{:S(2)}, u32[]{:S(2)}) collective-permute-start(f32[64,512]{1,0:T(8,128)S(1)} %get-tuple-element.47), channel_id=1, source_target_pairs={{0,6},{1,7},{2,4},{3,5},{4,2},{5,3},{6,0},{7,1},{8,14},{9,15},{10,... | collective-permute-start | bytes 393224 | tf_op jit(solution)/shard_map/ppermute | solution.py:208
  47.0 7.5 %collective-permute-start.17 = (f32[64,512]{1,0:T(8,128)S(1)}, f32[64,512]{1,0:T(8,128)S(1)}, u32[]{:S(2)}, u32[]{:S(2)}) collective-permute-start(f32[64,512]{1,0:T(8,128)S(1)} %get-tuple-element.48), channel_id=1, source_target_pairs={{0,7},{1,6},{2,5},{3,4},{4,3},{5,2},{6,1},{7,0},{8,15},{9,14},{10,... | collective-permute-start | bytes 393224 | tf_op jit(solution)/shard_map/ppermute | solution.py:208
  48.5 8.5 %collective-permute-start.11 = (f32[64,512]{1,0:T(8,128)S(1)}, f32[64,512]{1,0:T(8,128)S(1)}, u32[]{:S(2)}, u32[]{:S(2)}) collective-permute-start(f32[64,512]{1,0:T(8,128)S(1)} %get-tuple-element.41), channel_id=1, source_target_pairs={{0,1},{1,0},{2,3},{3,2},{4,5},{5,4},{6,7},{7,6},{8,9},{9,8},{10,11... | collective-permute-start | bytes 393224 | tf_op jit(solution)/shard_map/ppermute | solution.py:208
  49.8 11.0 %collective-permute-start.12 = (f32[64,512]{1,0:T(8,128)S(1)}, f32[64,512]{1,0:T(8,128)S(1)}, u32[]{:S(2)}, u32[]{:S(2)}) collective-permute-start(f32[64,512]{1,0:T(8,128)S(1)} %get-tuple-element.42), channel_id=1, source_target_pairs={{0,2},{1,3},{2,0},{3,1},{4,6},{5,7},{6,4},{7,5},{8,10},{9,11},{10,... | collective-permute-start | bytes 393224 | tf_op jit(solution)/shard_map/ppermute | solution.py:208
  50.5 10.3 %collective-permute-start.13 = (f32[64,512]{1,0:T(8,128)S(1)}, f32[64,512]{1,0:T(8,128)S(1)}, u32[]{:S(2)}, u32[]{:S(2)}) collective-permute-start(f32[64,512]{1,0:T(8,128)S(1)} %get-tuple-element.43), channel_id=1, source_target_pairs={{0,3},{1,2},{2,1},{3,0},{4,7},{5,6},{6,5},{7,4},{8,11},{9,10},{10,... | collective-permute-start | bytes 393224 | tf_op jit(solution)/shard_map/ppermute | solution.py:208

commit v4 on v3

--- a/solution.py
+++ b/solution.py
@@ -51,35 +51,36 @@
             for i, source in enumerate(sources)
         ]
 
-    for d in range(members):
+    order = list(reversed(range(half))) + list(range(half, members))
+    for d in order:
         for copy in copies(d):
             copy.start()
-    for d in range(members):
+    for d in order:
         for i, copy in enumerate(copies(d)):
             copy.wait()
             part = buffers[i][d].astype(jnp.float32)
             if d < half:
-                near[d][i] = part
+                near[half - 1 - d][i] = part
             else:
                 cross[d - half, i] = part
 
 
 def forward(half, swapped, *outs):
     for e in range(1, half):
-        outs[e - 1][...] = swapped[e, 0:2]
+        outs[half - 1 - e][...] = swapped[e, 0:2]
 
 
 def join_queries(half, width, gates, place, queries, swapped, *refs):
     outs = refs[gates:]
     me = place[0]
     for e in range(half):
-        outs[e][0] = queries[:, columns_of(me ^ e, width)].astype(jnp.float32)
-        outs[e][1] = swapped[e, 2]
+        outs[half - 1 - e][0] = queries[:, columns_of(me ^ e, width)].astype(jnp.float32)
+        outs[half - 1 - e][1] = swapped[e, 2]
 
 
 def gather_states(members, heads, docs, rows, place, lengths, *refs):
     half = members // CORES
-    parts = refs[:members]
+    parts = refs[:half][::-1] + refs[half:members][::-1]
     carry_out, total_out, key_blocks, value_blocks = refs[members + 1 :]
     me, base = place[0], place[1]
     row = lax.broadcasted_iota(jnp.int32, (rows, heads * HEAD_DIM), 0)
@@ -126,9 +127,9 @@
 
 def reach_back(members, heads, docs, rows, place, lengths, *refs):
     half = members // CORES
-    query_parts = refs[:half]
+    query_parts = refs[:half][::-1]
     carry, earlier = refs[half : half + 2]
-    outs = refs[half + 3 :]
+    outs = refs[half + 3 :][::-1]
     me, base = place[0], place[1]
     for e in range(half):
         for side in range(CORES):
@@ -207,6 +208,7 @@
         pairs = [(g, g - g % members + (g % members ^ d)) for g in range(devices)]
         return lax.ppermute(part, everyone, pairs)
 
+    downward = list(reversed(range(half)))
     block_bytes = rows * columns * 4
     parts = call(
         functools.partial(spread, members, width),
@@ -215,9 +217,8 @@
         [SMEM, HBM, HBM, HBM],
         [VMEM] * (half + 1),
         [pltpu.VMEM((members, rows, width), bf16)] * 3 + [pltpu.SemaphoreType.DMA((3, members))],
-        moved=4 * block_bytes,
-    )(place, queries, keys, values)
-    near_got = [parts[0]] + [swap(parts[e], e) for e in range(1, half)]
+    )(place, *[pltpu.with_memory_space_constraint(x, pltpu.HBM) for x in (queries, keys, values)])
+    near_got = [swap(part, e) if e else part for e, part in zip(downward, parts)]
     swapped = swap(parts[half], half)
     far_parts = call(
         functools.partial(forward, half),
@@ -227,8 +228,8 @@
         [VMEM] * (half - 1),
         moved=2 * block_bytes,
     )(swapped)
-    far_got = [swapped] + [swap(part, e + 1) for e, part in enumerate(far_parts)]
-    gates = near_got[1:]
+    far_got = [swap(part, e) for e, part in zip(downward, far_parts)] + [swapped]
+    gates = near_got[:-1]
     query_parts = call(
         functools.partial(join_queries, half, width, len(gates)),
         "join_queries",
@@ -237,7 +238,7 @@
         [VMEM] * half,
         moved=2 * block_bytes,
     )(place, queries, swapped, *gates)
-    query_got = [query_parts[0]] + [swap(query_parts[e], e) for e in range(1, half)]
+    query_got = [swap(part, e) if e else part for e, part in zip(downward, query_parts)]
 
     own = call(
         functools.partial(inside, head_count, docs, rows),
@@ -258,7 +259,7 @@
         [pltpu.VMEM((members, rows, width), bf16)] * 2,
         flops=2 * rows * HEAD_DIM * columns,
         moved=4 * block_bytes,
-    )(place, lengths, *near_got, *far_got, query_parts[0])
+    )(place, lengths, *near_got, *far_got, query_parts[-1])
     up = [(g, g + members) for g in range(devices - members)]
     moving = lax.ppermute(total, everyone, up)
     earlier = moving
@@ -277,11 +278,11 @@
         flops=2 * rows * HEAD_DIM * columns,
         moved=4 * block_bytes,
     )(place, lengths, *query_got, carry, earlier, own)
-    crossed_got = [crossed[0]] + [swap(crossed[d], d) for d in range(1, members)]
+    crossed_got = [swap(crossed[members - 1 - d], d) if d else crossed[-1] for d in range(members)]
 
     gain = norm_gain.reshape(1, columns)
-    first = [0] + list(range(half, members))
-    last = list(range(1, half))
+    last = [d for d in range(members) if d % half in (1, 2)]
+    first = [d for d in reversed(range(members)) if d not in last]
     out = None
     for chosen in (first, last):
         more = [] if out is None else [out]

time: 62.5 us -> 59.2 us (0.947)
  local copies, waits for them, and re-layouts: 3.14 us -> 0.02 us
  starting transfers between devices: 26.6 us -> 25.2 us
  Pallas kernels: 12.1 us -> 12.9 us
    unnamed x14 -> x10, local copies, waits for them, and re-layouts: 3.14 us -> 0.02 us
    ppermute x17, starting transfers between devices: 23.1 us -> 21.7 us  [swap(): return lax.ppermute(part, everyone, pairs)]
    pallas_call x1, Pallas kernels: 1.23 us -> 2.09 us  [body(): call(functools.partial(spread, members, width), 'spread', [shape(2, rows,...]
  transfers between devices with their start and end apart: 18 -> 18, of which waited for: 8 -> 12; matrix products, arithmetic and copies ran while one was open for 0% -> 0% of each run, Pallas kernels for 13% -> 14%
where the time goes in v4:
time: 59.2 us; the launch traced here: 59 us
  starting transfers between devices  25.2 us (43%)
  waiting for transfers between devices  20.7 us (35%)
  Pallas kernels  12.9 us (22%)
    ppermute x17, starting transfers between devices, swap(): return lax.ppermute(part, everyone, pairs)  21.7 us
    ppermute x17, waiting for transfers between devices, swap(): return lax.ppermute(part, everyone, pairs)  20.7 us
    pallas_call x1, Pallas kernels, body(): call(functools.partial(inside, head_count, docs, rows), 'inside', shape(r...  4.93 us
    ppermute x1, starting transfers between devices, body(): moving = lax.ppermute(total, everyone, up)  3.49 us
    pallas_call x2, Pallas kernels, body(): call(functools.partial(finish, chosen, heads, docs, rows), 'finish', shap...  2.95 us
    pallas_call x1, Pallas kernels, body(): call(functools.partial(spread, members, width), 'spread', [shape(2, rows,...  2.09 us
    pallas_call x1, Pallas kernels, body(): call(functools.partial(gather_states, members, heads, docs, rows), 'gathe...  1.22 us
  transfers between devices with their start and end apart: 18, of which 12 were waited for; matrix products, arithmetic and copies ran while one was open for 0% of the time, Pallas kernels for 14%

profile of v4, /device:TPU:0, one launch (start us, length us, event | category | flops | bytes accessed | tf_op | source)
XLA Modules:
  0.0 59.0 jit_solution(7622843376501490706)
XLA Ops:
  0.0 0.1 pad_add_fusion.place
  0.1 0.0 copy-start
  0.1 2.1 %spread.1 = (f32[2,64,512]{2,1,0:T(8,128)S(1)}, f32[2,64,512]{2,1,0:T(8,128)S(1)}, f32[2,64,512]{2,1,0:T(8,128)S(1)}, f32[2,64,512]{2,1,0:T(8,128)S(1)}, f32[4,3,64,512]{3,2,1,0:T(8,128)S(1)}) custom-call(s32[3]{0:T(128)S(1)} %pad_add_fusion.place, bf16[64,4096]{1,0:T(8,128)(2,1)} %queries.5, bf16[64,4096]{1,0:T(8,128)(2,1)} %keys.3, bf16[64,4096]{1,0:T(8,128)(2,1)} %values.3), custom_call_target="tpu_custom_call" | custom-call | tf_op jit(solution)/shard_map/spread/pallas_call | solution.py:213
  2.2 0.5 collective-permute-start
  2.7 3.5 %collective-permute-start.1 = (f32[2,64,512]{2,1,0:T(8,128)S(1)}, f32[2,64,512]{2,1,0:T(8,128)S(1)}, u32[]{:S(2)}, u32[]{:S(2)}) collective-permute-start(f32[2,64,512]{2,1,0:T(8,128)S(1)} %get-tuple-element.28), channel_id=1, source_target_pairs={{0,3},{1,2},{2,1},{3,0},{4,7},{5,6},{6,5},{7,4},{8,11},{9,10},{10,... | collective-permute-start | bytes 786440 | tf_op jit(solution)/shard_map/ppermute | solution.py:209
  6.2 0.5 collective-permute-start.2
  6.7 0.1 collective-permute-start.3
  6.9 0.0 collective-permute-done.swapped.refs_7_
  6.9 0.1 forward.1
  6.9 0.0 copy-start.4
  6.9 2.9 %collective-permute-start.7 = (f32[2,64,512]{2,1,0:T(8,128)S(1)}, f32[2,64,512]{2,1,0:T(8,128)S(1)}, u32[]{:S(2)}, u32[]{:S(2)}) collective-permute-start(f32[2,64,512]{2,1,0:T(8,128)S(1)} %get-tuple-element.36), channel_id=1, source_target_pairs={{0,3},{1,2},{2,1},{3,0},{4,7},{5,6},{6,5},{7,4},{8,11},{9,10},{10,... | collective-permute-start | bytes 786440 | tf_op jit(solution)/shard_map/ppermute | solution.py:209
  9.8 0.5 collective-permute-start.8
  10.3 3.1 %collective-permute-done.1.refs_0_ = f32[2,64,512]{2,1,0:T(8,128)S(1)} collective-permute-done((f32[2,64,512]{2,1,0:T(8,128)S(1)}, f32[2,64,512]{2,1,0:T(8,128)S(1)}, u32[]{:S(2)}, u32[]{:S(2)}) %collective-permute-start.1) | collective-permute-done | bytes 262176 | tf_op jit(solution)/shard_map/ppermute | solution.py:209
  13.4 1.9 %collective-permute-start.9 = (f32[2,64,512]{2,1,0:T(8,128)S(1)}, f32[2,64,512]{2,1,0:T(8,128)S(1)}, u32[]{:S(2)}, u32[]{:S(2)}) collective-permute-start(f32[2,64,512]{2,1,0:T(8,128)S(1)} %get-tuple-element.38), channel_id=1, source_target_pairs={{0,1},{1,0},{2,3},{3,2},{4,5},{5,4},{6,7},{7,6},{8,9},{9,8},{10,11... | collective-permute-start | bytes 786440 | tf_op jit(solution)/shard_map/ppermute | solution.py:209
  15.3 3.8 %collective-permute-done.2.refs_1_ = f32[2,64,512]{2,1,0:T(8,128)S(1)} collective-permute-done((f32[2,64,512]{2,1,0:T(8,128)S(1)}, f32[2,64,512]{2,1,0:T(8,128)S(1)}, u32[]{:S(2)}, u32[]{:S(2)}) %collective-permute-start.2) | collective-permute-done | bytes 262176 | tf_op jit(solution)/shard_map/ppermute | solution.py:209
  19.1 0.4 collective-permute-done.3.refs_2_
  19.5 0.0 copy-done
  19.5 0.6 %join_queries.1 = (f32[2,64,512]{2,1,0:T(8,128)S(1)}, f32[2,64,512]{2,1,0:T(8,128)S(1)}, f32[2,64,512]{2,1,0:T(8,128)S(1)}, f32[2,64,512]{2,1,0:T(8,128)S(1)}) custom-call(s32[3]{0:T(128)S(1)} %pad_add_fusion.place, bf16[64,4096]{1,0:T(8,128)(2,1)S(1)} %copy-done, f32[4,3,64,512]{3,2,1,0:T(8,128)S(1)} %collective-permute-done.swapped.refs_7_, ...), custom_call_target="tpu_custom_call" | custom-call | bytes 2097152 | tf_op jit(solution)/shard_map/join_queries/pallas_call | solution.py:233
  20.1 1.7 %collective-permute-start.4 = (f32[2,64,512]{2,1,0:T(8,128)S(1)}, f32[2,64,512]{2,1,0:T(8,128)S(1)}, u32[]{:S(2)}, u32[]{:S(2)}) collective-permute-start(f32[2,64,512]{2,1,0:T(8,128)S(1)} %get-tuple-element.31), channel_id=1, source_target_pairs={{0,3},{1,2},{2,1},{3,0},{4,7},{5,6},{6,5},{7,4},{8,11},{9,10},{10,... | collective-permute-start | bytes 786440 | tf_op jit(solution)/shard_map/ppermute | solution.py:209
  21.8 1.4 %collective-permute-start.5 = (f32[2,64,512]{2,1,0:T(8,128)S(1)}, f32[2,64,512]{2,1,0:T(8,128)S(1)}, u32[]{:S(2)}, u32[]{:S(2)}) collective-permute-start(f32[2,64,512]{2,1,0:T(8,128)S(1)} %get-tuple-element.32), channel_id=1, source_target_pairs={{0,2},{1,3},{2,0},{3,1},{4,6},{5,7},{6,4},{7,5},{8,10},{9,11},{10,... | collective-permute-start | bytes 786440 | tf_op jit(solution)/shard_map/ppermute | solution.py:209
  23.1 1.6 %collective-permute-done.7.refs_4_ = f32[2,64,512]{2,1,0:T(8,128)S(1)} collective-permute-done((f32[2,64,512]{2,1,0:T(8,128)S(1)}, f32[2,64,512]{2,1,0:T(8,128)S(1)}, u32[]{:S(2)}, u32[]{:S(2)}) %collective-permute-start.7) | collective-permute-done | bytes 262176 | tf_op jit(solution)/shard_map/ppermute | solution.py:209
  24.7 1.9 %collective-permute-start.6 = (f32[2,64,512]{2,1,0:T(8,128)S(1)}, f32[2,64,512]{2,1,0:T(8,128)S(1)}, u32[]{:S(2)}, u32[]{:S(2)}) collective-permute-start(f32[2,64,512]{2,1,0:T(8,128)S(1)} %get-tuple-element.33), channel_id=1, source_target_pairs={{0,1},{1,0},{2,3},{3,2},{4,5},{5,4},{6,7},{7,6},{8,9},{9,8},{10,11... | collective-permute-start | bytes 786440 | tf_op jit(solution)/shard_map/ppermute | solution.py:209
  26.6 3.7 %collective-permute-done.8.refs_5_ = f32[2,64,512]{2,1,0:T(8,128)S(1)} collective-permute-done((f32[2,64,512]{2,1,0:T(8,128)S(1)}, f32[2,64,512]{2,1,0:T(8,128)S(1)}, u32[]{:S(2)}, u32[]{:S(2)}) %collective-permute-start.8) | collective-permute-done | bytes 262176 | tf_op jit(solution)/shard_map/ppermute | solution.py:209
  30.3 0.5 collective-permute-done.9.refs_6_
  30.8 0.0 copy-done.4
  30.8 0.0 copy-start.1
  30.8 0.0 copy-start.2
  30.8 1.2 %gather_states.1 = (f32[8,4,128,128]{3,2,1,0:T(8,128)S(1)}, f32[4,128,128]{2,1,0:T(8,128)S(1)}) custom-call(s32[3]{0:T(128)S(1)} %pad_add_fusion.place, s32[16]{0:T(128)S(1)} %copy-done.4, f32[2,64,512]{2,1,0:T(8,128)S(1)} %collective-permute-done.1.refs_0_, f32[2,64,512]{2,1,0:T(8,128)S(1)} %collective-permute-done.2.refs_1_, ...), custom_call_target="tpu_custom_call" | custom-call | flops 67108864 | bytes 4194304 | tf_op jit(solution)/shard_map/gather_states/pallas_call | solution.py:253
  32.0 3.5 %collective-permute-start.10 = (f32[4,128,128]{2,1,0:T(8,128)S(1)}, f32[4,128,128]{2,1,0:T(8,128)S(1)}, u32[]{:S(2)}, u32[]{:S(2)}) collective-permute-start(f32[4,128,128]{2,1,0:T(8,128)S(1)} %get-tuple-element.40), channel_id=1, source_target_pairs={{0,8},{1,9},{2,10},{3,11},{4,12},{5,13},{6,14},{7,15},{8,16},{9,17... | collective-permute-start | bytes 786440 | tf_op jit(solution)/shard_map/ppermute | solution.py:264
  35.5 0.0 copy-done.1
  35.5 0.0 copy-done.2
  35.5 4.9 %inside.1.refs_6_.own = f32[64,4096]{1,0:T(8,128)S(1)} custom-call(s32[3]{0:T(128)S(1)} %pad_add_fusion.place, s32[16]{0:T(128)S(1)} %copy-done.4, bf16[64,4096]{1,0:T(8,128)(2,1)S(1)} %copy-done, bf16[64,4096]{1,0:T(8,128)(2,1)S(1)} %copy-done.1, bf16[64,4096]{1,0:T(8,128)(2,1)S(1)} %copy-done.2), custom_call_target="tpu_custom_call" | custom-call | flops 67108864 | bytes 3145728 | tf_op jit(solution)/shard_map/inside/pallas_call | solution.py:243
  40.5 0.0 collective-permute-done.4.refs_0_
  40.5 0.7 %collective-permute-done.5.refs_1_ = f32[2,64,512]{2,1,0:T(8,128)S(1)} collective-permute-done((f32[2,64,512]{2,1,0:T(8,128)S(1)}, f32[2,64,512]{2,1,0:T(8,128)S(1)}, u32[]{:S(2)}, u32[]{:S(2)}) %collective-permute-start.5) | collective-permute-done | bytes 262176 | tf_op jit(solution)/shard_map/ppermute | solution.py:209
  41.2 0.4 collective-permute-done.6.refs_2_
  41.6 0.0 collective-permute-done.10.refs_5_
  41.6 0.0 copy-start.3
  41.6 1.0 %reach_back.1 = (f32[64,512]{1,0:T(8,128)S(1)}, f32[64,512]{1,0:T(8,128)S(1)}, f32[64,512]{1,0:T(8,128)S(1)}, f32[64,512]{1,0:T(8,128)S(1)}, f32[64,512]{1,0:T(8...) custom-call(s32[3]{0:T(128)S(1)} %pad_add_fusion.place, s32[16]{0:T(128)S(1)} %copy-done.4, ...), custom_call_target="tpu_custom_call" | custom-call | flops 67108864 | bytes 4194304 | tf_op jit(solution)/shard_map/reach_back/pallas_call | solution.py:272
  42.6 0.8 %collective-permute-start.15 = (f32[64,512]{1,0:T(8,128)S(1)}, f32[64,512]{1,0:T(8,128)S(1)}, u32[]{:S(2)}, u32[]{:S(2)}) collective-permute-start(f32[64,512]{1,0:T(8,128)S(1)} %get-tuple-element.45), channel_id=1, source_target_pairs={{0,7},{1,6},{2,5},{3,4},{4,3},{5,2},{6,1},{7,0},{8,15},{9,14},{10,... | collective-permute-start | bytes 393224 | tf_op jit(solution)/shard_map/ppermute | solution.py:209
  43.4 0.8 %collective-permute-start.16 = (f32[64,512]{1,0:T(8,128)S(1)}, f32[64,512]{1,0:T(8,128)S(1)}, u32[]{:S(2)}, u32[]{:S(2)}) collective-permute-start(f32[64,512]{1,0:T(8,128)S(1)} %get-tuple-element.46), channel_id=1, source_target_pairs={{0,4},{1,5},{2,6},{3,7},{4,0},{5,1},{6,2},{7,3},{8,12},{9,13},{10,... | collective-permute-start | bytes 393224 | tf_op jit(solution)/shard_map/ppermute | solution.py:209
  44.2 1.5 %collective-permute-start.17 = (f32[64,512]{1,0:T(8,128)S(1)}, f32[64,512]{1,0:T(8,128)S(1)}, u32[]{:S(2)}, u32[]{:S(2)}) collective-permute-start(f32[64,512]{1,0:T(8,128)S(1)} %get-tuple-element.47), channel_id=1, source_target_pairs={{0,3},{1,2},{2,1},{3,0},{4,7},{5,6},{6,5},{7,4},{8,11},{9,10},{10,... | collective-permute-start | bytes 393224 | tf_op jit(solution)/shard_map/ppermute | solution.py:209
  45.7 1.5 %collective-permute-start.11 = (f32[64,512]{1,0:T(8,128)S(1)}, f32[64,512]{1,0:T(8,128)S(1)}, u32[]{:S(2)}, u32[]{:S(2)}) collective-permute-start(f32[64,512]{1,0:T(8,128)S(1)} %get-tuple-element.41), channel_id=1, source_target_pairs={{0,1},{1,0},{2,3},{3,2},{4,5},{5,4},{6,7},{7,6},{8,9},{9,8},{10,11... | collective-permute-start | bytes 393224 | tf_op jit(solution)/shard_map/ppermute | solution.py:209
  47.2 0.5 collective-permute-start.12
  47.7 1.7 %collective-permute-done.15.refs_0_ = f32[64,512]{1,0:T(8,128)S(1)} collective-permute-done((f32[64,512]{1,0:T(8,128)S(1)}, f32[64,512]{1,0:T(8,128)S(1)}, u32[]{:S(2)}, u32[]{:S(2)}) %collective-permute-start.15) | collective-permute-done | bytes 131104 | tf_op jit(solution)/shard_map/ppermute | solution.py:209
  49.4 1.2 %collective-permute-start.13 = (f32[64,512]{1,0:T(8,128)S(1)}, f32[64,512]{1,0:T(8,128)S(1)}, u32[]{:S(2)}, u32[]{:S(2)}) collective-permute-start(f32[64,512]{1,0:T(8,128)S(1)} %get-tuple-element.43), channel_id=1, source_target_pairs={{0,5},{1,4},{2,7},{3,6},{4,1},{5,0},{6,3},{7,2},{8,13},{9,12},{10,... | collective-permute-start | bytes 393224 | tf_op jit(solution)/shard_map/ppermute | solution.py:209
  50.6 0.0 collective-permute-done.16.refs_1_
  50.6 0.6 collective-permute-start.14
  51.1 0.8 %collective-permute-done.17.refs_2_ = f32[64,512]{1,0:T(8,128)S(1)} collective-permute-done((f32[64,512]{1,0:T(8,128)S(1)}, f32[64,512]{1,0:T(8,128)S(1)}, u32[]{:S(2)}, u32[]{:S(2)}) %collective-permute-start.17) | collective-permute-done | bytes 131104 | tf_op jit(solution)/shard_map/ppermute | solution.py:209
  52.0 0.0 copy-done.3
  52.0 1.5 %finish.2.refs_4_ = bf16[64,4096]{1,0:T(8,128)(2,1)} custom-call(s32[3]{0:T(128)S(1)} %pad_add_fusion.place, s32[16]{0:T(128)S(1)} %copy-done.4, f32[64,4096]{1,0:T(8,128)S(1)} %inside.1.refs_6_.own, f32[1,4096]{1,0:T(1,128)S(1)} %bitcast.4, f32[64,512]{1,0:T(8,128)S(1)} %collective-permute-done.15.refs_0_, f32[64,512]{1,0:T(8,128)S(1)} %collective-permute-done.16.refs_1_, ...), custom_call_target="tpu_custom_call" | custom-call | bytes 2097152 | tf_op jit(solution)/shard_map/finish/pallas_call | solution.py:289
  53.5 1.7 %collective-permute-done.11.refs_0_ = f32[64,512]{1,0:T(8,128)S(1)} collective-permute-done((f32[64,512]{1,0:T(8,128)S(1)}, f32[64,512]{1,0:T(8,128)S(1)}, u32[]{:S(2)}, u32[]{:S(2)}) %collective-permute-start.11) | collective-permute-done | bytes 131104 | tf_op jit(solution)/shard_map/ppermute | solution.py:209
  55.2 0.0 collective-permute-done.12.refs_1_
  55.2 2.4 %collective-permute-done.13.refs_2_ = f32[64,512]{1,0:T(8,128)S(1)} collective-permute-done((f32[64,512]{1,0:T(8,128)S(1)}, f32[64,512]{1,0:T(8,128)S(1)}, u32[]{:S(2)}, u32[]{:S(2)}) %collective-permute-start.13) | collective-permute-done | bytes 131104 | tf_op jit(solution)/shard_map/ppermute | solution.py:209
  57.5 0.0 collective-permute-done.14.refs_3_
  57.6 1.5 %finish.3 = bf16[64,4096]{1,0:T(8,128)(2,1)} custom-call(s32[3]{0:T(128)S(1)} %pad_add_fusion.place, s32[16]{0:T(128)S(1)} %copy-done.4, f32[64,4096]{1,0:T(8,128)S(1)} %inside.1.refs_6_.own, f32[1,4096]{1,0:T(1,128)S(1)} %bitcast.5, f32[64,512]{1,0:T(8,128)S(1)} %collective-permute-done.11.refs_0_, ...), custom_call_target="tpu_custom_call", output_to_operand_aliasing={{}: (8, {})} | custom-call | bytes 2097152 | tf_op jit(solution)/shard_map/finish/pallas_call | solution.py:289
Async XLA Ops:
  0.1 19.4 %copy-start = (bf16[64,4096]{1,0:T(8,128)(2,1)S(1)}, bf16[64,4096]{1,0:T(8,128)(2,1)}, u32[]{:S(2)}) copy-start(bf16[64,4096]{1,0:T(8,128)(2,1)} %queries.5) | copy-start | bytes 1572868
  2.2 4.7 %collective-permute-start = (f32[4,3,64,512]{3,2,1,0:T(8,128)S(1)}, f32[4,3,64,512]{3,2,1,0:T(8,128)S(1)}, u32[]{:S(2)}, u32[]{:S(2)}) collective-permute-start(f32[4,3,64,512]{3,2,1,0:T(8,128)S(1)} %get-tuple-element.27), channel_id=1, source_target_pairs={{0,4},{1,5},{2,6},{3,7},{4,0},{5,1},{6,2},{7,3},{8,12},{9,13},{10,... | collective-permute-start | bytes 4718600 | tf_op jit(solution)/shard_map/ppermute | solution.py:209
  2.7 10.7 %collective-permute-start.1 = (f32[2,64,512]{2,1,0:T(8,128)S(1)}, f32[2,64,512]{2,1,0:T(8,128)S(1)}, u32[]{:S(2)}, u32[]{:S(2)}) collective-permute-start(f32[2,64,512]{2,1,0:T(8,128)S(1)} %get-tuple-element.28), channel_id=1, source_target_pairs={{0,3},{1,2},{2,1},{3,0},{4,7},{5,6},{6,5},{7,4},{8,11},{9,10},{10,... | collective-permute-start | bytes 786440 | tf_op jit(solution)/shard_map/ppermute | solution.py:209
  6.2 12.9 %collective-permute-start.2 = (f32[2,64,512]{2,1,0:T(8,128)S(1)}, f32[2,64,512]{2,1,0:T(8,128)S(1)}, u32[]{:S(2)}, u32[]{:S(2)}) collective-permute-start(f32[2,64,512]{2,1,0:T(8,128)S(1)} %get-tuple-element.29), channel_id=1, source_target_pairs={{0,2},{1,3},{2,0},{3,1},{4,6},{5,7},{6,4},{7,5},{8,10},{9,11},{10,... | collective-permute-start | bytes 786440 | tf_op jit(solution)/shard_map/ppermute | solution.py:209
  6.7 12.8 %collective-permute-start.3 = (f32[2,64,512]{2,1,0:T(8,128)S(1)}, f32[2,64,512]{2,1,0:T(8,128)S(1)}, u32[]{:S(2)}, u32[]{:S(2)}) collective-permute-start(f32[2,64,512]{2,1,0:T(8,128)S(1)} %get-tuple-element.30), channel_id=1, source_target_pairs={{0,1},{1,0},{2,3},{3,2},{4,5},{5,4},{6,7},{7,6},{8,9},{9,8},{10,11... | collective-permute-start | bytes 786440 | tf_op jit(solution)/shard_map/ppermute | solution.py:209
  6.9 23.9 %copy-start.4 = (s32[16]{0:T(128)S(1)}, s32[16]{0:T(128)}, u32[]{:S(2)}) copy-start(s32[16]{0:T(128)} %lengths.9) | copy-start | bytes 196
  6.9 17.8 %collective-permute-start.7 = (f32[2,64,512]{2,1,0:T(8,128)S(1)}, f32[2,64,512]{2,1,0:T(8,128)S(1)}, u32[]{:S(2)}, u32[]{:S(2)}) collective-permute-start(f32[2,64,512]{2,1,0:T(8,128)S(1)} %get-tuple-element.36), channel_id=1, source_target_pairs={{0,3},{1,2},{2,1},{3,0},{4,7},{5,6},{6,5},{7,4},{8,11},{9,10},{10,... | collective-permute-start | bytes 786440 | tf_op jit(solution)/shard_map/ppermute | solution.py:209
  9.8 20.4 %collective-permute-start.8 = (f32[2,64,512]{2,1,0:T(8,128)S(1)}, f32[2,64,512]{2,1,0:T(8,128)S(1)}, u32[]{:S(2)}, u32[]{:S(2)}) collective-permute-start(f32[2,64,512]{2,1,0:T(8,128)S(1)} %get-tuple-element.37), channel_id=1, source_target_pairs={{0,2},{1,3},{2,0},{3,1},{4,6},{5,7},{6,4},{7,5},{8,10},{9,11},{10,... | collective-permute-start | bytes 786440 | tf_op jit(solution)/shard_map/ppermute | solution.py:209
  13.4 17.4 %collective-permute-start.9 = (f32[2,64,512]{2,1,0:T(8,128)S(1)}, f32[2,64,512]{2,1,0:T(8,128)S(1)}, u32[]{:S(2)}, u32[]{:S(2)}) collective-permute-start(f32[2,64,512]{2,1,0:T(8,128)S(1)} %get-tuple-element.38), channel_id=1, source_target_pairs={{0,1},{1,0},{2,3},{3,2},{4,5},{5,4},{6,7},{7,6},{8,9},{9,8},{10,11... | collective-permute-start | bytes 786440 | tf_op jit(solution)/shard_map/ppermute | solution.py:209
  20.1 20.3 %collective-permute-start.4 = (f32[2,64,512]{2,1,0:T(8,128)S(1)}, f32[2,64,512]{2,1,0:T(8,128)S(1)}, u32[]{:S(2)}, u32[]{:S(2)}) collective-permute-start(f32[2,64,512]{2,1,0:T(8,128)S(1)} %get-tuple-element.31), channel_id=1, source_target_pairs={{0,3},{1,2},{2,1},{3,0},{4,7},{5,6},{6,5},{7,4},{8,11},{9,10},{10,... | collective-permute-start | bytes 786440 | tf_op jit(solution)/shard_map/ppermute | solution.py:209
  21.8 19.4 %collective-permute-start.5 = (f32[2,64,512]{2,1,0:T(8,128)S(1)}, f32[2,64,512]{2,1,0:T(8,128)S(1)}, u32[]{:S(2)}, u32[]{:S(2)}) collective-permute-start(f32[2,64,512]{2,1,0:T(8,128)S(1)} %get-tuple-element.32), channel_id=1, source_target_pairs={{0,2},{1,3},{2,0},{3,1},{4,6},{5,7},{6,4},{7,5},{8,10},{9,11},{10,... | collective-permute-start | bytes 786440 | tf_op jit(solution)/shard_map/ppermute | solution.py:209
  24.7 16.9 %collective-permute-start.6 = (f32[2,64,512]{2,1,0:T(8,128)S(1)}, f32[2,64,512]{2,1,0:T(8,128)S(1)}, u32[]{:S(2)}, u32[]{:S(2)}) collective-permute-start(f32[2,64,512]{2,1,0:T(8,128)S(1)} %get-tuple-element.33), channel_id=1, source_target_pairs={{0,1},{1,0},{2,3},{3,2},{4,5},{5,4},{6,7},{7,6},{8,9},{9,8},{10,11... | collective-permute-start | bytes 786440 | tf_op jit(solution)/shard_map/ppermute | solution.py:209
  30.8 4.7 %copy-start.1 = (bf16[64,4096]{1,0:T(8,128)(2,1)S(1)}, bf16[64,4096]{1,0:T(8,128)(2,1)}, u32[]{:S(2)}) copy-start(bf16[64,4096]{1,0:T(8,128)(2,1)} %keys.3) | copy-start | bytes 1572868
  30.8 4.7 %copy-start.2 = (bf16[64,4096]{1,0:T(8,128)(2,1)S(1)}, bf16[64,4096]{1,0:T(8,128)(2,1)}, u32[]{:S(2)}) copy-start(bf16[64,4096]{1,0:T(8,128)(2,1)} %values.3) | copy-start | bytes 1572868
  32.0 9.6 %collective-permute-start.10 = (f32[4,128,128]{2,1,0:T(8,128)S(1)}, f32[4,128,128]{2,1,0:T(8,128)S(1)}, u32[]{:S(2)}, u32[]{:S(2)}) collective-permute-start(f32[4,128,128]{2,1,0:T(8,128)S(1)} %get-tuple-element.40), channel_id=1, source_target_pairs={{0,8},{1,9},{2,10},{3,11},{4,12},{5,13},{6,14},{7,15},{8,16},{9,17... | collective-permute-start | bytes 786440 | tf_op jit(solution)/shard_map/ppermute | solution.py:264
  41.6 10.4 %copy-start.3 = (f32[4096]{0:T(1024)S(1)}, f32[4096]{0:T(1024)}, u32[]{:S(2)}) copy-start(f32[4096]{0:T(1024)} %param.9) | copy-start | bytes 49156
  42.6 6.8 %collective-permute-start.15 = (f32[64,512]{1,0:T(8,128)S(1)}, f32[64,512]{1,0:T(8,128)S(1)}, u32[]{:S(2)}, u32[]{:S(2)}) collective-permute-start(f32[64,512]{1,0:T(8,128)S(1)} %get-tuple-element.45), channel_id=1, source_target_pairs={{0,7},{1,6},{2,5},{3,4},{4,3},{5,2},{6,1},{7,0},{8,15},{9,14},{10,... | collective-permute-start | bytes 393224 | tf_op jit(solution)/shard_map/ppermute | solution.py:209
  43.4 7.2 %collective-permute-start.16 = (f32[64,512]{1,0:T(8,128)S(1)}, f32[64,512]{1,0:T(8,128)S(1)}, u32[]{:S(2)}, u32[]{:S(2)}) collective-permute-start(f32[64,512]{1,0:T(8,128)S(1)} %get-tuple-element.46), channel_id=1, source_target_pairs={{0,4},{1,5},{2,6},{3,7},{4,0},{5,1},{6,2},{7,3},{8,12},{9,13},{10,... | collective-permute-start | bytes 393224 | tf_op jit(solution)/shard_map/ppermute | solution.py:209
  44.2 7.7 %collective-permute-start.17 = (f32[64,512]{1,0:T(8,128)S(1)}, f32[64,512]{1,0:T(8,128)S(1)}, u32[]{:S(2)}, u32[]{:S(2)}) collective-permute-start(f32[64,512]{1,0:T(8,128)S(1)} %get-tuple-element.47), channel_id=1, source_target_pairs={{0,3},{1,2},{2,1},{3,0},{4,7},{5,6},{6,5},{7,4},{8,11},{9,10},{10,... | collective-permute-start | bytes 393224 | tf_op jit(solution)/shard_map/ppermute | solution.py:209
  45.7 9.4 %collective-permute-start.11 = (f32[64,512]{1,0:T(8,128)S(1)}, f32[64,512]{1,0:T(8,128)S(1)}, u32[]{:S(2)}, u32[]{:S(2)}) collective-permute-start(f32[64,512]{1,0:T(8,128)S(1)} %get-tuple-element.41), channel_id=1, source_target_pairs={{0,1},{1,0},{2,3},{3,2},{4,5},{5,4},{6,7},{7,6},{8,9},{9,8},{10,11... | collective-permute-start | bytes 393224 | tf_op jit(solution)/shard_map/ppermute | solution.py:209
  47.2 7.9 %collective-permute-start.12 = (f32[64,512]{1,0:T(8,128)S(1)}, f32[64,512]{1,0:T(8,128)S(1)}, u32[]{:S(2)}, u32[]{:S(2)}) collective-permute-start(f32[64,512]{1,0:T(8,128)S(1)} %get-tuple-element.42), channel_id=1, source_target_pairs={{0,2},{1,3},{2,0},{3,1},{4,6},{5,7},{6,4},{7,5},{8,10},{9,11},{10,... | collective-permute-start | bytes 393224 | tf_op jit(solution)/shard_map/ppermute | solution.py:209
  49.4 8.1 %collective-permute-start.13 = (f32[64,512]{1,0:T(8,128)S(1)}, f32[64,512]{1,0:T(8,128)S(1)}, u32[]{:S(2)}, u32[]{:S(2)}) collective-permute-start(f32[64,512]{1,0:T(8,128)S(1)} %get-tuple-element.43), channel_id=1, source_target_pairs={{0,5},{1,4},{2,7},{3,6},{4,1},{5,0},{6,3},{7,2},{8,13},{9,12},{10,... | collective-permute-start | bytes 393224 | tf_op jit(solution)/shard_map/ppermute | solution.py:209
  50.6 7.0 %collective-permute-start.14 = (f32[64,512]{1,0:T(8,128)S(1)}, f32[64,512]{1,0:T(8,128)S(1)}, u32[]{:S(2)}, u32[]{:S(2)}) collective-permute-start(f32[64,512]{1,0:T(8,128)S(1)} %get-tuple-element.44), channel_id=1, source_target_pairs={{0,6},{1,7},{2,4},{3,5},{4,2},{5,3},{6,0},{7,1},{8,14},{9,15},{10,... | collective-permute-start | bytes 393224 | tf_op jit(solution)/shard_map/ppermute | solution.py:209

commit v5 on v4

--- a/solution.py
+++ b/solution.py
@@ -37,18 +37,17 @@
     return found, after
 
 
-def spread(members, width, place, queries, keys, values, *refs):
+def spread(members, width, place, keys, values, *refs):
     half = members // CORES
     near, cross = refs[:half], refs[half]
-    buffers, sems = refs[half + 1 : half + 4], refs[half + 4]
+    buffers, sems = refs[half + 1 : half + 3], refs[half + 3]
     me = place[0]
 
     def copies(d):
         span = columns_of(me ^ d, width)
-        sources = (keys, values) if d < half else (keys, values, queries)
         return [
             pltpu.make_async_copy(source.at[:, span], buffers[i].at[d], sems.at[i, d])
-            for i, source in enumerate(sources)
+            for i, source in enumerate((keys, values))
         ]
 
     order = list(reversed(range(half))) + list(range(half, members))
@@ -67,7 +66,12 @@
 
 def forward(half, swapped, *outs):
     for e in range(1, half):
-        outs[half - 1 - e][...] = swapped[e, 0:2]
+        outs[half - 1 - e][...] = swapped[e]
+
+
+def pick_queries(half, width, place, queries, out):
+    for e in range(half):
+        out[e] = queries[:, columns_of(place[0] ^ e ^ half, width)].astype(jnp.float32)
 
 
 def join_queries(half, width, gates, place, queries, swapped, *refs):
@@ -75,7 +79,7 @@
     me = place[0]
     for e in range(half):
         outs[half - 1 - e][0] = queries[:, columns_of(me ^ e, width)].astype(jnp.float32)
-        outs[half - 1 - e][1] = swapped[e, 2]
+        outs[half - 1 - e][1] = swapped[e]
 
 
 def gather_states(members, heads, docs, rows, place, lengths, *refs):
@@ -125,22 +129,20 @@
         out[:, span] = jnp.dot(weights, values[:, span], preferred_element_type=jnp.float32)
 
 
-def reach_back(members, heads, docs, rows, place, lengths, *refs):
+def reach_back(members, heads, docs, rows, chosen, gates, place, lengths, carry, earlier, *refs):
+    count = len(chosen)
     half = members // CORES
-    query_parts = refs[:half][::-1]
-    carry, earlier = refs[half : half + 2]
-    outs = refs[half + 3 :][::-1]
+    query_parts, outs = refs[:count], refs[count + gates :]
     me, base = place[0], place[1]
-    for e in range(half):
+    for n, e in enumerate(chosen):
         for side in range(CORES):
-            d = e ^ (side * half)
-            j = me ^ d
+            j = me ^ e ^ (side * half)
             first, _ = start_of(lengths, docs, base + j * rows)
             before = jnp.where(first < base, 1.0, 0.0).astype(jnp.float32)
             for h, span in enumerate(heads_of(heads)):
                 held = (carry[j, h] + before * earlier[h]).astype(jnp.bfloat16)
-                query = query_parts[e][side, :, span].astype(jnp.bfloat16)
-                outs[d][:, span] = jnp.dot(query, held, preferred_element_type=jnp.float32)
+                query = query_parts[n][side, :, span].astype(jnp.bfloat16)
+                outs[n * CORES + side][:, span] = jnp.dot(query, held, preferred_element_type=jnp.float32)
 
 
 def finish(chosen, heads, docs, rows, place, lengths, own, gain, *refs):
@@ -213,11 +215,11 @@
     parts = call(
         functools.partial(spread, members, width),
         "spread",
-        [shape(2, rows, width)] * half + [shape(half, 3, rows, width)],
-        [SMEM, HBM, HBM, HBM],
+        [shape(2, rows, width)] * half + [shape(half, 2, rows, width)],
+        [SMEM, HBM, HBM],
         [VMEM] * (half + 1),
-        [pltpu.VMEM((members, rows, width), bf16)] * 3 + [pltpu.SemaphoreType.DMA((3, members))],
-    )(place, *[pltpu.with_memory_space_constraint(x, pltpu.HBM) for x in (queries, keys, values)])
+        [pltpu.VMEM((members, rows, width), bf16)] * 2 + [pltpu.SemaphoreType.DMA((2, members))],
+    )(place, *[pltpu.with_memory_space_constraint(x, pltpu.HBM) for x in (keys, values)])
     near_got = [swap(part, e) if e else part for e, part in zip(downward, parts)]
     swapped = swap(parts[half], half)
     far_parts = call(
@@ -229,6 +231,15 @@
         moved=2 * block_bytes,
     )(swapped)
     far_got = [swap(part, e) for e, part in zip(downward, far_parts)] + [swapped]
+    picked = call(
+        functools.partial(pick_queries, half, width),
+        "pick_queries",
+        shape(half, rows, width),
+        [SMEM, VMEM],
+        VMEM,
+        moved=block_bytes,
+    )(place, queries)
+    swapped_queries = swap(picked, half)
     gates = near_got[:-1]
     query_parts = call(
         functools.partial(join_queries, half, width, len(gates)),
@@ -237,7 +248,7 @@
         [SMEM, VMEM, VMEM] + [ANY] * len(gates),
         [VMEM] * half,
         moved=2 * block_bytes,
-    )(place, queries, swapped, *gates)
+    )(place, queries, swapped_queries, *gates)
     query_got = [swap(part, e) if e else part for e, part in zip(downward, query_parts)]
 
     own = call(
@@ -269,22 +280,30 @@
         for k in range(2, min(reach, planes - 1) + 1):
             moving = lax.ppermute(moving, everyone, up)
             earlier = earlier + jnp.where(opens < base - (k - 1) * members * rows, moving, 0.0)
-    crossed = call(
-        functools.partial(reach_back, members, heads, docs, rows),
-        "reach_back",
-        [shape(rows, width)] * members,
-        [SMEM, SMEM] + [VMEM] * (half + 2) + [ANY],
-        [VMEM] * members,
-        flops=2 * rows * HEAD_DIM * columns,
-        moved=4 * block_bytes,
-    )(place, lengths, *query_got, carry, earlier, own)
-    crossed_got = [swap(crossed[members - 1 - d], d) if d else crossed[-1] for d in range(members)]
+    crossed_got = {}
+    late = [e for e in downward if e in (1, 2)]
+    soon = [e for e in downward if e not in late]
+    for chosen, gates in ((soon, [own]), (late, [])):
+        crossed = call(
+            functools.partial(reach_back, members, heads, docs, rows, chosen, len(gates)),
+            "reach_back",
+            [shape(rows, width)] * (CORES * len(chosen)),
+            [SMEM, SMEM] + [VMEM] * (len(chosen) + 2) + [ANY] * len(gates),
+            [VMEM] * (CORES * len(chosen)),
+            flops=2 * rows * HEAD_DIM * width * CORES * len(chosen),
+            moved=2 * block_bytes,
+        )(place, lengths, carry, earlier, *[query_got[half - 1 - e] for e in chosen], *gates)
+        for n, e in enumerate(chosen):
+            for side in range(CORES):
+                d = e ^ (side * half)
+                part = crossed[n * CORES + side]
+                crossed_got[d] = swap(part, d) if d else part
 
     gain = norm_gain.reshape(1, columns)
-    last = [d for d in range(members) if d % half in (1, 2)]
-    first = [d for d in reversed(range(members)) if d not in last]
     out = None
-    for chosen in (first, last):
+    groups = [[e ^ (side * half) for e in soon for side in range(CORES)]]
+    groups += [[e ^ (side * half) for e in late] for side in range(CORES)]
+    for chosen in groups:
         more = [] if out is None else [out]
         out = call(
             functools.partial(finish, chosen, heads, docs, rows),

time: 59.2 us -> 61.3 us (1.035)
  Pallas kernels: 12.9 us -> 15.4 us
  waiting for transfers between devices: 20.7 us -> 18.5 us
  local copies, waits for them, and re-layouts: 0.02 us -> 1.06 us
  starting transfers between devices: 25.2 us -> 26 us
    ppermute x17 -> x18, waiting for transfers between devices: 20.7 us -> 18.5 us  [swap(): return lax.ppermute(part, everyone, pairs)]
    pallas_call x1 -> x3, Pallas kernels: 1.02 us -> 2.38 us  [the longest x2 1.8 us: body(): call(functools.partial(reach_back, members, heads, docs, rows, chosen, le...]
    pallas_call x2 -> x3, Pallas kernels: 2.95 us -> 4.25 us  [body(): call(functools.partial(finish, chosen, heads, docs, rows), 'finish', shap...]
    unnamed x10 -> x12, local copies, waits for them, and re-layouts: 0.02 us -> 1.06 us
    ppermute x17 -> x18, starting transfers between devices: 21.7 us -> 22.5 us  [swap(): return lax.ppermute(part, everyone, pairs)]
  transfers between devices with their start and end apart: 18 -> 19, of which waited for: 12 -> 10; matrix products, arithmetic and copies ran while one was open for 0% -> 0% of each run, Pallas kernels for 14% -> 20%
where the time goes in v5:
time: 61.3 us; the launch traced here: 61.1 us
  starting transfers between devices  26 us (42%)
  waiting for transfers between devices  18.5 us (30%)
  Pallas kernels  15.4 us (25%)
  local copies, waits for them, and re-layouts  1.06 us (2%)
    ppermute x18, starting transfers between devices, swap(): return lax.ppermute(part, everyone, pairs)  22.5 us
    ppermute x18, waiting for transfers between devices, swap(): return lax.ppermute(part, everyone, pairs)  18.5 us
    pallas_call x1, Pallas kernels, body(): call(functools.partial(inside, head_count, docs, rows), 'inside', shape(r...  4.93 us
    pallas_call x3, Pallas kernels, body(): call(functools.partial(finish, chosen, heads, docs, rows), 'finish', shap...  4.25 us
    ppermute x1, starting transfers between devices, body(): moving = lax.ppermute(total, everyone, up)  3.5 us
    pallas_call x1, Pallas kernels, body(): call(functools.partial(spread, members, width), 'spread', [shape(2, rows,...  1.94 us
    pallas_call x2, Pallas kernels, body(): call(functools.partial(reach_back, members, heads, docs, rows, chosen, le...  1.8 us
  transfers between devices with their start and end apart: 19, of which 10 were waited for; matrix products, arithmetic and copies ran while one was open for 0% of the time, Pallas kernels for 20%

profile of v5, /device:TPU:0, one launch (start us, length us, event | category | flops | bytes accessed | tf_op | source)
XLA Modules:
  0.0 61.1 jit_solution(17905917455129478932)
XLA Ops:
  0.0 0.0 copy-start.1
  0.0 0.1 pad_add_fusion.place
  0.1 1.9 %spread.1 = (f32[2,64,512]{2,1,0:T(8,128)S(1)}, f32[2,64,512]{2,1,0:T(8,128)S(1)}, f32[2,64,512]{2,1,0:T(8,128)S(1)}, f32[2,64,512]{2,1,0:T(8,128)S(1)}, f32[4,2,64,512]{3,2,1,0:T(8,128)S(1)}) custom-call(s32[3]{0:T(128)S(1)} %pad_add_fusion.place, bf16[64,4096]{1,0:T(8,128)(2,1)} %keys.3, bf16[64,4096]{1,0:T(8,128)(2,1)} %values.3), custom_call_target="tpu_custom_call" | custom-call | tf_op jit(solution)/shard_map/spread/pallas_call | solution.py:215
  2.0 0.0 copy-start.5
  2.0 0.5 collective-permute-start.3
  2.6 0.0 copy-start
  2.6 1.0 %copy-done = bf16[64,4096]{1,0:T(8,128)(2,1)S(1)} copy-done((bf16[64,4096]{1,0:T(8,128)(2,1)S(1)}, bf16[64,4096]{1,0:T(8,128)(2,1)}, u32[]{:S(2)}) %copy-start) | copy-done | bytes 524312
  3.6 0.6 pick_queries.1
  4.2 0.1 collective-permute-start.7
  4.3 3.9 %collective-permute-start = (f32[2,64,512]{2,1,0:T(8,128)S(1)}, f32[2,64,512]{2,1,0:T(8,128)S(1)}, u32[]{:S(2)}, u32[]{:S(2)}) collective-permute-start(f32[2,64,512]{2,1,0:T(8,128)S(1)} %get-tuple-element.27), channel_id=1, source_target_pairs={{0,3},{1,2},{2,1},{3,0},{4,7},{5,6},{6,5},{7,4},{8,11},{9,10},{10,... | collective-permute-start | bytes 786440 | tf_op jit(solution)/shard_map/ppermute | solution.py:211
  8.2 0.5 collective-permute-start.1
  8.7 0.1 collective-permute-start.2
  8.8 0.0 collective-permute-done.3.swapped.refs_7_
  8.8 0.1 forward.1
  8.8 3.0 %collective-permute-start.4 = (f32[2,64,512]{2,1,0:T(8,128)S(1)}, f32[2,64,512]{2,1,0:T(8,128)S(1)}, u32[]{:S(2)}, u32[]{:S(2)}) collective-permute-start(f32[2,64,512]{2,1,0:T(8,128)S(1)} %get-tuple-element.32), channel_id=1, source_target_pairs={{0,3},{1,2},{2,1},{3,0},{4,7},{5,6},{6,5},{7,4},{8,11},{9,10},{10,... | collective-permute-start | bytes 786440 | tf_op jit(solution)/shard_map/ppermute | solution.py:211
  11.8 3.5 %collective-permute-done.refs_0_ = f32[2,64,512]{2,1,0:T(8,128)S(1)} collective-permute-done((f32[2,64,512]{2,1,0:T(8,128)S(1)}, f32[2,64,512]{2,1,0:T(8,128)S(1)}, u32[]{:S(2)}, u32[]{:S(2)}) %collective-permute-start) | collective-permute-done | bytes 262176 | tf_op jit(solution)/shard_map/ppermute | solution.py:211
  15.3 2.0 %collective-permute-start.5 = (f32[2,64,512]{2,1,0:T(8,128)S(1)}, f32[2,64,512]{2,1,0:T(8,128)S(1)}, u32[]{:S(2)}, u32[]{:S(2)}) collective-permute-start(f32[2,64,512]{2,1,0:T(8,128)S(1)} %get-tuple-element.33), channel_id=1, source_target_pairs={{0,2},{1,3},{2,0},{3,1},{4,6},{5,7},{6,4},{7,5},{8,10},{9,11},{10,... | collective-permute-start | bytes 786440 | tf_op jit(solution)/shard_map/ppermute | solution.py:211
  17.4 3.6 %collective-permute-done.1.refs_1_ = f32[2,64,512]{2,1,0:T(8,128)S(1)} collective-permute-done((f32[2,64,512]{2,1,0:T(8,128)S(1)}, f32[2,64,512]{2,1,0:T(8,128)S(1)}, u32[]{:S(2)}, u32[]{:S(2)}) %collective-permute-start.1) | collective-permute-done | bytes 262176 | tf_op jit(solution)/shard_map/ppermute | solution.py:211
  21.0 0.0 copy-start.2
  21.0 0.0 copy-start.3
  21.0 2.0 %collective-permute-start.6 = (f32[2,64,512]{2,1,0:T(8,128)S(1)}, f32[2,64,512]{2,1,0:T(8,128)S(1)}, u32[]{:S(2)}, u32[]{:S(2)}) collective-permute-start(f32[2,64,512]{2,1,0:T(8,128)S(1)} %get-tuple-element.34), channel_id=1, source_target_pairs={{0,1},{1,0},{2,3},{3,2},{4,5},{5,4},{6,7},{7,6},{8,9},{9,8},{10,11... | collective-permute-start | bytes 786440 | tf_op jit(solution)/shard_map/ppermute | solution.py:211
  23.0 0.0 collective-permute-done.2.refs_2_
  23.0 0.0 collective-permute-done.7.swapped
  23.0 0.0 copy-done.1
  23.0 0.6 %join_queries.1 = (f32[2,64,512]{2,1,0:T(8,128)S(1)}, f32[2,64,512]{2,1,0:T(8,128)S(1)}, f32[2,64,512]{2,1,0:T(8,128)S(1)}, f32[2,64,512]{2,1,0:T(8,128)S(1)}) custom-call(s32[3]{0:T(128)S(1)} %pad_add_fusion.place, bf16[64,4096]{1,0:T(8,128)(2,1)S(1)} %copy-done.1, f32[4,64,512]{2,1,0:T(8,128)S(1)} %collective-permute-done.7.swapped, ...), custom_call_target="tpu_custom_call" | custom-call | bytes 2097152 | tf_op jit(solution)/shard_map/join_queries/pallas_call | solution.py:244
  23.7 1.6 %collective-permute-start.15 = (f32[2,64,512]{2,1,0:T(8,128)S(1)}, f32[2,64,512]{2,1,0:T(8,128)S(1)}, u32[]{:S(2)}, u32[]{:S(2)}) collective-permute-start(f32[2,64,512]{2,1,0:T(8,128)S(1)} %get-tuple-element.44), channel_id=1, source_target_pairs={{0,3},{1,2},{2,1},{3,0},{4,7},{5,6},{6,5},{7,4},{8,11},{9,10},{10,... | collective-permute-start | bytes 786440 | tf_op jit(solution)/shard_map/ppermute | solution.py:211
  25.2 1.4 %collective-permute-done.4.refs_4_ = f32[2,64,512]{2,1,0:T(8,128)S(1)} collective-permute-done((f32[2,64,512]{2,1,0:T(8,128)S(1)}, f32[2,64,512]{2,1,0:T(8,128)S(1)}, u32[]{:S(2)}, u32[]{:S(2)}) %collective-permute-start.4) | collective-permute-done | bytes 262176 | tf_op jit(solution)/shard_map/ppermute | solution.py:211
  26.6 5.4 %collective-permute-done.5.refs_5_ = f32[2,64,512]{2,1,0:T(8,128)S(1)} collective-permute-done((f32[2,64,512]{2,1,0:T(8,128)S(1)}, f32[2,64,512]{2,1,0:T(8,128)S(1)}, u32[]{:S(2)}, u32[]{:S(2)}) %collective-permute-start.5) | collective-permute-done | bytes 262176 | tf_op jit(solution)/shard_map/ppermute | solution.py:211
  32.1 0.7 %collective-permute-done.6.refs_6_ = f32[2,64,512]{2,1,0:T(8,128)S(1)} collective-permute-done((f32[2,64,512]{2,1,0:T(8,128)S(1)}, f32[2,64,512]{2,1,0:T(8,128)S(1)}, u32[]{:S(2)}, u32[]{:S(2)}) %collective-permute-start.6) | collective-permute-done | bytes 262176 | tf_op jit(solution)/shard_map/ppermute | solution.py:211
  32.8 0.0 copy-done.5
  32.8 1.2 %gather_states.1 = (f32[8,4,128,128]{3,2,1,0:T(8,128)S(1)}, f32[4,128,128]{2,1,0:T(8,128)S(1)}) custom-call(s32[3]{0:T(128)S(1)} %pad_add_fusion.place, s32[16]{0:T(128)S(1)} %copy-done.5, f32[2,64,512]{2,1,0:T(8,128)S(1)} %collective-permute-done.refs_0_, f32[2,64,512]{2,1,0:T(8,128)S(1)} %collective-permute-done.1.refs_1_, ...), custom_call_target="tpu_custom_call" | custom-call | flops 67108864 | bytes 4194304 | tf_op jit(solution)/shard_map/gather_states/pallas_call | solution.py:264
  34.0 3.5 %collective-permute-start.8 = (f32[4,128,128]{2,1,0:T(8,128)S(1)}, f32[4,128,128]{2,1,0:T(8,128)S(1)}, u32[]{:S(2)}, u32[]{:S(2)}) collective-permute-start(f32[4,128,128]{2,1,0:T(8,128)S(1)} %get-tuple-element.37), channel_id=1, source_target_pairs={{0,8},{1,9},{2,10},{3,11},{4,12},{5,13},{6,14},{7,15},{8,16},{9,17... | collective-permute-start | bytes 786440 | tf_op jit(solution)/shard_map/ppermute | solution.py:275
  37.6 1.6 %collective-permute-start.10 = (f32[2,64,512]{2,1,0:T(8,128)S(1)}, f32[2,64,512]{2,1,0:T(8,128)S(1)}, u32[]{:S(2)}, u32[]{:S(2)}) collective-permute-start(f32[2,64,512]{2,1,0:T(8,128)S(1)} %get-tuple-element.39), channel_id=1, source_target_pairs={{0,1},{1,0},{2,3},{3,2},{4,5},{5,4},{6,7},{7,6},{8,9},{9,8},{10,11... | collective-permute-start | bytes 786440 | tf_op jit(solution)/shard_map/ppermute | solution.py:211
  39.1 0.5 collective-permute-start.9
  39.6 0.0 copy-done.2
  39.6 0.0 copy-done.3
  39.6 4.9 %inside.1.refs_2_.own = f32[64,4096]{1,0:T(8,128)S(1)} custom-call(s32[3]{0:T(128)S(1)} %pad_add_fusion.place, s32[16]{0:T(128)S(1)} %copy-done.5, bf16[64,4096]{1,0:T(8,128)(2,1)S(1)} %copy-done.1, bf16[64,4096]{1,0:T(8,128)(2,1)S(1)} %copy-done.2, bf16[64,4096]{1,0:T(8,128)(2,1)S(1)} %copy-done.3), custom_call_target="tpu_custom_call" | custom-call | flops 67108864 | bytes 3145728 | tf_op jit(solution)/shard_map/inside/pallas_call | solution.py:254
  44.5 0.0 collective-permute-done.15.refs_0_
  44.6 0.0 collective-permute-done.8.earlier
  44.6 0.9 %reach_back.3 = (f32[64,512]{1,0:T(8,128)S(1)}, f32[64,512]{1,0:T(8,128)S(1)}, f32[64,512]{1,0:T(8,128)S(1)}, f32[64,512]{1,0:T(8,128)S(1)}) custom-call(s32[3]{0:T(128)S(1)} %pad_add_fusion.place, s32[16]{0:T(128)S(1)} %copy-done.5, f32[8,4,128,128]{3,2,1,0:T(8,128)S(1)} %get-tuple-element.36.carry, f32[4,128,128]{2,1,0:T(8,128)S(1)} %collective-permute-done.8.earlier, ...), custom_call_target="tpu_custom_call" | custom-call | flops 33554432 | bytes 2097152 | tf_op jit(solution)/shard_map/reach_back/pallas_call | solution.py:287
  45.5 0.0 copy-start.4
  45.5 1.6 %collective-permute-start.16 = (f32[64,512]{1,0:T(8,128)S(1)}, f32[64,512]{1,0:T(8,128)S(1)}, u32[]{:S(2)}, u32[]{:S(2)}) collective-permute-start(f32[64,512]{1,0:T(8,128)S(1)} %get-tuple-element.45), channel_id=1, source_target_pairs={{0,3},{1,2},{2,1},{3,0},{4,7},{5,6},{6,5},{7,4},{8,11},{9,10},{10,... | collective-permute-start | bytes 393224 | tf_op jit(solution)/shard_map/ppermute | solution.py:211
  47.0 0.0 collective-permute-start.17
  47.0 1.5 %collective-permute-start.18 = (f32[64,512]{1,0:T(8,128)S(1)}, f32[64,512]{1,0:T(8,128)S(1)}, u32[]{:S(2)}, u32[]{:S(2)}) collective-permute-start(f32[64,512]{1,0:T(8,128)S(1)} %get-tuple-element.48), channel_id=1, source_target_pairs={{0,4},{1,5},{2,6},{3,7},{4,0},{5,1},{6,2},{7,3},{8,12},{9,13},{10,... | collective-permute-start | bytes 393224 | tf_op jit(solution)/shard_map/ppermute | solution.py:211
  48.6 0.0 collective-permute-done.10.refs_1_
  48.6 0.0 collective-permute-done.9.refs_0_
  48.6 0.9 %reach_back.2 = (f32[64,512]{1,0:T(8,128)S(1)}, f32[64,512]{1,0:T(8,128)S(1)}, f32[64,512]{1,0:T(8,128)S(1)}, f32[64,512]{1,0:T(8,128)S(1)}) custom-call(s32[3]{0:T(128)S(1)} %pad_add_fusion.place, s32[16]{0:T(128)S(1)} %copy-done.5, f32[8,4,128,128]{3,2,1,0:T(8,128)S(1)} %get-tuple-element.36.carry, f32[4,128,128]{2,1,0:T(8,128)S(1)} %collective-permute-done.8.earlier, ...), custom_call_target="tpu_custom_call" | custom-call | flops 33554432 | bytes 2097152 | tf_op jit(solution)/shard_map/reach_back/pallas_call | solution.py:287
  49.5 1.6 %collective-permute-start.13 = (f32[64,512]{1,0:T(8,128)S(1)}, f32[64,512]{1,0:T(8,128)S(1)}, u32[]{:S(2)}, u32[]{:S(2)}) collective-permute-start(f32[64,512]{1,0:T(8,128)S(1)} %get-tuple-element.42), channel_id=1, source_target_pairs={{0,2},{1,3},{2,0},{3,1},{4,6},{5,7},{6,4},{7,5},{8,10},{9,11},{10,... | collective-permute-start | bytes 393224 | tf_op jit(solution)/shard_map/ppermute | solution.py:211
  51.1 0.5 collective-permute-start.14
  51.6 0.3 collective-permute-done.16.refs_0_
  51.9 0.0 collective-permute-start.11
  52.0 1.9 %collective-permute-done.17.refs_1_ = f32[64,512]{1,0:T(8,128)S(1)} collective-permute-done((f32[64,512]{1,0:T(8,128)S(1)}, f32[64,512]{1,0:T(8,128)S(1)}, u32[]{:S(2)}, u32[]{:S(2)}) %collective-permute-start.17) | collective-permute-done | bytes 131104 | tf_op jit(solution)/shard_map/ppermute | solution.py:211
  53.8 1.5 %collective-permute-start.12 = (f32[64,512]{1,0:T(8,128)S(1)}, f32[64,512]{1,0:T(8,128)S(1)}, u32[]{:S(2)}, u32[]{:S(2)}) collective-permute-start(f32[64,512]{1,0:T(8,128)S(1)} %get-tuple-element.41), channel_id=1, source_target_pairs={{0,5},{1,4},{2,7},{3,6},{4,1},{5,0},{6,3},{7,2},{8,13},{9,12},{10,... | collective-permute-start | bytes 393224 | tf_op jit(solution)/shard_map/ppermute | solution.py:211
  55.3 0.0 collective-permute-done.18.refs_3_
  55.3 0.0 copy-done.4
  55.3 1.5 %finish.3.refs_2_ = bf16[64,4096]{1,0:T(8,128)(2,1)} custom-call(s32[3]{0:T(128)S(1)} %pad_add_fusion.place, s32[16]{0:T(128)S(1)} %copy-done.5, f32[64,4096]{1,0:T(8,128)S(1)} %inside.1.refs_2_.own, f32[1,4096]{1,0:T(1,128)S(1)} %bitcast.4, f32[64,512]{1,0:T(8,128)S(1)} %collective-permute-done.16.refs_0_, f32[64,512]{1,0:T(8,128)S(1)} %collective-permute-done.17.refs_1_, ...), custom_call_target="tpu_custom_call" | custom-call | bytes 2097152 | tf_op jit(solution)/shard_map/finish/pallas_call | solution.py:308
  56.8 0.3 collective-permute-done.13.refs_0_
  57.1 0.2 collective-permute-done.14.refs_1_
  57.3 1.4 %finish.4.refs_2_ = bf16[64,4096]{1,0:T(8,128)(2,1)} custom-call(s32[3]{0:T(128)S(1)} %pad_add_fusion.place, s32[16]{0:T(128)S(1)} %copy-done.5, f32[64,4096]{1,0:T(8,128)S(1)} %inside.1.refs_2_.own, f32[1,4096]{1,0:T(1,128)S(1)} %bitcast.5, f32[64,512]{1,0:T(8,128)S(1)} %collective-permute-done.13.refs_0_, ...), custom_call_target="tpu_custom_call", output_to_operand_aliasing={{}: (6, {})} | custom-call | bytes 2097152 | tf_op jit(solution)/shard_map/finish/pallas_call | solution.py:308
  58.7 1.0 %collective-permute-done.11.refs_0_ = f32[64,512]{1,0:T(8,128)S(1)} collective-permute-done((f32[64,512]{1,0:T(8,128)S(1)}, f32[64,512]{1,0:T(8,128)S(1)}, u32[]{:S(2)}, u32[]{:S(2)}) %collective-permute-start.11) | collective-permute-done | bytes 131104 | tf_op jit(solution)/shard_map/ppermute | solution.py:211
  59.8 0.0 collective-permute-done.12.refs_1_
  59.8 1.4 %finish.5 = bf16[64,4096]{1,0:T(8,128)(2,1)} custom-call(s32[3]{0:T(128)S(1)} %pad_add_fusion.place, s32[16]{0:T(128)S(1)} %copy-done.5, f32[64,4096]{1,0:T(8,128)S(1)} %inside.1.refs_2_.own, f32[1,4096]{1,0:T(1,128)S(1)} %bitcast.6, f32[64,512]{1,0:T(8,128)S(1)} %collective-permute-done.11.refs_0_, ...), custom_call_target="tpu_custom_call", output_to_operand_aliasing={{}: (6, {})} | custom-call | bytes 2097152 | tf_op jit(solution)/shard_map/finish/pallas_call | solution.py:308
Async XLA Ops:
  0.0 23.0 %copy-start.1 = (bf16[64,4096]{1,0:T(8,128)(2,1)S(1)}, bf16[64,4096]{1,0:T(8,128)(2,1)}, u32[]{:S(2)}) copy-start(bf16[64,4096]{1,0:T(8,128)(2,1)} %queries.5) | copy-start | bytes 1572868
  2.0 30.8 %copy-start.5 = (s32[16]{0:T(128)S(1)}, s32[16]{0:T(128)}, u32[]{:S(2)}) copy-start(s32[16]{0:T(128)} %lengths.13) | copy-start | bytes 196
  2.0 6.7 %collective-permute-start.3 = (f32[4,2,64,512]{3,2,1,0:T(8,128)S(1)}, f32[4,2,64,512]{3,2,1,0:T(8,128)S(1)}, u32[]{:S(2)}, u32[]{:S(2)}) collective-permute-start(f32[4,2,64,512]{3,2,1,0:T(8,128)S(1)} %get-tuple-element.31), channel_id=1, source_target_pairs={{0,4},{1,5},{2,6},{3,7},{4,0},{5,1},{6,2},{7,3},{8,12},{9,13},{10,... | collective-permute-start | bytes 3145736 | tf_op jit(solution)/shard_map/ppermute | solution.py:211
  2.6 1.0 %copy-start = (bf16[64,4096]{1,0:T(8,128)(2,1)S(1)}, bf16[64,4096]{1,0:T(8,128)(2,1)}, u32[]{:S(2)}) copy-start(bf16[64,4096]{1,0:T(8,128)(2,1)} %queries.5) | copy-start | bytes 1572868
  4.2 18.9 %collective-permute-start.7 = (f32[4,64,512]{2,1,0:T(8,128)S(1)}, f32[4,64,512]{2,1,0:T(8,128)S(1)}, u32[]{:S(2)}, u32[]{:S(2)}) collective-permute-start(f32[4,64,512]{2,1,0:T(8,128)S(1)} %pick_queries.1), channel_id=1, source_target_pairs={{0,4},{1,5},{2,6},{3,7},{4,0},{5,1},{6,2},{7,3},{8,12},{9,13},{10,... | collective-permute-start | bytes 1572872 | tf_op jit(solution)/shard_map/ppermute | solution.py:211
  4.3 11.0 %collective-permute-start = (f32[2,64,512]{2,1,0:T(8,128)S(1)}, f32[2,64,512]{2,1,0:T(8,128)S(1)}, u32[]{:S(2)}, u32[]{:S(2)}) collective-permute-start(f32[2,64,512]{2,1,0:T(8,128)S(1)} %get-tuple-element.27), channel_id=1, source_target_pairs={{0,3},{1,2},{2,1},{3,0},{4,7},{5,6},{6,5},{7,4},{8,11},{9,10},{10,... | collective-permute-start | bytes 786440 | tf_op jit(solution)/shard_map/ppermute | solution.py:211
  8.2 12.8 %collective-permute-start.1 = (f32[2,64,512]{2,1,0:T(8,128)S(1)}, f32[2,64,512]{2,1,0:T(8,128)S(1)}, u32[]{:S(2)}, u32[]{:S(2)}) collective-permute-start(f32[2,64,512]{2,1,0:T(8,128)S(1)} %get-tuple-element.28), channel_id=1, source_target_pairs={{0,2},{1,3},{2,0},{3,1},{4,6},{5,7},{6,4},{7,5},{8,10},{9,11},{10,... | collective-permute-start | bytes 786440 | tf_op jit(solution)/shard_map/ppermute | solution.py:211
  8.7 14.3 %collective-permute-start.2 = (f32[2,64,512]{2,1,0:T(8,128)S(1)}, f32[2,64,512]{2,1,0:T(8,128)S(1)}, u32[]{:S(2)}, u32[]{:S(2)}) collective-permute-start(f32[2,64,512]{2,1,0:T(8,128)S(1)} %get-tuple-element.29), channel_id=1, source_target_pairs={{0,1},{1,0},{2,3},{3,2},{4,5},{5,4},{6,7},{7,6},{8,9},{9,8},{10,11... | collective-permute-start | bytes 786440 | tf_op jit(solution)/shard_map/ppermute | solution.py:211
  8.8 17.8 %collective-permute-start.4 = (f32[2,64,512]{2,1,0:T(8,128)S(1)}, f32[2,64,512]{2,1,0:T(8,128)S(1)}, u32[]{:S(2)}, u32[]{:S(2)}) collective-permute-start(f32[2,64,512]{2,1,0:T(8,128)S(1)} %get-tuple-element.32), channel_id=1, source_target_pairs={{0,3},{1,2},{2,1},{3,0},{4,7},{5,6},{6,5},{7,4},{8,11},{9,10},{10,... | collective-permute-start | bytes 786440 | tf_op jit(solution)/shard_map/ppermute | solution.py:211
  15.3 16.7 %collective-permute-start.5 = (f32[2,64,512]{2,1,0:T(8,128)S(1)}, f32[2,64,512]{2,1,0:T(8,128)S(1)}, u32[]{:S(2)}, u32[]{:S(2)}) collective-permute-start(f32[2,64,512]{2,1,0:T(8,128)S(1)} %get-tuple-element.33), channel_id=1, source_target_pairs={{0,2},{1,3},{2,0},{3,1},{4,6},{5,7},{6,4},{7,5},{8,10},{9,11},{10,... | collective-permute-start | bytes 786440 | tf_op jit(solution)/shard_map/ppermute | solution.py:211
  21.0 18.6 %copy-start.2 = (bf16[64,4096]{1,0:T(8,128)(2,1)S(1)}, bf16[64,4096]{1,0:T(8,128)(2,1)}, u32[]{:S(2)}) copy-start(bf16[64,4096]{1,0:T(8,128)(2,1)} %keys.3) | copy-start | bytes 1572868
  21.0 18.6 %copy-start.3 = (bf16[64,4096]{1,0:T(8,128)(2,1)S(1)}, bf16[64,4096]{1,0:T(8,128)(2,1)}, u32[]{:S(2)}) copy-start(bf16[64,4096]{1,0:T(8,128)(2,1)} %values.3) | copy-start | bytes 1572868
  21.0 11.8 %collective-permute-start.6 = (f32[2,64,512]{2,1,0:T(8,128)S(1)}, f32[2,64,512]{2,1,0:T(8,128)S(1)}, u32[]{:S(2)}, u32[]{:S(2)}) collective-permute-start(f32[2,64,512]{2,1,0:T(8,128)S(1)} %get-tuple-element.34), channel_id=1, source_target_pairs={{0,1},{1,0},{2,3},{3,2},{4,5},{5,4},{6,7},{7,6},{8,9},{9,8},{10,11... | collective-permute-start | bytes 786440 | tf_op jit(solution)/shard_map/ppermute | solution.py:211
  23.7 20.9 %collective-permute-start.15 = (f32[2,64,512]{2,1,0:T(8,128)S(1)}, f32[2,64,512]{2,1,0:T(8,128)S(1)}, u32[]{:S(2)}, u32[]{:S(2)}) collective-permute-start(f32[2,64,512]{2,1,0:T(8,128)S(1)} %get-tuple-element.44), channel_id=1, source_target_pairs={{0,3},{1,2},{2,1},{3,0},{4,7},{5,6},{6,5},{7,4},{8,11},{9,10},{10,... | collective-permute-start | bytes 786440 | tf_op jit(solution)/shard_map/ppermute | solution.py:211
  34.0 10.5 %collective-permute-start.8 = (f32[4,128,128]{2,1,0:T(8,128)S(1)}, f32[4,128,128]{2,1,0:T(8,128)S(1)}, u32[]{:S(2)}, u32[]{:S(2)}) collective-permute-start(f32[4,128,128]{2,1,0:T(8,128)S(1)} %get-tuple-element.37), channel_id=1, source_target_pairs={{0,8},{1,9},{2,10},{3,11},{4,12},{5,13},{6,14},{7,15},{8,16},{9,17... | collective-permute-start | bytes 786440 | tf_op jit(solution)/shard_map/ppermute | solution.py:275
  37.6 11.0 %collective-permute-start.10 = (f32[2,64,512]{2,1,0:T(8,128)S(1)}, f32[2,64,512]{2,1,0:T(8,128)S(1)}, u32[]{:S(2)}, u32[]{:S(2)}) collective-permute-start(f32[2,64,512]{2,1,0:T(8,128)S(1)} %get-tuple-element.39), channel_id=1, source_target_pairs={{0,1},{1,0},{2,3},{3,2},{4,5},{5,4},{6,7},{7,6},{8,9},{9,8},{10,11... | collective-permute-start | bytes 786440 | tf_op jit(solution)/shard_map/ppermute | solution.py:211
  39.1 9.5 %collective-permute-start.9 = (f32[2,64,512]{2,1,0:T(8,128)S(1)}, f32[2,64,512]{2,1,0:T(8,128)S(1)}, u32[]{:S(2)}, u32[]{:S(2)}) collective-permute-start(f32[2,64,512]{2,1,0:T(8,128)S(1)} %get-tuple-element.38), channel_id=1, source_target_pairs={{0,2},{1,3},{2,0},{3,1},{4,6},{5,7},{6,4},{7,5},{8,10},{9,11},{10,... | collective-permute-start | bytes 786440 | tf_op jit(solution)/shard_map/ppermute | solution.py:211
  45.5 9.8 %copy-start.4 = (f32[4096]{0:T(1024)S(1)}, f32[4096]{0:T(1024)}, u32[]{:S(2)}) copy-start(f32[4096]{0:T(1024)} %param.9) | copy-start | bytes 49156
  45.5 6.4 %collective-permute-start.16 = (f32[64,512]{1,0:T(8,128)S(1)}, f32[64,512]{1,0:T(8,128)S(1)}, u32[]{:S(2)}, u32[]{:S(2)}) collective-permute-start(f32[64,512]{1,0:T(8,128)S(1)} %get-tuple-element.45), channel_id=1, source_target_pairs={{0,3},{1,2},{2,1},{3,0},{4,7},{5,6},{6,5},{7,4},{8,11},{9,10},{10,... | collective-permute-start | bytes 393224 | tf_op jit(solution)/shard_map/ppermute | solution.py:211
  47.0 6.8 %collective-permute-start.17 = (f32[64,512]{1,0:T(8,128)S(1)}, f32[64,512]{1,0:T(8,128)S(1)}, u32[]{:S(2)}, u32[]{:S(2)}) collective-permute-start(f32[64,512]{1,0:T(8,128)S(1)} %get-tuple-element.46), channel_id=1, source_target_pairs={{0,7},{1,6},{2,5},{3,4},{4,3},{5,2},{6,1},{7,0},{8,15},{9,14},{10,... | collective-permute-start | bytes 393224 | tf_op jit(solution)/shard_map/ppermute | solution.py:211
  47.0 8.3 %collective-permute-start.18 = (f32[64,512]{1,0:T(8,128)S(1)}, f32[64,512]{1,0:T(8,128)S(1)}, u32[]{:S(2)}, u32[]{:S(2)}) collective-permute-start(f32[64,512]{1,0:T(8,128)S(1)} %get-tuple-element.48), channel_id=1, source_target_pairs={{0,4},{1,5},{2,6},{3,7},{4,0},{5,1},{6,2},{7,3},{8,12},{9,13},{10,... | collective-permute-start | bytes 393224 | tf_op jit(solution)/shard_map/ppermute | solution.py:211
  49.5 7.6 %collective-permute-start.13 = (f32[64,512]{1,0:T(8,128)S(1)}, f32[64,512]{1,0:T(8,128)S(1)}, u32[]{:S(2)}, u32[]{:S(2)}) collective-permute-start(f32[64,512]{1,0:T(8,128)S(1)} %get-tuple-element.42), channel_id=1, source_target_pairs={{0,2},{1,3},{2,0},{3,1},{4,6},{5,7},{6,4},{7,5},{8,10},{9,11},{10,... | collective-permute-start | bytes 393224 | tf_op jit(solution)/shard_map/ppermute | solution.py:211
  51.1 6.2 %collective-permute-start.14 = (f32[64,512]{1,0:T(8,128)S(1)}, f32[64,512]{1,0:T(8,128)S(1)}, u32[]{:S(2)}, u32[]{:S(2)}) collective-permute-start(f32[64,512]{1,0:T(8,128)S(1)} %get-tuple-element.43), channel_id=1, source_target_pairs={{0,1},{1,0},{2,3},{3,2},{4,5},{5,4},{6,7},{7,6},{8,9},{9,8},{10,11... | collective-permute-start | bytes 393224 | tf_op jit(solution)/shard_map/ppermute | solution.py:211
  51.9 7.8 %collective-permute-start.11 = (f32[64,512]{1,0:T(8,128)S(1)}, f32[64,512]{1,0:T(8,128)S(1)}, u32[]{:S(2)}, u32[]{:S(2)}) collective-permute-start(f32[64,512]{1,0:T(8,128)S(1)} %get-tuple-element.40), channel_id=1, source_target_pairs={{0,6},{1,7},{2,4},{3,5},{4,2},{5,3},{6,0},{7,1},{8,14},{9,15},{10,... | collective-permute-start | bytes 393224 | tf_op jit(solution)/shard_map/ppermute | solution.py:211
  53.8 5.9 %collective-permute-start.12 = (f32[64,512]{1,0:T(8,128)S(1)}, f32[64,512]{1,0:T(8,128)S(1)}, u32[]{:S(2)}, u32[]{:S(2)}) collective-permute-start(f32[64,512]{1,0:T(8,128)S(1)} %get-tuple-element.41), channel_id=1, source_target_pairs={{0,5},{1,4},{2,7},{3,6},{4,1},{5,0},{6,3},{7,2},{8,13},{9,12},{10,... | collective-permute-start | bytes 393224 | tf_op jit(solution)/shard_map/ppermute | solution.py:211

commit v6 on v4

--- a/solution.py
+++ b/solution.py
@@ -22,6 +22,12 @@
     return pl.ds(pl.multiple_of(member * width, width), width)
 
 
+def position():
+    inner_count = lax.axis_size("inner")
+    index = lax.axis_index("outer") * inner_count + lax.axis_index("inner")
+    return index, index % (CORES * inner_count)
+
+
 def heads_of(heads):
     return [slice(h * HEAD_DIM, (h + 1) * HEAD_DIM) for h in range(heads)]
 
@@ -37,11 +43,11 @@
     return found, after
 
 
-def spread(members, width, place, queries, keys, values, *refs):
+def spread(members, width, queries, keys, values, *refs):
     half = members // CORES
     near, cross = refs[:half], refs[half]
     buffers, sems = refs[half + 1 : half + 4], refs[half + 4]
-    me = place[0]
+    _, me = position()
 
     def copies(d):
         span = columns_of(me ^ d, width)
@@ -70,30 +76,37 @@
         outs[half - 1 - e][...] = swapped[e, 0:2]
 
 
-def join_queries(half, width, gates, place, queries, swapped, *refs):
-    outs = refs[gates:]
-    me = place[0]
+def join_queries(members, width, rows, docs, gates, lengths, queries, swapped, *refs):
+    half = members // CORES
+    outs, table = refs[gates:-1], refs[-1]
+    index, me = position()
     for e in range(half):
         outs[half - 1 - e][0] = queries[:, columns_of(me ^ e, width)].astype(jnp.float32)
         outs[half - 1 - e][1] = swapped[e, 2]
-
-
-def gather_states(members, heads, docs, rows, place, lengths, *refs):
+    base = (index - me) * rows
+    for j in range(members + 1):
+        found, _ = start_of(lengths, docs, base + j * rows)
+        table[j : j + 1, :] = jnp.full((1, HEAD_DIM), found - base, jnp.int32)
+    _, after = start_of(lengths, docs, index * rows)
+    table[members + 1 : members + 2, :] = jnp.full((1, HEAD_DIM), after - index * rows, jnp.int32)
+
+
+def gather_states(members, heads, rows, table, *refs):
     half = members // CORES
     parts = refs[:half][::-1] + refs[half:members][::-1]
-    carry_out, total_out, key_blocks, value_blocks = refs[members + 1 :]
-    me, base = place[0], place[1]
-    row = lax.broadcasted_iota(jnp.int32, (rows, heads * HEAD_DIM), 0)
+    carry_out, total_out, key_blocks, value_blocks = refs[members:]
+    _, me = position()
+    row = lax.broadcasted_iota(jnp.int32, (rows, HEAD_DIM), 0)
     for d in range(members):
         j = me ^ d
-        since, _ = start_of(lengths, docs, base + (j + 1) * rows)
+        kept = row >= table[pl.ds(j + 1, 1), :] - j * rows
         key, value = (parts[d][0, 0], parts[d][0, 1]) if d == half else (parts[d][0], parts[d][1])
-        key_blocks[j] = jnp.where(row >= since - base - j * rows, key, 0.0).astype(jnp.bfloat16)
+        for span in heads_of(heads):
+            key_blocks[j, :, span] = jnp.where(kept, key[:, span], 0.0).astype(jnp.bfloat16)
         value_blocks[j] = value.astype(jnp.bfloat16)
     state = [jnp.zeros((HEAD_DIM, HEAD_DIM), jnp.float32) for _ in range(heads)]
     for j in range(members):
-        since, _ = start_of(lengths, docs, base + (j + 1) * rows)
-        keep = jnp.where(since <= base + j * rows, 1.0, 0.0).astype(jnp.float32)
+        keep = jnp.where(table[j + 1 : j + 2, :] <= j * rows, 1.0, 0.0).astype(jnp.float32)
         for h, span in enumerate(heads_of(heads)):
             carry_out[j, h] = state[h]
             own = lax.dot_general(
@@ -107,8 +120,8 @@
         total_out[h] = state[h]
 
 
-def inside(head_count, docs, rows, place, lengths, queries, keys, values, out):
-    begin = place[2]
+def inside(head_count, docs, rows, lengths, queries, keys, values, out):
+    begin = position()[0] * rows
     row = lax.broadcasted_iota(jnp.int32, (rows, rows), 0)
     lane = lax.broadcasted_iota(jnp.int32, (rows, rows), 1)
     since = jnp.zeros((rows, rows), jnp.int32)
@@ -125,33 +138,30 @@
         out[:, span] = jnp.dot(weights, values[:, span], preferred_element_type=jnp.float32)
 
 
-def reach_back(members, heads, docs, rows, place, lengths, *refs):
+def reach_back(members, heads, table, *refs):
     half = members // CORES
     query_parts = refs[:half][::-1]
     carry, earlier = refs[half : half + 2]
     outs = refs[half + 3 :][::-1]
-    me, base = place[0], place[1]
-    for e in range(half):
+    _, me = position()
+    for e in reversed(range(half)):
         for side in range(CORES):
             d = e ^ (side * half)
             j = me ^ d
-            first, _ = start_of(lengths, docs, base + j * rows)
-            before = jnp.where(first < base, 1.0, 0.0).astype(jnp.float32)
+            before = jnp.where(table[pl.ds(j, 1), :] < 0, 1.0, 0.0).astype(jnp.float32)
             for h, span in enumerate(heads_of(heads)):
                 held = (carry[j, h] + before * earlier[h]).astype(jnp.bfloat16)
                 query = query_parts[e][side, :, span].astype(jnp.bfloat16)
                 outs[d][:, span] = jnp.dot(query, held, preferred_element_type=jnp.float32)
 
 
-def finish(chosen, heads, docs, rows, place, lengths, own, gain, *refs):
+def finish(chosen, members, heads, rows, table, own, gain, *refs):
     count = len(chosen)
     parts, out = refs[:count], refs[-3]
     buffer, sems = refs[-2:]
     width = heads * HEAD_DIM
-    me, begin = place[0], place[2]
-    row = lax.broadcasted_iota(jnp.int32, (rows, HEAD_DIM), 0)
-    _, after = start_of(lengths, docs, begin)
-    continued = row < after - begin
+    _, me = position()
+    continued = lax.broadcasted_iota(jnp.int32, (rows, HEAD_DIM), 0) < table[members + 1 : members + 2, :]
     copies = []
     for i, d in enumerate(chosen):
         columns = columns_of(me ^ d, width)
@@ -184,9 +194,7 @@
     index = lax.axis_index("outer") * inner_count + lax.axis_index("inner")
     me = index % members
     base = (index - me) * rows
-    place = jnp.stack([me, base, index * rows]).astype(jnp.int32)
     f32, bf16 = jnp.float32, jnp.bfloat16
-    params = pltpu.CompilerParams(vmem_limit_bytes=48 * 1024 * 1024)
 
     def call(kernel, name, out_shape, in_specs, out_specs, scratch=(), flops=0, moved=0, aliases=None):
         return pl.pallas_call(
@@ -195,7 +203,7 @@
             in_specs=in_specs,
             out_specs=out_specs,
             scratch_shapes=scratch,
-            compiler_params=params,
+            compiler_params=pltpu.CompilerParams(vmem_limit_bytes=48 * 1024 * 1024),
             cost_estimate=pl.CostEstimate(flops=flops, bytes_accessed=moved, transcendentals=0),
             input_output_aliases=aliases or {},
             name=name,
@@ -214,10 +222,10 @@
         functools.partial(spread, members, width),
         "spread",
         [shape(2, rows, width)] * half + [shape(half, 3, rows, width)],
-        [SMEM, HBM, HBM, HBM],
+        [HBM, HBM, HBM],
         [VMEM] * (half + 1),
         [pltpu.VMEM((members, rows, width), bf16)] * 3 + [pltpu.SemaphoreType.DMA((3, members))],
-    )(place, *[pltpu.with_memory_space_constraint(x, pltpu.HBM) for x in (queries, keys, values)])
+    )(*[pltpu.with_memory_space_constraint(x, pltpu.HBM) for x in (queries, keys, values)])
     near_got = [swap(part, e) if e else part for e, part in zip(downward, parts)]
     swapped = swap(parts[half], half)
     far_parts = call(
@@ -230,36 +238,36 @@
     )(swapped)
     far_got = [swap(part, e) for e, part in zip(downward, far_parts)] + [swapped]
     gates = near_got[:-1]
-    query_parts = call(
-        functools.partial(join_queries, half, width, len(gates)),
+    *query_parts, table = call(
+        functools.partial(join_queries, members, width, rows, docs, len(gates)),
         "join_queries",
-        [shape(CORES, rows, width)] * half,
+        [shape(CORES, rows, width)] * half + [shape(members + 2, HEAD_DIM, dtype=jnp.int32)],
         [SMEM, VMEM, VMEM] + [ANY] * len(gates),
-        [VMEM] * half,
+        [VMEM] * (half + 1),
         moved=2 * block_bytes,
-    )(place, queries, swapped, *gates)
+    )(lengths, queries, swapped, *gates)
     query_got = [swap(part, e) if e else part for e, part in zip(downward, query_parts)]
 
     own = call(
         functools.partial(inside, head_count, docs, rows),
         "inside",
         shape(rows, columns),
-        [SMEM, SMEM, VMEM, VMEM, VMEM],
+        [SMEM, VMEM, VMEM, VMEM],
         VMEM,
         flops=4 * rows * rows * columns,
         moved=3 * block_bytes,
-    )(place, lengths, queries, keys, values)
+    )(lengths, queries, keys, values)
 
     carry, total = call(
-        functools.partial(gather_states, members, heads, docs, rows),
+        functools.partial(gather_states, members, heads, rows),
         "gather_states",
         [shape(members, heads, HEAD_DIM, HEAD_DIM), shape(heads, HEAD_DIM, HEAD_DIM)],
-        [SMEM, SMEM] + [VMEM] * members + [ANY],
+        [VMEM] * (members + 1),
         [VMEM] * 2,
         [pltpu.VMEM((members, rows, width), bf16)] * 2,
         flops=2 * rows * HEAD_DIM * columns,
         moved=4 * block_bytes,
-    )(place, lengths, *near_got, *far_got, query_parts[-1])
+    )(table, *near_got, *far_got)
     up = [(g, g + members) for g in range(devices - members)]
     moving = lax.ppermute(total, everyone, up)
     earlier = moving
@@ -270,32 +278,33 @@
             moving = lax.ppermute(moving, everyone, up)
             earlier = earlier + jnp.where(opens < base - (k - 1) * members * rows, moving, 0.0)
     crossed = call(
-        functools.partial(reach_back, members, heads, docs, rows),
+        functools.partial(reach_back, members, heads),
         "reach_back",
         [shape(rows, width)] * members,
-        [SMEM, SMEM] + [VMEM] * (half + 2) + [ANY],
+        [VMEM] * (half + 3) + [ANY],
         [VMEM] * members,
         flops=2 * rows * HEAD_DIM * columns,
         moved=4 * block_bytes,
-    )(place, lengths, *query_got, carry, earlier, own)
+    )(table, *query_got, carry, earlier, own)
     crossed_got = [swap(crossed[members - 1 - d], d) if d else crossed[-1] for d in range(members)]
 
     gain = norm_gain.reshape(1, columns)
     last = [d for d in range(members) if d % half in (1, 2)]
-    first = [d for d in reversed(range(members)) if d not in last]
+    first = [d for d in range(members) if d not in last]
+    first.sort(key=lambda d: (d != half, -d))
     out = None
     for chosen in (first, last):
         more = [] if out is None else [out]
         out = call(
-            functools.partial(finish, chosen, heads, docs, rows),
+            functools.partial(finish, chosen, members, heads, rows),
             "finish",
             shape(rows, columns, dtype=bf16),
-            [SMEM, SMEM, VMEM, VMEM] + [VMEM] * len(chosen) + [ANY] * len(more),
+            [VMEM] * (3 + len(chosen)) + [ANY] * len(more),
             ANY,
             [pltpu.VMEM((len(chosen), rows, width), bf16), pltpu.SemaphoreType.DMA((len(chosen),))],
             moved=2 * block_bytes,
-            aliases={4 + len(chosen): 0} if more else None,
-        )(place, lengths, own, gain, *[crossed_got[d] for d in chosen], *more)
+            aliases={3 + len(chosen): 0} if more else None,
+        )(table, own, gain, *[crossed_got[d] for d in chosen], *more)
     return out
 
 

time: 59.2 us -> 57.9 us (0.978)
  Pallas kernels: 12.9 us -> 10.3 us
  waiting for transfers between devices: 20.7 us -> 21.6 us
    pallas_call x5, Pallas kernels: 5.8 us -> 3.76 us  [the longest x2 1.8 us: body(): call(functools.partial(finish, chosen, members, heads, rows), 'finish', s...]
    ppermute x17, waiting for transfers between devices: 20.7 us -> 21.6 us  [swap(): return lax.ppermute(part, everyone, pairs)]
  transfers between devices with their start and end apart: 18 -> 18, of which waited for: 12 -> 13; matrix products, arithmetic and copies ran while one was open for 0% -> 0% of each run, Pallas kernels for 14% -> 13%
where the time goes in v6:
time: 57.9 us; the launch traced here: 57.7 us
  starting transfers between devices  25.7 us (44%)
  waiting for transfers between devices  21.6 us (37%)
  Pallas kernels  10.3 us (18%)
    ppermute x17, starting transfers between devices, swap(): return lax.ppermute(part, everyone, pairs)  22.2 us
    ppermute x17, waiting for transfers between devices, swap(): return lax.ppermute(part, everyone, pairs)  21.6 us
    pallas_call x1, Pallas kernels, body(): call(functools.partial(inside, head_count, docs, rows), 'inside', shape(r...  4.93 us
    ppermute x1, starting transfers between devices, body(): moving = lax.ppermute(total, everyone, up)  3.5 us
    pallas_call x2, Pallas kernels, body(): call(functools.partial(finish, chosen, members, heads, rows), 'finish', s...  1.8 us
    pallas_call x1, Pallas kernels, body(): call(functools.partial(spread, members, width), 'spread', [shape(2, rows,...  1.59 us
  transfers between devices with their start and end apart: 18, of which 13 were waited for; matrix products, arithmetic and copies ran while one was open for 0% of the time, Pallas kernels for 13%

profile of v6, /device:TPU:0, one launch (start us, length us, event | category | flops | bytes accessed | tf_op | source)
XLA Modules:
  0.0 57.7 jit_solution(12912509237005669645)
XLA Ops:
  0.0 0.0 copy-start
  0.0 0.0 copy-start.4
  0.0 1.6 %spread.1 = (f32[2,64,512]{2,1,0:T(8,128)S(1)}, f32[2,64,512]{2,1,0:T(8,128)S(1)}, f32[2,64,512]{2,1,0:T(8,128)S(1)}, f32[2,64,512]{2,1,0:T(8,128)S(1)}, f32[4,3,64,512]{3,2,1,0:T(8,128)S(1)}) custom-call(bf16[64,4096]{1,0:T(8,128)(2,1)} %queries.5, bf16[64,4096]{1,0:T(8,128)(2,1)} %keys.3, bf16[64,4096]{1,0:T(8,128)(2,1)} %values.3), custom_call_target="tpu_custom_call" | custom-call | tf_op jit(solution)/shard_map/spread/pallas_call | solution.py:221
  1.6 0.5 collective-permute-start
  2.1 3.5 %collective-permute-start.1 = (f32[2,64,512]{2,1,0:T(8,128)S(1)}, f32[2,64,512]{2,1,0:T(8,128)S(1)}, u32[]{:S(2)}, u32[]{:S(2)}) collective-permute-start(f32[2,64,512]{2,1,0:T(8,128)S(1)} %get-tuple-element.29), channel_id=1, source_target_pairs={{0,3},{1,2},{2,1},{3,0},{4,7},{5,6},{6,5},{7,4},{8,11},{9,10},{10,... | collective-permute-start | bytes 786440 | tf_op jit(solution)/shard_map/ppermute | solution.py:217
  5.6 0.5 collective-permute-start.2
  6.2 0.1 collective-permute-start.3
  6.3 0.0 collective-permute-done.swapped.refs_7_
  6.3 0.1 forward.1
  6.3 2.9 %collective-permute-start.7 = (f32[2,64,512]{2,1,0:T(8,128)S(1)}, f32[2,64,512]{2,1,0:T(8,128)S(1)}, u32[]{:S(2)}, u32[]{:S(2)}) collective-permute-start(f32[2,64,512]{2,1,0:T(8,128)S(1)} %get-tuple-element.38), channel_id=1, source_target_pairs={{0,3},{1,2},{2,1},{3,0},{4,7},{5,6},{6,5},{7,4},{8,11},{9,10},{10,... | collective-permute-start | bytes 786440 | tf_op jit(solution)/shard_map/ppermute | solution.py:217
  9.3 0.5 collective-permute-start.8
  9.8 3.1 %collective-permute-done.1.refs_0_ = f32[2,64,512]{2,1,0:T(8,128)S(1)} collective-permute-done((f32[2,64,512]{2,1,0:T(8,128)S(1)}, f32[2,64,512]{2,1,0:T(8,128)S(1)}, u32[]{:S(2)}, u32[]{:S(2)}) %collective-permute-start.1) | collective-permute-done | bytes 262176 | tf_op jit(solution)/shard_map/ppermute | solution.py:217
  12.8 1.9 %collective-permute-start.9 = (f32[2,64,512]{2,1,0:T(8,128)S(1)}, f32[2,64,512]{2,1,0:T(8,128)S(1)}, u32[]{:S(2)}, u32[]{:S(2)}) collective-permute-start(f32[2,64,512]{2,1,0:T(8,128)S(1)} %get-tuple-element.40), channel_id=1, source_target_pairs={{0,1},{1,0},{2,3},{3,2},{4,5},{5,4},{6,7},{7,6},{8,9},{9,8},{10,11... | collective-permute-start | bytes 786440 | tf_op jit(solution)/shard_map/ppermute | solution.py:217
  14.7 3.8 %collective-permute-done.2.refs_1_ = f32[2,64,512]{2,1,0:T(8,128)S(1)} collective-permute-done((f32[2,64,512]{2,1,0:T(8,128)S(1)}, f32[2,64,512]{2,1,0:T(8,128)S(1)}, u32[]{:S(2)}, u32[]{:S(2)}) %collective-permute-start.2) | collective-permute-done | bytes 262176 | tf_op jit(solution)/shard_map/ppermute | solution.py:217
  18.5 0.4 collective-permute-done.3.refs_2_
  18.9 0.0 copy-done
  18.9 0.0 copy-done.4
  18.9 0.7 %join_queries.1 = (f32[2,64,512]{2,1,0:T(8,128)S(1)}, f32[2,64,512]{2,1,0:T(8,128)S(1)}, f32[2,64,512]{2,1,0:T(8,128)S(1)}, f32[2,64,512]{2,1,0:T(8,128)S(1)}, s32[10,128]{1,0:T(8,128)S(1)}) custom-call(s32[16]{0:T(128)S(1)} %copy-done.4, bf16[64,4096]{1,0:T(8,128)(2,1)S(1)} %copy-done, f32[4,3,64,512]{3,2,1,0:T(8,128)S(1)} %collective-permute-done.swapped.refs_7_, ...), custom_call_target="tpu_custom_call" | custom-call | bytes 2097152 | tf_op jit(solution)/shard_map/join_queries/pallas_call | solution.py:241
  19.7 1.7 %collective-permute-start.4 = (f32[2,64,512]{2,1,0:T(8,128)S(1)}, f32[2,64,512]{2,1,0:T(8,128)S(1)}, u32[]{:S(2)}, u32[]{:S(2)}) collective-permute-start(f32[2,64,512]{2,1,0:T(8,128)S(1)} %get-tuple-element.33), channel_id=1, source_target_pairs={{0,3},{1,2},{2,1},{3,0},{4,7},{5,6},{6,5},{7,4},{8,11},{9,10},{10,... | collective-permute-start | bytes 786440 | tf_op jit(solution)/shard_map/ppermute | solution.py:217
  21.3 1.4 %collective-permute-start.5 = (f32[2,64,512]{2,1,0:T(8,128)S(1)}, f32[2,64,512]{2,1,0:T(8,128)S(1)}, u32[]{:S(2)}, u32[]{:S(2)}) collective-permute-start(f32[2,64,512]{2,1,0:T(8,128)S(1)} %get-tuple-element.34), channel_id=1, source_target_pairs={{0,2},{1,3},{2,0},{3,1},{4,6},{5,7},{6,4},{7,5},{8,10},{9,11},{10,... | collective-permute-start | bytes 786440 | tf_op jit(solution)/shard_map/ppermute | solution.py:217
  22.7 1.4 %collective-permute-done.7.refs_4_ = f32[2,64,512]{2,1,0:T(8,128)S(1)} collective-permute-done((f32[2,64,512]{2,1,0:T(8,128)S(1)}, f32[2,64,512]{2,1,0:T(8,128)S(1)}, u32[]{:S(2)}, u32[]{:S(2)}) %collective-permute-start.7) | collective-permute-done | bytes 262176 | tf_op jit(solution)/shard_map/ppermute | solution.py:217
  24.1 1.9 %collective-permute-start.6 = (f32[2,64,512]{2,1,0:T(8,128)S(1)}, f32[2,64,512]{2,1,0:T(8,128)S(1)}, u32[]{:S(2)}, u32[]{:S(2)}) collective-permute-start(f32[2,64,512]{2,1,0:T(8,128)S(1)} %get-tuple-element.35), channel_id=1, source_target_pairs={{0,1},{1,0},{2,3},{3,2},{4,5},{5,4},{6,7},{7,6},{8,9},{9,8},{10,11... | collective-permute-start | bytes 786440 | tf_op jit(solution)/shard_map/ppermute | solution.py:217
  26.0 3.7 %collective-permute-done.8.refs_5_ = f32[2,64,512]{2,1,0:T(8,128)S(1)} collective-permute-done((f32[2,64,512]{2,1,0:T(8,128)S(1)}, f32[2,64,512]{2,1,0:T(8,128)S(1)}, u32[]{:S(2)}, u32[]{:S(2)}) %collective-permute-start.8) | collective-permute-done | bytes 262176 | tf_op jit(solution)/shard_map/ppermute | solution.py:217
  29.7 0.5 collective-permute-done.9.refs_6_
  30.2 0.0 copy-start.1
  30.2 0.0 copy-start.2
  30.2 0.6 %gather_states.1 = (f32[8,4,128,128]{3,2,1,0:T(8,128)S(1)}, f32[4,128,128]{2,1,0:T(8,128)S(1)}) custom-call(s32[10,128]{1,0:T(8,128)S(1)} %get-tuple-element.32.table, f32[2,64,512]{2,1,0:T(8,128)S(1)} %collective-permute-done.1.refs_0_, f32[2,64,512]{2,1,0:T(8,128)S(1)} %collective-permute-done.2.refs_1_, f32[2,64,512]{2,1,0:T(8,128)S(1)} %collective-permute-done.3.refs_2_, ...), custom_call_target="tpu_custom_call" | custom-call | flops 67108864 | bytes 4194304 | tf_op jit(solution)/shard_map/gather_states/pallas_call | solution.py:261
  30.8 3.5 %collective-permute-start.10 = (f32[4,128,128]{2,1,0:T(8,128)S(1)}, f32[4,128,128]{2,1,0:T(8,128)S(1)}, u32[]{:S(2)}, u32[]{:S(2)}) collective-permute-start(f32[4,128,128]{2,1,0:T(8,128)S(1)} %get-tuple-element.42), channel_id=1, source_target_pairs={{0,8},{1,9},{2,10},{3,11},{4,12},{5,13},{6,14},{7,15},{8,16},{9,17... | collective-permute-start | bytes 786440 | tf_op jit(solution)/shard_map/ppermute | solution.py:272
  34.3 0.0 copy-done.1
  34.3 0.0 copy-done.2
  34.3 4.9 %inside.1.refs_6_.own = f32[64,4096]{1,0:T(8,128)S(1)} custom-call(s32[16]{0:T(128)S(1)} %copy-done.4, bf16[64,4096]{1,0:T(8,128)(2,1)S(1)} %copy-done, bf16[64,4096]{1,0:T(8,128)(2,1)S(1)} %copy-done.1, bf16[64,4096]{1,0:T(8,128)(2,1)S(1)} %copy-done.2), custom_call_target="tpu_custom_call" | custom-call | flops 67108864 | bytes 3145728 | tf_op jit(solution)/shard_map/inside/pallas_call | solution.py:251
  39.3 0.0 collective-permute-done.4.refs_0_
  39.3 1.4 %collective-permute-done.5.refs_1_ = f32[2,64,512]{2,1,0:T(8,128)S(1)} collective-permute-done((f32[2,64,512]{2,1,0:T(8,128)S(1)}, f32[2,64,512]{2,1,0:T(8,128)S(1)}, u32[]{:S(2)}, u32[]{:S(2)}) %collective-permute-start.5) | collective-permute-done | bytes 262176 | tf_op jit(solution)/shard_map/ppermute | solution.py:217
  40.6 0.4 collective-permute-done.6.refs_2_
  41.0 0.0 collective-permute-done.10.refs_5_
  41.0 0.0 copy-start.3
  41.0 0.6 %reach_back.1 = (f32[64,512]{1,0:T(8,128)S(1)}, f32[64,512]{1,0:T(8,128)S(1)}, f32[64,512]{1,0:T(8,128)S(1)}, f32[64,512]{1,0:T(8,128)S(1)}, f32[64,512]{1,0:T(8...) custom-call(s32[10,128]{1,0:T(8,128)S(1)} %get-tuple-element.32.table, ...), custom_call_target="tpu_custom_call" | custom-call | flops 67108864 | bytes 4194304 | tf_op jit(solution)/shard_map/reach_back/pallas_call | solution.py:280
  41.6 0.1 collective-permute-start.15
  41.7 1.5 %collective-permute-start.16 = (f32[64,512]{1,0:T(8,128)S(1)}, f32[64,512]{1,0:T(8,128)S(1)}, u32[]{:S(2)}, u32[]{:S(2)}) collective-permute-start(f32[64,512]{1,0:T(8,128)S(1)} %get-tuple-element.48), channel_id=1, source_target_pairs={{0,7},{1,6},{2,5},{3,4},{4,3},{5,2},{6,1},{7,0},{8,15},{9,14},{10,... | collective-permute-start | bytes 393224 | tf_op jit(solution)/shard_map/ppermute | solution.py:217
  43.3 1.5 %collective-permute-start.17 = (f32[64,512]{1,0:T(8,128)S(1)}, f32[64,512]{1,0:T(8,128)S(1)}, u32[]{:S(2)}, u32[]{:S(2)}) collective-permute-start(f32[64,512]{1,0:T(8,128)S(1)} %get-tuple-element.49), channel_id=1, source_target_pairs={{0,3},{1,2},{2,1},{3,0},{4,7},{5,6},{6,5},{7,4},{8,11},{9,10},{10,... | collective-permute-start | bytes 393224 | tf_op jit(solution)/shard_map/ppermute | solution.py:217
  44.8 1.5 %collective-permute-start.11 = (f32[64,512]{1,0:T(8,128)S(1)}, f32[64,512]{1,0:T(8,128)S(1)}, u32[]{:S(2)}, u32[]{:S(2)}) collective-permute-start(f32[64,512]{1,0:T(8,128)S(1)} %get-tuple-element.43), channel_id=1, source_target_pairs={{0,1},{1,0},{2,3},{3,2},{4,5},{5,4},{6,7},{7,6},{8,9},{9,8},{10,11... | collective-permute-start | bytes 393224 | tf_op jit(solution)/shard_map/ppermute | solution.py:217
  46.2 0.5 collective-permute-start.12
  46.8 0.0 collective-permute-done.15.refs_0_
  46.8 0.2 collective-permute-start.13
  47.0 0.9 %collective-permute-done.16.refs_1_ = f32[64,512]{1,0:T(8,128)S(1)} collective-permute-done((f32[64,512]{1,0:T(8,128)S(1)}, f32[64,512]{1,0:T(8,128)S(1)}, u32[]{:S(2)}, u32[]{:S(2)}) %collective-permute-start.16) | collective-permute-done | bytes 131104 | tf_op jit(solution)/shard_map/ppermute | solution.py:217
  47.9 2.0 %collective-permute-start.14 = (f32[64,512]{1,0:T(8,128)S(1)}, f32[64,512]{1,0:T(8,128)S(1)}, u32[]{:S(2)}, u32[]{:S(2)}) collective-permute-start(f32[64,512]{1,0:T(8,128)S(1)} %get-tuple-element.46), channel_id=1, source_target_pairs={{0,6},{1,7},{2,4},{3,5},{4,2},{5,3},{6,0},{7,1},{8,14},{9,15},{10,... | collective-permute-start | bytes 393224 | tf_op jit(solution)/shard_map/ppermute | solution.py:217
  49.9 2.0 %collective-permute-done.17.refs_2_ = f32[64,512]{1,0:T(8,128)S(1)} collective-permute-done((f32[64,512]{1,0:T(8,128)S(1)}, f32[64,512]{1,0:T(8,128)S(1)}, u32[]{:S(2)}, u32[]{:S(2)}) %collective-permute-start.17) | collective-permute-done | bytes 131104 | tf_op jit(solution)/shard_map/ppermute | solution.py:217
  51.9 0.0 copy-done.3
  51.9 0.9 %finish.2.refs_4_ = bf16[64,4096]{1,0:T(8,128)(2,1)} custom-call(s32[10,128]{1,0:T(8,128)S(1)} %get-tuple-element.32.table, f32[64,4096]{1,0:T(8,128)S(1)} %inside.1.refs_6_.own, f32[1,4096]{1,0:T(1,128)S(1)} %bitcast.1, f32[64,512]{1,0:T(8,128)S(1)} %collective-permute-done.15.refs_0_, f32[64,512]{1,0:T(8,128)S(1)} %collective-permute-done.16.refs_1_, ...), custom_call_target="tpu_custom_call" | custom-call | bytes 2097152 | tf_op jit(solution)/shard_map/finish/pallas_call | solution.py:298
  52.8 1.8 %collective-permute-done.11.refs_0_ = f32[64,512]{1,0:T(8,128)S(1)} collective-permute-done((f32[64,512]{1,0:T(8,128)S(1)}, f32[64,512]{1,0:T(8,128)S(1)}, u32[]{:S(2)}, u32[]{:S(2)}) %collective-permute-start.11) | collective-permute-done | bytes 131104 | tf_op jit(solution)/shard_map/ppermute | solution.py:217
  54.6 0.0 collective-permute-done.12.refs_1_
  54.6 1.7 %collective-permute-done.13.refs_2_ = f32[64,512]{1,0:T(8,128)S(1)} collective-permute-done((f32[64,512]{1,0:T(8,128)S(1)}, f32[64,512]{1,0:T(8,128)S(1)}, u32[]{:S(2)}, u32[]{:S(2)}) %collective-permute-start.13) | collective-permute-done | bytes 131104 | tf_op jit(solution)/shard_map/ppermute | solution.py:217
  56.3 0.5 collective-permute-done.14.refs_3_
  56.8 0.9 %finish.3 = bf16[64,4096]{1,0:T(8,128)(2,1)} custom-call(s32[10,128]{1,0:T(8,128)S(1)} %get-tuple-element.32.table, f32[64,4096]{1,0:T(8,128)S(1)} %inside.1.refs_6_.own, f32[1,4096]{1,0:T(1,128)S(1)} %bitcast.2, f32[64,512]{1,0:T(8,128)S(1)} %collective-permute-done.11.refs_0_, ...), custom_call_target="tpu_custom_call", output_to_operand_aliasing={{}: (7, {})} | custom-call | bytes 2097152 | tf_op jit(solution)/shard_map/finish/pallas_call | solution.py:298
Async XLA Ops:
  0.0 18.9 %copy-start = (bf16[64,4096]{1,0:T(8,128)(2,1)S(1)}, bf16[64,4096]{1,0:T(8,128)(2,1)}, u32[]{:S(2)}) copy-start(bf16[64,4096]{1,0:T(8,128)(2,1)} %queries.5) | copy-start | bytes 1572868
  0.0 18.9 %copy-start.4 = (s32[16]{0:T(128)S(1)}, s32[16]{0:T(128)}, u32[]{:S(2)}) copy-start(s32[16]{0:T(128)} %lengths.3) | copy-start | bytes 196
  1.6 4.7 %collective-permute-start = (f32[4,3,64,512]{3,2,1,0:T(8,128)S(1)}, f32[4,3,64,512]{3,2,1,0:T(8,128)S(1)}, u32[]{:S(2)}, u32[]{:S(2)}) collective-permute-start(f32[4,3,64,512]{3,2,1,0:T(8,128)S(1)} %get-tuple-element.28), channel_id=1, source_target_pairs={{0,4},{1,5},{2,6},{3,7},{4,0},{5,1},{6,2},{7,3},{8,12},{9,13},{10,... | collective-permute-start | bytes 4718600 | tf_op jit(solution)/shard_map/ppermute | solution.py:217
  2.1 10.7 %collective-permute-start.1 = (f32[2,64,512]{2,1,0:T(8,128)S(1)}, f32[2,64,512]{2,1,0:T(8,128)S(1)}, u32[]{:S(2)}, u32[]{:S(2)}) collective-permute-start(f32[2,64,512]{2,1,0:T(8,128)S(1)} %get-tuple-element.29), channel_id=1, source_target_pairs={{0,3},{1,2},{2,1},{3,0},{4,7},{5,6},{6,5},{7,4},{8,11},{9,10},{10,... | collective-permute-start | bytes 786440 | tf_op jit(solution)/shard_map/ppermute | solution.py:217
  5.6 12.9 %collective-permute-start.2 = (f32[2,64,512]{2,1,0:T(8,128)S(1)}, f32[2,64,512]{2,1,0:T(8,128)S(1)}, u32[]{:S(2)}, u32[]{:S(2)}) collective-permute-start(f32[2,64,512]{2,1,0:T(8,128)S(1)} %get-tuple-element.30), channel_id=1, source_target_pairs={{0,2},{1,3},{2,0},{3,1},{4,6},{5,7},{6,4},{7,5},{8,10},{9,11},{10,... | collective-permute-start | bytes 786440 | tf_op jit(solution)/shard_map/ppermute | solution.py:217
  6.2 12.8 %collective-permute-start.3 = (f32[2,64,512]{2,1,0:T(8,128)S(1)}, f32[2,64,512]{2,1,0:T(8,128)S(1)}, u32[]{:S(2)}, u32[]{:S(2)}) collective-permute-start(f32[2,64,512]{2,1,0:T(8,128)S(1)} %get-tuple-element.31), channel_id=1, source_target_pairs={{0,1},{1,0},{2,3},{3,2},{4,5},{5,4},{6,7},{7,6},{8,9},{9,8},{10,11... | collective-permute-start | bytes 786440 | tf_op jit(solution)/shard_map/ppermute | solution.py:217
  6.3 17.8 %collective-permute-start.7 = (f32[2,64,512]{2,1,0:T(8,128)S(1)}, f32[2,64,512]{2,1,0:T(8,128)S(1)}, u32[]{:S(2)}, u32[]{:S(2)}) collective-permute-start(f32[2,64,512]{2,1,0:T(8,128)S(1)} %get-tuple-element.38), channel_id=1, source_target_pairs={{0,3},{1,2},{2,1},{3,0},{4,7},{5,6},{6,5},{7,4},{8,11},{9,10},{10,... | collective-permute-start | bytes 786440 | tf_op jit(solution)/shard_map/ppermute | solution.py:217
  9.3 20.5 %collective-permute-start.8 = (f32[2,64,512]{2,1,0:T(8,128)S(1)}, f32[2,64,512]{2,1,0:T(8,128)S(1)}, u32[]{:S(2)}, u32[]{:S(2)}) collective-permute-start(f32[2,64,512]{2,1,0:T(8,128)S(1)} %get-tuple-element.39), channel_id=1, source_target_pairs={{0,2},{1,3},{2,0},{3,1},{4,6},{5,7},{6,4},{7,5},{8,10},{9,11},{10,... | collective-permute-start | bytes 786440 | tf_op jit(solution)/shard_map/ppermute | solution.py:217
  12.8 17.4 %collective-permute-start.9 = (f32[2,64,512]{2,1,0:T(8,128)S(1)}, f32[2,64,512]{2,1,0:T(8,128)S(1)}, u32[]{:S(2)}, u32[]{:S(2)}) collective-permute-start(f32[2,64,512]{2,1,0:T(8,128)S(1)} %get-tuple-element.40), channel_id=1, source_target_pairs={{0,1},{1,0},{2,3},{3,2},{4,5},{5,4},{6,7},{7,6},{8,9},{9,8},{10,11... | collective-permute-start | bytes 786440 | tf_op jit(solution)/shard_map/ppermute | solution.py:217
  19.7 19.6 %collective-permute-start.4 = (f32[2,64,512]{2,1,0:T(8,128)S(1)}, f32[2,64,512]{2,1,0:T(8,128)S(1)}, u32[]{:S(2)}, u32[]{:S(2)}) collective-permute-start(f32[2,64,512]{2,1,0:T(8,128)S(1)} %get-tuple-element.33), channel_id=1, source_target_pairs={{0,3},{1,2},{2,1},{3,0},{4,7},{5,6},{6,5},{7,4},{8,11},{9,10},{10,... | collective-permute-start | bytes 786440 | tf_op jit(solution)/shard_map/ppermute | solution.py:217
  21.3 19.3 %collective-permute-start.5 = (f32[2,64,512]{2,1,0:T(8,128)S(1)}, f32[2,64,512]{2,1,0:T(8,128)S(1)}, u32[]{:S(2)}, u32[]{:S(2)}) collective-permute-start(f32[2,64,512]{2,1,0:T(8,128)S(1)} %get-tuple-element.34), channel_id=1, source_target_pairs={{0,2},{1,3},{2,0},{3,1},{4,6},{5,7},{6,4},{7,5},{8,10},{9,11},{10,... | collective-permute-start | bytes 786440 | tf_op jit(solution)/shard_map/ppermute | solution.py:217
  24.1 16.9 %collective-permute-start.6 = (f32[2,64,512]{2,1,0:T(8,128)S(1)}, f32[2,64,512]{2,1,0:T(8,128)S(1)}, u32[]{:S(2)}, u32[]{:S(2)}) collective-permute-start(f32[2,64,512]{2,1,0:T(8,128)S(1)} %get-tuple-element.35), channel_id=1, source_target_pairs={{0,1},{1,0},{2,3},{3,2},{4,5},{5,4},{6,7},{7,6},{8,9},{9,8},{10,11... | collective-permute-start | bytes 786440 | tf_op jit(solution)/shard_map/ppermute | solution.py:217
  30.2 4.1 %copy-start.1 = (bf16[64,4096]{1,0:T(8,128)(2,1)S(1)}, bf16[64,4096]{1,0:T(8,128)(2,1)}, u32[]{:S(2)}) copy-start(bf16[64,4096]{1,0:T(8,128)(2,1)} %keys.3) | copy-start | bytes 1572868
  30.2 4.1 %copy-start.2 = (bf16[64,4096]{1,0:T(8,128)(2,1)S(1)}, bf16[64,4096]{1,0:T(8,128)(2,1)}, u32[]{:S(2)}) copy-start(bf16[64,4096]{1,0:T(8,128)(2,1)} %values.3) | copy-start | bytes 1572868
  30.8 10.2 %collective-permute-start.10 = (f32[4,128,128]{2,1,0:T(8,128)S(1)}, f32[4,128,128]{2,1,0:T(8,128)S(1)}, u32[]{:S(2)}, u32[]{:S(2)}) collective-permute-start(f32[4,128,128]{2,1,0:T(8,128)S(1)} %get-tuple-element.42), channel_id=1, source_target_pairs={{0,8},{1,9},{2,10},{3,11},{4,12},{5,13},{6,14},{7,15},{8,16},{9,17... | collective-permute-start | bytes 786440 | tf_op jit(solution)/shard_map/ppermute | solution.py:272
  41.0 10.9 %copy-start.3 = (f32[4096]{0:T(1024)S(1)}, f32[4096]{0:T(1024)}, u32[]{:S(2)}) copy-start(f32[4096]{0:T(1024)} %param.9) | copy-start | bytes 49156
  41.6 5.1 %collective-permute-start.15 = (f32[64,512]{1,0:T(8,128)S(1)}, f32[64,512]{1,0:T(8,128)S(1)}, u32[]{:S(2)}, u32[]{:S(2)}) collective-permute-start(f32[64,512]{1,0:T(8,128)S(1)} %get-tuple-element.47), channel_id=1, source_target_pairs={{0,4},{1,5},{2,6},{3,7},{4,0},{5,1},{6,2},{7,3},{8,12},{9,13},{10,... | collective-permute-start | bytes 393224 | tf_op jit(solution)/shard_map/ppermute | solution.py:217
  41.7 6.2 %collective-permute-start.16 = (f32[64,512]{1,0:T(8,128)S(1)}, f32[64,512]{1,0:T(8,128)S(1)}, u32[]{:S(2)}, u32[]{:S(2)}) collective-permute-start(f32[64,512]{1,0:T(8,128)S(1)} %get-tuple-element.48), channel_id=1, source_target_pairs={{0,7},{1,6},{2,5},{3,4},{4,3},{5,2},{6,1},{7,0},{8,15},{9,14},{10,... | collective-permute-start | bytes 393224 | tf_op jit(solution)/shard_map/ppermute | solution.py:217
  43.3 8.6 %collective-permute-start.17 = (f32[64,512]{1,0:T(8,128)S(1)}, f32[64,512]{1,0:T(8,128)S(1)}, u32[]{:S(2)}, u32[]{:S(2)}) collective-permute-start(f32[64,512]{1,0:T(8,128)S(1)} %get-tuple-element.49), channel_id=1, source_target_pairs={{0,3},{1,2},{2,1},{3,0},{4,7},{5,6},{6,5},{7,4},{8,11},{9,10},{10,... | collective-permute-start | bytes 393224 | tf_op jit(solution)/shard_map/ppermute | solution.py:217
  44.8 9.8 %collective-permute-start.11 = (f32[64,512]{1,0:T(8,128)S(1)}, f32[64,512]{1,0:T(8,128)S(1)}, u32[]{:S(2)}, u32[]{:S(2)}) collective-permute-start(f32[64,512]{1,0:T(8,128)S(1)} %get-tuple-element.43), channel_id=1, source_target_pairs={{0,1},{1,0},{2,3},{3,2},{4,5},{5,4},{6,7},{7,6},{8,9},{9,8},{10,11... | collective-permute-start | bytes 393224 | tf_op jit(solution)/shard_map/ppermute | solution.py:217
  46.2 8.3 %collective-permute-start.12 = (f32[64,512]{1,0:T(8,128)S(1)}, f32[64,512]{1,0:T(8,128)S(1)}, u32[]{:S(2)}, u32[]{:S(2)}) collective-permute-start(f32[64,512]{1,0:T(8,128)S(1)} %get-tuple-element.44), channel_id=1, source_target_pairs={{0,2},{1,3},{2,0},{3,1},{4,6},{5,7},{6,4},{7,5},{8,10},{9,11},{10,... | collective-permute-start | bytes 393224 | tf_op jit(solution)/shard_map/ppermute | solution.py:217
  46.8 9.5 %collective-permute-start.13 = (f32[64,512]{1,0:T(8,128)S(1)}, f32[64,512]{1,0:T(8,128)S(1)}, u32[]{:S(2)}, u32[]{:S(2)}) collective-permute-start(f32[64,512]{1,0:T(8,128)S(1)} %get-tuple-element.45), channel_id=1, source_target_pairs={{0,5},{1,4},{2,7},{3,6},{4,1},{5,0},{6,3},{7,2},{8,13},{9,12},{10,... | collective-permute-start | bytes 393224 | tf_op jit(solution)/shard_map/ppermute | solution.py:217
  47.9 8.9 %collective-permute-start.14 = (f32[64,512]{1,0:T(8,128)S(1)}, f32[64,512]{1,0:T(8,128)S(1)}, u32[]{:S(2)}, u32[]{:S(2)}) collective-permute-start(f32[64,512]{1,0:T(8,128)S(1)} %get-tuple-element.46), channel_id=1, source_target_pairs={{0,6},{1,7},{2,4},{3,5},{4,2},{5,3},{6,0},{7,1},{8,14},{9,15},{10,... | collective-permute-start | bytes 393224 | tf_op jit(solution)/shard_map/ppermute | solution.py:217

commit v7 on v6

--- a/solution.py
+++ b/solution.py
@@ -94,7 +94,7 @@
 def gather_states(members, heads, rows, table, *refs):
     half = members // CORES
     parts = refs[:half][::-1] + refs[half:members][::-1]
-    carry_out, total_out, key_blocks, value_blocks = refs[members:]
+    carry_out, total_out, key_blocks, value_blocks = refs[members + 1 :]
     _, me = position()
     row = lax.broadcasted_iota(jnp.int32, (rows, HEAD_DIM), 0)
     for d in range(members):
@@ -138,21 +138,19 @@
         out[:, span] = jnp.dot(weights, values[:, span], preferred_element_type=jnp.float32)
 
 
-def reach_back(members, heads, table, *refs):
+def reach_back(members, heads, chosen, gates, table, carry, earlier, *refs):
+    count = len(chosen)
     half = members // CORES
-    query_parts = refs[:half][::-1]
-    carry, earlier = refs[half : half + 2]
-    outs = refs[half + 3 :][::-1]
+    query_parts, outs = refs[:count], refs[count + gates :]
     _, me = position()
-    for e in reversed(range(half)):
+    for n, e in enumerate(chosen):
         for side in range(CORES):
-            d = e ^ (side * half)
-            j = me ^ d
+            j = me ^ e ^ (side * half)
             before = jnp.where(table[pl.ds(j, 1), :] < 0, 1.0, 0.0).astype(jnp.float32)
             for h, span in enumerate(heads_of(heads)):
                 held = (carry[j, h] + before * earlier[h]).astype(jnp.bfloat16)
-                query = query_parts[e][side, :, span].astype(jnp.bfloat16)
-                outs[d][:, span] = jnp.dot(query, held, preferred_element_type=jnp.float32)
+                query = query_parts[n][side, :, span].astype(jnp.bfloat16)
+                outs[n * CORES + side][:, span] = jnp.dot(query, held, preferred_element_type=jnp.float32)
 
 
 def finish(chosen, members, heads, rows, table, own, gain, *refs):
@@ -203,7 +201,7 @@
             in_specs=in_specs,
             out_specs=out_specs,
             scratch_shapes=scratch,
-            compiler_params=pltpu.CompilerParams(vmem_limit_bytes=48 * 1024 * 1024),
+            compiler_params=pltpu.CompilerParams(vmem_limit_bytes=16 * 1024 * 1024),
             cost_estimate=pl.CostEstimate(flops=flops, bytes_accessed=moved, transcendentals=0),
             input_output_aliases=aliases or {},
             name=name,
@@ -262,12 +260,12 @@
         functools.partial(gather_states, members, heads, rows),
         "gather_states",
         [shape(members, heads, HEAD_DIM, HEAD_DIM), shape(heads, HEAD_DIM, HEAD_DIM)],
-        [VMEM] * (members + 1),
+        [VMEM] * (members + 1) + [ANY],
         [VMEM] * 2,
         [pltpu.VMEM((members, rows, width), bf16)] * 2,
         flops=2 * rows * HEAD_DIM * columns,
         moved=4 * block_bytes,
-    )(table, *near_got, *far_got)
+    )(table, *near_got, *far_got, own)
     up = [(g, g + members) for g in range(devices - members)]
     moving = lax.ppermute(total, everyone, up)
     earlier = moving
@@ -277,23 +275,30 @@
         for k in range(2, min(reach, planes - 1) + 1):
             moving = lax.ppermute(moving, everyone, up)
             earlier = earlier + jnp.where(opens < base - (k - 1) * members * rows, moving, 0.0)
-    crossed = call(
-        functools.partial(reach_back, members, heads),
-        "reach_back",
-        [shape(rows, width)] * members,
-        [VMEM] * (half + 3) + [ANY],
-        [VMEM] * members,
-        flops=2 * rows * HEAD_DIM * columns,
-        moved=4 * block_bytes,
-    )(table, *query_got, carry, earlier, own)
-    crossed_got = [swap(crossed[members - 1 - d], d) if d else crossed[-1] for d in range(members)]
+    crossed_got = {}
+    late = [e for e in downward if e in (1, 2)]
+    soon = [e for e in downward if e not in late]
+    for chosen, gates in ((soon, []), (late, [])):
+        crossed = call(
+            functools.partial(reach_back, members, heads, chosen, len(gates)),
+            "reach_back",
+            [shape(rows, width)] * (CORES * len(chosen)),
+            [VMEM] * (len(chosen) + 3) + [ANY] * len(gates),
+            [VMEM] * (CORES * len(chosen)),
+            flops=2 * rows * HEAD_DIM * width * CORES * len(chosen),
+            moved=2 * block_bytes,
+        )(table, carry, earlier, *[query_got[half - 1 - e] for e in chosen], *gates)
+        for n, e in enumerate(chosen):
+            for side in range(CORES):
+                d = e ^ (side * half)
+                part = crossed[n * CORES + side]
+                crossed_got[d] = swap(part, d) if d else part
 
     gain = norm_gain.reshape(1, columns)
-    last = [d for d in range(members) if d % half in (1, 2)]
-    first = [d for d in range(members) if d not in last]
-    first.sort(key=lambda d: (d != half, -d))
     out = None
-    for chosen in (first, last):
+    groups = [[e ^ (side * half) for e in soon for side in range(CORES)]]
+    groups += [[e ^ (side * half) for e in late for side in range(CORES)]]
+    for chosen in groups:
         more = [] if out is None else [out]
         out = call(
             functools.partial(finish, chosen, members, heads, rows),

time: 57.9 us -> 55.6 us (0.960)
  starting transfers between devices: 25.7 us -> 24 us
  waiting for transfers between devices: 21.6 us -> 20.8 us
    ppermute x17, waiting for transfers between devices: 21.6 us -> 17.4 us  [swap(): return lax.ppermute(part, everyone, pairs)]
    ppermute x1, waiting for transfers between devices: 0.01 us -> 3.36 us  [body(): moving = lax.ppermute(total, everyone, up)]
    ppermute x17, starting transfers between devices: 22.2 us -> 20.5 us  [swap(): return lax.ppermute(part, everyone, pairs)]
  transfers between devices with their start and end apart: 18 -> 18, of which waited for: 13 -> 9; matrix products, arithmetic and copies ran while one was open for 0% -> 0% of each run, Pallas kernels for 13% -> 14%
where the time goes in v7:
time: 55.6 us; the launch traced here: 55.4 us
  starting transfers between devices  24 us (43%)
  waiting for transfers between devices  20.8 us (37%)
  Pallas kernels  10.5 us (19%)
    ppermute x17, starting transfers between devices, swap(): return lax.ppermute(part, everyone, pairs)  20.5 us
    ppermute x17, waiting for transfers between devices, swap(): return lax.ppermute(part, everyone, pairs)  17.4 us
    pallas_call x1, Pallas kernels, body(): call(functools.partial(inside, head_count, docs, rows), 'inside', shape(r...  4.93 us
    ppermute x1, starting transfers between devices, body(): moving = lax.ppermute(total, everyone, up)  3.5 us
    ppermute x1, waiting for transfers between devices, body(): moving = lax.ppermute(total, everyone, up)  3.36 us
    pallas_call x2, Pallas kernels, body(): call(functools.partial(finish, chosen, members, heads, rows), 'finish', s...  1.81 us
    pallas_call x1, Pallas kernels, body(): call(functools.partial(spread, members, width), 'spread', [shape(2, rows,...  1.67 us
  transfers between devices with their start and end apart: 18, of which 9 were waited for; matrix products, arithmetic and copies ran while one was open for 0% of the time, Pallas kernels for 14%

profile of v7, /device:TPU:0, one launch (start us, length us, event | category | flops | bytes accessed | tf_op | source)
XLA Modules:
  0.0 55.4 jit_solution(10305178088777079485)
XLA Ops:
  0.0 0.0 copy-start
  0.0 0.0 copy-start.2
  0.0 0.0 copy-start.1
  0.0 0.0 copy-start.4
  0.0 1.7 %spread.1 = (f32[2,64,512]{2,1,0:T(8,128)S(1)}, f32[2,64,512]{2,1,0:T(8,128)S(1)}, f32[2,64,512]{2,1,0:T(8,128)S(1)}, f32[2,64,512]{2,1,0:T(8,128)S(1)}, f32[4,3,64,512]{3,2,1,0:T(8,128)S(1)}) custom-call(bf16[64,4096]{1,0:T(8,128)(2,1)} %queries.5, bf16[64,4096]{1,0:T(8,128)(2,1)} %keys.3, bf16[64,4096]{1,0:T(8,128)(2,1)} %values.3), custom_call_target="tpu_custom_call" | custom-call | tf_op jit(solution)/shard_map/spread/pallas_call | solution.py:219
  1.7 0.5 collective-permute-start
  2.2 3.5 %collective-permute-start.1 = (f32[2,64,512]{2,1,0:T(8,128)S(1)}, f32[2,64,512]{2,1,0:T(8,128)S(1)}, u32[]{:S(2)}, u32[]{:S(2)}) collective-permute-start(f32[2,64,512]{2,1,0:T(8,128)S(1)} %get-tuple-element.29), channel_id=1, source_target_pairs={{0,3},{1,2},{2,1},{3,0},{4,7},{5,6},{6,5},{7,4},{8,11},{9,10},{10,... | collective-permute-start | bytes 786440 | tf_op jit(solution)/shard_map/ppermute | solution.py:215
  5.7 0.5 collective-permute-start.2
  6.2 0.1 collective-permute-start.3
  6.4 0.0 collective-permute-done.swapped.refs_7_
  6.4 0.1 forward.1
  6.4 2.9 %collective-permute-start.4 = (f32[2,64,512]{2,1,0:T(8,128)S(1)}, f32[2,64,512]{2,1,0:T(8,128)S(1)}, u32[]{:S(2)}, u32[]{:S(2)}) collective-permute-start(f32[2,64,512]{2,1,0:T(8,128)S(1)} %get-tuple-element.34), channel_id=1, source_target_pairs={{0,3},{1,2},{2,1},{3,0},{4,7},{5,6},{6,5},{7,4},{8,11},{9,10},{10,... | collective-permute-start | bytes 786440 | tf_op jit(solution)/shard_map/ppermute | solution.py:215
  9.3 0.5 collective-permute-start.5
  9.9 3.1 %collective-permute-done.1.refs_0_ = f32[2,64,512]{2,1,0:T(8,128)S(1)} collective-permute-done((f32[2,64,512]{2,1,0:T(8,128)S(1)}, f32[2,64,512]{2,1,0:T(8,128)S(1)}, u32[]{:S(2)}, u32[]{:S(2)}) %collective-permute-start.1) | collective-permute-done | bytes 262176 | tf_op jit(solution)/shard_map/ppermute | solution.py:215
  12.9 1.9 %collective-permute-start.6 = (f32[2,64,512]{2,1,0:T(8,128)S(1)}, f32[2,64,512]{2,1,0:T(8,128)S(1)}, u32[]{:S(2)}, u32[]{:S(2)}) collective-permute-start(f32[2,64,512]{2,1,0:T(8,128)S(1)} %get-tuple-element.36), channel_id=1, source_target_pairs={{0,1},{1,0},{2,3},{3,2},{4,5},{5,4},{6,7},{7,6},{8,9},{9,8},{10,11... | collective-permute-start | bytes 786440 | tf_op jit(solution)/shard_map/ppermute | solution.py:215
  14.8 0.0 copy-done
  14.8 0.0 copy-done.2
  14.8 0.0 copy-done.1
  14.8 0.0 copy-done.4
  14.8 4.9 %inside.1.refs_8_.own = f32[64,4096]{1,0:T(8,128)S(1)} custom-call(s32[16]{0:T(128)S(1)} %copy-done.4, bf16[64,4096]{1,0:T(8,128)(2,1)S(1)} %copy-done, bf16[64,4096]{1,0:T(8,128)(2,1)S(1)} %copy-done.1, bf16[64,4096]{1,0:T(8,128)(2,1)S(1)} %copy-done.2), custom_call_target="tpu_custom_call" | custom-call | flops 67108864 | bytes 3145728 | tf_op jit(solution)/shard_map/inside/pallas_call | solution.py:249
  19.8 0.0 collective-permute-done.2.refs_1_
  19.8 0.0 collective-permute-done.3.refs_2_
  19.8 0.7 %join_queries.1 = (f32[2,64,512]{2,1,0:T(8,128)S(1)}, f32[2,64,512]{2,1,0:T(8,128)S(1)}, f32[2,64,512]{2,1,0:T(8,128)S(1)}, f32[2,64,512]{2,1,0:T(8,128)S(1)}, s32[10,128]{1,0:T(8,128)S(1)}) custom-call(s32[16]{0:T(128)S(1)} %copy-done.4, bf16[64,4096]{1,0:T(8,128)(2,1)S(1)} %copy-done, f32[4,3,64,512]{3,2,1,0:T(8,128)S(1)} %collective-permute-done.swapped.refs_7_, ...), custom_call_target="tpu_custom_call" | custom-call | bytes 2097152 | tf_op jit(solution)/shard_map/join_queries/pallas_call | solution.py:239
  20.5 1.6 %collective-permute-start.14 = (f32[2,64,512]{2,1,0:T(8,128)S(1)}, f32[2,64,512]{2,1,0:T(8,128)S(1)}, u32[]{:S(2)}, u32[]{:S(2)}) collective-permute-start(f32[2,64,512]{2,1,0:T(8,128)S(1)} %get-tuple-element.45), channel_id=1, source_target_pairs={{0,3},{1,2},{2,1},{3,0},{4,7},{5,6},{6,5},{7,4},{8,11},{9,10},{10,... | collective-permute-start | bytes 786440 | tf_op jit(solution)/shard_map/ppermute | solution.py:215
  22.1 2.1 %collective-permute-done.4.refs_4_ = f32[2,64,512]{2,1,0:T(8,128)S(1)} collective-permute-done((f32[2,64,512]{2,1,0:T(8,128)S(1)}, f32[2,64,512]{2,1,0:T(8,128)S(1)}, u32[]{:S(2)}, u32[]{:S(2)}) %collective-permute-start.4) | collective-permute-done | bytes 262176 | tf_op jit(solution)/shard_map/ppermute | solution.py:215
  24.2 5.4 %collective-permute-done.5.refs_5_ = f32[2,64,512]{2,1,0:T(8,128)S(1)} collective-permute-done((f32[2,64,512]{2,1,0:T(8,128)S(1)}, f32[2,64,512]{2,1,0:T(8,128)S(1)}, u32[]{:S(2)}, u32[]{:S(2)}) %collective-permute-start.5) | collective-permute-done | bytes 262176 | tf_op jit(solution)/shard_map/ppermute | solution.py:215
  29.7 0.6 %collective-permute-done.6.refs_6_ = f32[2,64,512]{2,1,0:T(8,128)S(1)} collective-permute-done((f32[2,64,512]{2,1,0:T(8,128)S(1)}, f32[2,64,512]{2,1,0:T(8,128)S(1)}, u32[]{:S(2)}, u32[]{:S(2)}) %collective-permute-start.6) | collective-permute-done | bytes 262176 | tf_op jit(solution)/shard_map/ppermute | solution.py:215
  30.3 0.6 %gather_states.1 = (f32[8,4,128,128]{3,2,1,0:T(8,128)S(1)}, f32[4,128,128]{2,1,0:T(8,128)S(1)}) custom-call(s32[10,128]{1,0:T(8,128)S(1)} %get-tuple-element.32.table, f32[2,64,512]{2,1,0:T(8,128)S(1)} %collective-permute-done.1.refs_0_, f32[2,64,512]{2,1,0:T(8,128)S(1)} %collective-permute-done.2.refs_1_, f32[2,64,512]{2,1,0:T(8,128)S(1)} %collective-permute-done.3.refs_2_, ...), custom_call_target="tpu_custom_call" | custom-call | flops 67108864 | bytes 4194304 | tf_op jit(solution)/shard_map/gather_states/pallas_call | solution.py:259
  30.9 3.5 %collective-permute-start.7 = (f32[4,128,128]{2,1,0:T(8,128)S(1)}, f32[4,128,128]{2,1,0:T(8,128)S(1)}, u32[]{:S(2)}, u32[]{:S(2)}) collective-permute-start(f32[4,128,128]{2,1,0:T(8,128)S(1)} %get-tuple-element.38), channel_id=1, source_target_pairs={{0,8},{1,9},{2,10},{3,11},{4,12},{5,13},{6,14},{7,15},{8,16},{9,17... | collective-permute-start | bytes 786440 | tf_op jit(solution)/shard_map/ppermute | solution.py:270
  34.4 1.4 %collective-permute-start.8 = (f32[2,64,512]{2,1,0:T(8,128)S(1)}, f32[2,64,512]{2,1,0:T(8,128)S(1)}, u32[]{:S(2)}, u32[]{:S(2)}) collective-permute-start(f32[2,64,512]{2,1,0:T(8,128)S(1)} %get-tuple-element.39), channel_id=1, source_target_pairs={{0,2},{1,3},{2,0},{3,1},{4,6},{5,7},{6,4},{7,5},{8,10},{9,11},{10,... | collective-permute-start | bytes 786440 | tf_op jit(solution)/shard_map/ppermute | solution.py:215
  35.8 0.7 %collective-permute-start.9 = (f32[2,64,512]{2,1,0:T(8,128)S(1)}, f32[2,64,512]{2,1,0:T(8,128)S(1)}, u32[]{:S(2)}, u32[]{:S(2)}) collective-permute-start(f32[2,64,512]{2,1,0:T(8,128)S(1)} %get-tuple-element.40), channel_id=1, source_target_pairs={{0,1},{1,0},{2,3},{3,2},{4,5},{5,4},{6,7},{7,6},{8,9},{9,8},{10,11... | collective-permute-start | bytes 786440 | tf_op jit(solution)/shard_map/ppermute | solution.py:215
  36.5 0.0 collective-permute-done.14.refs_0_
  36.5 3.4 %collective-permute-done.7.earlier = f32[4,128,128]{2,1,0:T(8,128)S(1)} collective-permute-done((f32[4,128,128]{2,1,0:T(8,128)S(1)}, f32[4,128,128]{2,1,0:T(8,128)S(1)}, u32[]{:S(2)}, u32[]{:S(2)}) %collective-permute-start.7) | collective-permute-done | bytes 262176 | tf_op jit(solution)/shard_map/ppermute | solution.py:270
  39.8 0.4 reach_back.3
  40.2 0.0 copy-start.3
  40.2 1.0 %collective-permute-start.15 = (f32[64,512]{1,0:T(8,128)S(1)}, f32[64,512]{1,0:T(8,128)S(1)}, u32[]{:S(2)}, u32[]{:S(2)}) collective-permute-start(f32[64,512]{1,0:T(8,128)S(1)} %get-tuple-element.47), channel_id=1, source_target_pairs={{0,3},{1,2},{2,1},{3,0},{4,7},{5,6},{6,5},{7,4},{8,11},{9,10},{10,... | collective-permute-start | bytes 393224 | tf_op jit(solution)/shard_map/ppermute | solution.py:215
  41.2 0.2 collective-permute-start.16
  41.4 1.9 %collective-permute-start.17 = (f32[64,512]{1,0:T(8,128)S(1)}, f32[64,512]{1,0:T(8,128)S(1)}, u32[]{:S(2)}, u32[]{:S(2)}) collective-permute-start(f32[64,512]{1,0:T(8,128)S(1)} %get-tuple-element.50), channel_id=1, source_target_pairs={{0,4},{1,5},{2,6},{3,7},{4,0},{5,1},{6,2},{7,3},{8,12},{9,13},{10,... | collective-permute-start | bytes 393224 | tf_op jit(solution)/shard_map/ppermute | solution.py:215
  43.3 0.0 collective-permute-done.8.refs_0_
  43.3 0.5 collective-permute-done.9.refs_1_
  43.8 0.3 reach_back.2
  44.1 1.1 %collective-permute-start.10 = (f32[64,512]{1,0:T(8,128)S(1)}, f32[64,512]{1,0:T(8,128)S(1)}, u32[]{:S(2)}, u32[]{:S(2)}) collective-permute-start(f32[64,512]{1,0:T(8,128)S(1)} %get-tuple-element.41), channel_id=1, source_target_pairs={{0,2},{1,3},{2,0},{3,1},{4,6},{5,7},{6,4},{7,5},{8,10},{9,11},{10,... | collective-permute-start | bytes 393224 | tf_op jit(solution)/shard_map/ppermute | solution.py:215
  45.2 0.0 collective-permute-start.11
  45.2 2.1 %collective-permute-done.15.refs_0_ = f32[64,512]{1,0:T(8,128)S(1)} collective-permute-done((f32[64,512]{1,0:T(8,128)S(1)}, f32[64,512]{1,0:T(8,128)S(1)}, u32[]{:S(2)}, u32[]{:S(2)}) %collective-permute-start.15) | collective-permute-done | bytes 131104 | tf_op jit(solution)/shard_map/ppermute | solution.py:215
  47.3 0.9 %collective-permute-start.12 = (f32[64,512]{1,0:T(8,128)S(1)}, f32[64,512]{1,0:T(8,128)S(1)}, u32[]{:S(2)}, u32[]{:S(2)}) collective-permute-start(f32[64,512]{1,0:T(8,128)S(1)} %get-tuple-element.43), channel_id=1, source_target_pairs={{0,1},{1,0},{2,3},{3,2},{4,5},{5,4},{6,7},{7,6},{8,9},{9,8},{10,11... | collective-permute-start | bytes 393224 | tf_op jit(solution)/shard_map/ppermute | solution.py:215
  48.2 0.0 collective-permute-done.16.refs_1_
  48.2 1.8 %collective-permute-start.13 = (f32[64,512]{1,0:T(8,128)S(1)}, f32[64,512]{1,0:T(8,128)S(1)}, u32[]{:S(2)}, u32[]{:S(2)}) collective-permute-start(f32[64,512]{1,0:T(8,128)S(1)} %get-tuple-element.44), channel_id=1, source_target_pairs={{0,5},{1,4},{2,7},{3,6},{4,1},{5,0},{6,3},{7,2},{8,13},{9,12},{10,... | collective-permute-start | bytes 393224 | tf_op jit(solution)/shard_map/ppermute | solution.py:215
  50.0 0.0 collective-permute-done.17.refs_3_
  50.0 0.0 copy-done.3
  50.0 0.9 %finish.2.refs_4_ = bf16[64,4096]{1,0:T(8,128)(2,1)} custom-call(s32[10,128]{1,0:T(8,128)S(1)} %get-tuple-element.32.table, f32[64,4096]{1,0:T(8,128)S(1)} %inside.1.refs_8_.own, f32[1,4096]{1,0:T(1,128)S(1)} %bitcast.1, f32[64,512]{1,0:T(8,128)S(1)} %collective-permute-done.15.refs_0_, f32[64,512]{1,0:T(8,128)S(1)} %collective-permute-done.16.refs_1_, ...), custom_call_target="tpu_custom_call" | custom-call | bytes 2097152 | tf_op jit(solution)/shard_map/finish/pallas_call | solution.py:303
  50.9 1.0 %collective-permute-done.10.refs_0_ = f32[64,512]{1,0:T(8,128)S(1)} collective-permute-done((f32[64,512]{1,0:T(8,128)S(1)}, f32[64,512]{1,0:T(8,128)S(1)}, u32[]{:S(2)}, u32[]{:S(2)}) %collective-permute-start.10) | collective-permute-done | bytes 131104 | tf_op jit(solution)/shard_map/ppermute | solution.py:215
  51.8 2.6 %collective-permute-done.11.refs_1_ = f32[64,512]{1,0:T(8,128)S(1)} collective-permute-done((f32[64,512]{1,0:T(8,128)S(1)}, f32[64,512]{1,0:T(8,128)S(1)}, u32[]{:S(2)}, u32[]{:S(2)}) %collective-permute-start.11) | collective-permute-done | bytes 131104 | tf_op jit(solution)/shard_map/ppermute | solution.py:215
  54.5 0.0 collective-permute-done.12.refs_2_
  54.5 0.0 collective-permute-done.13.refs_3_
  54.5 0.9 %finish.3 = bf16[64,4096]{1,0:T(8,128)(2,1)} custom-call(s32[10,128]{1,0:T(8,128)S(1)} %get-tuple-element.32.table, f32[64,4096]{1,0:T(8,128)S(1)} %inside.1.refs_8_.own, f32[1,4096]{1,0:T(1,128)S(1)} %bitcast.2, f32[64,512]{1,0:T(8,128)S(1)} %collective-permute-done.10.refs_0_, ...), custom_call_target="tpu_custom_call", output_to_operand_aliasing={{}: (7, {})} | custom-call | bytes 2097152 | tf_op jit(solution)/shard_map/finish/pallas_call | solution.py:303
Async XLA Ops:
  0.0 14.8 %copy-start = (bf16[64,4096]{1,0:T(8,128)(2,1)S(1)}, bf16[64,4096]{1,0:T(8,128)(2,1)}, u32[]{:S(2)}) copy-start(bf16[64,4096]{1,0:T(8,128)(2,1)} %queries.5) | copy-start | bytes 1572868
  0.0 14.8 %copy-start.2 = (bf16[64,4096]{1,0:T(8,128)(2,1)S(1)}, bf16[64,4096]{1,0:T(8,128)(2,1)}, u32[]{:S(2)}) copy-start(bf16[64,4096]{1,0:T(8,128)(2,1)} %values.3) | copy-start | bytes 1572868
  0.0 14.8 %copy-start.1 = (bf16[64,4096]{1,0:T(8,128)(2,1)S(1)}, bf16[64,4096]{1,0:T(8,128)(2,1)}, u32[]{:S(2)}) copy-start(bf16[64,4096]{1,0:T(8,128)(2,1)} %keys.3) | copy-start | bytes 1572868
  0.0 14.8 %copy-start.4 = (s32[16]{0:T(128)S(1)}, s32[16]{0:T(128)}, u32[]{:S(2)}) copy-start(s32[16]{0:T(128)} %lengths.3) | copy-start | bytes 196
  1.7 4.7 %collective-permute-start = (f32[4,3,64,512]{3,2,1,0:T(8,128)S(1)}, f32[4,3,64,512]{3,2,1,0:T(8,128)S(1)}, u32[]{:S(2)}, u32[]{:S(2)}) collective-permute-start(f32[4,3,64,512]{3,2,1,0:T(8,128)S(1)} %get-tuple-element.28), channel_id=1, source_target_pairs={{0,4},{1,5},{2,6},{3,7},{4,0},{5,1},{6,2},{7,3},{8,12},{9,13},{10,... | collective-permute-start | bytes 4718600 | tf_op jit(solution)/shard_map/ppermute | solution.py:215
  2.2 10.7 %collective-permute-start.1 = (f32[2,64,512]{2,1,0:T(8,128)S(1)}, f32[2,64,512]{2,1,0:T(8,128)S(1)}, u32[]{:S(2)}, u32[]{:S(2)}) collective-permute-start(f32[2,64,512]{2,1,0:T(8,128)S(1)} %get-tuple-element.29), channel_id=1, source_target_pairs={{0,3},{1,2},{2,1},{3,0},{4,7},{5,6},{6,5},{7,4},{8,11},{9,10},{10,... | collective-permute-start | bytes 786440 | tf_op jit(solution)/shard_map/ppermute | solution.py:215
  5.7 14.0 %collective-permute-start.2 = (f32[2,64,512]{2,1,0:T(8,128)S(1)}, f32[2,64,512]{2,1,0:T(8,128)S(1)}, u32[]{:S(2)}, u32[]{:S(2)}) collective-permute-start(f32[2,64,512]{2,1,0:T(8,128)S(1)} %get-tuple-element.30), channel_id=1, source_target_pairs={{0,2},{1,3},{2,0},{3,1},{4,6},{5,7},{6,4},{7,5},{8,10},{9,11},{10,... | collective-permute-start | bytes 786440 | tf_op jit(solution)/shard_map/ppermute | solution.py:215
  6.2 13.5 %collective-permute-start.3 = (f32[2,64,512]{2,1,0:T(8,128)S(1)}, f32[2,64,512]{2,1,0:T(8,128)S(1)}, u32[]{:S(2)}, u32[]{:S(2)}) collective-permute-start(f32[2,64,512]{2,1,0:T(8,128)S(1)} %get-tuple-element.31), channel_id=1, source_target_pairs={{0,1},{1,0},{2,3},{3,2},{4,5},{5,4},{6,7},{7,6},{8,9},{9,8},{10,11... | collective-permute-start | bytes 786440 | tf_op jit(solution)/shard_map/ppermute | solution.py:215
  6.4 17.8 %collective-permute-start.4 = (f32[2,64,512]{2,1,0:T(8,128)S(1)}, f32[2,64,512]{2,1,0:T(8,128)S(1)}, u32[]{:S(2)}, u32[]{:S(2)}) collective-permute-start(f32[2,64,512]{2,1,0:T(8,128)S(1)} %get-tuple-element.34), channel_id=1, source_target_pairs={{0,3},{1,2},{2,1},{3,0},{4,7},{5,6},{6,5},{7,4},{8,11},{9,10},{10,... | collective-permute-start | bytes 786440 | tf_op jit(solution)/shard_map/ppermute | solution.py:215
  9.3 20.3 %collective-permute-start.5 = (f32[2,64,512]{2,1,0:T(8,128)S(1)}, f32[2,64,512]{2,1,0:T(8,128)S(1)}, u32[]{:S(2)}, u32[]{:S(2)}) collective-permute-start(f32[2,64,512]{2,1,0:T(8,128)S(1)} %get-tuple-element.35), channel_id=1, source_target_pairs={{0,2},{1,3},{2,0},{3,1},{4,6},{5,7},{6,4},{7,5},{8,10},{9,11},{10,... | collective-permute-start | bytes 786440 | tf_op jit(solution)/shard_map/ppermute | solution.py:215
  12.9 17.4 %collective-permute-start.6 = (f32[2,64,512]{2,1,0:T(8,128)S(1)}, f32[2,64,512]{2,1,0:T(8,128)S(1)}, u32[]{:S(2)}, u32[]{:S(2)}) collective-permute-start(f32[2,64,512]{2,1,0:T(8,128)S(1)} %get-tuple-element.36), channel_id=1, source_target_pairs={{0,1},{1,0},{2,3},{3,2},{4,5},{5,4},{6,7},{7,6},{8,9},{9,8},{10,11... | collective-permute-start | bytes 786440 | tf_op jit(solution)/shard_map/ppermute | solution.py:215
  20.5 15.9 %collective-permute-start.14 = (f32[2,64,512]{2,1,0:T(8,128)S(1)}, f32[2,64,512]{2,1,0:T(8,128)S(1)}, u32[]{:S(2)}, u32[]{:S(2)}) collective-permute-start(f32[2,64,512]{2,1,0:T(8,128)S(1)} %get-tuple-element.45), channel_id=1, source_target_pairs={{0,3},{1,2},{2,1},{3,0},{4,7},{5,6},{6,5},{7,4},{8,11},{9,10},{10,... | collective-permute-start | bytes 786440 | tf_op jit(solution)/shard_map/ppermute | solution.py:215
  30.9 8.9 %collective-permute-start.7 = (f32[4,128,128]{2,1,0:T(8,128)S(1)}, f32[4,128,128]{2,1,0:T(8,128)S(1)}, u32[]{:S(2)}, u32[]{:S(2)}) collective-permute-start(f32[4,128,128]{2,1,0:T(8,128)S(1)} %get-tuple-element.38), channel_id=1, source_target_pairs={{0,8},{1,9},{2,10},{3,11},{4,12},{5,13},{6,14},{7,15},{8,16},{9,17... | collective-permute-start | bytes 786440 | tf_op jit(solution)/shard_map/ppermute | solution.py:270
  34.4 8.9 %collective-permute-start.8 = (f32[2,64,512]{2,1,0:T(8,128)S(1)}, f32[2,64,512]{2,1,0:T(8,128)S(1)}, u32[]{:S(2)}, u32[]{:S(2)}) collective-permute-start(f32[2,64,512]{2,1,0:T(8,128)S(1)} %get-tuple-element.39), channel_id=1, source_target_pairs={{0,2},{1,3},{2,0},{3,1},{4,6},{5,7},{6,4},{7,5},{8,10},{9,11},{10,... | collective-permute-start | bytes 786440 | tf_op jit(solution)/shard_map/ppermute | solution.py:215
  35.8 8.0 %collective-permute-start.9 = (f32[2,64,512]{2,1,0:T(8,128)S(1)}, f32[2,64,512]{2,1,0:T(8,128)S(1)}, u32[]{:S(2)}, u32[]{:S(2)}) collective-permute-start(f32[2,64,512]{2,1,0:T(8,128)S(1)} %get-tuple-element.40), channel_id=1, source_target_pairs={{0,1},{1,0},{2,3},{3,2},{4,5},{5,4},{6,7},{7,6},{8,9},{9,8},{10,11... | collective-permute-start | bytes 786440 | tf_op jit(solution)/shard_map/ppermute | solution.py:215
  40.2 9.8 %copy-start.3 = (f32[4096]{0:T(1024)S(1)}, f32[4096]{0:T(1024)}, u32[]{:S(2)}) copy-start(f32[4096]{0:T(1024)} %param.9) | copy-start | bytes 49156
  40.2 7.1 %collective-permute-start.15 = (f32[64,512]{1,0:T(8,128)S(1)}, f32[64,512]{1,0:T(8,128)S(1)}, u32[]{:S(2)}, u32[]{:S(2)}) collective-permute-start(f32[64,512]{1,0:T(8,128)S(1)} %get-tuple-element.47), channel_id=1, source_target_pairs={{0,3},{1,2},{2,1},{3,0},{4,7},{5,6},{6,5},{7,4},{8,11},{9,10},{10,... | collective-permute-start | bytes 393224 | tf_op jit(solution)/shard_map/ppermute | solution.py:215
  41.2 7.0 %collective-permute-start.16 = (f32[64,512]{1,0:T(8,128)S(1)}, f32[64,512]{1,0:T(8,128)S(1)}, u32[]{:S(2)}, u32[]{:S(2)}) collective-permute-start(f32[64,512]{1,0:T(8,128)S(1)} %get-tuple-element.48), channel_id=1, source_target_pairs={{0,7},{1,6},{2,5},{3,4},{4,3},{5,2},{6,1},{7,0},{8,15},{9,14},{10,... | collective-permute-start | bytes 393224 | tf_op jit(solution)/shard_map/ppermute | solution.py:215
  41.4 8.6 %collective-permute-start.17 = (f32[64,512]{1,0:T(8,128)S(1)}, f32[64,512]{1,0:T(8,128)S(1)}, u32[]{:S(2)}, u32[]{:S(2)}) collective-permute-start(f32[64,512]{1,0:T(8,128)S(1)} %get-tuple-element.50), channel_id=1, source_target_pairs={{0,4},{1,5},{2,6},{3,7},{4,0},{5,1},{6,2},{7,3},{8,12},{9,13},{10,... | collective-permute-start | bytes 393224 | tf_op jit(solution)/shard_map/ppermute | solution.py:215
  44.1 7.7 %collective-permute-start.10 = (f32[64,512]{1,0:T(8,128)S(1)}, f32[64,512]{1,0:T(8,128)S(1)}, u32[]{:S(2)}, u32[]{:S(2)}) collective-permute-start(f32[64,512]{1,0:T(8,128)S(1)} %get-tuple-element.41), channel_id=1, source_target_pairs={{0,2},{1,3},{2,0},{3,1},{4,6},{5,7},{6,4},{7,5},{8,10},{9,11},{10,... | collective-permute-start | bytes 393224 | tf_op jit(solution)/shard_map/ppermute | solution.py:215
  45.2 9.2 %collective-permute-start.11 = (f32[64,512]{1,0:T(8,128)S(1)}, f32[64,512]{1,0:T(8,128)S(1)}, u32[]{:S(2)}, u32[]{:S(2)}) collective-permute-start(f32[64,512]{1,0:T(8,128)S(1)} %get-tuple-element.42), channel_id=1, source_target_pairs={{0,6},{1,7},{2,4},{3,5},{4,2},{5,3},{6,0},{7,1},{8,14},{9,15},{10,... | collective-permute-start | bytes 393224 | tf_op jit(solution)/shard_map/ppermute | solution.py:215
  47.3 7.2 %collective-permute-start.12 = (f32[64,512]{1,0:T(8,128)S(1)}, f32[64,512]{1,0:T(8,128)S(1)}, u32[]{:S(2)}, u32[]{:S(2)}) collective-permute-start(f32[64,512]{1,0:T(8,128)S(1)} %get-tuple-element.43), channel_id=1, source_target_pairs={{0,1},{1,0},{2,3},{3,2},{4,5},{5,4},{6,7},{7,6},{8,9},{9,8},{10,11... | collective-permute-start | bytes 393224 | tf_op jit(solution)/shard_map/ppermute | solution.py:215
  48.2 6.3 %collective-permute-start.13 = (f32[64,512]{1,0:T(8,128)S(1)}, f32[64,512]{1,0:T(8,128)S(1)}, u32[]{:S(2)}, u32[]{:S(2)}) collective-permute-start(f32[64,512]{1,0:T(8,128)S(1)} %get-tuple-element.44), channel_id=1, source_target_pairs={{0,5},{1,4},{2,7},{3,6},{4,1},{5,0},{6,3},{7,2},{8,13},{9,12},{10,... | collective-permute-start | bytes 393224 | tf_op jit(solution)/shard_map/ppermute | solution.py:215

commit v8 on v7

--- a/solution.py
+++ b/solution.py
@@ -276,9 +276,10 @@
             moving = lax.ppermute(moving, everyone, up)
             earlier = earlier + jnp.where(opens < base - (k - 1) * members * rows, moving, 0.0)
     crossed_got = {}
-    late = [e for e in downward if e in (1, 2)]
+    late = [e for e in downward if e in (0, 1, 2)]
     soon = [e for e in downward if e not in late]
-    for chosen, gates in ((soon, []), (late, [])):
+    gates = []
+    for chosen in (soon, late):
         crossed = call(
             functools.partial(reach_back, members, heads, chosen, len(gates)),
             "reach_back",
@@ -293,11 +294,12 @@
                 d = e ^ (side * half)
                 part = crossed[n * CORES + side]
                 crossed_got[d] = swap(part, d) if d else part
+        gates = crossed[:1]
 
     gain = norm_gain.reshape(1, columns)
     out = None
-    groups = [[e ^ (side * half) for e in soon for side in range(CORES)]]
-    groups += [[e ^ (side * half) for e in late for side in range(CORES)]]
+    groups = [[0] + [e ^ (side * half) for e in soon for side in range(CORES)]]
+    groups += [[half] + [e ^ (side * half) for e in late if e for side in range(CORES)]]
     for chosen in groups:
         more = [] if out is None else [out]
         out = call(

time: 55.6 us -> 55.6 us (level)
  transfers between devices with their start and end apart: 18 -> 18, of which waited for: 9 -> 10; matrix products, arithmetic and copies ran while one was open for 0% -> 0% of each run, Pallas kernels for 14% -> 14%
where the time goes in v8:
time: 55.6 us; the launch traced here: 55.5 us
  starting transfers between devices  23.6 us (42%)
  waiting for transfers between devices  21.3 us (38%)
  Pallas kernels  10.5 us (19%)
    ppermute x17, starting transfers between devices, swap(): return lax.ppermute(part, everyone, pairs)  20.1 us
    ppermute x17, waiting for transfers between devices, swap(): return lax.ppermute(part, everyone, pairs)  17.9 us
    pallas_call x1, Pallas kernels, body(): call(functools.partial(inside, head_count, docs, rows), 'inside', shape(r...  4.93 us
    ppermute x1, starting transfers between devices, body(): moving = lax.ppermute(total, everyone, up)  3.5 us
    ppermute x1, waiting for transfers between devices, body(): moving = lax.ppermute(total, everyone, up)  3.36 us
    pallas_call x2, Pallas kernels, body(): call(functools.partial(finish, chosen, members, heads, rows), 'finish', s...  1.8 us
    pallas_call x1, Pallas kernels, body(): call(functools.partial(spread, members, width), 'spread', [shape(2, rows,...  1.67 us
  transfers between devices with their start and end apart: 18, of which 10 were waited for; matrix products, arithmetic and copies ran while one was open for 0% of the time, Pallas kernels for 14%

profile of v8, /device:TPU:0, one launch (start us, length us, event | category | flops | bytes accessed | tf_op | source)
XLA Modules:
  0.0 55.5 jit_solution(17835548249270654288)
XLA Ops:
  0.0 0.0 copy-start
  0.0 0.0 copy-start.2
  0.0 0.0 copy-start.1
  0.0 0.0 copy-start.4
  0.0 1.7 %spread.1 = (f32[2,64,512]{2,1,0:T(8,128)S(1)}, f32[2,64,512]{2,1,0:T(8,128)S(1)}, f32[2,64,512]{2,1,0:T(8,128)S(1)}, f32[2,64,512]{2,1,0:T(8,128)S(1)}, f32[4,3,64,512]{3,2,1,0:T(8,128)S(1)}) custom-call(bf16[64,4096]{1,0:T(8,128)(2,1)} %queries.5, bf16[64,4096]{1,0:T(8,128)(2,1)} %keys.3, bf16[64,4096]{1,0:T(8,128)(2,1)} %values.3), custom_call_target="tpu_custom_call" | custom-call | tf_op jit(solution)/shard_map/spread/pallas_call | solution.py:219
  1.7 0.5 collective-permute-start
  2.2 3.5 %collective-permute-start.1 = (f32[2,64,512]{2,1,0:T(8,128)S(1)}, f32[2,64,512]{2,1,0:T(8,128)S(1)}, u32[]{:S(2)}, u32[]{:S(2)}) collective-permute-start(f32[2,64,512]{2,1,0:T(8,128)S(1)} %get-tuple-element.29), channel_id=1, source_target_pairs={{0,3},{1,2},{2,1},{3,0},{4,7},{5,6},{6,5},{7,4},{8,11},{9,10},{10,... | collective-permute-start | bytes 786440 | tf_op jit(solution)/shard_map/ppermute | solution.py:215
  5.7 0.5 collective-permute-start.2
  6.2 0.1 collective-permute-start.3
  6.4 0.0 collective-permute-done.swapped.refs_7_
  6.4 0.1 forward.1
  6.4 2.9 %collective-permute-start.4 = (f32[2,64,512]{2,1,0:T(8,128)S(1)}, f32[2,64,512]{2,1,0:T(8,128)S(1)}, u32[]{:S(2)}, u32[]{:S(2)}) collective-permute-start(f32[2,64,512]{2,1,0:T(8,128)S(1)} %get-tuple-element.34), channel_id=1, source_target_pairs={{0,3},{1,2},{2,1},{3,0},{4,7},{5,6},{6,5},{7,4},{8,11},{9,10},{10,... | collective-permute-start | bytes 786440 | tf_op jit(solution)/shard_map/ppermute | solution.py:215
  9.3 0.5 collective-permute-start.5
  9.9 3.1 %collective-permute-done.1.refs_0_ = f32[2,64,512]{2,1,0:T(8,128)S(1)} collective-permute-done((f32[2,64,512]{2,1,0:T(8,128)S(1)}, f32[2,64,512]{2,1,0:T(8,128)S(1)}, u32[]{:S(2)}, u32[]{:S(2)}) %collective-permute-start.1) | collective-permute-done | bytes 262176 | tf_op jit(solution)/shard_map/ppermute | solution.py:215
  12.9 1.9 %collective-permute-start.6 = (f32[2,64,512]{2,1,0:T(8,128)S(1)}, f32[2,64,512]{2,1,0:T(8,128)S(1)}, u32[]{:S(2)}, u32[]{:S(2)}) collective-permute-start(f32[2,64,512]{2,1,0:T(8,128)S(1)} %get-tuple-element.36), channel_id=1, source_target_pairs={{0,1},{1,0},{2,3},{3,2},{4,5},{5,4},{6,7},{7,6},{8,9},{9,8},{10,11... | collective-permute-start | bytes 786440 | tf_op jit(solution)/shard_map/ppermute | solution.py:215
  14.8 0.0 copy-done
  14.8 0.0 copy-done.2
  14.8 0.0 copy-done.1
  14.8 0.0 copy-done.4
  14.8 4.9 %inside.1.refs_8_.own = f32[64,4096]{1,0:T(8,128)S(1)} custom-call(s32[16]{0:T(128)S(1)} %copy-done.4, bf16[64,4096]{1,0:T(8,128)(2,1)S(1)} %copy-done, bf16[64,4096]{1,0:T(8,128)(2,1)S(1)} %copy-done.1, bf16[64,4096]{1,0:T(8,128)(2,1)S(1)} %copy-done.2), custom_call_target="tpu_custom_call" | custom-call | flops 67108864 | bytes 3145728 | tf_op jit(solution)/shard_map/inside/pallas_call | solution.py:249
  19.8 0.0 collective-permute-done.2.refs_1_
  19.8 0.0 collective-permute-done.3.refs_2_
  19.8 0.7 %join_queries.1 = (f32[2,64,512]{2,1,0:T(8,128)S(1)}, f32[2,64,512]{2,1,0:T(8,128)S(1)}, f32[2,64,512]{2,1,0:T(8,128)S(1)}, f32[2,64,512]{2,1,0:T(8,128)S(1)}, s32[10,128]{1,0:T(8,128)S(1)}) custom-call(s32[16]{0:T(128)S(1)} %copy-done.4, bf16[64,4096]{1,0:T(8,128)(2,1)S(1)} %copy-done, f32[4,3,64,512]{3,2,1,0:T(8,128)S(1)} %collective-permute-done.swapped.refs_7_, ...), custom_call_target="tpu_custom_call" | custom-call | bytes 2097152 | tf_op jit(solution)/shard_map/join_queries/pallas_call | solution.py:239
  20.5 1.6 %collective-permute-start.10 = (f32[2,64,512]{2,1,0:T(8,128)S(1)}, f32[2,64,512]{2,1,0:T(8,128)S(1)}, u32[]{:S(2)}, u32[]{:S(2)}) collective-permute-start(f32[2,64,512]{2,1,0:T(8,128)S(1)} %get-tuple-element.42), channel_id=1, source_target_pairs={{0,3},{1,2},{2,1},{3,0},{4,7},{5,6},{6,5},{7,4},{8,11},{9,10},{10,... | collective-permute-start | bytes 786440 | tf_op jit(solution)/shard_map/ppermute | solution.py:215
  22.1 2.1 %collective-permute-done.4.refs_4_ = f32[2,64,512]{2,1,0:T(8,128)S(1)} collective-permute-done((f32[2,64,512]{2,1,0:T(8,128)S(1)}, f32[2,64,512]{2,1,0:T(8,128)S(1)}, u32[]{:S(2)}, u32[]{:S(2)}) %collective-permute-start.4) | collective-permute-done | bytes 262176 | tf_op jit(solution)/shard_map/ppermute | solution.py:215
  24.2 5.4 %collective-permute-done.5.refs_5_ = f32[2,64,512]{2,1,0:T(8,128)S(1)} collective-permute-done((f32[2,64,512]{2,1,0:T(8,128)S(1)}, f32[2,64,512]{2,1,0:T(8,128)S(1)}, u32[]{:S(2)}, u32[]{:S(2)}) %collective-permute-start.5) | collective-permute-done | bytes 262176 | tf_op jit(solution)/shard_map/ppermute | solution.py:215
  29.7 0.6 %collective-permute-done.6.refs_6_ = f32[2,64,512]{2,1,0:T(8,128)S(1)} collective-permute-done((f32[2,64,512]{2,1,0:T(8,128)S(1)}, f32[2,64,512]{2,1,0:T(8,128)S(1)}, u32[]{:S(2)}, u32[]{:S(2)}) %collective-permute-start.6) | collective-permute-done | bytes 262176 | tf_op jit(solution)/shard_map/ppermute | solution.py:215
  30.3 0.6 %gather_states.1 = (f32[8,4,128,128]{3,2,1,0:T(8,128)S(1)}, f32[4,128,128]{2,1,0:T(8,128)S(1)}) custom-call(s32[10,128]{1,0:T(8,128)S(1)} %get-tuple-element.32.table, f32[2,64,512]{2,1,0:T(8,128)S(1)} %collective-permute-done.1.refs_0_, f32[2,64,512]{2,1,0:T(8,128)S(1)} %collective-permute-done.2.refs_1_, f32[2,64,512]{2,1,0:T(8,128)S(1)} %collective-permute-done.3.refs_2_, ...), custom_call_target="tpu_custom_call" | custom-call | flops 67108864 | bytes 4194304 | tf_op jit(solution)/shard_map/gather_states/pallas_call | solution.py:259
  30.9 3.5 %collective-permute-start.7 = (f32[4,128,128]{2,1,0:T(8,128)S(1)}, f32[4,128,128]{2,1,0:T(8,128)S(1)}, u32[]{:S(2)}, u32[]{:S(2)}) collective-permute-start(f32[4,128,128]{2,1,0:T(8,128)S(1)} %get-tuple-element.38), channel_id=1, source_target_pairs={{0,8},{1,9},{2,10},{3,11},{4,12},{5,13},{6,14},{7,15},{8,16},{9,17... | collective-permute-start | bytes 786440 | tf_op jit(solution)/shard_map/ppermute | solution.py:270
  34.4 1.4 %collective-permute-start.8 = (f32[2,64,512]{2,1,0:T(8,128)S(1)}, f32[2,64,512]{2,1,0:T(8,128)S(1)}, u32[]{:S(2)}, u32[]{:S(2)}) collective-permute-start(f32[2,64,512]{2,1,0:T(8,128)S(1)} %get-tuple-element.39), channel_id=1, source_target_pairs={{0,2},{1,3},{2,0},{3,1},{4,6},{5,7},{6,4},{7,5},{8,10},{9,11},{10,... | collective-permute-start | bytes 786440 | tf_op jit(solution)/shard_map/ppermute | solution.py:215
  35.8 0.7 %collective-permute-start.9 = (f32[2,64,512]{2,1,0:T(8,128)S(1)}, f32[2,64,512]{2,1,0:T(8,128)S(1)}, u32[]{:S(2)}, u32[]{:S(2)}) collective-permute-start(f32[2,64,512]{2,1,0:T(8,128)S(1)} %get-tuple-element.40), channel_id=1, source_target_pairs={{0,1},{1,0},{2,3},{3,2},{4,5},{5,4},{6,7},{7,6},{8,9},{9,8},{10,11... | collective-permute-start | bytes 786440 | tf_op jit(solution)/shard_map/ppermute | solution.py:215
  36.5 0.0 collective-permute-done.10.refs_0_
  36.5 3.4 %collective-permute-done.7.earlier = f32[4,128,128]{2,1,0:T(8,128)S(1)} collective-permute-done((f32[4,128,128]{2,1,0:T(8,128)S(1)}, f32[4,128,128]{2,1,0:T(8,128)S(1)}, u32[]{:S(2)}, u32[]{:S(2)}) %collective-permute-start.7) | collective-permute-done | bytes 262176 | tf_op jit(solution)/shard_map/ppermute | solution.py:270
  39.8 0.2 reach_back.2
  40.1 0.1 collective-permute-start.17
  40.2 1.4 %collective-permute-start.16 = (f32[64,512]{1,0:T(8,128)S(1)}, f32[64,512]{1,0:T(8,128)S(1)}, u32[]{:S(2)}, u32[]{:S(2)}) collective-permute-start(f32[64,512]{1,0:T(8,128)S(1)} %get-tuple-element.43.refs_3_), channel_id=1, source_target_pairs={{0,3},{1,2},{2,1},{3,0},{4,7},{5,6},{6,5},{7,4},{8,11},{9,10},{10,... | collective-permute-start | bytes 393224 | tf_op jit(solution)/shard_map/ppermute | solution.py:215
  41.5 0.6 %collective-permute-done.8.refs_0_ = f32[2,64,512]{2,1,0:T(8,128)S(1)} collective-permute-done((f32[2,64,512]{2,1,0:T(8,128)S(1)}, f32[2,64,512]{2,1,0:T(8,128)S(1)}, u32[]{:S(2)}, u32[]{:S(2)}) %collective-permute-start.8) | collective-permute-done | bytes 262176 | tf_op jit(solution)/shard_map/ppermute | solution.py:215
  42.1 1.2 %collective-permute-done.9.refs_1_ = f32[2,64,512]{2,1,0:T(8,128)S(1)} collective-permute-done((f32[2,64,512]{2,1,0:T(8,128)S(1)}, f32[2,64,512]{2,1,0:T(8,128)S(1)}, u32[]{:S(2)}, u32[]{:S(2)}) %collective-permute-start.9) | collective-permute-done | bytes 262176 | tf_op jit(solution)/shard_map/ppermute | solution.py:215
  43.4 0.0 copy-start.3
  43.4 0.5 reach_back.3
  43.9 0.1 collective-permute-start.11
  43.9 1.0 %collective-permute-start.12 = (f32[64,512]{1,0:T(8,128)S(1)}, f32[64,512]{1,0:T(8,128)S(1)}, u32[]{:S(2)}, u32[]{:S(2)}) collective-permute-start(f32[64,512]{1,0:T(8,128)S(1)} %get-tuple-element.45), channel_id=1, source_target_pairs={{0,2},{1,3},{2,0},{3,1},{4,6},{5,7},{6,4},{7,5},{8,10},{9,11},{10,... | collective-permute-start | bytes 393224 | tf_op jit(solution)/shard_map/ppermute | solution.py:215
  45.0 0.8 %collective-permute-start.13 = (f32[64,512]{1,0:T(8,128)S(1)}, f32[64,512]{1,0:T(8,128)S(1)}, u32[]{:S(2)}, u32[]{:S(2)}) collective-permute-start(f32[64,512]{1,0:T(8,128)S(1)} %get-tuple-element.46), channel_id=1, source_target_pairs={{0,6},{1,7},{2,4},{3,5},{4,2},{5,3},{6,0},{7,1},{8,14},{9,15},{10,... | collective-permute-start | bytes 393224 | tf_op jit(solution)/shard_map/ppermute | solution.py:215
  45.8 1.1 %collective-permute-done.17.refs_2_ = f32[64,512]{1,0:T(8,128)S(1)} collective-permute-done((f32[64,512]{1,0:T(8,128)S(1)}, f32[64,512]{1,0:T(8,128)S(1)}, u32[]{:S(2)}, u32[]{:S(2)}) %collective-permute-start.17) | collective-permute-done | bytes 131104 | tf_op jit(solution)/shard_map/ppermute | solution.py:215
  46.9 1.6 %collective-permute-start.14 = (f32[64,512]{1,0:T(8,128)S(1)}, f32[64,512]{1,0:T(8,128)S(1)}, u32[]{:S(2)}, u32[]{:S(2)}) collective-permute-start(f32[64,512]{1,0:T(8,128)S(1)} %get-tuple-element.47), channel_id=1, source_target_pairs={{0,1},{1,0},{2,3},{3,2},{4,5},{5,4},{6,7},{7,6},{8,9},{9,8},{10,11... | collective-permute-start | bytes 393224 | tf_op jit(solution)/shard_map/ppermute | solution.py:215
  48.5 0.0 collective-permute-done.16.refs_1_
  48.5 1.5 %collective-permute-start.15 = (f32[64,512]{1,0:T(8,128)S(1)}, f32[64,512]{1,0:T(8,128)S(1)}, u32[]{:S(2)}, u32[]{:S(2)}) collective-permute-start(f32[64,512]{1,0:T(8,128)S(1)} %get-tuple-element.48), channel_id=1, source_target_pairs={{0,5},{1,4},{2,7},{3,6},{4,1},{5,0},{6,3},{7,2},{8,13},{9,12},{10,... | collective-permute-start | bytes 393224 | tf_op jit(solution)/shard_map/ppermute | solution.py:215
  50.0 0.0 copy-done.3
  50.0 0.9 %finish.2.refs_5_ = bf16[64,4096]{1,0:T(8,128)(2,1)} custom-call(s32[10,128]{1,0:T(8,128)S(1)} %get-tuple-element.32.table, f32[64,4096]{1,0:T(8,128)S(1)} %inside.1.refs_8_.own, f32[1,4096]{1,0:T(1,128)S(1)} %bitcast.1, f32[64,512]{1,0:T(8,128)S(1)} %get-tuple-element.49.refs_0_, f32[64,512]{1,0:T(8,128)S(1)} %collective-permute-done.16.refs_1_, ...), custom_call_target="tpu_custom_call" | custom-call | bytes 2097152 | tf_op jit(solution)/shard_map/finish/pallas_call | solution.py:305
  50.8 0.0 collective-permute-done.11.refs_0_
  50.8 0.9 %collective-permute-done.12.refs_1_ = f32[64,512]{1,0:T(8,128)S(1)} collective-permute-done((f32[64,512]{1,0:T(8,128)S(1)}, f32[64,512]{1,0:T(8,128)S(1)}, u32[]{:S(2)}, u32[]{:S(2)}) %collective-permute-start.12) | collective-permute-done | bytes 131104 | tf_op jit(solution)/shard_map/ppermute | solution.py:215
  51.8 2.7 %collective-permute-done.13.refs_2_ = f32[64,512]{1,0:T(8,128)S(1)} collective-permute-done((f32[64,512]{1,0:T(8,128)S(1)}, f32[64,512]{1,0:T(8,128)S(1)}, u32[]{:S(2)}, u32[]{:S(2)}) %collective-permute-start.13) | collective-permute-done | bytes 131104 | tf_op jit(solution)/shard_map/ppermute | solution.py:215
  54.5 0.0 collective-permute-done.14.refs_3_
  54.5 0.0 collective-permute-done.15.refs_4_
  54.5 0.9 %finish.3 = bf16[64,4096]{1,0:T(8,128)(2,1)} custom-call(s32[10,128]{1,0:T(8,128)S(1)} %get-tuple-element.32.table, f32[64,4096]{1,0:T(8,128)S(1)} %inside.1.refs_8_.own, f32[1,4096]{1,0:T(1,128)S(1)} %bitcast.2, f32[64,512]{1,0:T(8,128)S(1)} %collective-permute-done.11.refs_0_, ...), custom_call_target="tpu_custom_call", output_to_operand_aliasing={{}: (8, {})} | custom-call | bytes 2097152 | tf_op jit(solution)/shard_map/finish/pallas_call | solution.py:305
Async XLA Ops:
  0.0 14.8 %copy-start = (bf16[64,4096]{1,0:T(8,128)(2,1)S(1)}, bf16[64,4096]{1,0:T(8,128)(2,1)}, u32[]{:S(2)}) copy-start(bf16[64,4096]{1,0:T(8,128)(2,1)} %queries.5) | copy-start | bytes 1572868
  0.0 14.8 %copy-start.2 = (bf16[64,4096]{1,0:T(8,128)(2,1)S(1)}, bf16[64,4096]{1,0:T(8,128)(2,1)}, u32[]{:S(2)}) copy-start(bf16[64,4096]{1,0:T(8,128)(2,1)} %values.3) | copy-start | bytes 1572868
  0.0 14.8 %copy-start.1 = (bf16[64,4096]{1,0:T(8,128)(2,1)S(1)}, bf16[64,4096]{1,0:T(8,128)(2,1)}, u32[]{:S(2)}) copy-start(bf16[64,4096]{1,0:T(8,128)(2,1)} %keys.3) | copy-start | bytes 1572868
  0.0 14.8 %copy-start.4 = (s32[16]{0:T(128)S(1)}, s32[16]{0:T(128)}, u32[]{:S(2)}) copy-start(s32[16]{0:T(128)} %lengths.3) | copy-start | bytes 196
  1.7 4.7 %collective-permute-start = (f32[4,3,64,512]{3,2,1,0:T(8,128)S(1)}, f32[4,3,64,512]{3,2,1,0:T(8,128)S(1)}, u32[]{:S(2)}, u32[]{:S(2)}) collective-permute-start(f32[4,3,64,512]{3,2,1,0:T(8,128)S(1)} %get-tuple-element.28), channel_id=1, source_target_pairs={{0,4},{1,5},{2,6},{3,7},{4,0},{5,1},{6,2},{7,3},{8,12},{9,13},{10,... | collective-permute-start | bytes 4718600 | tf_op jit(solution)/shard_map/ppermute | solution.py:215
  2.2 10.7 %collective-permute-start.1 = (f32[2,64,512]{2,1,0:T(8,128)S(1)}, f32[2,64,512]{2,1,0:T(8,128)S(1)}, u32[]{:S(2)}, u32[]{:S(2)}) collective-permute-start(f32[2,64,512]{2,1,0:T(8,128)S(1)} %get-tuple-element.29), channel_id=1, source_target_pairs={{0,3},{1,2},{2,1},{3,0},{4,7},{5,6},{6,5},{7,4},{8,11},{9,10},{10,... | collective-permute-start | bytes 786440 | tf_op jit(solution)/shard_map/ppermute | solution.py:215
  5.7 14.0 %collective-permute-start.2 = (f32[2,64,512]{2,1,0:T(8,128)S(1)}, f32[2,64,512]{2,1,0:T(8,128)S(1)}, u32[]{:S(2)}, u32[]{:S(2)}) collective-permute-start(f32[2,64,512]{2,1,0:T(8,128)S(1)} %get-tuple-element.30), channel_id=1, source_target_pairs={{0,2},{1,3},{2,0},{3,1},{4,6},{5,7},{6,4},{7,5},{8,10},{9,11},{10,... | collective-permute-start | bytes 786440 | tf_op jit(solution)/shard_map/ppermute | solution.py:215
  6.2 13.5 %collective-permute-start.3 = (f32[2,64,512]{2,1,0:T(8,128)S(1)}, f32[2,64,512]{2,1,0:T(8,128)S(1)}, u32[]{:S(2)}, u32[]{:S(2)}) collective-permute-start(f32[2,64,512]{2,1,0:T(8,128)S(1)} %get-tuple-element.31), channel_id=1, source_target_pairs={{0,1},{1,0},{2,3},{3,2},{4,5},{5,4},{6,7},{7,6},{8,9},{9,8},{10,11... | collective-permute-start | bytes 786440 | tf_op jit(solution)/shard_map/ppermute | solution.py:215
  6.4 17.8 %collective-permute-start.4 = (f32[2,64,512]{2,1,0:T(8,128)S(1)}, f32[2,64,512]{2,1,0:T(8,128)S(1)}, u32[]{:S(2)}, u32[]{:S(2)}) collective-permute-start(f32[2,64,512]{2,1,0:T(8,128)S(1)} %get-tuple-element.34), channel_id=1, source_target_pairs={{0,3},{1,2},{2,1},{3,0},{4,7},{5,6},{6,5},{7,4},{8,11},{9,10},{10,... | collective-permute-start | bytes 786440 | tf_op jit(solution)/shard_map/ppermute | solution.py:215
  9.3 20.3 %collective-permute-start.5 = (f32[2,64,512]{2,1,0:T(8,128)S(1)}, f32[2,64,512]{2,1,0:T(8,128)S(1)}, u32[]{:S(2)}, u32[]{:S(2)}) collective-permute-start(f32[2,64,512]{2,1,0:T(8,128)S(1)} %get-tuple-element.35), channel_id=1, source_target_pairs={{0,2},{1,3},{2,0},{3,1},{4,6},{5,7},{6,4},{7,5},{8,10},{9,11},{10,... | collective-permute-start | bytes 786440 | tf_op jit(solution)/shard_map/ppermute | solution.py:215
  12.9 17.4 %collective-permute-start.6 = (f32[2,64,512]{2,1,0:T(8,128)S(1)}, f32[2,64,512]{2,1,0:T(8,128)S(1)}, u32[]{:S(2)}, u32[]{:S(2)}) collective-permute-start(f32[2,64,512]{2,1,0:T(8,128)S(1)} %get-tuple-element.36), channel_id=1, source_target_pairs={{0,1},{1,0},{2,3},{3,2},{4,5},{5,4},{6,7},{7,6},{8,9},{9,8},{10,11... | collective-permute-start | bytes 786440 | tf_op jit(solution)/shard_map/ppermute | solution.py:215
  20.5 15.9 %collective-permute-start.10 = (f32[2,64,512]{2,1,0:T(8,128)S(1)}, f32[2,64,512]{2,1,0:T(8,128)S(1)}, u32[]{:S(2)}, u32[]{:S(2)}) collective-permute-start(f32[2,64,512]{2,1,0:T(8,128)S(1)} %get-tuple-element.42), channel_id=1, source_target_pairs={{0,3},{1,2},{2,1},{3,0},{4,7},{5,6},{6,5},{7,4},{8,11},{9,10},{10,... | collective-permute-start | bytes 786440 | tf_op jit(solution)/shard_map/ppermute | solution.py:215
  30.9 8.9 %collective-permute-start.7 = (f32[4,128,128]{2,1,0:T(8,128)S(1)}, f32[4,128,128]{2,1,0:T(8,128)S(1)}, u32[]{:S(2)}, u32[]{:S(2)}) collective-permute-start(f32[4,128,128]{2,1,0:T(8,128)S(1)} %get-tuple-element.38), channel_id=1, source_target_pairs={{0,8},{1,9},{2,10},{3,11},{4,12},{5,13},{6,14},{7,15},{8,16},{9,17... | collective-permute-start | bytes 786440 | tf_op jit(solution)/shard_map/ppermute | solution.py:270
  34.4 7.7 %collective-permute-start.8 = (f32[2,64,512]{2,1,0:T(8,128)S(1)}, f32[2,64,512]{2,1,0:T(8,128)S(1)}, u32[]{:S(2)}, u32[]{:S(2)}) collective-permute-start(f32[2,64,512]{2,1,0:T(8,128)S(1)} %get-tuple-element.39), channel_id=1, source_target_pairs={{0,2},{1,3},{2,0},{3,1},{4,6},{5,7},{6,4},{7,5},{8,10},{9,11},{10,... | collective-permute-start | bytes 786440 | tf_op jit(solution)/shard_map/ppermute | solution.py:215
  35.8 7.6 %collective-permute-start.9 = (f32[2,64,512]{2,1,0:T(8,128)S(1)}, f32[2,64,512]{2,1,0:T(8,128)S(1)}, u32[]{:S(2)}, u32[]{:S(2)}) collective-permute-start(f32[2,64,512]{2,1,0:T(8,128)S(1)} %get-tuple-element.40), channel_id=1, source_target_pairs={{0,1},{1,0},{2,3},{3,2},{4,5},{5,4},{6,7},{7,6},{8,9},{9,8},{10,11... | collective-permute-start | bytes 786440 | tf_op jit(solution)/shard_map/ppermute | solution.py:215
  40.1 6.8 %collective-permute-start.17 = (f32[64,512]{1,0:T(8,128)S(1)}, f32[64,512]{1,0:T(8,128)S(1)}, u32[]{:S(2)}, u32[]{:S(2)}) collective-permute-start(f32[64,512]{1,0:T(8,128)S(1)} %get-tuple-element.50), channel_id=1, source_target_pairs={{0,7},{1,6},{2,5},{3,4},{4,3},{5,2},{6,1},{7,0},{8,15},{9,14},{10,... | collective-permute-start | bytes 393224 | tf_op jit(solution)/shard_map/ppermute | solution.py:215
  40.2 8.3 %collective-permute-start.16 = (f32[64,512]{1,0:T(8,128)S(1)}, f32[64,512]{1,0:T(8,128)S(1)}, u32[]{:S(2)}, u32[]{:S(2)}) collective-permute-start(f32[64,512]{1,0:T(8,128)S(1)} %get-tuple-element.43.refs_3_), channel_id=1, source_target_pairs={{0,3},{1,2},{2,1},{3,0},{4,7},{5,6},{6,5},{7,4},{8,11},{9,10},{10,... | collective-permute-start | bytes 393224 | tf_op jit(solution)/shard_map/ppermute | solution.py:215
  43.4 6.6 %copy-start.3 = (f32[4096]{0:T(1024)S(1)}, f32[4096]{0:T(1024)}, u32[]{:S(2)}) copy-start(f32[4096]{0:T(1024)} %param.9) | copy-start | bytes 49156
  43.9 7.0 %collective-permute-start.11 = (f32[64,512]{1,0:T(8,128)S(1)}, f32[64,512]{1,0:T(8,128)S(1)}, u32[]{:S(2)}, u32[]{:S(2)}) collective-permute-start(f32[64,512]{1,0:T(8,128)S(1)} %get-tuple-element.44), channel_id=1, source_target_pairs={{0,4},{1,5},{2,6},{3,7},{4,0},{5,1},{6,2},{7,3},{8,12},{9,13},{10,... | collective-permute-start | bytes 393224 | tf_op jit(solution)/shard_map/ppermute | solution.py:215
  43.9 7.9 %collective-permute-start.12 = (f32[64,512]{1,0:T(8,128)S(1)}, f32[64,512]{1,0:T(8,128)S(1)}, u32[]{:S(2)}, u32[]{:S(2)}) collective-permute-start(f32[64,512]{1,0:T(8,128)S(1)} %get-tuple-element.45), channel_id=1, source_target_pairs={{0,2},{1,3},{2,0},{3,1},{4,6},{5,7},{6,4},{7,5},{8,10},{9,11},{10,... | collective-permute-start | bytes 393224 | tf_op jit(solution)/shard_map/ppermute | solution.py:215
  45.0 9.5 %collective-permute-start.13 = (f32[64,512]{1,0:T(8,128)S(1)}, f32[64,512]{1,0:T(8,128)S(1)}, u32[]{:S(2)}, u32[]{:S(2)}) collective-permute-start(f32[64,512]{1,0:T(8,128)S(1)} %get-tuple-element.46), channel_id=1, source_target_pairs={{0,6},{1,7},{2,4},{3,5},{4,2},{5,3},{6,0},{7,1},{8,14},{9,15},{10,... | collective-permute-start | bytes 393224 | tf_op jit(solution)/shard_map/ppermute | solution.py:215
  46.9 7.6 %collective-permute-start.14 = (f32[64,512]{1,0:T(8,128)S(1)}, f32[64,512]{1,0:T(8,128)S(1)}, u32[]{:S(2)}, u32[]{:S(2)}) collective-permute-start(f32[64,512]{1,0:T(8,128)S(1)} %get-tuple-element.47), channel_id=1, source_target_pairs={{0,1},{1,0},{2,3},{3,2},{4,5},{5,4},{6,7},{7,6},{8,9},{9,8},{10,11... | collective-permute-start | bytes 393224 | tf_op jit(solution)/shard_map/ppermute | solution.py:215
  48.5 6.0 %collective-permute-start.15 = (f32[64,512]{1,0:T(8,128)S(1)}, f32[64,512]{1,0:T(8,128)S(1)}, u32[]{:S(2)}, u32[]{:S(2)}) collective-permute-start(f32[64,512]{1,0:T(8,128)S(1)} %get-tuple-element.48), channel_id=1, source_target_pairs={{0,5},{1,4},{2,7},{3,6},{4,1},{5,0},{6,3},{7,2},{8,13},{9,12},{10,... | collective-permute-start | bytes 393224 | tf_op jit(solution)/shard_map/ppermute | solution.py:215

commit v9 on v8

--- a/solution.py
+++ b/solution.py
@@ -235,7 +235,7 @@
         moved=2 * block_bytes,
     )(swapped)
     far_got = [swap(part, e) for e, part in zip(downward, far_parts)] + [swapped]
-    gates = near_got[:-1]
+    gates = [*near_got[:-1], far_got[0]]
     *query_parts, table = call(
         functools.partial(join_queries, members, width, rows, docs, len(gates)),
         "join_queries",
@@ -276,7 +276,7 @@
             moving = lax.ppermute(moving, everyone, up)
             earlier = earlier + jnp.where(opens < base - (k - 1) * members * rows, moving, 0.0)
     crossed_got = {}
-    late = [e for e in downward if e in (0, 1, 2)]
+    late = [e for e in (1, 2, 0) if e < half]
     soon = [e for e in downward if e not in late]
     gates = []
     for chosen in (soon, late):
@@ -299,7 +299,7 @@
     gain = norm_gain.reshape(1, columns)
     out = None
     groups = [[0] + [e ^ (side * half) for e in soon for side in range(CORES)]]
-    groups += [[half] + [e ^ (side * half) for e in late if e for side in range(CORES)]]
+    groups += [[e ^ (side * half) for side in range(CORES) for e in late if e] + [half]]
     for chosen in groups:
         more = [] if out is None else [out]
         out = call(

time: 55.6 us -> 58.5 us (1.052)
  waiting for transfers between devices: 21.3 us -> 24 us
    ppermute x17, waiting for transfers between devices: 17.9 us -> 20.6 us  [swap(): return lax.ppermute(part, everyone, pairs)]
where the time goes in v9:
time: 58.5 us; the launch traced here: 58.3 us
  waiting for transfers between devices  24 us (41%)
  starting transfers between devices  23.7 us (41%)
  Pallas kernels  10.5 us (18%)
    ppermute x17, waiting for transfers between devices, swap(): return lax.ppermute(part, everyone, pairs)  20.6 us
    ppermute x17, starting transfers between devices, swap(): return lax.ppermute(part, everyone, pairs)  20.2 us
    pallas_call x1, Pallas kernels, body(): call(functools.partial(inside, head_count, docs, rows), 'inside', shape(r...  4.93 us
    ppermute x1, starting transfers between devices, body(): moving = lax.ppermute(total, everyone, up)  3.5 us
    ppermute x1, waiting for transfers between devices, body(): moving = lax.ppermute(total, everyone, up)  3.36 us
    pallas_call x2, Pallas kernels, body(): call(functools.partial(finish, chosen, members, heads, rows), 'finish', s...  1.81 us
    pallas_call x1, Pallas kernels, body(): call(functools.partial(spread, members, width), 'spread', [shape(2, rows,...  1.67 us
  transfers between devices with their start and end apart: 18, of which 10 were waited for; matrix products, arithmetic and copies ran while one was open for 0% of the time, Pallas kernels for 14%

profile of v9, /device:TPU:0, one launch (start us, length us, event | category | flops | bytes accessed | tf_op | source)
XLA Modules:
  0.0 58.3 jit_solution(5061566195074419781)
XLA Ops:
  0.0 0.0 copy-start
  0.0 0.0 copy-start.2
  0.0 0.0 copy-start.1
  0.0 0.0 copy-start.4
  0.0 1.7 %spread.1 = (f32[2,64,512]{2,1,0:T(8,128)S(1)}, f32[2,64,512]{2,1,0:T(8,128)S(1)}, f32[2,64,512]{2,1,0:T(8,128)S(1)}, f32[2,64,512]{2,1,0:T(8,128)S(1)}, f32[4,3,64,512]{3,2,1,0:T(8,128)S(1)}) custom-call(bf16[64,4096]{1,0:T(8,128)(2,1)} %queries.5, bf16[64,4096]{1,0:T(8,128)(2,1)} %keys.3, bf16[64,4096]{1,0:T(8,128)(2,1)} %values.3), custom_call_target="tpu_custom_call" | custom-call | tf_op jit(solution)/shard_map/spread/pallas_call | solution.py:219
  1.7 0.5 collective-permute-start
  2.2 3.5 %collective-permute-start.1 = (f32[2,64,512]{2,1,0:T(8,128)S(1)}, f32[2,64,512]{2,1,0:T(8,128)S(1)}, u32[]{:S(2)}, u32[]{:S(2)}) collective-permute-start(f32[2,64,512]{2,1,0:T(8,128)S(1)} %get-tuple-element.29), channel_id=1, source_target_pairs={{0,3},{1,2},{2,1},{3,0},{4,7},{5,6},{6,5},{7,4},{8,11},{9,10},{10,... | collective-permute-start | bytes 786440 | tf_op jit(solution)/shard_map/ppermute | solution.py:215
  5.7 0.5 collective-permute-start.2
  6.2 0.1 collective-permute-start.3
  6.4 0.0 collective-permute-done.swapped.refs_7_
  6.4 0.1 forward.1
  6.4 2.9 %collective-permute-start.4 = (f32[2,64,512]{2,1,0:T(8,128)S(1)}, f32[2,64,512]{2,1,0:T(8,128)S(1)}, u32[]{:S(2)}, u32[]{:S(2)}) collective-permute-start(f32[2,64,512]{2,1,0:T(8,128)S(1)} %get-tuple-element.32), channel_id=1, source_target_pairs={{0,3},{1,2},{2,1},{3,0},{4,7},{5,6},{6,5},{7,4},{8,11},{9,10},{10,... | collective-permute-start | bytes 786440 | tf_op jit(solution)/shard_map/ppermute | solution.py:215
  9.3 0.5 collective-permute-start.5
  9.9 3.1 %collective-permute-done.1.refs_0_ = f32[2,64,512]{2,1,0:T(8,128)S(1)} collective-permute-done((f32[2,64,512]{2,1,0:T(8,128)S(1)}, f32[2,64,512]{2,1,0:T(8,128)S(1)}, u32[]{:S(2)}, u32[]{:S(2)}) %collective-permute-start.1) | collective-permute-done | bytes 262176 | tf_op jit(solution)/shard_map/ppermute | solution.py:215
  12.9 1.9 %collective-permute-start.6 = (f32[2,64,512]{2,1,0:T(8,128)S(1)}, f32[2,64,512]{2,1,0:T(8,128)S(1)}, u32[]{:S(2)}, u32[]{:S(2)}) collective-permute-start(f32[2,64,512]{2,1,0:T(8,128)S(1)} %get-tuple-element.36), channel_id=1, source_target_pairs={{0,1},{1,0},{2,3},{3,2},{4,5},{5,4},{6,7},{7,6},{8,9},{9,8},{10,11... | collective-permute-start | bytes 786440 | tf_op jit(solution)/shard_map/ppermute | solution.py:215
  14.8 0.0 copy-done
  14.8 0.0 copy-done.2
  14.8 0.0 copy-done.1
  14.8 0.0 copy-done.4
  14.8 4.9 %inside.1.refs_8_.own = f32[64,4096]{1,0:T(8,128)S(1)} custom-call(s32[16]{0:T(128)S(1)} %copy-done.4, bf16[64,4096]{1,0:T(8,128)(2,1)S(1)} %copy-done, bf16[64,4096]{1,0:T(8,128)(2,1)S(1)} %copy-done.1, bf16[64,4096]{1,0:T(8,128)(2,1)S(1)} %copy-done.2), custom_call_target="tpu_custom_call" | custom-call | flops 67108864 | bytes 3145728 | tf_op jit(solution)/shard_map/inside/pallas_call | solution.py:249
  19.8 0.0 collective-permute-done.2.refs_1_
  19.8 0.0 collective-permute-done.3.refs_2_
  19.8 4.4 %collective-permute-done.4.refs_3_.refs_4_ = f32[2,64,512]{2,1,0:T(8,128)S(1)} collective-permute-done((f32[2,64,512]{2,1,0:T(8,128)S(1)}, f32[2,64,512]{2,1,0:T(8,128)S(1)}, u32[]{:S(2)}, u32[]{:S(2)}) %collective-permute-start.4) | collective-permute-done | bytes 262176 | tf_op jit(solution)/shard_map/ppermute | solution.py:215
  24.2 0.7 %join_queries.1 = (f32[2,64,512]{2,1,0:T(8,128)S(1)}, f32[2,64,512]{2,1,0:T(8,128)S(1)}, f32[2,64,512]{2,1,0:T(8,128)S(1)}, f32[2,64,512]{2,1,0:T(8,128)S(1)}, s32[10,128]{1,0:T(8,128)S(1)}) custom-call(s32[16]{0:T(128)S(1)} %copy-done.4, bf16[64,4096]{1,0:T(8,128)(2,1)S(1)} %copy-done, f32[4,3,64,512]{3,2,1,0:T(8,128)S(1)} %collective-permute-done.swapped.refs_7_, ...), custom_call_target="tpu_custom_call" | custom-call | bytes 2097152 | tf_op jit(solution)/shard_map/join_queries/pallas_call | solution.py:239
  25.0 2.9 %collective-permute-start.10 = (f32[2,64,512]{2,1,0:T(8,128)S(1)}, f32[2,64,512]{2,1,0:T(8,128)S(1)}, u32[]{:S(2)}, u32[]{:S(2)}) collective-permute-start(f32[2,64,512]{2,1,0:T(8,128)S(1)} %get-tuple-element.42), channel_id=1, source_target_pairs={{0,3},{1,2},{2,1},{3,0},{4,7},{5,6},{6,5},{7,4},{8,11},{9,10},{10,... | collective-permute-start | bytes 786440 | tf_op jit(solution)/shard_map/ppermute | solution.py:215
  27.9 1.8 %collective-permute-done.5.refs_5_ = f32[2,64,512]{2,1,0:T(8,128)S(1)} collective-permute-done((f32[2,64,512]{2,1,0:T(8,128)S(1)}, f32[2,64,512]{2,1,0:T(8,128)S(1)}, u32[]{:S(2)}, u32[]{:S(2)}) %collective-permute-start.5) | collective-permute-done | bytes 262176 | tf_op jit(solution)/shard_map/ppermute | solution.py:215
  29.7 0.6 %collective-permute-done.6.refs_6_ = f32[2,64,512]{2,1,0:T(8,128)S(1)} collective-permute-done((f32[2,64,512]{2,1,0:T(8,128)S(1)}, f32[2,64,512]{2,1,0:T(8,128)S(1)}, u32[]{:S(2)}, u32[]{:S(2)}) %collective-permute-start.6) | collective-permute-done | bytes 262176 | tf_op jit(solution)/shard_map/ppermute | solution.py:215
  30.3 0.6 %gather_states.1 = (f32[8,4,128,128]{3,2,1,0:T(8,128)S(1)}, f32[4,128,128]{2,1,0:T(8,128)S(1)}) custom-call(s32[10,128]{1,0:T(8,128)S(1)} %get-tuple-element.33.table, f32[2,64,512]{2,1,0:T(8,128)S(1)} %collective-permute-done.1.refs_0_, f32[2,64,512]{2,1,0:T(8,128)S(1)} %collective-permute-done.2.refs_1_, f32[2,64,512]{2,1,0:T(8,128)S(1)} %collective-permute-done.3.refs_2_, ...), custom_call_target="tpu_custom_call" | custom-call | flops 67108864 | bytes 4194304 | tf_op jit(solution)/shard_map/gather_states/pallas_call | solution.py:259
  30.9 3.5 %collective-permute-start.7 = (f32[4,128,128]{2,1,0:T(8,128)S(1)}, f32[4,128,128]{2,1,0:T(8,128)S(1)}, u32[]{:S(2)}, u32[]{:S(2)}) collective-permute-start(f32[4,128,128]{2,1,0:T(8,128)S(1)} %get-tuple-element.38), channel_id=1, source_target_pairs={{0,8},{1,9},{2,10},{3,11},{4,12},{5,13},{6,14},{7,15},{8,16},{9,17... | collective-permute-start | bytes 786440 | tf_op jit(solution)/shard_map/ppermute | solution.py:270
  34.4 1.6 %collective-permute-start.8 = (f32[2,64,512]{2,1,0:T(8,128)S(1)}, f32[2,64,512]{2,1,0:T(8,128)S(1)}, u32[]{:S(2)}, u32[]{:S(2)}) collective-permute-start(f32[2,64,512]{2,1,0:T(8,128)S(1)} %get-tuple-element.39), channel_id=1, source_target_pairs={{0,1},{1,0},{2,3},{3,2},{4,5},{5,4},{6,7},{7,6},{8,9},{9,8},{10,11... | collective-permute-start | bytes 786440 | tf_op jit(solution)/shard_map/ppermute | solution.py:215
  36.0 0.5 collective-permute-start.9
  36.5 0.0 collective-permute-done.10.refs_0_
  36.5 3.4 %collective-permute-done.7.earlier = f32[4,128,128]{2,1,0:T(8,128)S(1)} collective-permute-done((f32[4,128,128]{2,1,0:T(8,128)S(1)}, f32[4,128,128]{2,1,0:T(8,128)S(1)}, u32[]{:S(2)}, u32[]{:S(2)}) %collective-permute-start.7) | collective-permute-done | bytes 262176 | tf_op jit(solution)/shard_map/ppermute | solution.py:270
  39.8 0.2 reach_back.2
  40.1 0.1 collective-permute-start.17
  40.2 1.4 %collective-permute-start.16 = (f32[64,512]{1,0:T(8,128)S(1)}, f32[64,512]{1,0:T(8,128)S(1)}, u32[]{:S(2)}, u32[]{:S(2)}) collective-permute-start(f32[64,512]{1,0:T(8,128)S(1)} %get-tuple-element.43.refs_3_), channel_id=1, source_target_pairs={{0,3},{1,2},{2,1},{3,0},{4,7},{5,6},{6,5},{7,4},{8,11},{9,10},{10,... | collective-permute-start | bytes 393224 | tf_op jit(solution)/shard_map/ppermute | solution.py:215
  41.5 0.6 %collective-permute-done.8.refs_0_ = f32[2,64,512]{2,1,0:T(8,128)S(1)} collective-permute-done((f32[2,64,512]{2,1,0:T(8,128)S(1)}, f32[2,64,512]{2,1,0:T(8,128)S(1)}, u32[]{:S(2)}, u32[]{:S(2)}) %collective-permute-start.8) | collective-permute-done | bytes 262176 | tf_op jit(solution)/shard_map/ppermute | solution.py:215
  42.1 6.9 %collective-permute-done.9.refs_1_ = f32[2,64,512]{2,1,0:T(8,128)S(1)} collective-permute-done((f32[2,64,512]{2,1,0:T(8,128)S(1)}, f32[2,64,512]{2,1,0:T(8,128)S(1)}, u32[]{:S(2)}, u32[]{:S(2)}) %collective-permute-start.9) | collective-permute-done | bytes 262176 | tf_op jit(solution)/shard_map/ppermute | solution.py:215
  49.1 0.0 copy-start.3
  49.1 0.5 reach_back.3
  49.5 0.1 collective-permute-start.11
  49.6 2.0 %collective-permute-start.12 = (f32[64,512]{1,0:T(8,128)S(1)}, f32[64,512]{1,0:T(8,128)S(1)}, u32[]{:S(2)}, u32[]{:S(2)}) collective-permute-start(f32[64,512]{1,0:T(8,128)S(1)} %get-tuple-element.45), channel_id=1, source_target_pairs={{0,2},{1,3},{2,0},{3,1},{4,6},{5,7},{6,4},{7,5},{8,10},{9,11},{10,... | collective-permute-start | bytes 393224 | tf_op jit(solution)/shard_map/ppermute | solution.py:215
  51.6 0.0 collective-permute-start.13
  51.6 0.0 collective-permute-done.17.refs_2_
  51.6 1.7 %collective-permute-start.14 = (f32[64,512]{1,0:T(8,128)S(1)}, f32[64,512]{1,0:T(8,128)S(1)}, u32[]{:S(2)}, u32[]{:S(2)}) collective-permute-start(f32[64,512]{1,0:T(8,128)S(1)} %get-tuple-element.47), channel_id=1, source_target_pairs={{0,6},{1,7},{2,4},{3,5},{4,2},{5,3},{6,0},{7,1},{8,14},{9,15},{10,... | collective-permute-start | bytes 393224 | tf_op jit(solution)/shard_map/ppermute | solution.py:215
  53.4 0.0 collective-permute-done.16.refs_1_
  53.4 0.0 collective-permute-start.15
  53.4 0.0 copy-done.3
  53.4 0.9 %finish.2.refs_5_ = bf16[64,4096]{1,0:T(8,128)(2,1)} custom-call(s32[10,128]{1,0:T(8,128)S(1)} %get-tuple-element.33.table, f32[64,4096]{1,0:T(8,128)S(1)} %inside.1.refs_8_.own, f32[1,4096]{1,0:T(1,128)S(1)} %bitcast.1, f32[64,512]{1,0:T(8,128)S(1)} %get-tuple-element.49.refs_0_, f32[64,512]{1,0:T(8,128)S(1)} %collective-permute-done.16.refs_1_, ...), custom_call_target="tpu_custom_call" | custom-call | bytes 2097152 | tf_op jit(solution)/shard_map/finish/pallas_call | solution.py:305
  54.3 0.3 collective-permute-done.11.refs_0_
  54.6 0.5 collective-permute-done.12.refs_1_
  55.0 2.3 %collective-permute-done.13.refs_2_ = f32[64,512]{1,0:T(8,128)S(1)} collective-permute-done((f32[64,512]{1,0:T(8,128)S(1)}, f32[64,512]{1,0:T(8,128)S(1)}, u32[]{:S(2)}, u32[]{:S(2)}) %collective-permute-start.13) | collective-permute-done | bytes 131104 | tf_op jit(solution)/shard_map/ppermute | solution.py:215
  57.4 0.0 collective-permute-done.14.refs_3_
  57.4 0.0 collective-permute-done.15.refs_4_
  57.4 0.9 %finish.3 = bf16[64,4096]{1,0:T(8,128)(2,1)} custom-call(s32[10,128]{1,0:T(8,128)S(1)} %get-tuple-element.33.table, f32[64,4096]{1,0:T(8,128)S(1)} %inside.1.refs_8_.own, f32[1,4096]{1,0:T(1,128)S(1)} %bitcast.2, f32[64,512]{1,0:T(8,128)S(1)} %collective-permute-done.11.refs_0_, ...), custom_call_target="tpu_custom_call", output_to_operand_aliasing={{}: (8, {})} | custom-call | bytes 2097152 | tf_op jit(solution)/shard_map/finish/pallas_call | solution.py:305
Async XLA Ops:
  0.0 14.8 %copy-start = (bf16[64,4096]{1,0:T(8,128)(2,1)S(1)}, bf16[64,4096]{1,0:T(8,128)(2,1)}, u32[]{:S(2)}) copy-start(bf16[64,4096]{1,0:T(8,128)(2,1)} %queries.5) | copy-start | bytes 1572868
  0.0 14.8 %copy-start.2 = (bf16[64,4096]{1,0:T(8,128)(2,1)S(1)}, bf16[64,4096]{1,0:T(8,128)(2,1)}, u32[]{:S(2)}) copy-start(bf16[64,4096]{1,0:T(8,128)(2,1)} %values.3) | copy-start | bytes 1572868
  0.0 14.8 %copy-start.1 = (bf16[64,4096]{1,0:T(8,128)(2,1)S(1)}, bf16[64,4096]{1,0:T(8,128)(2,1)}, u32[]{:S(2)}) copy-start(bf16[64,4096]{1,0:T(8,128)(2,1)} %keys.3) | copy-start | bytes 1572868
  0.0 14.8 %copy-start.4 = (s32[16]{0:T(128)S(1)}, s32[16]{0:T(128)}, u32[]{:S(2)}) copy-start(s32[16]{0:T(128)} %lengths.3) | copy-start | bytes 196
  1.7 4.7 %collective-permute-start = (f32[4,3,64,512]{3,2,1,0:T(8,128)S(1)}, f32[4,3,64,512]{3,2,1,0:T(8,128)S(1)}, u32[]{:S(2)}, u32[]{:S(2)}) collective-permute-start(f32[4,3,64,512]{3,2,1,0:T(8,128)S(1)} %get-tuple-element.28), channel_id=1, source_target_pairs={{0,4},{1,5},{2,6},{3,7},{4,0},{5,1},{6,2},{7,3},{8,12},{9,13},{10,... | collective-permute-start | bytes 4718600 | tf_op jit(solution)/shard_map/ppermute | solution.py:215
  2.2 10.7 %collective-permute-start.1 = (f32[2,64,512]{2,1,0:T(8,128)S(1)}, f32[2,64,512]{2,1,0:T(8,128)S(1)}, u32[]{:S(2)}, u32[]{:S(2)}) collective-permute-start(f32[2,64,512]{2,1,0:T(8,128)S(1)} %get-tuple-element.29), channel_id=1, source_target_pairs={{0,3},{1,2},{2,1},{3,0},{4,7},{5,6},{6,5},{7,4},{8,11},{9,10},{10,... | collective-permute-start | bytes 786440 | tf_op jit(solution)/shard_map/ppermute | solution.py:215
  5.7 14.0 %collective-permute-start.2 = (f32[2,64,512]{2,1,0:T(8,128)S(1)}, f32[2,64,512]{2,1,0:T(8,128)S(1)}, u32[]{:S(2)}, u32[]{:S(2)}) collective-permute-start(f32[2,64,512]{2,1,0:T(8,128)S(1)} %get-tuple-element.30), channel_id=1, source_target_pairs={{0,2},{1,3},{2,0},{3,1},{4,6},{5,7},{6,4},{7,5},{8,10},{9,11},{10,... | collective-permute-start | bytes 786440 | tf_op jit(solution)/shard_map/ppermute | solution.py:215
  6.2 13.5 %collective-permute-start.3 = (f32[2,64,512]{2,1,0:T(8,128)S(1)}, f32[2,64,512]{2,1,0:T(8,128)S(1)}, u32[]{:S(2)}, u32[]{:S(2)}) collective-permute-start(f32[2,64,512]{2,1,0:T(8,128)S(1)} %get-tuple-element.31), channel_id=1, source_target_pairs={{0,1},{1,0},{2,3},{3,2},{4,5},{5,4},{6,7},{7,6},{8,9},{9,8},{10,11... | collective-permute-start | bytes 786440 | tf_op jit(solution)/shard_map/ppermute | solution.py:215
  6.4 17.8 %collective-permute-start.4 = (f32[2,64,512]{2,1,0:T(8,128)S(1)}, f32[2,64,512]{2,1,0:T(8,128)S(1)}, u32[]{:S(2)}, u32[]{:S(2)}) collective-permute-start(f32[2,64,512]{2,1,0:T(8,128)S(1)} %get-tuple-element.32), channel_id=1, source_target_pairs={{0,3},{1,2},{2,1},{3,0},{4,7},{5,6},{6,5},{7,4},{8,11},{9,10},{10,... | collective-permute-start | bytes 786440 | tf_op jit(solution)/shard_map/ppermute | solution.py:215
  9.3 20.3 %collective-permute-start.5 = (f32[2,64,512]{2,1,0:T(8,128)S(1)}, f32[2,64,512]{2,1,0:T(8,128)S(1)}, u32[]{:S(2)}, u32[]{:S(2)}) collective-permute-start(f32[2,64,512]{2,1,0:T(8,128)S(1)} %get-tuple-element.35), channel_id=1, source_target_pairs={{0,2},{1,3},{2,0},{3,1},{4,6},{5,7},{6,4},{7,5},{8,10},{9,11},{10,... | collective-permute-start | bytes 786440 | tf_op jit(solution)/shard_map/ppermute | solution.py:215
  12.9 17.4 %collective-permute-start.6 = (f32[2,64,512]{2,1,0:T(8,128)S(1)}, f32[2,64,512]{2,1,0:T(8,128)S(1)}, u32[]{:S(2)}, u32[]{:S(2)}) collective-permute-start(f32[2,64,512]{2,1,0:T(8,128)S(1)} %get-tuple-element.36), channel_id=1, source_target_pairs={{0,1},{1,0},{2,3},{3,2},{4,5},{5,4},{6,7},{7,6},{8,9},{9,8},{10,11... | collective-permute-start | bytes 786440 | tf_op jit(solution)/shard_map/ppermute | solution.py:215
  25.0 11.5 %collective-permute-start.10 = (f32[2,64,512]{2,1,0:T(8,128)S(1)}, f32[2,64,512]{2,1,0:T(8,128)S(1)}, u32[]{:S(2)}, u32[]{:S(2)}) collective-permute-start(f32[2,64,512]{2,1,0:T(8,128)S(1)} %get-tuple-element.42), channel_id=1, source_target_pairs={{0,3},{1,2},{2,1},{3,0},{4,7},{5,6},{6,5},{7,4},{8,11},{9,10},{10,... | collective-permute-start | bytes 786440 | tf_op jit(solution)/shard_map/ppermute | solution.py:215
  30.9 8.9 %collective-permute-start.7 = (f32[4,128,128]{2,1,0:T(8,128)S(1)}, f32[4,128,128]{2,1,0:T(8,128)S(1)}, u32[]{:S(2)}, u32[]{:S(2)}) collective-permute-start(f32[4,128,128]{2,1,0:T(8,128)S(1)} %get-tuple-element.38), channel_id=1, source_target_pairs={{0,8},{1,9},{2,10},{3,11},{4,12},{5,13},{6,14},{7,15},{8,16},{9,17... | collective-permute-start | bytes 786440 | tf_op jit(solution)/shard_map/ppermute | solution.py:270
  34.4 7.7 %collective-permute-start.8 = (f32[2,64,512]{2,1,0:T(8,128)S(1)}, f32[2,64,512]{2,1,0:T(8,128)S(1)}, u32[]{:S(2)}, u32[]{:S(2)}) collective-permute-start(f32[2,64,512]{2,1,0:T(8,128)S(1)} %get-tuple-element.39), channel_id=1, source_target_pairs={{0,1},{1,0},{2,3},{3,2},{4,5},{5,4},{6,7},{7,6},{8,9},{9,8},{10,11... | collective-permute-start | bytes 786440 | tf_op jit(solution)/shard_map/ppermute | solution.py:215
  36.0 13.1 %collective-permute-start.9 = (f32[2,64,512]{2,1,0:T(8,128)S(1)}, f32[2,64,512]{2,1,0:T(8,128)S(1)}, u32[]{:S(2)}, u32[]{:S(2)}) collective-permute-start(f32[2,64,512]{2,1,0:T(8,128)S(1)} %get-tuple-element.40), channel_id=1, source_target_pairs={{0,2},{1,3},{2,0},{3,1},{4,6},{5,7},{6,4},{7,5},{8,10},{9,11},{10,... | collective-permute-start | bytes 786440 | tf_op jit(solution)/shard_map/ppermute | solution.py:215
  40.1 11.6 %collective-permute-start.17 = (f32[64,512]{1,0:T(8,128)S(1)}, f32[64,512]{1,0:T(8,128)S(1)}, u32[]{:S(2)}, u32[]{:S(2)}) collective-permute-start(f32[64,512]{1,0:T(8,128)S(1)} %get-tuple-element.50), channel_id=1, source_target_pairs={{0,7},{1,6},{2,5},{3,4},{4,3},{5,2},{6,1},{7,0},{8,15},{9,14},{10,... | collective-permute-start | bytes 393224 | tf_op jit(solution)/shard_map/ppermute | solution.py:215
  40.2 13.2 %collective-permute-start.16 = (f32[64,512]{1,0:T(8,128)S(1)}, f32[64,512]{1,0:T(8,128)S(1)}, u32[]{:S(2)}, u32[]{:S(2)}) collective-permute-start(f32[64,512]{1,0:T(8,128)S(1)} %get-tuple-element.43.refs_3_), channel_id=1, source_target_pairs={{0,3},{1,2},{2,1},{3,0},{4,7},{5,6},{6,5},{7,4},{8,11},{9,10},{10,... | collective-permute-start | bytes 393224 | tf_op jit(solution)/shard_map/ppermute | solution.py:215
  49.1 4.3 %copy-start.3 = (f32[4096]{0:T(1024)S(1)}, f32[4096]{0:T(1024)}, u32[]{:S(2)}) copy-start(f32[4096]{0:T(1024)} %param.9) | copy-start | bytes 49156
  49.5 5.0 %collective-permute-start.11 = (f32[64,512]{1,0:T(8,128)S(1)}, f32[64,512]{1,0:T(8,128)S(1)}, u32[]{:S(2)}, u32[]{:S(2)}) collective-permute-start(f32[64,512]{1,0:T(8,128)S(1)} %get-tuple-element.44), channel_id=1, source_target_pairs={{0,1},{1,0},{2,3},{3,2},{4,5},{5,4},{6,7},{7,6},{8,9},{9,8},{10,11... | collective-permute-start | bytes 393224 | tf_op jit(solution)/shard_map/ppermute | solution.py:215
  49.6 5.4 %collective-permute-start.12 = (f32[64,512]{1,0:T(8,128)S(1)}, f32[64,512]{1,0:T(8,128)S(1)}, u32[]{:S(2)}, u32[]{:S(2)}) collective-permute-start(f32[64,512]{1,0:T(8,128)S(1)} %get-tuple-element.45), channel_id=1, source_target_pairs={{0,2},{1,3},{2,0},{3,1},{4,6},{5,7},{6,4},{7,5},{8,10},{9,11},{10,... | collective-permute-start | bytes 393224 | tf_op jit(solution)/shard_map/ppermute | solution.py:215
  51.6 5.8 %collective-permute-start.13 = (f32[64,512]{1,0:T(8,128)S(1)}, f32[64,512]{1,0:T(8,128)S(1)}, u32[]{:S(2)}, u32[]{:S(2)}) collective-permute-start(f32[64,512]{1,0:T(8,128)S(1)} %get-tuple-element.46), channel_id=1, source_target_pairs={{0,5},{1,4},{2,7},{3,6},{4,1},{5,0},{6,3},{7,2},{8,13},{9,12},{10,... | collective-permute-start | bytes 393224 | tf_op jit(solution)/shard_map/ppermute | solution.py:215
  51.6 5.7 %collective-permute-start.14 = (f32[64,512]{1,0:T(8,128)S(1)}, f32[64,512]{1,0:T(8,128)S(1)}, u32[]{:S(2)}, u32[]{:S(2)}) collective-permute-start(f32[64,512]{1,0:T(8,128)S(1)} %get-tuple-element.47), channel_id=1, source_target_pairs={{0,6},{1,7},{2,4},{3,5},{4,2},{5,3},{6,0},{7,1},{8,14},{9,15},{10,... | collective-permute-start | bytes 393224 | tf_op jit(solution)/shard_map/ppermute | solution.py:215
  53.4 4.0 %collective-permute-start.15 = (f32[64,512]{1,0:T(8,128)S(1)}, f32[64,512]{1,0:T(8,128)S(1)}, u32[]{:S(2)}, u32[]{:S(2)}) collective-permute-start(f32[64,512]{1,0:T(8,128)S(1)} %get-tuple-element.48), channel_id=1, source_target_pairs={{0,4},{1,5},{2,6},{3,7},{4,0},{5,1},{6,2},{7,3},{8,12},{9,13},{10,... | collective-permute-start | bytes 393224 | tf_op jit(solution)/shard_map/ppermute | solution.py:215

commit v10 on v8

--- a/solution.py
+++ b/solution.py
@@ -28,6 +28,11 @@
     return index, index % (CORES * inner_count)
 
 
+def ranked(count, *first):
+    first = [e for e in first if e < count]
+    return [e for e in range(count) if e not in first and e > max(first)] + first
+
+
 def heads_of(heads):
     return [slice(h * HEAD_DIM, (h + 1) * HEAD_DIM) for h in range(heads)]
 
@@ -43,7 +48,7 @@
     return found, after
 
 
-def spread(members, width, queries, keys, values, *refs):
+def spread(members, width, near_order, queries, keys, values, *refs):
     half = members // CORES
     near, cross = refs[:half], refs[half]
     buffers, sems = refs[half + 1 : half + 4], refs[half + 4]
@@ -57,7 +62,7 @@
             for i, source in enumerate(sources)
         ]
 
-    order = list(reversed(range(half))) + list(range(half, members))
+    order = near_order + list(range(half, members))
     for d in order:
         for copy in copies(d):
             copy.start()
@@ -66,23 +71,23 @@
             copy.wait()
             part = buffers[i][d].astype(jnp.float32)
             if d < half:
-                near[half - 1 - d][i] = part
+                near[near_order.index(d)][i] = part
             else:
                 cross[d - half, i] = part
 
 
-def forward(half, swapped, *outs):
-    for e in range(1, half):
-        outs[half - 1 - e][...] = swapped[e, 0:2]
-
-
-def join_queries(members, width, rows, docs, gates, lengths, queries, swapped, *refs):
+def forward(order, swapped, *outs):
+    for n, e in enumerate(order):
+        outs[n][...] = swapped[e, 0:2]
+
+
+def join_queries(members, width, order, rows, docs, gates, lengths, queries, swapped, *refs):
     half = members // CORES
     outs, table = refs[gates:-1], refs[-1]
     index, me = position()
-    for e in range(half):
-        outs[half - 1 - e][0] = queries[:, columns_of(me ^ e, width)].astype(jnp.float32)
-        outs[half - 1 - e][1] = swapped[e, 2]
+    for n, e in enumerate(order):
+        outs[n][0] = queries[:, columns_of(me ^ e, width)].astype(jnp.float32)
+        outs[n][1] = swapped[e, 2]
     base = (index - me) * rows
     for j in range(members + 1):
         found, _ = start_of(lengths, docs, base + j * rows)
@@ -91,9 +96,9 @@
     table[members + 1 : members + 2, :] = jnp.full((1, HEAD_DIM), after - index * rows, jnp.int32)
 
 
-def gather_states(members, heads, rows, table, *refs):
+def gather_states(members, heads, rows, order, table, *refs):
     half = members // CORES
-    parts = refs[:half][::-1] + refs[half:members][::-1]
+    parts = dict(zip(order, refs))
     carry_out, total_out, key_blocks, value_blocks = refs[members + 1 :]
     _, me = position()
     row = lax.broadcasted_iota(jnp.int32, (rows, HEAD_DIM), 0)
@@ -214,37 +219,39 @@
         pairs = [(g, g - g % members + (g % members ^ d)) for g in range(devices)]
         return lax.ppermute(part, everyone, pairs)
 
-    downward = list(reversed(range(half)))
+    near_order = ranked(half, 2, 1, 3, 0)
+    far_order = ranked(half, 3, 2, 1, 0)[:-1]
+    query_order = ranked(half, 3, 2, 1, 0)
     block_bytes = rows * columns * 4
     parts = call(
-        functools.partial(spread, members, width),
+        functools.partial(spread, members, width, near_order),
         "spread",
         [shape(2, rows, width)] * half + [shape(half, 3, rows, width)],
         [HBM, HBM, HBM],
         [VMEM] * (half + 1),
         [pltpu.VMEM((members, rows, width), bf16)] * 3 + [pltpu.SemaphoreType.DMA((3, members))],
     )(*[pltpu.with_memory_space_constraint(x, pltpu.HBM) for x in (queries, keys, values)])
-    near_got = [swap(part, e) if e else part for e, part in zip(downward, parts)]
+    near_got = [swap(part, e) if e else part for e, part in zip(near_order, parts)]
     swapped = swap(parts[half], half)
     far_parts = call(
-        functools.partial(forward, half),
+        functools.partial(forward, far_order),
         "forward",
         [shape(2, rows, width)] * (half - 1),
         [VMEM],
         [VMEM] * (half - 1),
         moved=2 * block_bytes,
     )(swapped)
-    far_got = [swap(part, e) for e, part in zip(downward, far_parts)] + [swapped]
+    far_got = [swap(part, e) for e, part in zip(far_order, far_parts)] + [swapped]
     gates = near_got[:-1]
     *query_parts, table = call(
-        functools.partial(join_queries, members, width, rows, docs, len(gates)),
+        functools.partial(join_queries, members, width, query_order, rows, docs, len(gates)),
         "join_queries",
         [shape(CORES, rows, width)] * half + [shape(members + 2, HEAD_DIM, dtype=jnp.int32)],
         [SMEM, VMEM, VMEM] + [ANY] * len(gates),
         [VMEM] * (half + 1),
         moved=2 * block_bytes,
     )(lengths, queries, swapped, *gates)
-    query_got = [swap(part, e) if e else part for e, part in zip(downward, query_parts)]
+    query_got = [swap(part, e) if e else part for e, part in zip(query_order, query_parts)]
 
     own = call(
         functools.partial(inside, head_count, docs, rows),
@@ -257,7 +264,7 @@
     )(lengths, queries, keys, values)
 
     carry, total = call(
-        functools.partial(gather_states, members, heads, rows),
+        functools.partial(gather_states, members, heads, rows, near_order + [e + half for e in far_order + [0]]),
         "gather_states",
         [shape(members, heads, HEAD_DIM, HEAD_DIM), shape(heads, HEAD_DIM, HEAD_DIM)],
         [VMEM] * (members + 1) + [ANY],
@@ -276,8 +283,8 @@
             moving = lax.ppermute(moving, everyone, up)
             earlier = earlier + jnp.where(opens < base - (k - 1) * members * rows, moving, 0.0)
     crossed_got = {}
-    late = [e for e in downward if e in (0, 1, 2)]
-    soon = [e for e in downward if e not in late]
+    late = [e for e in (2, 1, 0,) if e < half]
+    soon = [e for e in ranked(half, 3) if e not in late]
     gates = []
     for chosen in (soon, late):
         crossed = call(
@@ -288,7 +295,7 @@
             [VMEM] * (CORES * len(chosen)),
             flops=2 * rows * HEAD_DIM * width * CORES * len(chosen),
             moved=2 * block_bytes,
-        )(table, carry, earlier, *[query_got[half - 1 - e] for e in chosen], *gates)
+        )(table, carry, earlier, *[query_got[query_order.index(e)] for e in chosen], *gates)
         for n, e in enumerate(chosen):
             for side in range(CORES):
                 d = e ^ (side * half)
@@ -298,8 +305,10 @@
 
     gain = norm_gain.reshape(1, columns)
     out = None
-    groups = [[0] + [e ^ (side * half) for e in soon for side in range(CORES)]]
-    groups += [[half] + [e ^ (side * half) for e in late if e for side in range(CORES)]]
+    listed = [[(0, 0), (3, 1), (3, 0)], [(0, 1), (1, 0), (2, 0), (1, 1), (2, 1)]]
+    named = [pair for group in listed for pair in group]
+    listed[0] += [(e, side) for e in soon for side in range(CORES) if (e, side) not in named]
+    groups = [[e + side * half for e, side in group] for group in listed]
     for chosen in groups:
         more = [] if out is None else [out]
         out = call(

time: 55.6 us -> 54.8 us (0.986)
  waiting for transfers between devices: 21.3 us -> 19.1 us
  starting transfers between devices: 23.6 us -> 24.9 us
    ppermute x17, starting transfers between devices: 20.1 us -> 21.4 us  [swap(): return lax.ppermute(part, everyone, pairs)]
    ppermute x1, waiting for transfers between devices: 3.36 us -> 2.19 us  [body(): moving = lax.ppermute(total, everyone, up)]
    ppermute x17, waiting for transfers between devices: 17.9 us -> 16.9 us  [swap(): return lax.ppermute(part, everyone, pairs)]
  transfers between devices with their start and end apart: 18 -> 18, of which waited for: 10 -> 13; matrix products, arithmetic and copies ran while one was open for 0% -> 0% of each run, Pallas kernels for 14% -> 14%
where the time goes in v10:
time: 54.8 us; the launch traced here: 54.7 us
  starting transfers between devices  24.9 us (45%)
  waiting for transfers between devices  19.1 us (35%)
  Pallas kernels  10.5 us (19%)
    ppermute x17, starting transfers between devices, swap(): return lax.ppermute(part, everyone, pairs)  21.4 us
    ppermute x17, waiting for transfers between devices, swap(): return lax.ppermute(part, everyone, pairs)  16.9 us
    pallas_call x1, Pallas kernels, body(): call(functools.partial(inside, head_count, docs, rows), 'inside', shape(r...  4.93 us
    ppermute x1, starting transfers between devices, body(): moving = lax.ppermute(total, everyone, up)  3.5 us
    ppermute x1, waiting for transfers between devices, body(): moving = lax.ppermute(total, everyone, up)  2.19 us
    pallas_call x2, Pallas kernels, body(): call(functools.partial(finish, chosen, members, heads, rows), 'finish', s...  1.8 us
    pallas_call x1, Pallas kernels, body(): call(functools.partial(spread, members, width, near_order), 'spread', [sh...  1.67 us
  transfers between devices with their start and end apart: 18, of which 13 were waited for; matrix products, arithmetic and copies ran while one was open for 0% of the time, Pallas kernels for 14%

profile of v10, /device:TPU:0, one launch (start us, length us, event | category | flops | bytes accessed | tf_op | source)
XLA Modules:
  0.0 54.7 jit_solution(1348855947180692358)
XLA Ops:
  0.0 0.0 copy-start
  0.0 0.0 copy-start.2
  0.0 0.0 copy-start.1
  0.0 0.0 copy-start.4
  0.0 1.7 %spread.1 = (f32[2,64,512]{2,1,0:T(8,128)S(1)}, f32[2,64,512]{2,1,0:T(8,128)S(1)}, f32[2,64,512]{2,1,0:T(8,128)S(1)}, f32[2,64,512]{2,1,0:T(8,128)S(1)}, f32[4,3,64,512]{3,2,1,0:T(8,128)S(1)}) custom-call(bf16[64,4096]{1,0:T(8,128)(2,1)} %queries.5, bf16[64,4096]{1,0:T(8,128)(2,1)} %keys.3, bf16[64,4096]{1,0:T(8,128)(2,1)} %values.3), custom_call_target="tpu_custom_call" | custom-call | tf_op jit(solution)/shard_map/spread/pallas_call | solution.py:226
  1.7 0.5 collective-permute-start
  2.2 2.6 %collective-permute-start.1 = (f32[2,64,512]{2,1,0:T(8,128)S(1)}, f32[2,64,512]{2,1,0:T(8,128)S(1)}, u32[]{:S(2)}, u32[]{:S(2)}) collective-permute-start(f32[2,64,512]{2,1,0:T(8,128)S(1)} %get-tuple-element.29), channel_id=1, source_target_pairs={{0,2},{1,3},{2,0},{3,1},{4,6},{5,7},{6,4},{7,5},{8,10},{9,11},{10,... | collective-permute-start | bytes 786440 | tf_op jit(solution)/shard_map/ppermute | solution.py:220
  4.8 1.5 %collective-permute-start.2 = (f32[2,64,512]{2,1,0:T(8,128)S(1)}, f32[2,64,512]{2,1,0:T(8,128)S(1)}, u32[]{:S(2)}, u32[]{:S(2)}) collective-permute-start(f32[2,64,512]{2,1,0:T(8,128)S(1)} %get-tuple-element.30), channel_id=1, source_target_pairs={{0,1},{1,0},{2,3},{3,2},{4,5},{5,4},{6,7},{7,6},{8,9},{9,8},{10,11... | collective-permute-start | bytes 786440 | tf_op jit(solution)/shard_map/ppermute | solution.py:220
  6.3 0.0 collective-permute-start.3
  6.3 0.0 collective-permute-done.swapped.refs_7_
  6.4 0.1 forward.1
  6.4 2.9 %collective-permute-start.4 = (f32[2,64,512]{2,1,0:T(8,128)S(1)}, f32[2,64,512]{2,1,0:T(8,128)S(1)}, u32[]{:S(2)}, u32[]{:S(2)}) collective-permute-start(f32[2,64,512]{2,1,0:T(8,128)S(1)} %get-tuple-element.34), channel_id=1, source_target_pairs={{0,3},{1,2},{2,1},{3,0},{4,7},{5,6},{6,5},{7,4},{8,11},{9,10},{10,... | collective-permute-start | bytes 786440 | tf_op jit(solution)/shard_map/ppermute | solution.py:220
  9.3 0.5 collective-permute-start.5
  9.9 1.9 %collective-permute-done.1.refs_0_ = f32[2,64,512]{2,1,0:T(8,128)S(1)} collective-permute-done((f32[2,64,512]{2,1,0:T(8,128)S(1)}, f32[2,64,512]{2,1,0:T(8,128)S(1)}, u32[]{:S(2)}, u32[]{:S(2)}) %collective-permute-start.1) | collective-permute-done | bytes 262176 | tf_op jit(solution)/shard_map/ppermute | solution.py:220
  11.7 2.2 %collective-permute-start.6 = (f32[2,64,512]{2,1,0:T(8,128)S(1)}, f32[2,64,512]{2,1,0:T(8,128)S(1)}, u32[]{:S(2)}, u32[]{:S(2)}) collective-permute-start(f32[2,64,512]{2,1,0:T(8,128)S(1)} %get-tuple-element.36), channel_id=1, source_target_pairs={{0,1},{1,0},{2,3},{3,2},{4,5},{5,4},{6,7},{7,6},{8,9},{9,8},{10,11... | collective-permute-start | bytes 786440 | tf_op jit(solution)/shard_map/ppermute | solution.py:220
  13.9 0.0 copy-done
  13.9 0.0 copy-done.2
  13.9 0.0 copy-done.1
  13.9 0.0 copy-done.4
  13.9 4.9 %inside.1.refs_8_.own = f32[64,4096]{1,0:T(8,128)S(1)} custom-call(s32[16]{0:T(128)S(1)} %copy-done.4, bf16[64,4096]{1,0:T(8,128)(2,1)S(1)} %copy-done, bf16[64,4096]{1,0:T(8,128)(2,1)S(1)} %copy-done.1, bf16[64,4096]{1,0:T(8,128)(2,1)S(1)} %copy-done.2), custom_call_target="tpu_custom_call" | custom-call | flops 67108864 | bytes 3145728 | tf_op jit(solution)/shard_map/inside/pallas_call | solution.py:256
  18.9 0.0 collective-permute-done.2.refs_1_
  18.9 0.3 collective-permute-done.3.refs_2_
  19.2 0.7 %join_queries.1 = (f32[2,64,512]{2,1,0:T(8,128)S(1)}, f32[2,64,512]{2,1,0:T(8,128)S(1)}, f32[2,64,512]{2,1,0:T(8,128)S(1)}, f32[2,64,512]{2,1,0:T(8,128)S(1)}, s32[10,128]{1,0:T(8,128)S(1)}) custom-call(s32[16]{0:T(128)S(1)} %copy-done.4, bf16[64,4096]{1,0:T(8,128)(2,1)S(1)} %copy-done, f32[4,3,64,512]{3,2,1,0:T(8,128)S(1)} %collective-permute-done.swapped.refs_7_, ...), custom_call_target="tpu_custom_call" | custom-call | bytes 2097152 | tf_op jit(solution)/shard_map/join_queries/pallas_call | solution.py:246
  19.9 3.0 %collective-permute-start.10 = (f32[2,64,512]{2,1,0:T(8,128)S(1)}, f32[2,64,512]{2,1,0:T(8,128)S(1)}, u32[]{:S(2)}, u32[]{:S(2)}) collective-permute-start(f32[2,64,512]{2,1,0:T(8,128)S(1)} %get-tuple-element.42), channel_id=1, source_target_pairs={{0,3},{1,2},{2,1},{3,0},{4,7},{5,6},{6,5},{7,4},{8,11},{9,10},{10,... | collective-permute-start | bytes 786440 | tf_op jit(solution)/shard_map/ppermute | solution.py:220
  22.9 1.8 %collective-permute-done.4.refs_4_ = f32[2,64,512]{2,1,0:T(8,128)S(1)} collective-permute-done((f32[2,64,512]{2,1,0:T(8,128)S(1)}, f32[2,64,512]{2,1,0:T(8,128)S(1)}, u32[]{:S(2)}, u32[]{:S(2)}) %collective-permute-start.4) | collective-permute-done | bytes 262176 | tf_op jit(solution)/shard_map/ppermute | solution.py:220
  24.7 3.8 %collective-permute-done.5.refs_5_ = f32[2,64,512]{2,1,0:T(8,128)S(1)} collective-permute-done((f32[2,64,512]{2,1,0:T(8,128)S(1)}, f32[2,64,512]{2,1,0:T(8,128)S(1)}, u32[]{:S(2)}, u32[]{:S(2)}) %collective-permute-start.5) | collective-permute-done | bytes 262176 | tf_op jit(solution)/shard_map/ppermute | solution.py:220
  28.6 2.3 %collective-permute-done.6.refs_6_ = f32[2,64,512]{2,1,0:T(8,128)S(1)} collective-permute-done((f32[2,64,512]{2,1,0:T(8,128)S(1)}, f32[2,64,512]{2,1,0:T(8,128)S(1)}, u32[]{:S(2)}, u32[]{:S(2)}) %collective-permute-start.6) | collective-permute-done | bytes 262176 | tf_op jit(solution)/shard_map/ppermute | solution.py:220
  30.9 0.6 %gather_states.1 = (f32[8,4,128,128]{3,2,1,0:T(8,128)S(1)}, f32[4,128,128]{2,1,0:T(8,128)S(1)}) custom-call(s32[10,128]{1,0:T(8,128)S(1)} %get-tuple-element.32.table, f32[2,64,512]{2,1,0:T(8,128)S(1)} %collective-permute-done.1.refs_0_, f32[2,64,512]{2,1,0:T(8,128)S(1)} %collective-permute-done.2.refs_1_, f32[2,64,512]{2,1,0:T(8,128)S(1)} %collective-permute-done.3.refs_2_, ...), custom_call_target="tpu_custom_call" | custom-call | flops 67108864 | bytes 4194304 | tf_op jit(solution)/shard_map/gather_states/pallas_call | solution.py:266
  31.5 3.5 %collective-permute-start.7 = (f32[4,128,128]{2,1,0:T(8,128)S(1)}, f32[4,128,128]{2,1,0:T(8,128)S(1)}, u32[]{:S(2)}, u32[]{:S(2)}) collective-permute-start(f32[4,128,128]{2,1,0:T(8,128)S(1)} %get-tuple-element.38), channel_id=1, source_target_pairs={{0,8},{1,9},{2,10},{3,11},{4,12},{5,13},{6,14},{7,15},{8,16},{9,17... | collective-permute-start | bytes 786440 | tf_op jit(solution)/shard_map/ppermute | solution.py:277
  35.0 0.6 %collective-permute-start.8 = (f32[2,64,512]{2,1,0:T(8,128)S(1)}, f32[2,64,512]{2,1,0:T(8,128)S(1)}, u32[]{:S(2)}, u32[]{:S(2)}) collective-permute-start(f32[2,64,512]{2,1,0:T(8,128)S(1)} %get-tuple-element.39), channel_id=1, source_target_pairs={{0,2},{1,3},{2,0},{3,1},{4,6},{5,7},{6,4},{7,5},{8,10},{9,11},{10,... | collective-permute-start | bytes 786440 | tf_op jit(solution)/shard_map/ppermute | solution.py:220
  35.5 1.5 %collective-permute-start.9 = (f32[2,64,512]{2,1,0:T(8,128)S(1)}, f32[2,64,512]{2,1,0:T(8,128)S(1)}, u32[]{:S(2)}, u32[]{:S(2)}) collective-permute-start(f32[2,64,512]{2,1,0:T(8,128)S(1)} %get-tuple-element.40), channel_id=1, source_target_pairs={{0,1},{1,0},{2,3},{3,2},{4,5},{5,4},{6,7},{7,6},{8,9},{9,8},{10,11... | collective-permute-start | bytes 786440 | tf_op jit(solution)/shard_map/ppermute | solution.py:220
  37.0 0.0 collective-permute-done.10.refs_0_
  37.0 2.2 %collective-permute-done.7.earlier = f32[4,128,128]{2,1,0:T(8,128)S(1)} collective-permute-done((f32[4,128,128]{2,1,0:T(8,128)S(1)}, f32[4,128,128]{2,1,0:T(8,128)S(1)}, u32[]{:S(2)}, u32[]{:S(2)}) %collective-permute-start.7) | collective-permute-done | bytes 262176 | tf_op jit(solution)/shard_map/ppermute | solution.py:277
  39.2 0.2 reach_back.2
  39.5 0.1 collective-permute-start.16
  39.5 1.6 %collective-permute-start.17 = (f32[64,512]{1,0:T(8,128)S(1)}, f32[64,512]{1,0:T(8,128)S(1)}, u32[]{:S(2)}, u32[]{:S(2)}) collective-permute-start(f32[64,512]{1,0:T(8,128)S(1)} %get-tuple-element.43.refs_3_), channel_id=1, source_target_pairs={{0,3},{1,2},{2,1},{3,0},{4,7},{5,6},{6,5},{7,4},{8,11},{9,10},{10,... | collective-permute-start | bytes 393224 | tf_op jit(solution)/shard_map/ppermute | solution.py:220
  41.1 0.4 collective-permute-done.8.refs_0_
  41.5 0.4 collective-permute-done.9.refs_1_
  41.9 0.0 copy-start.3
  41.9 0.5 reach_back.3
  42.4 0.4 collective-permute-start.11
  42.8 1.5 %collective-permute-start.12 = (f32[64,512]{1,0:T(8,128)S(1)}, f32[64,512]{1,0:T(8,128)S(1)}, u32[]{:S(2)}, u32[]{:S(2)}) collective-permute-start(f32[64,512]{1,0:T(8,128)S(1)} %get-tuple-element.45), channel_id=1, source_target_pairs={{0,1},{1,0},{2,3},{3,2},{4,5},{5,4},{6,7},{7,6},{8,9},{9,8},{10,11... | collective-permute-start | bytes 393224 | tf_op jit(solution)/shard_map/ppermute | solution.py:220
  44.3 1.2 %collective-permute-start.13 = (f32[64,512]{1,0:T(8,128)S(1)}, f32[64,512]{1,0:T(8,128)S(1)}, u32[]{:S(2)}, u32[]{:S(2)}) collective-permute-start(f32[64,512]{1,0:T(8,128)S(1)} %get-tuple-element.46), channel_id=1, source_target_pairs={{0,2},{1,3},{2,0},{3,1},{4,6},{5,7},{6,4},{7,5},{8,10},{9,11},{10,... | collective-permute-start | bytes 393224 | tf_op jit(solution)/shard_map/ppermute | solution.py:220
  45.5 0.7 %collective-permute-done.16.refs_1_ = f32[64,512]{1,0:T(8,128)S(1)} collective-permute-done((f32[64,512]{1,0:T(8,128)S(1)}, f32[64,512]{1,0:T(8,128)S(1)}, u32[]{:S(2)}, u32[]{:S(2)}) %collective-permute-start.16) | collective-permute-done | bytes 131104 | tf_op jit(solution)/shard_map/ppermute | solution.py:220
  46.3 0.0 collective-permute-start.14
  46.3 1.7 %collective-permute-done.17.refs_2_ = f32[64,512]{1,0:T(8,128)S(1)} collective-permute-done((f32[64,512]{1,0:T(8,128)S(1)}, f32[64,512]{1,0:T(8,128)S(1)}, u32[]{:S(2)}, u32[]{:S(2)}) %collective-permute-start.17) | collective-permute-done | bytes 131104 | tf_op jit(solution)/shard_map/ppermute | solution.py:220
  48.0 1.3 %collective-permute-start.15 = (f32[64,512]{1,0:T(8,128)S(1)}, f32[64,512]{1,0:T(8,128)S(1)}, u32[]{:S(2)}, u32[]{:S(2)}) collective-permute-start(f32[64,512]{1,0:T(8,128)S(1)} %get-tuple-element.48), channel_id=1, source_target_pairs={{0,6},{1,7},{2,4},{3,5},{4,2},{5,3},{6,0},{7,1},{8,14},{9,15},{10,... | collective-permute-start | bytes 393224 | tf_op jit(solution)/shard_map/ppermute | solution.py:220
  49.3 0.0 copy-done.3
  49.3 0.9 %finish.2.refs_5_ = bf16[64,4096]{1,0:T(8,128)(2,1)} custom-call(s32[10,128]{1,0:T(8,128)S(1)} %get-tuple-element.32.table, f32[64,4096]{1,0:T(8,128)S(1)} %inside.1.refs_8_.own, f32[1,4096]{1,0:T(1,128)S(1)} %bitcast.1, f32[64,512]{1,0:T(8,128)S(1)} %get-tuple-element.49.refs_0_, f32[64,512]{1,0:T(8,128)S(1)} %collective-permute-done.16.refs_1_, ...), custom_call_target="tpu_custom_call" | custom-call | bytes 2097152 | tf_op jit(solution)/shard_map/finish/pallas_call | solution.py:314
  50.1 0.0 collective-permute-done.11.refs_0_
  50.2 0.8 %collective-permute-done.12.refs_1_ = f32[64,512]{1,0:T(8,128)S(1)} collective-permute-done((f32[64,512]{1,0:T(8,128)S(1)}, f32[64,512]{1,0:T(8,128)S(1)}, u32[]{:S(2)}, u32[]{:S(2)}) %collective-permute-start.12) | collective-permute-done | bytes 131104 | tf_op jit(solution)/shard_map/ppermute | solution.py:220
  51.0 0.4 collective-permute-done.13.refs_2_
  51.4 2.3 %collective-permute-done.14.refs_3_ = f32[64,512]{1,0:T(8,128)S(1)} collective-permute-done((f32[64,512]{1,0:T(8,128)S(1)}, f32[64,512]{1,0:T(8,128)S(1)}, u32[]{:S(2)}, u32[]{:S(2)}) %collective-permute-start.14) | collective-permute-done | bytes 131104 | tf_op jit(solution)/shard_map/ppermute | solution.py:220
  53.7 0.0 collective-permute-done.15.refs_4_
  53.7 0.9 %finish.3 = bf16[64,4096]{1,0:T(8,128)(2,1)} custom-call(s32[10,128]{1,0:T(8,128)S(1)} %get-tuple-element.32.table, f32[64,4096]{1,0:T(8,128)S(1)} %inside.1.refs_8_.own, f32[1,4096]{1,0:T(1,128)S(1)} %bitcast.2, f32[64,512]{1,0:T(8,128)S(1)} %collective-permute-done.11.refs_0_, ...), custom_call_target="tpu_custom_call", output_to_operand_aliasing={{}: (8, {})} | custom-call | bytes 2097152 | tf_op jit(solution)/shard_map/finish/pallas_call | solution.py:314
Async XLA Ops:
  0.0 13.9 %copy-start = (bf16[64,4096]{1,0:T(8,128)(2,1)S(1)}, bf16[64,4096]{1,0:T(8,128)(2,1)}, u32[]{:S(2)}) copy-start(bf16[64,4096]{1,0:T(8,128)(2,1)} %queries.5) | copy-start | bytes 1572868
  0.0 13.9 %copy-start.2 = (bf16[64,4096]{1,0:T(8,128)(2,1)S(1)}, bf16[64,4096]{1,0:T(8,128)(2,1)}, u32[]{:S(2)}) copy-start(bf16[64,4096]{1,0:T(8,128)(2,1)} %values.3) | copy-start | bytes 1572868
  0.0 13.9 %copy-start.1 = (bf16[64,4096]{1,0:T(8,128)(2,1)S(1)}, bf16[64,4096]{1,0:T(8,128)(2,1)}, u32[]{:S(2)}) copy-start(bf16[64,4096]{1,0:T(8,128)(2,1)} %keys.3) | copy-start | bytes 1572868
  0.0 13.9 %copy-start.4 = (s32[16]{0:T(128)S(1)}, s32[16]{0:T(128)}, u32[]{:S(2)}) copy-start(s32[16]{0:T(128)} %lengths.3) | copy-start | bytes 196
  1.7 4.7 %collective-permute-start = (f32[4,3,64,512]{3,2,1,0:T(8,128)S(1)}, f32[4,3,64,512]{3,2,1,0:T(8,128)S(1)}, u32[]{:S(2)}, u32[]{:S(2)}) collective-permute-start(f32[4,3,64,512]{3,2,1,0:T(8,128)S(1)} %get-tuple-element.28), channel_id=1, source_target_pairs={{0,4},{1,5},{2,6},{3,7},{4,0},{5,1},{6,2},{7,3},{8,12},{9,13},{10,... | collective-permute-start | bytes 4718600 | tf_op jit(solution)/shard_map/ppermute | solution.py:220
  2.2 9.5 %collective-permute-start.1 = (f32[2,64,512]{2,1,0:T(8,128)S(1)}, f32[2,64,512]{2,1,0:T(8,128)S(1)}, u32[]{:S(2)}, u32[]{:S(2)}) collective-permute-start(f32[2,64,512]{2,1,0:T(8,128)S(1)} %get-tuple-element.29), channel_id=1, source_target_pairs={{0,2},{1,3},{2,0},{3,1},{4,6},{5,7},{6,4},{7,5},{8,10},{9,11},{10,... | collective-permute-start | bytes 786440 | tf_op jit(solution)/shard_map/ppermute | solution.py:220
  4.8 14.1 %collective-permute-start.2 = (f32[2,64,512]{2,1,0:T(8,128)S(1)}, f32[2,64,512]{2,1,0:T(8,128)S(1)}, u32[]{:S(2)}, u32[]{:S(2)}) collective-permute-start(f32[2,64,512]{2,1,0:T(8,128)S(1)} %get-tuple-element.30), channel_id=1, source_target_pairs={{0,1},{1,0},{2,3},{3,2},{4,5},{5,4},{6,7},{7,6},{8,9},{9,8},{10,11... | collective-permute-start | bytes 786440 | tf_op jit(solution)/shard_map/ppermute | solution.py:220
  6.3 12.9 %collective-permute-start.3 = (f32[2,64,512]{2,1,0:T(8,128)S(1)}, f32[2,64,512]{2,1,0:T(8,128)S(1)}, u32[]{:S(2)}, u32[]{:S(2)}) collective-permute-start(f32[2,64,512]{2,1,0:T(8,128)S(1)} %get-tuple-element.31), channel_id=1, source_target_pairs={{0,3},{1,2},{2,1},{3,0},{4,7},{5,6},{6,5},{7,4},{8,11},{9,10},{10,... | collective-permute-start | bytes 786440 | tf_op jit(solution)/shard_map/ppermute | solution.py:220
  6.4 18.3 %collective-permute-start.4 = (f32[2,64,512]{2,1,0:T(8,128)S(1)}, f32[2,64,512]{2,1,0:T(8,128)S(1)}, u32[]{:S(2)}, u32[]{:S(2)}) collective-permute-start(f32[2,64,512]{2,1,0:T(8,128)S(1)} %get-tuple-element.34), channel_id=1, source_target_pairs={{0,3},{1,2},{2,1},{3,0},{4,7},{5,6},{6,5},{7,4},{8,11},{9,10},{10,... | collective-permute-start | bytes 786440 | tf_op jit(solution)/shard_map/ppermute | solution.py:220
  9.3 19.2 %collective-permute-start.5 = (f32[2,64,512]{2,1,0:T(8,128)S(1)}, f32[2,64,512]{2,1,0:T(8,128)S(1)}, u32[]{:S(2)}, u32[]{:S(2)}) collective-permute-start(f32[2,64,512]{2,1,0:T(8,128)S(1)} %get-tuple-element.35), channel_id=1, source_target_pairs={{0,2},{1,3},{2,0},{3,1},{4,6},{5,7},{6,4},{7,5},{8,10},{9,11},{10,... | collective-permute-start | bytes 786440 | tf_op jit(solution)/shard_map/ppermute | solution.py:220
  11.7 19.1 %collective-permute-start.6 = (f32[2,64,512]{2,1,0:T(8,128)S(1)}, f32[2,64,512]{2,1,0:T(8,128)S(1)}, u32[]{:S(2)}, u32[]{:S(2)}) collective-permute-start(f32[2,64,512]{2,1,0:T(8,128)S(1)} %get-tuple-element.36), channel_id=1, source_target_pairs={{0,1},{1,0},{2,3},{3,2},{4,5},{5,4},{6,7},{7,6},{8,9},{9,8},{10,11... | collective-permute-start | bytes 786440 | tf_op jit(solution)/shard_map/ppermute | solution.py:220
  19.9 17.1 %collective-permute-start.10 = (f32[2,64,512]{2,1,0:T(8,128)S(1)}, f32[2,64,512]{2,1,0:T(8,128)S(1)}, u32[]{:S(2)}, u32[]{:S(2)}) collective-permute-start(f32[2,64,512]{2,1,0:T(8,128)S(1)} %get-tuple-element.42), channel_id=1, source_target_pairs={{0,3},{1,2},{2,1},{3,0},{4,7},{5,6},{6,5},{7,4},{8,11},{9,10},{10,... | collective-permute-start | bytes 786440 | tf_op jit(solution)/shard_map/ppermute | solution.py:220
  31.5 7.8 %collective-permute-start.7 = (f32[4,128,128]{2,1,0:T(8,128)S(1)}, f32[4,128,128]{2,1,0:T(8,128)S(1)}, u32[]{:S(2)}, u32[]{:S(2)}) collective-permute-start(f32[4,128,128]{2,1,0:T(8,128)S(1)} %get-tuple-element.38), channel_id=1, source_target_pairs={{0,8},{1,9},{2,10},{3,11},{4,12},{5,13},{6,14},{7,15},{8,16},{9,17... | collective-permute-start | bytes 786440 | tf_op jit(solution)/shard_map/ppermute | solution.py:277
  35.0 6.6 %collective-permute-start.8 = (f32[2,64,512]{2,1,0:T(8,128)S(1)}, f32[2,64,512]{2,1,0:T(8,128)S(1)}, u32[]{:S(2)}, u32[]{:S(2)}) collective-permute-start(f32[2,64,512]{2,1,0:T(8,128)S(1)} %get-tuple-element.39), channel_id=1, source_target_pairs={{0,2},{1,3},{2,0},{3,1},{4,6},{5,7},{6,4},{7,5},{8,10},{9,11},{10,... | collective-permute-start | bytes 786440 | tf_op jit(solution)/shard_map/ppermute | solution.py:220
  35.5 6.4 %collective-permute-start.9 = (f32[2,64,512]{2,1,0:T(8,128)S(1)}, f32[2,64,512]{2,1,0:T(8,128)S(1)}, u32[]{:S(2)}, u32[]{:S(2)}) collective-permute-start(f32[2,64,512]{2,1,0:T(8,128)S(1)} %get-tuple-element.40), channel_id=1, source_target_pairs={{0,1},{1,0},{2,3},{3,2},{4,5},{5,4},{6,7},{7,6},{8,9},{9,8},{10,11... | collective-permute-start | bytes 786440 | tf_op jit(solution)/shard_map/ppermute | solution.py:220
  39.5 6.8 %collective-permute-start.16 = (f32[64,512]{1,0:T(8,128)S(1)}, f32[64,512]{1,0:T(8,128)S(1)}, u32[]{:S(2)}, u32[]{:S(2)}) collective-permute-start(f32[64,512]{1,0:T(8,128)S(1)} %get-tuple-element.50), channel_id=1, source_target_pairs={{0,7},{1,6},{2,5},{3,4},{4,3},{5,2},{6,1},{7,0},{8,15},{9,14},{10,... | collective-permute-start | bytes 393224 | tf_op jit(solution)/shard_map/ppermute | solution.py:220
  39.5 8.4 %collective-permute-start.17 = (f32[64,512]{1,0:T(8,128)S(1)}, f32[64,512]{1,0:T(8,128)S(1)}, u32[]{:S(2)}, u32[]{:S(2)}) collective-permute-start(f32[64,512]{1,0:T(8,128)S(1)} %get-tuple-element.43.refs_3_), channel_id=1, source_target_pairs={{0,3},{1,2},{2,1},{3,0},{4,7},{5,6},{6,5},{7,4},{8,11},{9,10},{10,... | collective-permute-start | bytes 393224 | tf_op jit(solution)/shard_map/ppermute | solution.py:220
  41.9 7.4 %copy-start.3 = (f32[4096]{0:T(1024)S(1)}, f32[4096]{0:T(1024)}, u32[]{:S(2)}) copy-start(f32[4096]{0:T(1024)} %param.9) | copy-start | bytes 49156
  42.4 7.8 %collective-permute-start.11 = (f32[64,512]{1,0:T(8,128)S(1)}, f32[64,512]{1,0:T(8,128)S(1)}, u32[]{:S(2)}, u32[]{:S(2)}) collective-permute-start(f32[64,512]{1,0:T(8,128)S(1)} %get-tuple-element.44), channel_id=1, source_target_pairs={{0,4},{1,5},{2,6},{3,7},{4,0},{5,1},{6,2},{7,3},{8,12},{9,13},{10,... | collective-permute-start | bytes 393224 | tf_op jit(solution)/shard_map/ppermute | solution.py:220
  42.8 8.2 %collective-permute-start.12 = (f32[64,512]{1,0:T(8,128)S(1)}, f32[64,512]{1,0:T(8,128)S(1)}, u32[]{:S(2)}, u32[]{:S(2)}) collective-permute-start(f32[64,512]{1,0:T(8,128)S(1)} %get-tuple-element.45), channel_id=1, source_target_pairs={{0,1},{1,0},{2,3},{3,2},{4,5},{5,4},{6,7},{7,6},{8,9},{9,8},{10,11... | collective-permute-start | bytes 393224 | tf_op jit(solution)/shard_map/ppermute | solution.py:220
  44.3 7.1 %collective-permute-start.13 = (f32[64,512]{1,0:T(8,128)S(1)}, f32[64,512]{1,0:T(8,128)S(1)}, u32[]{:S(2)}, u32[]{:S(2)}) collective-permute-start(f32[64,512]{1,0:T(8,128)S(1)} %get-tuple-element.46), channel_id=1, source_target_pairs={{0,2},{1,3},{2,0},{3,1},{4,6},{5,7},{6,4},{7,5},{8,10},{9,11},{10,... | collective-permute-start | bytes 393224 | tf_op jit(solution)/shard_map/ppermute | solution.py:220
  46.3 7.4 %collective-permute-start.14 = (f32[64,512]{1,0:T(8,128)S(1)}, f32[64,512]{1,0:T(8,128)S(1)}, u32[]{:S(2)}, u32[]{:S(2)}) collective-permute-start(f32[64,512]{1,0:T(8,128)S(1)} %get-tuple-element.47), channel_id=1, source_target_pairs={{0,5},{1,4},{2,7},{3,6},{4,1},{5,0},{6,3},{7,2},{8,13},{9,12},{10,... | collective-permute-start | bytes 393224 | tf_op jit(solution)/shard_map/ppermute | solution.py:220
  48.0 5.7 %collective-permute-start.15 = (f32[64,512]{1,0:T(8,128)S(1)}, f32[64,512]{1,0:T(8,128)S(1)}, u32[]{:S(2)}, u32[]{:S(2)}) collective-permute-start(f32[64,512]{1,0:T(8,128)S(1)} %get-tuple-element.48), channel_id=1, source_target_pairs={{0,6},{1,7},{2,4},{3,5},{4,2},{5,3},{6,0},{7,1},{8,14},{9,15},{10,... | collective-permute-start | bytes 393224 | tf_op jit(solution)/shard_map/ppermute | solution.py:220

commit v11 on v10

--- a/solution.py
+++ b/solution.py
@@ -51,29 +51,27 @@
 def spread(members, width, near_order, queries, keys, values, *refs):
     half = members // CORES
     near, cross = refs[:half], refs[half]
-    buffers, sems = refs[half + 1 : half + 4], refs[half + 4]
+    near_buffer, cross_buffer, sems = refs[half + 1 :]
     _, me = position()
-
-    def copies(d):
-        span = columns_of(me ^ d, width)
-        sources = (keys, values) if d < half else (keys, values, queries)
-        return [
-            pltpu.make_async_copy(source.at[:, span], buffers[i].at[d], sems.at[i, d])
-            for i, source in enumerate(sources)
-        ]
-
-    order = near_order + list(range(half, members))
-    for d in order:
-        for copy in copies(d):
-            copy.start()
-    for d in order:
-        for i, copy in enumerate(copies(d)):
-            copy.wait()
-            part = buffers[i][d].astype(jnp.float32)
-            if d < half:
-                near[near_order.index(d)][i] = part
-            else:
-                cross[d - half, i] = part
+    side = me // half
+    near_copies = [
+        pltpu.make_async_copy(source.at[:, columns_of(side, half * width)], near_buffer.at[i], sems.at[0, i])
+        for i, source in enumerate((keys, values))
+    ]
+    cross_copies = [
+        pltpu.make_async_copy(source.at[:, columns_of(1 - side, half * width)], cross_buffer.at[i], sems.at[1, i])
+        for i, source in enumerate((keys, values, queries))
+    ]
+    for copy in near_copies + cross_copies:
+        copy.start()
+    for i, copy in enumerate(near_copies):
+        copy.wait()
+        for n, d in enumerate(near_order):
+            near[n][i] = near_buffer[i, :, columns_of((me ^ d) % half, width)].astype(jnp.float32)
+    for i, copy in enumerate(cross_copies):
+        copy.wait()
+        for e in range(half):
+            cross[e, i] = cross_buffer[i, :, columns_of((me ^ e) % half, width)].astype(jnp.float32)
 
 
 def forward(order, swapped, *outs):
@@ -155,7 +153,7 @@
             for h, span in enumerate(heads_of(heads)):
                 held = (carry[j, h] + before * earlier[h]).astype(jnp.bfloat16)
                 query = query_parts[n][side, :, span].astype(jnp.bfloat16)
-                outs[n * CORES + side][:, span] = jnp.dot(query, held, preferred_element_type=jnp.float32)
+                outs[n * CORES + 1 - side][:, span] = jnp.dot(query, held, preferred_element_type=jnp.float32)
 
 
 def finish(chosen, members, heads, rows, table, own, gain, *refs):
@@ -229,7 +227,11 @@
         [shape(2, rows, width)] * half + [shape(half, 3, rows, width)],
         [HBM, HBM, HBM],
         [VMEM] * (half + 1),
-        [pltpu.VMEM((members, rows, width), bf16)] * 3 + [pltpu.SemaphoreType.DMA((3, members))],
+        [
+            pltpu.VMEM((2, rows, half * width), bf16),
+            pltpu.VMEM((3, rows, half * width), bf16),
+            pltpu.SemaphoreType.DMA((CORES, 3)),
+        ],
     )(*[pltpu.with_memory_space_constraint(x, pltpu.HBM) for x in (queries, keys, values)])
     near_got = [swap(part, e) if e else part for e, part in zip(near_order, parts)]
     swapped = swap(parts[half], half)
@@ -283,7 +285,7 @@
             moving = lax.ppermute(moving, everyone, up)
             earlier = earlier + jnp.where(opens < base - (k - 1) * members * rows, moving, 0.0)
     crossed_got = {}
-    late = [e for e in (2, 1, 0,) if e < half]
+    late = [e for e in (2, 0, 1,) if e < half]
     soon = [e for e in ranked(half, 3) if e not in late]
     gates = []
     for chosen in (soon, late):
@@ -297,9 +299,9 @@
             moved=2 * block_bytes,
         )(table, carry, earlier, *[query_got[query_order.index(e)] for e in chosen], *gates)
         for n, e in enumerate(chosen):
-            for side in range(CORES):
+            for side in reversed(range(CORES)):
                 d = e ^ (side * half)
-                part = crossed[n * CORES + side]
+                part = crossed[n * CORES + 1 - side]
                 crossed_got[d] = swap(part, d) if d else part
         gates = crossed[:1]
 

time: 54.8 us -> 54.5 us (level)
  transfers between devices with their start and end apart: 18 -> 18, of which waited for: 13 -> 13; matrix products, arithmetic and copies ran while one was open for 0% -> 0% of each run, Pallas kernels for 14% -> 15%
where the time goes in v11:
time: 54.5 us; the launch traced here: 54.4 us
  starting transfers between devices  24.5 us (45%)
  waiting for transfers between devices  19.4 us (36%)
  Pallas kernels  10.3 us (19%)
    ppermute x17, starting transfers between devices, swap(): return lax.ppermute(part, everyone, pairs)  21 us
    ppermute x17, waiting for transfers between devices, swap(): return lax.ppermute(part, everyone, pairs)  17.2 us
    pallas_call x1, Pallas kernels, body(): call(functools.partial(inside, head_count, docs, rows), 'inside', shape(r...  4.93 us
    ppermute x1, starting transfers between devices, body(): moving = lax.ppermute(total, everyone, up)  3.5 us
    ppermute x1, waiting for transfers between devices, body(): moving = lax.ppermute(total, everyone, up)  2.19 us
    pallas_call x2, Pallas kernels, body(): call(functools.partial(finish, chosen, members, heads, rows), 'finish', s...  1.8 us
    pallas_call x1, Pallas kernels, body(): call(functools.partial(spread, members, width, near_order), 'spread', [sh...  1.48 us
  transfers between devices with their start and end apart: 18, of which 13 were waited for; matrix products, arithmetic and copies ran while one was open for 0% of the time, Pallas kernels for 15%

profile of v11, /device:TPU:0, one launch (start us, length us, event | category | flops | bytes accessed | tf_op | source)
XLA Modules:
  0.0 54.4 jit_solution(2079307140392329770)
XLA Ops:
  0.0 0.0 copy-start
  0.0 0.0 copy-start.2
  0.0 0.0 copy-start.1
  0.0 0.0 copy-start.4
  0.0 1.5 %spread.1 = (f32[2,64,512]{2,1,0:T(8,128)S(1)}, f32[2,64,512]{2,1,0:T(8,128)S(1)}, f32[2,64,512]{2,1,0:T(8,128)S(1)}, f32[2,64,512]{2,1,0:T(8,128)S(1)}, f32[4,3,64,512]{3,2,1,0:T(8,128)S(1)}) custom-call(bf16[64,4096]{1,0:T(8,128)(2,1)} %queries.5, bf16[64,4096]{1,0:T(8,128)(2,1)} %keys.3, bf16[64,4096]{1,0:T(8,128)(2,1)} %values.3), custom_call_target="tpu_custom_call" | custom-call | tf_op jit(solution)/shard_map/spread/pallas_call | solution.py:224
  1.5 0.5 collective-permute-start
  2.0 2.6 %collective-permute-start.1 = (f32[2,64,512]{2,1,0:T(8,128)S(1)}, f32[2,64,512]{2,1,0:T(8,128)S(1)}, u32[]{:S(2)}, u32[]{:S(2)}) collective-permute-start(f32[2,64,512]{2,1,0:T(8,128)S(1)} %get-tuple-element.29), channel_id=1, source_target_pairs={{0,2},{1,3},{2,0},{3,1},{4,6},{5,7},{6,4},{7,5},{8,10},{9,11},{10,... | collective-permute-start | bytes 786440 | tf_op jit(solution)/shard_map/ppermute | solution.py:218
  4.6 1.5 %collective-permute-start.2 = (f32[2,64,512]{2,1,0:T(8,128)S(1)}, f32[2,64,512]{2,1,0:T(8,128)S(1)}, u32[]{:S(2)}, u32[]{:S(2)}) collective-permute-start(f32[2,64,512]{2,1,0:T(8,128)S(1)} %get-tuple-element.30), channel_id=1, source_target_pairs={{0,1},{1,0},{2,3},{3,2},{4,5},{5,4},{6,7},{7,6},{8,9},{9,8},{10,11... | collective-permute-start | bytes 786440 | tf_op jit(solution)/shard_map/ppermute | solution.py:218
  6.1 0.0 collective-permute-start.3
  6.2 0.0 collective-permute-done.swapped.refs_7_
  6.2 0.1 forward.1
  6.2 2.9 %collective-permute-start.4 = (f32[2,64,512]{2,1,0:T(8,128)S(1)}, f32[2,64,512]{2,1,0:T(8,128)S(1)}, u32[]{:S(2)}, u32[]{:S(2)}) collective-permute-start(f32[2,64,512]{2,1,0:T(8,128)S(1)} %get-tuple-element.34), channel_id=1, source_target_pairs={{0,3},{1,2},{2,1},{3,0},{4,7},{5,6},{6,5},{7,4},{8,11},{9,10},{10,... | collective-permute-start | bytes 786440 | tf_op jit(solution)/shard_map/ppermute | solution.py:218
  9.2 0.5 collective-permute-start.5
  9.7 1.9 %collective-permute-done.1.refs_0_ = f32[2,64,512]{2,1,0:T(8,128)S(1)} collective-permute-done((f32[2,64,512]{2,1,0:T(8,128)S(1)}, f32[2,64,512]{2,1,0:T(8,128)S(1)}, u32[]{:S(2)}, u32[]{:S(2)}) %collective-permute-start.1) | collective-permute-done | bytes 262176 | tf_op jit(solution)/shard_map/ppermute | solution.py:218
  11.5 2.2 %collective-permute-start.6 = (f32[2,64,512]{2,1,0:T(8,128)S(1)}, f32[2,64,512]{2,1,0:T(8,128)S(1)}, u32[]{:S(2)}, u32[]{:S(2)}) collective-permute-start(f32[2,64,512]{2,1,0:T(8,128)S(1)} %get-tuple-element.36), channel_id=1, source_target_pairs={{0,1},{1,0},{2,3},{3,2},{4,5},{5,4},{6,7},{7,6},{8,9},{9,8},{10,11... | collective-permute-start | bytes 786440 | tf_op jit(solution)/shard_map/ppermute | solution.py:218
  13.7 0.0 copy-done
  13.7 0.0 copy-done.2
  13.7 0.0 copy-done.1
  13.8 0.0 copy-done.4
  13.8 4.9 %inside.1.refs_8_.own = f32[64,4096]{1,0:T(8,128)S(1)} custom-call(s32[16]{0:T(128)S(1)} %copy-done.4, bf16[64,4096]{1,0:T(8,128)(2,1)S(1)} %copy-done, bf16[64,4096]{1,0:T(8,128)(2,1)S(1)} %copy-done.1, bf16[64,4096]{1,0:T(8,128)(2,1)S(1)} %copy-done.2), custom_call_target="tpu_custom_call" | custom-call | flops 67108864 | bytes 3145728 | tf_op jit(solution)/shard_map/inside/pallas_call | solution.py:258
  18.7 0.0 collective-permute-done.2.refs_1_
  18.7 0.3 collective-permute-done.3.refs_2_
  19.0 0.7 %join_queries.1 = (f32[2,64,512]{2,1,0:T(8,128)S(1)}, f32[2,64,512]{2,1,0:T(8,128)S(1)}, f32[2,64,512]{2,1,0:T(8,128)S(1)}, f32[2,64,512]{2,1,0:T(8,128)S(1)}, s32[10,128]{1,0:T(8,128)S(1)}) custom-call(s32[16]{0:T(128)S(1)} %copy-done.4, bf16[64,4096]{1,0:T(8,128)(2,1)S(1)} %copy-done, f32[4,3,64,512]{3,2,1,0:T(8,128)S(1)} %collective-permute-done.swapped.refs_7_, ...), custom_call_target="tpu_custom_call" | custom-call | bytes 2097152 | tf_op jit(solution)/shard_map/join_queries/pallas_call | solution.py:248
  19.7 3.0 %collective-permute-start.10 = (f32[2,64,512]{2,1,0:T(8,128)S(1)}, f32[2,64,512]{2,1,0:T(8,128)S(1)}, u32[]{:S(2)}, u32[]{:S(2)}) collective-permute-start(f32[2,64,512]{2,1,0:T(8,128)S(1)} %get-tuple-element.42), channel_id=1, source_target_pairs={{0,3},{1,2},{2,1},{3,0},{4,7},{5,6},{6,5},{7,4},{8,11},{9,10},{10,... | collective-permute-start | bytes 786440 | tf_op jit(solution)/shard_map/ppermute | solution.py:218
  22.7 1.8 %collective-permute-done.4.refs_4_ = f32[2,64,512]{2,1,0:T(8,128)S(1)} collective-permute-done((f32[2,64,512]{2,1,0:T(8,128)S(1)}, f32[2,64,512]{2,1,0:T(8,128)S(1)}, u32[]{:S(2)}, u32[]{:S(2)}) %collective-permute-start.4) | collective-permute-done | bytes 262176 | tf_op jit(solution)/shard_map/ppermute | solution.py:218
  24.5 3.8 %collective-permute-done.5.refs_5_ = f32[2,64,512]{2,1,0:T(8,128)S(1)} collective-permute-done((f32[2,64,512]{2,1,0:T(8,128)S(1)}, f32[2,64,512]{2,1,0:T(8,128)S(1)}, u32[]{:S(2)}, u32[]{:S(2)}) %collective-permute-start.5) | collective-permute-done | bytes 262176 | tf_op jit(solution)/shard_map/ppermute | solution.py:218
  28.4 2.3 %collective-permute-done.6.refs_6_ = f32[2,64,512]{2,1,0:T(8,128)S(1)} collective-permute-done((f32[2,64,512]{2,1,0:T(8,128)S(1)}, f32[2,64,512]{2,1,0:T(8,128)S(1)}, u32[]{:S(2)}, u32[]{:S(2)}) %collective-permute-start.6) | collective-permute-done | bytes 262176 | tf_op jit(solution)/shard_map/ppermute | solution.py:218
  30.7 0.6 %gather_states.1 = (f32[8,4,128,128]{3,2,1,0:T(8,128)S(1)}, f32[4,128,128]{2,1,0:T(8,128)S(1)}) custom-call(s32[10,128]{1,0:T(8,128)S(1)} %get-tuple-element.32.table, f32[2,64,512]{2,1,0:T(8,128)S(1)} %collective-permute-done.1.refs_0_, f32[2,64,512]{2,1,0:T(8,128)S(1)} %collective-permute-done.2.refs_1_, f32[2,64,512]{2,1,0:T(8,128)S(1)} %collective-permute-done.3.refs_2_, ...), custom_call_target="tpu_custom_call" | custom-call | flops 67108864 | bytes 4194304 | tf_op jit(solution)/shard_map/gather_states/pallas_call | solution.py:268
  31.3 3.5 %collective-permute-start.7 = (f32[4,128,128]{2,1,0:T(8,128)S(1)}, f32[4,128,128]{2,1,0:T(8,128)S(1)}, u32[]{:S(2)}, u32[]{:S(2)}) collective-permute-start(f32[4,128,128]{2,1,0:T(8,128)S(1)} %get-tuple-element.38), channel_id=1, source_target_pairs={{0,8},{1,9},{2,10},{3,11},{4,12},{5,13},{6,14},{7,15},{8,16},{9,17... | collective-permute-start | bytes 786440 | tf_op jit(solution)/shard_map/ppermute | solution.py:279
  34.8 0.6 %collective-permute-start.8 = (f32[2,64,512]{2,1,0:T(8,128)S(1)}, f32[2,64,512]{2,1,0:T(8,128)S(1)}, u32[]{:S(2)}, u32[]{:S(2)}) collective-permute-start(f32[2,64,512]{2,1,0:T(8,128)S(1)} %get-tuple-element.39), channel_id=1, source_target_pairs={{0,2},{1,3},{2,0},{3,1},{4,6},{5,7},{6,4},{7,5},{8,10},{9,11},{10,... | collective-permute-start | bytes 786440 | tf_op jit(solution)/shard_map/ppermute | solution.py:218
  35.4 1.5 %collective-permute-start.9 = (f32[2,64,512]{2,1,0:T(8,128)S(1)}, f32[2,64,512]{2,1,0:T(8,128)S(1)}, u32[]{:S(2)}, u32[]{:S(2)}) collective-permute-start(f32[2,64,512]{2,1,0:T(8,128)S(1)} %get-tuple-element.41), channel_id=1, source_target_pairs={{0,1},{1,0},{2,3},{3,2},{4,5},{5,4},{6,7},{7,6},{8,9},{9,8},{10,11... | collective-permute-start | bytes 786440 | tf_op jit(solution)/shard_map/ppermute | solution.py:218
  36.9 0.0 collective-permute-done.10.refs_0_
  36.9 2.2 %collective-permute-done.7.earlier = f32[4,128,128]{2,1,0:T(8,128)S(1)} collective-permute-done((f32[4,128,128]{2,1,0:T(8,128)S(1)}, f32[4,128,128]{2,1,0:T(8,128)S(1)}, u32[]{:S(2)}, u32[]{:S(2)}) %collective-permute-start.7) | collective-permute-done | bytes 262176 | tf_op jit(solution)/shard_map/ppermute | solution.py:279
  39.1 0.2 reach_back.2
  39.3 1.6 %collective-permute-start.17 = (f32[64,512]{1,0:T(8,128)S(1)}, f32[64,512]{1,0:T(8,128)S(1)}, u32[]{:S(2)}, u32[]{:S(2)}) collective-permute-start(f32[64,512]{1,0:T(8,128)S(1)} %get-tuple-element.50), channel_id=1, source_target_pairs={{0,3},{1,2},{2,1},{3,0},{4,7},{5,6},{6,5},{7,4},{8,11},{9,10},{10,... | collective-permute-start | bytes 393224 | tf_op jit(solution)/shard_map/ppermute | solution.py:218
  40.8 0.0 collective-permute-start.16
  40.8 1.4 %collective-permute-done.8.refs_0_ = f32[2,64,512]{2,1,0:T(8,128)S(1)} collective-permute-done((f32[2,64,512]{2,1,0:T(8,128)S(1)}, f32[2,64,512]{2,1,0:T(8,128)S(1)}, u32[]{:S(2)}, u32[]{:S(2)}) %collective-permute-start.8) | collective-permute-done | bytes 262176 | tf_op jit(solution)/shard_map/ppermute | solution.py:218
  42.3 0.9 %collective-permute-done.9.refs_2_ = f32[2,64,512]{2,1,0:T(8,128)S(1)} collective-permute-done((f32[2,64,512]{2,1,0:T(8,128)S(1)}, f32[2,64,512]{2,1,0:T(8,128)S(1)}, u32[]{:S(2)}, u32[]{:S(2)}) %collective-permute-start.9) | collective-permute-done | bytes 262176 | tf_op jit(solution)/shard_map/ppermute | solution.py:218
  43.2 0.0 copy-start.3
  43.2 0.5 reach_back.3
  43.6 0.1 collective-permute-start.11
  43.7 1.6 %collective-permute-start.12 = (f32[64,512]{1,0:T(8,128)S(1)}, f32[64,512]{1,0:T(8,128)S(1)}, u32[]{:S(2)}, u32[]{:S(2)}) collective-permute-start(f32[64,512]{1,0:T(8,128)S(1)} %get-tuple-element.45), channel_id=1, source_target_pairs={{0,1},{1,0},{2,3},{3,2},{4,5},{5,4},{6,7},{7,6},{8,9},{9,8},{10,11... | collective-permute-start | bytes 393224 | tf_op jit(solution)/shard_map/ppermute | solution.py:218
  45.3 1.8 %collective-permute-start.13 = (f32[64,512]{1,0:T(8,128)S(1)}, f32[64,512]{1,0:T(8,128)S(1)}, u32[]{:S(2)}, u32[]{:S(2)}) collective-permute-start(f32[64,512]{1,0:T(8,128)S(1)} %get-tuple-element.46), channel_id=1, source_target_pairs={{0,2},{1,3},{2,0},{3,1},{4,6},{5,7},{6,4},{7,5},{8,10},{9,11},{10,... | collective-permute-start | bytes 393224 | tf_op jit(solution)/shard_map/ppermute | solution.py:218
  47.0 0.0 collective-permute-done.17.refs_2_
  47.0 0.0 collective-permute-start.14
  47.0 0.6 %collective-permute-done.16.refs_1_ = f32[64,512]{1,0:T(8,128)S(1)} collective-permute-done((f32[64,512]{1,0:T(8,128)S(1)}, f32[64,512]{1,0:T(8,128)S(1)}, u32[]{:S(2)}, u32[]{:S(2)}) %collective-permute-start.16) | collective-permute-done | bytes 131104 | tf_op jit(solution)/shard_map/ppermute | solution.py:218
  47.6 0.7 %collective-permute-start.15 = (f32[64,512]{1,0:T(8,128)S(1)}, f32[64,512]{1,0:T(8,128)S(1)}, u32[]{:S(2)}, u32[]{:S(2)}) collective-permute-start(f32[64,512]{1,0:T(8,128)S(1)} %get-tuple-element.48), channel_id=1, source_target_pairs={{0,6},{1,7},{2,4},{3,5},{4,2},{5,3},{6,0},{7,1},{8,14},{9,15},{10,... | collective-permute-start | bytes 393224 | tf_op jit(solution)/shard_map/ppermute | solution.py:218
  48.3 0.0 copy-done.3
  48.3 0.9 %finish.2.refs_5_ = bf16[64,4096]{1,0:T(8,128)(2,1)} custom-call(s32[10,128]{1,0:T(8,128)S(1)} %get-tuple-element.32.table, f32[64,4096]{1,0:T(8,128)S(1)} %inside.1.refs_8_.own, f32[1,4096]{1,0:T(1,128)S(1)} %bitcast.1, f32[64,512]{1,0:T(8,128)S(1)} %get-tuple-element.49.refs_0_, f32[64,512]{1,0:T(8,128)S(1)} %collective-permute-done.16.refs_1_, ...), custom_call_target="tpu_custom_call" | custom-call | bytes 2097152 | tf_op jit(solution)/shard_map/finish/pallas_call | solution.py:316
  49.2 0.0 collective-permute-done.11.refs_0_
  49.2 1.0 %collective-permute-done.12.refs_1_ = f32[64,512]{1,0:T(8,128)S(1)} collective-permute-done((f32[64,512]{1,0:T(8,128)S(1)}, f32[64,512]{1,0:T(8,128)S(1)}, u32[]{:S(2)}, u32[]{:S(2)}) %collective-permute-start.12) | collective-permute-done | bytes 131104 | tf_op jit(solution)/shard_map/ppermute | solution.py:218
  50.2 1.4 %collective-permute-done.13.refs_2_ = f32[64,512]{1,0:T(8,128)S(1)} collective-permute-done((f32[64,512]{1,0:T(8,128)S(1)}, f32[64,512]{1,0:T(8,128)S(1)}, u32[]{:S(2)}, u32[]{:S(2)}) %collective-permute-start.13) | collective-permute-done | bytes 131104 | tf_op jit(solution)/shard_map/ppermute | solution.py:218
  51.6 1.3 %collective-permute-done.14.refs_3_ = f32[64,512]{1,0:T(8,128)S(1)} collective-permute-done((f32[64,512]{1,0:T(8,128)S(1)}, f32[64,512]{1,0:T(8,128)S(1)}, u32[]{:S(2)}, u32[]{:S(2)}) %collective-permute-start.14) | collective-permute-done | bytes 131104 | tf_op jit(solution)/shard_map/ppermute | solution.py:218
  52.9 0.5 collective-permute-done.15.refs_4_
  53.4 0.9 %finish.3 = bf16[64,4096]{1,0:T(8,128)(2,1)} custom-call(s32[10,128]{1,0:T(8,128)S(1)} %get-tuple-element.32.table, f32[64,4096]{1,0:T(8,128)S(1)} %inside.1.refs_8_.own, f32[1,4096]{1,0:T(1,128)S(1)} %bitcast.2, f32[64,512]{1,0:T(8,128)S(1)} %collective-permute-done.11.refs_0_, ...), custom_call_target="tpu_custom_call", output_to_operand_aliasing={{}: (8, {})} | custom-call | bytes 2097152 | tf_op jit(solution)/shard_map/finish/pallas_call | solution.py:316
Async XLA Ops:
  0.0 13.7 %copy-start = (bf16[64,4096]{1,0:T(8,128)(2,1)S(1)}, bf16[64,4096]{1,0:T(8,128)(2,1)}, u32[]{:S(2)}) copy-start(bf16[64,4096]{1,0:T(8,128)(2,1)} %queries.5) | copy-start | bytes 1572868
  0.0 13.7 %copy-start.2 = (bf16[64,4096]{1,0:T(8,128)(2,1)S(1)}, bf16[64,4096]{1,0:T(8,128)(2,1)}, u32[]{:S(2)}) copy-start(bf16[64,4096]{1,0:T(8,128)(2,1)} %values.3) | copy-start | bytes 1572868
  0.0 13.7 %copy-start.1 = (bf16[64,4096]{1,0:T(8,128)(2,1)S(1)}, bf16[64,4096]{1,0:T(8,128)(2,1)}, u32[]{:S(2)}) copy-start(bf16[64,4096]{1,0:T(8,128)(2,1)} %keys.3) | copy-start | bytes 1572868
  0.0 13.7 %copy-start.4 = (s32[16]{0:T(128)S(1)}, s32[16]{0:T(128)}, u32[]{:S(2)}) copy-start(s32[16]{0:T(128)} %lengths.3) | copy-start | bytes 196
  1.5 4.7 %collective-permute-start = (f32[4,3,64,512]{3,2,1,0:T(8,128)S(1)}, f32[4,3,64,512]{3,2,1,0:T(8,128)S(1)}, u32[]{:S(2)}, u32[]{:S(2)}) collective-permute-start(f32[4,3,64,512]{3,2,1,0:T(8,128)S(1)} %get-tuple-element.28), channel_id=1, source_target_pairs={{0,4},{1,5},{2,6},{3,7},{4,0},{5,1},{6,2},{7,3},{8,12},{9,13},{10,... | collective-permute-start | bytes 4718600 | tf_op jit(solution)/shard_map/ppermute | solution.py:218
  2.0 9.5 %collective-permute-start.1 = (f32[2,64,512]{2,1,0:T(8,128)S(1)}, f32[2,64,512]{2,1,0:T(8,128)S(1)}, u32[]{:S(2)}, u32[]{:S(2)}) collective-permute-start(f32[2,64,512]{2,1,0:T(8,128)S(1)} %get-tuple-element.29), channel_id=1, source_target_pairs={{0,2},{1,3},{2,0},{3,1},{4,6},{5,7},{6,4},{7,5},{8,10},{9,11},{10,... | collective-permute-start | bytes 786440 | tf_op jit(solution)/shard_map/ppermute | solution.py:218
  4.6 14.1 %collective-permute-start.2 = (f32[2,64,512]{2,1,0:T(8,128)S(1)}, f32[2,64,512]{2,1,0:T(8,128)S(1)}, u32[]{:S(2)}, u32[]{:S(2)}) collective-permute-start(f32[2,64,512]{2,1,0:T(8,128)S(1)} %get-tuple-element.30), channel_id=1, source_target_pairs={{0,1},{1,0},{2,3},{3,2},{4,5},{5,4},{6,7},{7,6},{8,9},{9,8},{10,11... | collective-permute-start | bytes 786440 | tf_op jit(solution)/shard_map/ppermute | solution.py:218
  6.1 12.9 %collective-permute-start.3 = (f32[2,64,512]{2,1,0:T(8,128)S(1)}, f32[2,64,512]{2,1,0:T(8,128)S(1)}, u32[]{:S(2)}, u32[]{:S(2)}) collective-permute-start(f32[2,64,512]{2,1,0:T(8,128)S(1)} %get-tuple-element.31), channel_id=1, source_target_pairs={{0,3},{1,2},{2,1},{3,0},{4,7},{5,6},{6,5},{7,4},{8,11},{9,10},{10,... | collective-permute-start | bytes 786440 | tf_op jit(solution)/shard_map/ppermute | solution.py:218
  6.2 18.3 %collective-permute-start.4 = (f32[2,64,512]{2,1,0:T(8,128)S(1)}, f32[2,64,512]{2,1,0:T(8,128)S(1)}, u32[]{:S(2)}, u32[]{:S(2)}) collective-permute-start(f32[2,64,512]{2,1,0:T(8,128)S(1)} %get-tuple-element.34), channel_id=1, source_target_pairs={{0,3},{1,2},{2,1},{3,0},{4,7},{5,6},{6,5},{7,4},{8,11},{9,10},{10,... | collective-permute-start | bytes 786440 | tf_op jit(solution)/shard_map/ppermute | solution.py:218
  9.2 19.2 %collective-permute-start.5 = (f32[2,64,512]{2,1,0:T(8,128)S(1)}, f32[2,64,512]{2,1,0:T(8,128)S(1)}, u32[]{:S(2)}, u32[]{:S(2)}) collective-permute-start(f32[2,64,512]{2,1,0:T(8,128)S(1)} %get-tuple-element.35), channel_id=1, source_target_pairs={{0,2},{1,3},{2,0},{3,1},{4,6},{5,7},{6,4},{7,5},{8,10},{9,11},{10,... | collective-permute-start | bytes 786440 | tf_op jit(solution)/shard_map/ppermute | solution.py:218
  11.5 19.1 %collective-permute-start.6 = (f32[2,64,512]{2,1,0:T(8,128)S(1)}, f32[2,64,512]{2,1,0:T(8,128)S(1)}, u32[]{:S(2)}, u32[]{:S(2)}) collective-permute-start(f32[2,64,512]{2,1,0:T(8,128)S(1)} %get-tuple-element.36), channel_id=1, source_target_pairs={{0,1},{1,0},{2,3},{3,2},{4,5},{5,4},{6,7},{7,6},{8,9},{9,8},{10,11... | collective-permute-start | bytes 786440 | tf_op jit(solution)/shard_map/ppermute | solution.py:218
  19.7 17.1 %collective-permute-start.10 = (f32[2,64,512]{2,1,0:T(8,128)S(1)}, f32[2,64,512]{2,1,0:T(8,128)S(1)}, u32[]{:S(2)}, u32[]{:S(2)}) collective-permute-start(f32[2,64,512]{2,1,0:T(8,128)S(1)} %get-tuple-element.42), channel_id=1, source_target_pairs={{0,3},{1,2},{2,1},{3,0},{4,7},{5,6},{6,5},{7,4},{8,11},{9,10},{10,... | collective-permute-start | bytes 786440 | tf_op jit(solution)/shard_map/ppermute | solution.py:218
  31.3 7.8 %collective-permute-start.7 = (f32[4,128,128]{2,1,0:T(8,128)S(1)}, f32[4,128,128]{2,1,0:T(8,128)S(1)}, u32[]{:S(2)}, u32[]{:S(2)}) collective-permute-start(f32[4,128,128]{2,1,0:T(8,128)S(1)} %get-tuple-element.38), channel_id=1, source_target_pairs={{0,8},{1,9},{2,10},{3,11},{4,12},{5,13},{6,14},{7,15},{8,16},{9,17... | collective-permute-start | bytes 786440 | tf_op jit(solution)/shard_map/ppermute | solution.py:279
  34.8 7.5 %collective-permute-start.8 = (f32[2,64,512]{2,1,0:T(8,128)S(1)}, f32[2,64,512]{2,1,0:T(8,128)S(1)}, u32[]{:S(2)}, u32[]{:S(2)}) collective-permute-start(f32[2,64,512]{2,1,0:T(8,128)S(1)} %get-tuple-element.39), channel_id=1, source_target_pairs={{0,2},{1,3},{2,0},{3,1},{4,6},{5,7},{6,4},{7,5},{8,10},{9,11},{10,... | collective-permute-start | bytes 786440 | tf_op jit(solution)/shard_map/ppermute | solution.py:218
  35.4 7.8 %collective-permute-start.9 = (f32[2,64,512]{2,1,0:T(8,128)S(1)}, f32[2,64,512]{2,1,0:T(8,128)S(1)}, u32[]{:S(2)}, u32[]{:S(2)}) collective-permute-start(f32[2,64,512]{2,1,0:T(8,128)S(1)} %get-tuple-element.41), channel_id=1, source_target_pairs={{0,1},{1,0},{2,3},{3,2},{4,5},{5,4},{6,7},{7,6},{8,9},{9,8},{10,11... | collective-permute-start | bytes 786440 | tf_op jit(solution)/shard_map/ppermute | solution.py:218
  39.3 7.7 %collective-permute-start.17 = (f32[64,512]{1,0:T(8,128)S(1)}, f32[64,512]{1,0:T(8,128)S(1)}, u32[]{:S(2)}, u32[]{:S(2)}) collective-permute-start(f32[64,512]{1,0:T(8,128)S(1)} %get-tuple-element.50), channel_id=1, source_target_pairs={{0,3},{1,2},{2,1},{3,0},{4,7},{5,6},{6,5},{7,4},{8,11},{9,10},{10,... | collective-permute-start | bytes 393224 | tf_op jit(solution)/shard_map/ppermute | solution.py:218
  40.8 6.8 %collective-permute-start.16 = (f32[64,512]{1,0:T(8,128)S(1)}, f32[64,512]{1,0:T(8,128)S(1)}, u32[]{:S(2)}, u32[]{:S(2)}) collective-permute-start(f32[64,512]{1,0:T(8,128)S(1)} %get-tuple-element.43.refs_3_), channel_id=1, source_target_pairs={{0,7},{1,6},{2,5},{3,4},{4,3},{5,2},{6,1},{7,0},{8,15},{9,14},{10,... | collective-permute-start | bytes 393224 | tf_op jit(solution)/shard_map/ppermute | solution.py:218
  43.2 5.2 %copy-start.3 = (f32[4096]{0:T(1024)S(1)}, f32[4096]{0:T(1024)}, u32[]{:S(2)}) copy-start(f32[4096]{0:T(1024)} %param.9) | copy-start | bytes 49156
  43.6 5.5 %collective-permute-start.11 = (f32[64,512]{1,0:T(8,128)S(1)}, f32[64,512]{1,0:T(8,128)S(1)}, u32[]{:S(2)}, u32[]{:S(2)}) collective-permute-start(f32[64,512]{1,0:T(8,128)S(1)} %get-tuple-element.44), channel_id=1, source_target_pairs={{0,4},{1,5},{2,6},{3,7},{4,0},{5,1},{6,2},{7,3},{8,12},{9,13},{10,... | collective-permute-start | bytes 393224 | tf_op jit(solution)/shard_map/ppermute | solution.py:218
  43.7 6.5 %collective-permute-start.12 = (f32[64,512]{1,0:T(8,128)S(1)}, f32[64,512]{1,0:T(8,128)S(1)}, u32[]{:S(2)}, u32[]{:S(2)}) collective-permute-start(f32[64,512]{1,0:T(8,128)S(1)} %get-tuple-element.45), channel_id=1, source_target_pairs={{0,1},{1,0},{2,3},{3,2},{4,5},{5,4},{6,7},{7,6},{8,9},{9,8},{10,11... | collective-permute-start | bytes 393224 | tf_op jit(solution)/shard_map/ppermute | solution.py:218
  45.3 6.3 %collective-permute-start.13 = (f32[64,512]{1,0:T(8,128)S(1)}, f32[64,512]{1,0:T(8,128)S(1)}, u32[]{:S(2)}, u32[]{:S(2)}) collective-permute-start(f32[64,512]{1,0:T(8,128)S(1)} %get-tuple-element.46), channel_id=1, source_target_pairs={{0,2},{1,3},{2,0},{3,1},{4,6},{5,7},{6,4},{7,5},{8,10},{9,11},{10,... | collective-permute-start | bytes 393224 | tf_op jit(solution)/shard_map/ppermute | solution.py:218
  47.0 5.9 %collective-permute-start.14 = (f32[64,512]{1,0:T(8,128)S(1)}, f32[64,512]{1,0:T(8,128)S(1)}, u32[]{:S(2)}, u32[]{:S(2)}) collective-permute-start(f32[64,512]{1,0:T(8,128)S(1)} %get-tuple-element.47), channel_id=1, source_target_pairs={{0,5},{1,4},{2,7},{3,6},{4,1},{5,0},{6,3},{7,2},{8,13},{9,12},{10,... | collective-permute-start | bytes 393224 | tf_op jit(solution)/shard_map/ppermute | solution.py:218
  47.6 5.8 %collective-permute-start.15 = (f32[64,512]{1,0:T(8,128)S(1)}, f32[64,512]{1,0:T(8,128)S(1)}, u32[]{:S(2)}, u32[]{:S(2)}) collective-permute-start(f32[64,512]{1,0:T(8,128)S(1)} %get-tuple-element.48), channel_id=1, source_target_pairs={{0,6},{1,7},{2,4},{3,5},{4,2},{5,3},{6,0},{7,1},{8,14},{9,15},{10,... | collective-permute-start | bytes 393224 | tf_op jit(solution)/shard_map/ppermute | solution.py:218

commit v12 on v11

--- a/solution.py
+++ b/solution.py
@@ -307,7 +307,7 @@
 
     gain = norm_gain.reshape(1, columns)
     out = None
-    listed = [[(0, 0), (3, 1), (3, 0)], [(0, 1), (1, 0), (2, 0), (1, 1), (2, 1)]]
+    listed = [[(0, 0), (3, 1), (3, 0)], [(1, 0), (2, 0), (0, 1), (1, 1), (2, 1)]]
     named = [pair for group in listed for pair in group]
     listed[0] += [(e, side) for e in soon for side in range(CORES) if (e, side) not in named]
     groups = [[e + side * half for e, side in group] for group in listed]

time: 54.5 us -> 54.4 us (level)
  waiting for transfers between devices: 19.4 us -> 18.8 us
    ppermute x17, waiting for transfers between devices: 17.2 us -> 16.6 us  [swap(): return lax.ppermute(part, everyone, pairs)]
where the time goes in v12:
time: 54.4 us; the launch traced here: 53.9 us
  starting transfers between devices  24.7 us (45%)
  waiting for transfers between devices  18.8 us (35%)
  Pallas kernels  10.3 us (19%)
    ppermute x17, starting transfers between devices, swap(): return lax.ppermute(part, everyone, pairs)  21.2 us
    ppermute x17, waiting for transfers between devices, swap(): return lax.ppermute(part, everyone, pairs)  16.6 us
    pallas_call x1, Pallas kernels, body(): call(functools.partial(inside, head_count, docs, rows), 'inside', shape(r...  4.93 us
    ppermute x1, starting transfers between devices, body(): moving = lax.ppermute(total, everyone, up)  3.5 us
    ppermute x1, waiting for transfers between devices, body(): moving = lax.ppermute(total, everyone, up)  2.19 us
    pallas_call x2, Pallas kernels, body(): call(functools.partial(finish, chosen, members, heads, rows), 'finish', s...  1.8 us
    pallas_call x1, Pallas kernels, body(): call(functools.partial(spread, members, width, near_order), 'spread', [sh...  1.48 us
  transfers between devices with their start and end apart: 18, of which 13 were waited for; matrix products, arithmetic and copies ran while one was open for 0% of the time, Pallas kernels for 15%

profile of v12, /device:TPU:0, one launch (start us, length us, event | category | flops | bytes accessed | tf_op | source)
XLA Modules:
  0.0 53.9 jit_solution(1247542969174287255)
XLA Ops:
  0.0 0.0 copy-start
  0.0 0.0 copy-start.2
  0.0 0.0 copy-start.1
  0.0 0.0 copy-start.4
  0.0 1.5 %spread.1 = (f32[2,64,512]{2,1,0:T(8,128)S(1)}, f32[2,64,512]{2,1,0:T(8,128)S(1)}, f32[2,64,512]{2,1,0:T(8,128)S(1)}, f32[2,64,512]{2,1,0:T(8,128)S(1)}, f32[4,3,64,512]{3,2,1,0:T(8,128)S(1)}) custom-call(bf16[64,4096]{1,0:T(8,128)(2,1)} %queries.5, bf16[64,4096]{1,0:T(8,128)(2,1)} %keys.3, bf16[64,4096]{1,0:T(8,128)(2,1)} %values.3), custom_call_target="tpu_custom_call" | custom-call | tf_op jit(solution)/shard_map/spread/pallas_call | solution.py:224
  1.5 0.5 collective-permute-start
  2.0 2.6 %collective-permute-start.1 = (f32[2,64,512]{2,1,0:T(8,128)S(1)}, f32[2,64,512]{2,1,0:T(8,128)S(1)}, u32[]{:S(2)}, u32[]{:S(2)}) collective-permute-start(f32[2,64,512]{2,1,0:T(8,128)S(1)} %get-tuple-element.29), channel_id=1, source_target_pairs={{0,2},{1,3},{2,0},{3,1},{4,6},{5,7},{6,4},{7,5},{8,10},{9,11},{10,... | collective-permute-start | bytes 786440 | tf_op jit(solution)/shard_map/ppermute | solution.py:218
  4.6 1.5 %collective-permute-start.2 = (f32[2,64,512]{2,1,0:T(8,128)S(1)}, f32[2,64,512]{2,1,0:T(8,128)S(1)}, u32[]{:S(2)}, u32[]{:S(2)}) collective-permute-start(f32[2,64,512]{2,1,0:T(8,128)S(1)} %get-tuple-element.30), channel_id=1, source_target_pairs={{0,1},{1,0},{2,3},{3,2},{4,5},{5,4},{6,7},{7,6},{8,9},{9,8},{10,11... | collective-permute-start | bytes 786440 | tf_op jit(solution)/shard_map/ppermute | solution.py:218
  6.1 0.0 collective-permute-start.3
  6.2 0.0 collective-permute-done.swapped.refs_7_
  6.2 0.1 forward.1
  6.2 2.9 %collective-permute-start.4 = (f32[2,64,512]{2,1,0:T(8,128)S(1)}, f32[2,64,512]{2,1,0:T(8,128)S(1)}, u32[]{:S(2)}, u32[]{:S(2)}) collective-permute-start(f32[2,64,512]{2,1,0:T(8,128)S(1)} %get-tuple-element.34), channel_id=1, source_target_pairs={{0,3},{1,2},{2,1},{3,0},{4,7},{5,6},{6,5},{7,4},{8,11},{9,10},{10,... | collective-permute-start | bytes 786440 | tf_op jit(solution)/shard_map/ppermute | solution.py:218
  9.2 0.5 collective-permute-start.5
  9.7 1.9 %collective-permute-done.1.refs_0_ = f32[2,64,512]{2,1,0:T(8,128)S(1)} collective-permute-done((f32[2,64,512]{2,1,0:T(8,128)S(1)}, f32[2,64,512]{2,1,0:T(8,128)S(1)}, u32[]{:S(2)}, u32[]{:S(2)}) %collective-permute-start.1) | collective-permute-done | bytes 262176 | tf_op jit(solution)/shard_map/ppermute | solution.py:218
  11.5 2.2 %collective-permute-start.6 = (f32[2,64,512]{2,1,0:T(8,128)S(1)}, f32[2,64,512]{2,1,0:T(8,128)S(1)}, u32[]{:S(2)}, u32[]{:S(2)}) collective-permute-start(f32[2,64,512]{2,1,0:T(8,128)S(1)} %get-tuple-element.36), channel_id=1, source_target_pairs={{0,1},{1,0},{2,3},{3,2},{4,5},{5,4},{6,7},{7,6},{8,9},{9,8},{10,11... | collective-permute-start | bytes 786440 | tf_op jit(solution)/shard_map/ppermute | solution.py:218
  13.7 0.0 copy-done
  13.7 0.0 copy-done.2
  13.7 0.0 copy-done.1
  13.8 0.0 copy-done.4
  13.8 4.9 %inside.1.refs_8_.own = f32[64,4096]{1,0:T(8,128)S(1)} custom-call(s32[16]{0:T(128)S(1)} %copy-done.4, bf16[64,4096]{1,0:T(8,128)(2,1)S(1)} %copy-done, bf16[64,4096]{1,0:T(8,128)(2,1)S(1)} %copy-done.1, bf16[64,4096]{1,0:T(8,128)(2,1)S(1)} %copy-done.2), custom_call_target="tpu_custom_call" | custom-call | flops 67108864 | bytes 3145728 | tf_op jit(solution)/shard_map/inside/pallas_call | solution.py:258
  18.7 0.0 collective-permute-done.2.refs_1_
  18.7 0.3 collective-permute-done.3.refs_2_
  19.0 0.7 %join_queries.1 = (f32[2,64,512]{2,1,0:T(8,128)S(1)}, f32[2,64,512]{2,1,0:T(8,128)S(1)}, f32[2,64,512]{2,1,0:T(8,128)S(1)}, f32[2,64,512]{2,1,0:T(8,128)S(1)}, s32[10,128]{1,0:T(8,128)S(1)}) custom-call(s32[16]{0:T(128)S(1)} %copy-done.4, bf16[64,4096]{1,0:T(8,128)(2,1)S(1)} %copy-done, f32[4,3,64,512]{3,2,1,0:T(8,128)S(1)} %collective-permute-done.swapped.refs_7_, ...), custom_call_target="tpu_custom_call" | custom-call | bytes 2097152 | tf_op jit(solution)/shard_map/join_queries/pallas_call | solution.py:248
  19.7 3.0 %collective-permute-start.10 = (f32[2,64,512]{2,1,0:T(8,128)S(1)}, f32[2,64,512]{2,1,0:T(8,128)S(1)}, u32[]{:S(2)}, u32[]{:S(2)}) collective-permute-start(f32[2,64,512]{2,1,0:T(8,128)S(1)} %get-tuple-element.42), channel_id=1, source_target_pairs={{0,3},{1,2},{2,1},{3,0},{4,7},{5,6},{6,5},{7,4},{8,11},{9,10},{10,... | collective-permute-start | bytes 786440 | tf_op jit(solution)/shard_map/ppermute | solution.py:218
  22.7 1.8 %collective-permute-done.4.refs_4_ = f32[2,64,512]{2,1,0:T(8,128)S(1)} collective-permute-done((f32[2,64,512]{2,1,0:T(8,128)S(1)}, f32[2,64,512]{2,1,0:T(8,128)S(1)}, u32[]{:S(2)}, u32[]{:S(2)}) %collective-permute-start.4) | collective-permute-done | bytes 262176 | tf_op jit(solution)/shard_map/ppermute | solution.py:218
  24.5 3.8 %collective-permute-done.5.refs_5_ = f32[2,64,512]{2,1,0:T(8,128)S(1)} collective-permute-done((f32[2,64,512]{2,1,0:T(8,128)S(1)}, f32[2,64,512]{2,1,0:T(8,128)S(1)}, u32[]{:S(2)}, u32[]{:S(2)}) %collective-permute-start.5) | collective-permute-done | bytes 262176 | tf_op jit(solution)/shard_map/ppermute | solution.py:218
  28.4 2.3 %collective-permute-done.6.refs_6_ = f32[2,64,512]{2,1,0:T(8,128)S(1)} collective-permute-done((f32[2,64,512]{2,1,0:T(8,128)S(1)}, f32[2,64,512]{2,1,0:T(8,128)S(1)}, u32[]{:S(2)}, u32[]{:S(2)}) %collective-permute-start.6) | collective-permute-done | bytes 262176 | tf_op jit(solution)/shard_map/ppermute | solution.py:218
  30.7 0.6 %gather_states.1 = (f32[8,4,128,128]{3,2,1,0:T(8,128)S(1)}, f32[4,128,128]{2,1,0:T(8,128)S(1)}) custom-call(s32[10,128]{1,0:T(8,128)S(1)} %get-tuple-element.32.table, f32[2,64,512]{2,1,0:T(8,128)S(1)} %collective-permute-done.1.refs_0_, f32[2,64,512]{2,1,0:T(8,128)S(1)} %collective-permute-done.2.refs_1_, f32[2,64,512]{2,1,0:T(8,128)S(1)} %collective-permute-done.3.refs_2_, ...), custom_call_target="tpu_custom_call" | custom-call | flops 67108864 | bytes 4194304 | tf_op jit(solution)/shard_map/gather_states/pallas_call | solution.py:268
  31.3 3.5 %collective-permute-start.7 = (f32[4,128,128]{2,1,0:T(8,128)S(1)}, f32[4,128,128]{2,1,0:T(8,128)S(1)}, u32[]{:S(2)}, u32[]{:S(2)}) collective-permute-start(f32[4,128,128]{2,1,0:T(8,128)S(1)} %get-tuple-element.38), channel_id=1, source_target_pairs={{0,8},{1,9},{2,10},{3,11},{4,12},{5,13},{6,14},{7,15},{8,16},{9,17... | collective-permute-start | bytes 786440 | tf_op jit(solution)/shard_map/ppermute | solution.py:279
  34.8 0.6 %collective-permute-start.8 = (f32[2,64,512]{2,1,0:T(8,128)S(1)}, f32[2,64,512]{2,1,0:T(8,128)S(1)}, u32[]{:S(2)}, u32[]{:S(2)}) collective-permute-start(f32[2,64,512]{2,1,0:T(8,128)S(1)} %get-tuple-element.39), channel_id=1, source_target_pairs={{0,2},{1,3},{2,0},{3,1},{4,6},{5,7},{6,4},{7,5},{8,10},{9,11},{10,... | collective-permute-start | bytes 786440 | tf_op jit(solution)/shard_map/ppermute | solution.py:218
  35.4 1.5 %collective-permute-start.9 = (f32[2,64,512]{2,1,0:T(8,128)S(1)}, f32[2,64,512]{2,1,0:T(8,128)S(1)}, u32[]{:S(2)}, u32[]{:S(2)}) collective-permute-start(f32[2,64,512]{2,1,0:T(8,128)S(1)} %get-tuple-element.41), channel_id=1, source_target_pairs={{0,1},{1,0},{2,3},{3,2},{4,5},{5,4},{6,7},{7,6},{8,9},{9,8},{10,11... | collective-permute-start | bytes 786440 | tf_op jit(solution)/shard_map/ppermute | solution.py:218
  36.9 0.0 collective-permute-done.10.refs_0_
  36.9 2.2 %collective-permute-done.7.earlier = f32[4,128,128]{2,1,0:T(8,128)S(1)} collective-permute-done((f32[4,128,128]{2,1,0:T(8,128)S(1)}, f32[4,128,128]{2,1,0:T(8,128)S(1)}, u32[]{:S(2)}, u32[]{:S(2)}) %collective-permute-start.7) | collective-permute-done | bytes 262176 | tf_op jit(solution)/shard_map/ppermute | solution.py:279
  39.1 0.2 reach_back.2
  39.3 1.6 %collective-permute-start.17 = (f32[64,512]{1,0:T(8,128)S(1)}, f32[64,512]{1,0:T(8,128)S(1)}, u32[]{:S(2)}, u32[]{:S(2)}) collective-permute-start(f32[64,512]{1,0:T(8,128)S(1)} %get-tuple-element.50), channel_id=1, source_target_pairs={{0,3},{1,2},{2,1},{3,0},{4,7},{5,6},{6,5},{7,4},{8,11},{9,10},{10,... | collective-permute-start | bytes 393224 | tf_op jit(solution)/shard_map/ppermute | solution.py:218
  40.8 0.0 collective-permute-start.16
  40.8 1.4 %collective-permute-done.8.refs_0_ = f32[2,64,512]{2,1,0:T(8,128)S(1)} collective-permute-done((f32[2,64,512]{2,1,0:T(8,128)S(1)}, f32[2,64,512]{2,1,0:T(8,128)S(1)}, u32[]{:S(2)}, u32[]{:S(2)}) %collective-permute-start.8) | collective-permute-done | bytes 262176 | tf_op jit(solution)/shard_map/ppermute | solution.py:218
  42.3 0.9 %collective-permute-done.9.refs_2_ = f32[2,64,512]{2,1,0:T(8,128)S(1)} collective-permute-done((f32[2,64,512]{2,1,0:T(8,128)S(1)}, f32[2,64,512]{2,1,0:T(8,128)S(1)}, u32[]{:S(2)}, u32[]{:S(2)}) %collective-permute-start.9) | collective-permute-done | bytes 262176 | tf_op jit(solution)/shard_map/ppermute | solution.py:218
  43.2 0.0 copy-start.3
  43.2 0.5 reach_back.3
  43.6 1.6 %collective-permute-start.11 = (f32[64,512]{1,0:T(8,128)S(1)}, f32[64,512]{1,0:T(8,128)S(1)}, u32[]{:S(2)}, u32[]{:S(2)}) collective-permute-start(f32[64,512]{1,0:T(8,128)S(1)} %get-tuple-element.44), channel_id=1, source_target_pairs={{0,1},{1,0},{2,3},{3,2},{4,5},{5,4},{6,7},{7,6},{8,9},{9,8},{10,11... | collective-permute-start | bytes 393224 | tf_op jit(solution)/shard_map/ppermute | solution.py:218
  45.2 1.8 %collective-permute-start.12 = (f32[64,512]{1,0:T(8,128)S(1)}, f32[64,512]{1,0:T(8,128)S(1)}, u32[]{:S(2)}, u32[]{:S(2)}) collective-permute-start(f32[64,512]{1,0:T(8,128)S(1)} %get-tuple-element.45), channel_id=1, source_target_pairs={{0,2},{1,3},{2,0},{3,1},{4,6},{5,7},{6,4},{7,5},{8,10},{9,11},{10,... | collective-permute-start | bytes 393224 | tf_op jit(solution)/shard_map/ppermute | solution.py:218
  47.0 0.0 collective-permute-start.13
  47.0 0.0 collective-permute-done.17.refs_2_
  47.0 0.4 collective-permute-start.14
  47.4 0.3 collective-permute-done.16.refs_1_
  47.7 0.6 %collective-permute-start.15 = (f32[64,512]{1,0:T(8,128)S(1)}, f32[64,512]{1,0:T(8,128)S(1)}, u32[]{:S(2)}, u32[]{:S(2)}) collective-permute-start(f32[64,512]{1,0:T(8,128)S(1)} %get-tuple-element.48), channel_id=1, source_target_pairs={{0,6},{1,7},{2,4},{3,5},{4,2},{5,3},{6,0},{7,1},{8,14},{9,15},{10,... | collective-permute-start | bytes 393224 | tf_op jit(solution)/shard_map/ppermute | solution.py:218
  48.3 0.0 copy-done.3
  48.3 0.9 %finish.2.refs_5_ = bf16[64,4096]{1,0:T(8,128)(2,1)} custom-call(s32[10,128]{1,0:T(8,128)S(1)} %get-tuple-element.32.table, f32[64,4096]{1,0:T(8,128)S(1)} %inside.1.refs_8_.own, f32[1,4096]{1,0:T(1,128)S(1)} %bitcast.1, f32[64,512]{1,0:T(8,128)S(1)} %get-tuple-element.49.refs_0_, f32[64,512]{1,0:T(8,128)S(1)} %collective-permute-done.16.refs_1_, ...), custom_call_target="tpu_custom_call" | custom-call | bytes 2097152 | tf_op jit(solution)/shard_map/finish/pallas_call | solution.py:316
  49.2 1.0 %collective-permute-done.11.refs_0_ = f32[64,512]{1,0:T(8,128)S(1)} collective-permute-done((f32[64,512]{1,0:T(8,128)S(1)}, f32[64,512]{1,0:T(8,128)S(1)}, u32[]{:S(2)}, u32[]{:S(2)}) %collective-permute-start.11) | collective-permute-done | bytes 131104 | tf_op jit(solution)/shard_map/ppermute | solution.py:218
  50.1 1.4 %collective-permute-done.12.refs_1_ = f32[64,512]{1,0:T(8,128)S(1)} collective-permute-done((f32[64,512]{1,0:T(8,128)S(1)}, f32[64,512]{1,0:T(8,128)S(1)}, u32[]{:S(2)}, u32[]{:S(2)}) %collective-permute-start.12) | collective-permute-done | bytes 131104 | tf_op jit(solution)/shard_map/ppermute | solution.py:218
  51.5 0.0 collective-permute-done.13.refs_2_
  51.5 0.9 %collective-permute-done.14.refs_3_ = f32[64,512]{1,0:T(8,128)S(1)} collective-permute-done((f32[64,512]{1,0:T(8,128)S(1)}, f32[64,512]{1,0:T(8,128)S(1)}, u32[]{:S(2)}, u32[]{:S(2)}) %collective-permute-start.14) | collective-permute-done | bytes 131104 | tf_op jit(solution)/shard_map/ppermute | solution.py:218
  52.5 0.6 %collective-permute-done.15.refs_4_ = f32[64,512]{1,0:T(8,128)S(1)} collective-permute-done((f32[64,512]{1,0:T(8,128)S(1)}, f32[64,512]{1,0:T(8,128)S(1)}, u32[]{:S(2)}, u32[]{:S(2)}) %collective-permute-start.15) | collective-permute-done | bytes 131104 | tf_op jit(solution)/shard_map/ppermute | solution.py:218
  53.0 0.9 %finish.3 = bf16[64,4096]{1,0:T(8,128)(2,1)} custom-call(s32[10,128]{1,0:T(8,128)S(1)} %get-tuple-element.32.table, f32[64,4096]{1,0:T(8,128)S(1)} %inside.1.refs_8_.own, f32[1,4096]{1,0:T(1,128)S(1)} %bitcast.2, f32[64,512]{1,0:T(8,128)S(1)} %collective-permute-done.11.refs_0_, ...), custom_call_target="tpu_custom_call", output_to_operand_aliasing={{}: (8, {})} | custom-call | bytes 2097152 | tf_op jit(solution)/shard_map/finish/pallas_call | solution.py:316
Async XLA Ops:
  0.0 13.7 %copy-start = (bf16[64,4096]{1,0:T(8,128)(2,1)S(1)}, bf16[64,4096]{1,0:T(8,128)(2,1)}, u32[]{:S(2)}) copy-start(bf16[64,4096]{1,0:T(8,128)(2,1)} %queries.5) | copy-start | bytes 1572868
  0.0 13.7 %copy-start.2 = (bf16[64,4096]{1,0:T(8,128)(2,1)S(1)}, bf16[64,4096]{1,0:T(8,128)(2,1)}, u32[]{:S(2)}) copy-start(bf16[64,4096]{1,0:T(8,128)(2,1)} %values.3) | copy-start | bytes 1572868
  0.0 13.7 %copy-start.1 = (bf16[64,4096]{1,0:T(8,128)(2,1)S(1)}, bf16[64,4096]{1,0:T(8,128)(2,1)}, u32[]{:S(2)}) copy-start(bf16[64,4096]{1,0:T(8,128)(2,1)} %keys.3) | copy-start | bytes 1572868
  0.0 13.7 %copy-start.4 = (s32[16]{0:T(128)S(1)}, s32[16]{0:T(128)}, u32[]{:S(2)}) copy-start(s32[16]{0:T(128)} %lengths.3) | copy-start | bytes 196
  1.5 4.7 %collective-permute-start = (f32[4,3,64,512]{3,2,1,0:T(8,128)S(1)}, f32[4,3,64,512]{3,2,1,0:T(8,128)S(1)}, u32[]{:S(2)}, u32[]{:S(2)}) collective-permute-start(f32[4,3,64,512]{3,2,1,0:T(8,128)S(1)} %get-tuple-element.28), channel_id=1, source_target_pairs={{0,4},{1,5},{2,6},{3,7},{4,0},{5,1},{6,2},{7,3},{8,12},{9,13},{10,... | collective-permute-start | bytes 4718600 | tf_op jit(solution)/shard_map/ppermute | solution.py:218
  2.0 9.5 %collective-permute-start.1 = (f32[2,64,512]{2,1,0:T(8,128)S(1)}, f32[2,64,512]{2,1,0:T(8,128)S(1)}, u32[]{:S(2)}, u32[]{:S(2)}) collective-permute-start(f32[2,64,512]{2,1,0:T(8,128)S(1)} %get-tuple-element.29), channel_id=1, source_target_pairs={{0,2},{1,3},{2,0},{3,1},{4,6},{5,7},{6,4},{7,5},{8,10},{9,11},{10,... | collective-permute-start | bytes 786440 | tf_op jit(solution)/shard_map/ppermute | solution.py:218
  4.6 14.1 %collective-permute-start.2 = (f32[2,64,512]{2,1,0:T(8,128)S(1)}, f32[2,64,512]{2,1,0:T(8,128)S(1)}, u32[]{:S(2)}, u32[]{:S(2)}) collective-permute-start(f32[2,64,512]{2,1,0:T(8,128)S(1)} %get-tuple-element.30), channel_id=1, source_target_pairs={{0,1},{1,0},{2,3},{3,2},{4,5},{5,4},{6,7},{7,6},{8,9},{9,8},{10,11... | collective-permute-start | bytes 786440 | tf_op jit(solution)/shard_map/ppermute | solution.py:218
  6.1 12.9 %collective-permute-start.3 = (f32[2,64,512]{2,1,0:T(8,128)S(1)}, f32[2,64,512]{2,1,0:T(8,128)S(1)}, u32[]{:S(2)}, u32[]{:S(2)}) collective-permute-start(f32[2,64,512]{2,1,0:T(8,128)S(1)} %get-tuple-element.31), channel_id=1, source_target_pairs={{0,3},{1,2},{2,1},{3,0},{4,7},{5,6},{6,5},{7,4},{8,11},{9,10},{10,... | collective-permute-start | bytes 786440 | tf_op jit(solution)/shard_map/ppermute | solution.py:218
  6.2 18.3 %collective-permute-start.4 = (f32[2,64,512]{2,1,0:T(8,128)S(1)}, f32[2,64,512]{2,1,0:T(8,128)S(1)}, u32[]{:S(2)}, u32[]{:S(2)}) collective-permute-start(f32[2,64,512]{2,1,0:T(8,128)S(1)} %get-tuple-element.34), channel_id=1, source_target_pairs={{0,3},{1,2},{2,1},{3,0},{4,7},{5,6},{6,5},{7,4},{8,11},{9,10},{10,... | collective-permute-start | bytes 786440 | tf_op jit(solution)/shard_map/ppermute | solution.py:218
  9.2 19.2 %collective-permute-start.5 = (f32[2,64,512]{2,1,0:T(8,128)S(1)}, f32[2,64,512]{2,1,0:T(8,128)S(1)}, u32[]{:S(2)}, u32[]{:S(2)}) collective-permute-start(f32[2,64,512]{2,1,0:T(8,128)S(1)} %get-tuple-element.35), channel_id=1, source_target_pairs={{0,2},{1,3},{2,0},{3,1},{4,6},{5,7},{6,4},{7,5},{8,10},{9,11},{10,... | collective-permute-start | bytes 786440 | tf_op jit(solution)/shard_map/ppermute | solution.py:218
  11.5 19.1 %collective-permute-start.6 = (f32[2,64,512]{2,1,0:T(8,128)S(1)}, f32[2,64,512]{2,1,0:T(8,128)S(1)}, u32[]{:S(2)}, u32[]{:S(2)}) collective-permute-start(f32[2,64,512]{2,1,0:T(8,128)S(1)} %get-tuple-element.36), channel_id=1, source_target_pairs={{0,1},{1,0},{2,3},{3,2},{4,5},{5,4},{6,7},{7,6},{8,9},{9,8},{10,11... | collective-permute-start | bytes 786440 | tf_op jit(solution)/shard_map/ppermute | solution.py:218
  19.7 17.1 %collective-permute-start.10 = (f32[2,64,512]{2,1,0:T(8,128)S(1)}, f32[2,64,512]{2,1,0:T(8,128)S(1)}, u32[]{:S(2)}, u32[]{:S(2)}) collective-permute-start(f32[2,64,512]{2,1,0:T(8,128)S(1)} %get-tuple-element.42), channel_id=1, source_target_pairs={{0,3},{1,2},{2,1},{3,0},{4,7},{5,6},{6,5},{7,4},{8,11},{9,10},{10,... | collective-permute-start | bytes 786440 | tf_op jit(solution)/shard_map/ppermute | solution.py:218
  31.3 7.8 %collective-permute-start.7 = (f32[4,128,128]{2,1,0:T(8,128)S(1)}, f32[4,128,128]{2,1,0:T(8,128)S(1)}, u32[]{:S(2)}, u32[]{:S(2)}) collective-permute-start(f32[4,128,128]{2,1,0:T(8,128)S(1)} %get-tuple-element.38), channel_id=1, source_target_pairs={{0,8},{1,9},{2,10},{3,11},{4,12},{5,13},{6,14},{7,15},{8,16},{9,17... | collective-permute-start | bytes 786440 | tf_op jit(solution)/shard_map/ppermute | solution.py:279
  34.8 7.5 %collective-permute-start.8 = (f32[2,64,512]{2,1,0:T(8,128)S(1)}, f32[2,64,512]{2,1,0:T(8,128)S(1)}, u32[]{:S(2)}, u32[]{:S(2)}) collective-permute-start(f32[2,64,512]{2,1,0:T(8,128)S(1)} %get-tuple-element.39), channel_id=1, source_target_pairs={{0,2},{1,3},{2,0},{3,1},{4,6},{5,7},{6,4},{7,5},{8,10},{9,11},{10,... | collective-permute-start | bytes 786440 | tf_op jit(solution)/shard_map/ppermute | solution.py:218
  35.4 7.8 %collective-permute-start.9 = (f32[2,64,512]{2,1,0:T(8,128)S(1)}, f32[2,64,512]{2,1,0:T(8,128)S(1)}, u32[]{:S(2)}, u32[]{:S(2)}) collective-permute-start(f32[2,64,512]{2,1,0:T(8,128)S(1)} %get-tuple-element.41), channel_id=1, source_target_pairs={{0,1},{1,0},{2,3},{3,2},{4,5},{5,4},{6,7},{7,6},{8,9},{9,8},{10,11... | collective-permute-start | bytes 786440 | tf_op jit(solution)/shard_map/ppermute | solution.py:218
  39.3 7.7 %collective-permute-start.17 = (f32[64,512]{1,0:T(8,128)S(1)}, f32[64,512]{1,0:T(8,128)S(1)}, u32[]{:S(2)}, u32[]{:S(2)}) collective-permute-start(f32[64,512]{1,0:T(8,128)S(1)} %get-tuple-element.50), channel_id=1, source_target_pairs={{0,3},{1,2},{2,1},{3,0},{4,7},{5,6},{6,5},{7,4},{8,11},{9,10},{10,... | collective-permute-start | bytes 393224 | tf_op jit(solution)/shard_map/ppermute | solution.py:218
  40.8 6.8 %collective-permute-start.16 = (f32[64,512]{1,0:T(8,128)S(1)}, f32[64,512]{1,0:T(8,128)S(1)}, u32[]{:S(2)}, u32[]{:S(2)}) collective-permute-start(f32[64,512]{1,0:T(8,128)S(1)} %get-tuple-element.43.refs_3_), channel_id=1, source_target_pairs={{0,7},{1,6},{2,5},{3,4},{4,3},{5,2},{6,1},{7,0},{8,15},{9,14},{10,... | collective-permute-start | bytes 393224 | tf_op jit(solution)/shard_map/ppermute | solution.py:218
  43.2 5.2 %copy-start.3 = (f32[4096]{0:T(1024)S(1)}, f32[4096]{0:T(1024)}, u32[]{:S(2)}) copy-start(f32[4096]{0:T(1024)} %param.9) | copy-start | bytes 49156
  43.6 6.5 %collective-permute-start.11 = (f32[64,512]{1,0:T(8,128)S(1)}, f32[64,512]{1,0:T(8,128)S(1)}, u32[]{:S(2)}, u32[]{:S(2)}) collective-permute-start(f32[64,512]{1,0:T(8,128)S(1)} %get-tuple-element.44), channel_id=1, source_target_pairs={{0,1},{1,0},{2,3},{3,2},{4,5},{5,4},{6,7},{7,6},{8,9},{9,8},{10,11... | collective-permute-start | bytes 393224 | tf_op jit(solution)/shard_map/ppermute | solution.py:218
  45.2 6.3 %collective-permute-start.12 = (f32[64,512]{1,0:T(8,128)S(1)}, f32[64,512]{1,0:T(8,128)S(1)}, u32[]{:S(2)}, u32[]{:S(2)}) collective-permute-start(f32[64,512]{1,0:T(8,128)S(1)} %get-tuple-element.45), channel_id=1, source_target_pairs={{0,2},{1,3},{2,0},{3,1},{4,6},{5,7},{6,4},{7,5},{8,10},{9,11},{10,... | collective-permute-start | bytes 393224 | tf_op jit(solution)/shard_map/ppermute | solution.py:218
  47.0 4.6 %collective-permute-start.13 = (f32[64,512]{1,0:T(8,128)S(1)}, f32[64,512]{1,0:T(8,128)S(1)}, u32[]{:S(2)}, u32[]{:S(2)}) collective-permute-start(f32[64,512]{1,0:T(8,128)S(1)} %get-tuple-element.46), channel_id=1, source_target_pairs={{0,4},{1,5},{2,6},{3,7},{4,0},{5,1},{6,2},{7,3},{8,12},{9,13},{10,... | collective-permute-start | bytes 393224 | tf_op jit(solution)/shard_map/ppermute | solution.py:218
  47.0 5.5 %collective-permute-start.14 = (f32[64,512]{1,0:T(8,128)S(1)}, f32[64,512]{1,0:T(8,128)S(1)}, u32[]{:S(2)}, u32[]{:S(2)}) collective-permute-start(f32[64,512]{1,0:T(8,128)S(1)} %get-tuple-element.47), channel_id=1, source_target_pairs={{0,5},{1,4},{2,7},{3,6},{4,1},{5,0},{6,3},{7,2},{8,13},{9,12},{10,... | collective-permute-start | bytes 393224 | tf_op jit(solution)/shard_map/ppermute | solution.py:218
  47.7 5.3 %collective-permute-start.15 = (f32[64,512]{1,0:T(8,128)S(1)}, f32[64,512]{1,0:T(8,128)S(1)}, u32[]{:S(2)}, u32[]{:S(2)}) collective-permute-start(f32[64,512]{1,0:T(8,128)S(1)} %get-tuple-element.48), channel_id=1, source_target_pairs={{0,6},{1,7},{2,4},{3,5},{4,2},{5,3},{6,0},{7,1},{8,14},{9,15},{10,... | collective-permute-start | bytes 393224 | tf_op jit(solution)/shard_map/ppermute | solution.py:218

commit v13 on v11

--- a/solution.py
+++ b/solution.py
@@ -244,7 +244,7 @@
         moved=2 * block_bytes,
     )(swapped)
     far_got = [swap(part, e) for e, part in zip(far_order, far_parts)] + [swapped]
-    gates = near_got[:-1]
+    gates = near_got[:1]
     *query_parts, table = call(
         functools.partial(join_queries, members, width, query_order, rows, docs, len(gates)),
         "join_queries",

time: 54.5 us -> 54.5 us (level)
  waiting for transfers between devices: 19.4 us -> 20.8 us
  starting transfers between devices: 24.5 us -> 23.1 us
    ppermute x17, starting transfers between devices: 21 us -> 19.6 us  [swap(): return lax.ppermute(part, everyone, pairs)]
    ppermute x17, waiting for transfers between devices: 17.2 us -> 18.6 us  [swap(): return lax.ppermute(part, everyone, pairs)]
  transfers between devices with their start and end apart: 18 -> 18, of which waited for: 13 -> 12; matrix products, arithmetic and copies ran while one was open for 0% -> 0% of each run, Pallas kernels for 15% -> 15%
where the time goes in v13:
time: 54.5 us; the launch traced here: 54.4 us
  starting transfers between devices  23.1 us (42%)
  waiting for transfers between devices  20.8 us (38%)
  Pallas kernels  10.3 us (19%)
    ppermute x17, starting transfers between devices, swap(): return lax.ppermute(part, everyone, pairs)  19.6 us
    ppermute x17, waiting for transfers between devices, swap(): return lax.ppermute(part, everyone, pairs)  18.6 us
    pallas_call x1, Pallas kernels, body(): call(functools.partial(inside, head_count, docs, rows), 'inside', shape(r...  4.93 us
    ppermute x1, starting transfers between devices, body(): moving = lax.ppermute(total, everyone, up)  3.5 us
    ppermute x1, waiting for transfers between devices, body(): moving = lax.ppermute(total, everyone, up)  2.19 us
    pallas_call x2, Pallas kernels, body(): call(functools.partial(finish, chosen, members, heads, rows), 'finish', s...  1.8 us
    pallas_call x1, Pallas kernels, body(): call(functools.partial(spread, members, width, near_order), 'spread', [sh...  1.48 us
  transfers between devices with their start and end apart: 18, of which 12 were waited for; matrix products, arithmetic and copies ran while one was open for 0% of the time, Pallas kernels for 15%

profile of v13, /device:TPU:0, one launch (start us, length us, event | category | flops | bytes accessed | tf_op | source)
XLA Modules:
  0.0 54.4 jit_solution(9393268583609613632)
XLA Ops:
  0.0 0.0 copy-start
  0.0 0.0 copy-start.2
  0.0 0.0 copy-start.1
  0.0 0.0 copy-start.4
  0.0 1.5 %spread.1 = (f32[2,64,512]{2,1,0:T(8,128)S(1)}, f32[2,64,512]{2,1,0:T(8,128)S(1)}, f32[2,64,512]{2,1,0:T(8,128)S(1)}, f32[2,64,512]{2,1,0:T(8,128)S(1)}, f32[4,3,64,512]{3,2,1,0:T(8,128)S(1)}) custom-call(bf16[64,4096]{1,0:T(8,128)(2,1)} %queries.5, bf16[64,4096]{1,0:T(8,128)(2,1)} %keys.3, bf16[64,4096]{1,0:T(8,128)(2,1)} %values.3), custom_call_target="tpu_custom_call" | custom-call | tf_op jit(solution)/shard_map/spread/pallas_call | solution.py:224
  1.5 0.5 collective-permute-start
  2.0 2.6 %collective-permute-start.1 = (f32[2,64,512]{2,1,0:T(8,128)S(1)}, f32[2,64,512]{2,1,0:T(8,128)S(1)}, u32[]{:S(2)}, u32[]{:S(2)}) collective-permute-start(f32[2,64,512]{2,1,0:T(8,128)S(1)} %get-tuple-element.29), channel_id=1, source_target_pairs={{0,2},{1,3},{2,0},{3,1},{4,6},{5,7},{6,4},{7,5},{8,10},{9,11},{10,... | collective-permute-start | bytes 786440 | tf_op jit(solution)/shard_map/ppermute | solution.py:218
  4.6 1.5 %collective-permute-start.2 = (f32[2,64,512]{2,1,0:T(8,128)S(1)}, f32[2,64,512]{2,1,0:T(8,128)S(1)}, u32[]{:S(2)}, u32[]{:S(2)}) collective-permute-start(f32[2,64,512]{2,1,0:T(8,128)S(1)} %get-tuple-element.31), channel_id=1, source_target_pairs={{0,1},{1,0},{2,3},{3,2},{4,5},{5,4},{6,7},{7,6},{8,9},{9,8},{10,11... | collective-permute-start | bytes 786440 | tf_op jit(solution)/shard_map/ppermute | solution.py:218
  6.1 0.0 collective-permute-start.3
  6.2 0.0 collective-permute-done.swapped.refs_7_
  6.2 0.1 forward.1
  6.2 2.9 %collective-permute-start.4 = (f32[2,64,512]{2,1,0:T(8,128)S(1)}, f32[2,64,512]{2,1,0:T(8,128)S(1)}, u32[]{:S(2)}, u32[]{:S(2)}) collective-permute-start(f32[2,64,512]{2,1,0:T(8,128)S(1)} %get-tuple-element.34), channel_id=1, source_target_pairs={{0,3},{1,2},{2,1},{3,0},{4,7},{5,6},{6,5},{7,4},{8,11},{9,10},{10,... | collective-permute-start | bytes 786440 | tf_op jit(solution)/shard_map/ppermute | solution.py:218
  9.2 0.5 collective-permute-start.5
  9.7 1.9 %collective-permute-done.1.refs_0_ = f32[2,64,512]{2,1,0:T(8,128)S(1)} collective-permute-done((f32[2,64,512]{2,1,0:T(8,128)S(1)}, f32[2,64,512]{2,1,0:T(8,128)S(1)}, u32[]{:S(2)}, u32[]{:S(2)}) %collective-permute-start.1) | collective-permute-done | bytes 262176 | tf_op jit(solution)/shard_map/ppermute | solution.py:218
  11.5 2.2 %collective-permute-start.6 = (f32[2,64,512]{2,1,0:T(8,128)S(1)}, f32[2,64,512]{2,1,0:T(8,128)S(1)}, u32[]{:S(2)}, u32[]{:S(2)}) collective-permute-start(f32[2,64,512]{2,1,0:T(8,128)S(1)} %get-tuple-element.36), channel_id=1, source_target_pairs={{0,1},{1,0},{2,3},{3,2},{4,5},{5,4},{6,7},{7,6},{8,9},{9,8},{10,11... | collective-permute-start | bytes 786440 | tf_op jit(solution)/shard_map/ppermute | solution.py:218
  13.7 0.0 copy-done
  13.7 0.0 copy-done.2
  13.7 0.0 copy-done.1
  13.8 0.0 copy-done.4
  13.8 4.9 %inside.1.refs_8_.own = f32[64,4096]{1,0:T(8,128)S(1)} custom-call(s32[16]{0:T(128)S(1)} %copy-done.4, bf16[64,4096]{1,0:T(8,128)(2,1)S(1)} %copy-done, bf16[64,4096]{1,0:T(8,128)(2,1)S(1)} %copy-done.1, bf16[64,4096]{1,0:T(8,128)(2,1)S(1)} %copy-done.2), custom_call_target="tpu_custom_call" | custom-call | flops 67108864 | bytes 3145728 | tf_op jit(solution)/shard_map/inside/pallas_call | solution.py:258
  18.7 0.8 %join_queries.1 = (f32[2,64,512]{2,1,0:T(8,128)S(1)}, f32[2,64,512]{2,1,0:T(8,128)S(1)}, f32[2,64,512]{2,1,0:T(8,128)S(1)}, f32[2,64,512]{2,1,0:T(8,128)S(1)}, s32[10,128]{1,0:T(8,128)S(1)}) custom-call(s32[16]{0:T(128)S(1)} %copy-done.4, bf16[64,4096]{1,0:T(8,128)(2,1)S(1)} %copy-done, f32[4,3,64,512]{3,2,1,0:T(8,128)S(1)} %collective-permute-done.swapped.refs_7_, ...), custom_call_target="tpu_custom_call" | custom-call | bytes 2097152 | tf_op jit(solution)/shard_map/join_queries/pallas_call | solution.py:248
  19.4 0.0 collective-permute-done.2.refs_1_
  19.5 1.6 %collective-permute-start.10 = (f32[2,64,512]{2,1,0:T(8,128)S(1)}, f32[2,64,512]{2,1,0:T(8,128)S(1)}, u32[]{:S(2)}, u32[]{:S(2)}) collective-permute-start(f32[2,64,512]{2,1,0:T(8,128)S(1)} %get-tuple-element.42), channel_id=1, source_target_pairs={{0,3},{1,2},{2,1},{3,0},{4,7},{5,6},{6,5},{7,4},{8,11},{9,10},{10,... | collective-permute-start | bytes 786440 | tf_op jit(solution)/shard_map/ppermute | solution.py:218
  21.0 0.0 collective-permute-done.3.refs_2_
  21.0 3.5 %collective-permute-done.4.refs_4_ = f32[2,64,512]{2,1,0:T(8,128)S(1)} collective-permute-done((f32[2,64,512]{2,1,0:T(8,128)S(1)}, f32[2,64,512]{2,1,0:T(8,128)S(1)}, u32[]{:S(2)}, u32[]{:S(2)}) %collective-permute-start.4) | collective-permute-done | bytes 262176 | tf_op jit(solution)/shard_map/ppermute | solution.py:218
  24.5 3.8 %collective-permute-done.5.refs_5_ = f32[2,64,512]{2,1,0:T(8,128)S(1)} collective-permute-done((f32[2,64,512]{2,1,0:T(8,128)S(1)}, f32[2,64,512]{2,1,0:T(8,128)S(1)}, u32[]{:S(2)}, u32[]{:S(2)}) %collective-permute-start.5) | collective-permute-done | bytes 262176 | tf_op jit(solution)/shard_map/ppermute | solution.py:218
  28.4 2.3 %collective-permute-done.6.refs_6_ = f32[2,64,512]{2,1,0:T(8,128)S(1)} collective-permute-done((f32[2,64,512]{2,1,0:T(8,128)S(1)}, f32[2,64,512]{2,1,0:T(8,128)S(1)}, u32[]{:S(2)}, u32[]{:S(2)}) %collective-permute-start.6) | collective-permute-done | bytes 262176 | tf_op jit(solution)/shard_map/ppermute | solution.py:218
  30.7 0.6 %gather_states.1 = (f32[8,4,128,128]{3,2,1,0:T(8,128)S(1)}, f32[4,128,128]{2,1,0:T(8,128)S(1)}) custom-call(s32[10,128]{1,0:T(8,128)S(1)} %get-tuple-element.30.table, f32[2,64,512]{2,1,0:T(8,128)S(1)} %collective-permute-done.1.refs_0_, f32[2,64,512]{2,1,0:T(8,128)S(1)} %collective-permute-done.2.refs_1_, f32[2,64,512]{2,1,0:T(8,128)S(1)} %collective-permute-done.3.refs_2_, ...), custom_call_target="tpu_custom_call" | custom-call | flops 67108864 | bytes 4194304 | tf_op jit(solution)/shard_map/gather_states/pallas_call | solution.py:268
  31.3 3.5 %collective-permute-start.7 = (f32[4,128,128]{2,1,0:T(8,128)S(1)}, f32[4,128,128]{2,1,0:T(8,128)S(1)}, u32[]{:S(2)}, u32[]{:S(2)}) collective-permute-start(f32[4,128,128]{2,1,0:T(8,128)S(1)} %get-tuple-element.38), channel_id=1, source_target_pairs={{0,8},{1,9},{2,10},{3,11},{4,12},{5,13},{6,14},{7,15},{8,16},{9,17... | collective-permute-start | bytes 786440 | tf_op jit(solution)/shard_map/ppermute | solution.py:279
  34.8 0.6 %collective-permute-start.8 = (f32[2,64,512]{2,1,0:T(8,128)S(1)}, f32[2,64,512]{2,1,0:T(8,128)S(1)}, u32[]{:S(2)}, u32[]{:S(2)}) collective-permute-start(f32[2,64,512]{2,1,0:T(8,128)S(1)} %get-tuple-element.39), channel_id=1, source_target_pairs={{0,2},{1,3},{2,0},{3,1},{4,6},{5,7},{6,4},{7,5},{8,10},{9,11},{10,... | collective-permute-start | bytes 786440 | tf_op jit(solution)/shard_map/ppermute | solution.py:218
  35.4 1.5 %collective-permute-start.9 = (f32[2,64,512]{2,1,0:T(8,128)S(1)}, f32[2,64,512]{2,1,0:T(8,128)S(1)}, u32[]{:S(2)}, u32[]{:S(2)}) collective-permute-start(f32[2,64,512]{2,1,0:T(8,128)S(1)} %get-tuple-element.41), channel_id=1, source_target_pairs={{0,1},{1,0},{2,3},{3,2},{4,5},{5,4},{6,7},{7,6},{8,9},{9,8},{10,11... | collective-permute-start | bytes 786440 | tf_op jit(solution)/shard_map/ppermute | solution.py:218
  36.9 0.0 collective-permute-done.10.refs_0_
  36.9 2.2 %collective-permute-done.7.earlier = f32[4,128,128]{2,1,0:T(8,128)S(1)} collective-permute-done((f32[4,128,128]{2,1,0:T(8,128)S(1)}, f32[4,128,128]{2,1,0:T(8,128)S(1)}, u32[]{:S(2)}, u32[]{:S(2)}) %collective-permute-start.7) | collective-permute-done | bytes 262176 | tf_op jit(solution)/shard_map/ppermute | solution.py:279
  39.1 0.2 reach_back.2
  39.3 1.6 %collective-permute-start.17 = (f32[64,512]{1,0:T(8,128)S(1)}, f32[64,512]{1,0:T(8,128)S(1)}, u32[]{:S(2)}, u32[]{:S(2)}) collective-permute-start(f32[64,512]{1,0:T(8,128)S(1)} %get-tuple-element.50), channel_id=1, source_target_pairs={{0,3},{1,2},{2,1},{3,0},{4,7},{5,6},{6,5},{7,4},{8,11},{9,10},{10,... | collective-permute-start | bytes 393224 | tf_op jit(solution)/shard_map/ppermute | solution.py:218
  40.8 0.0 collective-permute-start.16
  40.8 1.4 %collective-permute-done.8.refs_0_ = f32[2,64,512]{2,1,0:T(8,128)S(1)} collective-permute-done((f32[2,64,512]{2,1,0:T(8,128)S(1)}, f32[2,64,512]{2,1,0:T(8,128)S(1)}, u32[]{:S(2)}, u32[]{:S(2)}) %collective-permute-start.8) | collective-permute-done | bytes 262176 | tf_op jit(solution)/shard_map/ppermute | solution.py:218
  42.3 0.9 %collective-permute-done.9.refs_2_ = f32[2,64,512]{2,1,0:T(8,128)S(1)} collective-permute-done((f32[2,64,512]{2,1,0:T(8,128)S(1)}, f32[2,64,512]{2,1,0:T(8,128)S(1)}, u32[]{:S(2)}, u32[]{:S(2)}) %collective-permute-start.9) | collective-permute-done | bytes 262176 | tf_op jit(solution)/shard_map/ppermute | solution.py:218
  43.1 0.0 copy-start.3
  43.1 0.5 reach_back.3
  43.6 0.1 collective-permute-start.11
  43.7 1.6 %collective-permute-start.12 = (f32[64,512]{1,0:T(8,128)S(1)}, f32[64,512]{1,0:T(8,128)S(1)}, u32[]{:S(2)}, u32[]{:S(2)}) collective-permute-start(f32[64,512]{1,0:T(8,128)S(1)} %get-tuple-element.45), channel_id=1, source_target_pairs={{0,1},{1,0},{2,3},{3,2},{4,5},{5,4},{6,7},{7,6},{8,9},{9,8},{10,11... | collective-permute-start | bytes 393224 | tf_op jit(solution)/shard_map/ppermute | solution.py:218
  45.3 1.8 %collective-permute-start.13 = (f32[64,512]{1,0:T(8,128)S(1)}, f32[64,512]{1,0:T(8,128)S(1)}, u32[]{:S(2)}, u32[]{:S(2)}) collective-permute-start(f32[64,512]{1,0:T(8,128)S(1)} %get-tuple-element.46), channel_id=1, source_target_pairs={{0,2},{1,3},{2,0},{3,1},{4,6},{5,7},{6,4},{7,5},{8,10},{9,11},{10,... | collective-permute-start | bytes 393224 | tf_op jit(solution)/shard_map/ppermute | solution.py:218
  47.0 0.0 collective-permute-done.17.refs_2_
  47.0 0.0 collective-permute-start.14
  47.0 0.6 %collective-permute-done.16.refs_1_ = f32[64,512]{1,0:T(8,128)S(1)} collective-permute-done((f32[64,512]{1,0:T(8,128)S(1)}, f32[64,512]{1,0:T(8,128)S(1)}, u32[]{:S(2)}, u32[]{:S(2)}) %collective-permute-start.16) | collective-permute-done | bytes 131104 | tf_op jit(solution)/shard_map/ppermute | solution.py:218
  47.6 0.7 %collective-permute-start.15 = (f32[64,512]{1,0:T(8,128)S(1)}, f32[64,512]{1,0:T(8,128)S(1)}, u32[]{:S(2)}, u32[]{:S(2)}) collective-permute-start(f32[64,512]{1,0:T(8,128)S(1)} %get-tuple-element.48), channel_id=1, source_target_pairs={{0,6},{1,7},{2,4},{3,5},{4,2},{5,3},{6,0},{7,1},{8,14},{9,15},{10,... | collective-permute-start | bytes 393224 | tf_op jit(solution)/shard_map/ppermute | solution.py:218
  48.3 0.0 copy-done.3
  48.3 0.9 %finish.2.refs_5_ = bf16[64,4096]{1,0:T(8,128)(2,1)} custom-call(s32[10,128]{1,0:T(8,128)S(1)} %get-tuple-element.30.table, f32[64,4096]{1,0:T(8,128)S(1)} %inside.1.refs_8_.own, f32[1,4096]{1,0:T(1,128)S(1)} %bitcast.1, f32[64,512]{1,0:T(8,128)S(1)} %get-tuple-element.49.refs_0_, f32[64,512]{1,0:T(8,128)S(1)} %collective-permute-done.16.refs_1_, ...), custom_call_target="tpu_custom_call" | custom-call | bytes 2097152 | tf_op jit(solution)/shard_map/finish/pallas_call | solution.py:316
  49.2 0.0 collective-permute-done.11.refs_0_
  49.2 1.0 %collective-permute-done.12.refs_1_ = f32[64,512]{1,0:T(8,128)S(1)} collective-permute-done((f32[64,512]{1,0:T(8,128)S(1)}, f32[64,512]{1,0:T(8,128)S(1)}, u32[]{:S(2)}, u32[]{:S(2)}) %collective-permute-start.12) | collective-permute-done | bytes 131104 | tf_op jit(solution)/shard_map/ppermute | solution.py:218
  50.2 1.4 %collective-permute-done.13.refs_2_ = f32[64,512]{1,0:T(8,128)S(1)} collective-permute-done((f32[64,512]{1,0:T(8,128)S(1)}, f32[64,512]{1,0:T(8,128)S(1)}, u32[]{:S(2)}, u32[]{:S(2)}) %collective-permute-start.13) | collective-permute-done | bytes 131104 | tf_op jit(solution)/shard_map/ppermute | solution.py:218
  51.6 1.3 %collective-permute-done.14.refs_3_ = f32[64,512]{1,0:T(8,128)S(1)} collective-permute-done((f32[64,512]{1,0:T(8,128)S(1)}, f32[64,512]{1,0:T(8,128)S(1)}, u32[]{:S(2)}, u32[]{:S(2)}) %collective-permute-start.14) | collective-permute-done | bytes 131104 | tf_op jit(solution)/shard_map/ppermute | solution.py:218
  52.9 0.5 collective-permute-done.15.refs_4_
  53.4 0.9 %finish.3 = bf16[64,4096]{1,0:T(8,128)(2,1)} custom-call(s32[10,128]{1,0:T(8,128)S(1)} %get-tuple-element.30.table, f32[64,4096]{1,0:T(8,128)S(1)} %inside.1.refs_8_.own, f32[1,4096]{1,0:T(1,128)S(1)} %bitcast.2, f32[64,512]{1,0:T(8,128)S(1)} %collective-permute-done.11.refs_0_, ...), custom_call_target="tpu_custom_call", output_to_operand_aliasing={{}: (8, {})} | custom-call | bytes 2097152 | tf_op jit(solution)/shard_map/finish/pallas_call | solution.py:316
Async XLA Ops:
  0.0 13.7 %copy-start = (bf16[64,4096]{1,0:T(8,128)(2,1)S(1)}, bf16[64,4096]{1,0:T(8,128)(2,1)}, u32[]{:S(2)}) copy-start(bf16[64,4096]{1,0:T(8,128)(2,1)} %queries.5) | copy-start | bytes 1572868
  0.0 13.7 %copy-start.2 = (bf16[64,4096]{1,0:T(8,128)(2,1)S(1)}, bf16[64,4096]{1,0:T(8,128)(2,1)}, u32[]{:S(2)}) copy-start(bf16[64,4096]{1,0:T(8,128)(2,1)} %values.3) | copy-start | bytes 1572868
  0.0 13.7 %copy-start.1 = (bf16[64,4096]{1,0:T(8,128)(2,1)S(1)}, bf16[64,4096]{1,0:T(8,128)(2,1)}, u32[]{:S(2)}) copy-start(bf16[64,4096]{1,0:T(8,128)(2,1)} %keys.3) | copy-start | bytes 1572868
  0.0 13.7 %copy-start.4 = (s32[16]{0:T(128)S(1)}, s32[16]{0:T(128)}, u32[]{:S(2)}) copy-start(s32[16]{0:T(128)} %lengths.3) | copy-start | bytes 196
  1.5 4.7 %collective-permute-start = (f32[4,3,64,512]{3,2,1,0:T(8,128)S(1)}, f32[4,3,64,512]{3,2,1,0:T(8,128)S(1)}, u32[]{:S(2)}, u32[]{:S(2)}) collective-permute-start(f32[4,3,64,512]{3,2,1,0:T(8,128)S(1)} %get-tuple-element.28), channel_id=1, source_target_pairs={{0,4},{1,5},{2,6},{3,7},{4,0},{5,1},{6,2},{7,3},{8,12},{9,13},{10,... | collective-permute-start | bytes 4718600 | tf_op jit(solution)/shard_map/ppermute | solution.py:218
  2.0 9.5 %collective-permute-start.1 = (f32[2,64,512]{2,1,0:T(8,128)S(1)}, f32[2,64,512]{2,1,0:T(8,128)S(1)}, u32[]{:S(2)}, u32[]{:S(2)}) collective-permute-start(f32[2,64,512]{2,1,0:T(8,128)S(1)} %get-tuple-element.29), channel_id=1, source_target_pairs={{0,2},{1,3},{2,0},{3,1},{4,6},{5,7},{6,4},{7,5},{8,10},{9,11},{10,... | collective-permute-start | bytes 786440 | tf_op jit(solution)/shard_map/ppermute | solution.py:218
  4.6 14.8 %collective-permute-start.2 = (f32[2,64,512]{2,1,0:T(8,128)S(1)}, f32[2,64,512]{2,1,0:T(8,128)S(1)}, u32[]{:S(2)}, u32[]{:S(2)}) collective-permute-start(f32[2,64,512]{2,1,0:T(8,128)S(1)} %get-tuple-element.31), channel_id=1, source_target_pairs={{0,1},{1,0},{2,3},{3,2},{4,5},{5,4},{6,7},{7,6},{8,9},{9,8},{10,11... | collective-permute-start | bytes 786440 | tf_op jit(solution)/shard_map/ppermute | solution.py:218
  6.1 14.9 %collective-permute-start.3 = (f32[2,64,512]{2,1,0:T(8,128)S(1)}, f32[2,64,512]{2,1,0:T(8,128)S(1)}, u32[]{:S(2)}, u32[]{:S(2)}) collective-permute-start(f32[2,64,512]{2,1,0:T(8,128)S(1)} %get-tuple-element.32), channel_id=1, source_target_pairs={{0,3},{1,2},{2,1},{3,0},{4,7},{5,6},{6,5},{7,4},{8,11},{9,10},{10,... | collective-permute-start | bytes 786440 | tf_op jit(solution)/shard_map/ppermute | solution.py:218
  6.2 18.3 %collective-permute-start.4 = (f32[2,64,512]{2,1,0:T(8,128)S(1)}, f32[2,64,512]{2,1,0:T(8,128)S(1)}, u32[]{:S(2)}, u32[]{:S(2)}) collective-permute-start(f32[2,64,512]{2,1,0:T(8,128)S(1)} %get-tuple-element.34), channel_id=1, source_target_pairs={{0,3},{1,2},{2,1},{3,0},{4,7},{5,6},{6,5},{7,4},{8,11},{9,10},{10,... | collective-permute-start | bytes 786440 | tf_op jit(solution)/shard_map/ppermute | solution.py:218
  9.2 19.2 %collective-permute-start.5 = (f32[2,64,512]{2,1,0:T(8,128)S(1)}, f32[2,64,512]{2,1,0:T(8,128)S(1)}, u32[]{:S(2)}, u32[]{:S(2)}) collective-permute-start(f32[2,64,512]{2,1,0:T(8,128)S(1)} %get-tuple-element.35), channel_id=1, source_target_pairs={{0,2},{1,3},{2,0},{3,1},{4,6},{5,7},{6,4},{7,5},{8,10},{9,11},{10,... | collective-permute-start | bytes 786440 | tf_op jit(solution)/shard_map/ppermute | solution.py:218
  11.5 19.1 %collective-permute-start.6 = (f32[2,64,512]{2,1,0:T(8,128)S(1)}, f32[2,64,512]{2,1,0:T(8,128)S(1)}, u32[]{:S(2)}, u32[]{:S(2)}) collective-permute-start(f32[2,64,512]{2,1,0:T(8,128)S(1)} %get-tuple-element.36), channel_id=1, source_target_pairs={{0,1},{1,0},{2,3},{3,2},{4,5},{5,4},{6,7},{7,6},{8,9},{9,8},{10,11... | collective-permute-start | bytes 786440 | tf_op jit(solution)/shard_map/ppermute | solution.py:218
  19.5 17.4 %collective-permute-start.10 = (f32[2,64,512]{2,1,0:T(8,128)S(1)}, f32[2,64,512]{2,1,0:T(8,128)S(1)}, u32[]{:S(2)}, u32[]{:S(2)}) collective-permute-start(f32[2,64,512]{2,1,0:T(8,128)S(1)} %get-tuple-element.42), channel_id=1, source_target_pairs={{0,3},{1,2},{2,1},{3,0},{4,7},{5,6},{6,5},{7,4},{8,11},{9,10},{10,... | collective-permute-start | bytes 786440 | tf_op jit(solution)/shard_map/ppermute | solution.py:218
  31.3 7.8 %collective-permute-start.7 = (f32[4,128,128]{2,1,0:T(8,128)S(1)}, f32[4,128,128]{2,1,0:T(8,128)S(1)}, u32[]{:S(2)}, u32[]{:S(2)}) collective-permute-start(f32[4,128,128]{2,1,0:T(8,128)S(1)} %get-tuple-element.38), channel_id=1, source_target_pairs={{0,8},{1,9},{2,10},{3,11},{4,12},{5,13},{6,14},{7,15},{8,16},{9,17... | collective-permute-start | bytes 786440 | tf_op jit(solution)/shard_map/ppermute | solution.py:279
  34.8 7.5 %collective-permute-start.8 = (f32[2,64,512]{2,1,0:T(8,128)S(1)}, f32[2,64,512]{2,1,0:T(8,128)S(1)}, u32[]{:S(2)}, u32[]{:S(2)}) collective-permute-start(f32[2,64,512]{2,1,0:T(8,128)S(1)} %get-tuple-element.39), channel_id=1, source_target_pairs={{0,2},{1,3},{2,0},{3,1},{4,6},{5,7},{6,4},{7,5},{8,10},{9,11},{10,... | collective-permute-start | bytes 786440 | tf_op jit(solution)/shard_map/ppermute | solution.py:218
  35.4 7.8 %collective-permute-start.9 = (f32[2,64,512]{2,1,0:T(8,128)S(1)}, f32[2,64,512]{2,1,0:T(8,128)S(1)}, u32[]{:S(2)}, u32[]{:S(2)}) collective-permute-start(f32[2,64,512]{2,1,0:T(8,128)S(1)} %get-tuple-element.41), channel_id=1, source_target_pairs={{0,1},{1,0},{2,3},{3,2},{4,5},{5,4},{6,7},{7,6},{8,9},{9,8},{10,11... | collective-permute-start | bytes 786440 | tf_op jit(solution)/shard_map/ppermute | solution.py:218
  39.3 7.8 %collective-permute-start.17 = (f32[64,512]{1,0:T(8,128)S(1)}, f32[64,512]{1,0:T(8,128)S(1)}, u32[]{:S(2)}, u32[]{:S(2)}) collective-permute-start(f32[64,512]{1,0:T(8,128)S(1)} %get-tuple-element.50), channel_id=1, source_target_pairs={{0,3},{1,2},{2,1},{3,0},{4,7},{5,6},{6,5},{7,4},{8,11},{9,10},{10,... | collective-permute-start | bytes 393224 | tf_op jit(solution)/shard_map/ppermute | solution.py:218
  40.8 6.8 %collective-permute-start.16 = (f32[64,512]{1,0:T(8,128)S(1)}, f32[64,512]{1,0:T(8,128)S(1)}, u32[]{:S(2)}, u32[]{:S(2)}) collective-permute-start(f32[64,512]{1,0:T(8,128)S(1)} %get-tuple-element.43.refs_3_), channel_id=1, source_target_pairs={{0,7},{1,6},{2,5},{3,4},{4,3},{5,2},{6,1},{7,0},{8,15},{9,14},{10,... | collective-permute-start | bytes 393224 | tf_op jit(solution)/shard_map/ppermute | solution.py:218
  43.1 5.1 %copy-start.3 = (f32[4096]{0:T(1024)S(1)}, f32[4096]{0:T(1024)}, u32[]{:S(2)}) copy-start(f32[4096]{0:T(1024)} %param.9) | copy-start | bytes 49156
  43.6 5.5 %collective-permute-start.11 = (f32[64,512]{1,0:T(8,128)S(1)}, f32[64,512]{1,0:T(8,128)S(1)}, u32[]{:S(2)}, u32[]{:S(2)}) collective-permute-start(f32[64,512]{1,0:T(8,128)S(1)} %get-tuple-element.44), channel_id=1, source_target_pairs={{0,4},{1,5},{2,6},{3,7},{4,0},{5,1},{6,2},{7,3},{8,12},{9,13},{10,... | collective-permute-start | bytes 393224 | tf_op jit(solution)/shard_map/ppermute | solution.py:218
  43.7 6.5 %collective-permute-start.12 = (f32[64,512]{1,0:T(8,128)S(1)}, f32[64,512]{1,0:T(8,128)S(1)}, u32[]{:S(2)}, u32[]{:S(2)}) collective-permute-start(f32[64,512]{1,0:T(8,128)S(1)} %get-tuple-element.45), channel_id=1, source_target_pairs={{0,1},{1,0},{2,3},{3,2},{4,5},{5,4},{6,7},{7,6},{8,9},{9,8},{10,11... | collective-permute-start | bytes 393224 | tf_op jit(solution)/shard_map/ppermute | solution.py:218
  45.3 6.3 %collective-permute-start.13 = (f32[64,512]{1,0:T(8,128)S(1)}, f32[64,512]{1,0:T(8,128)S(1)}, u32[]{:S(2)}, u32[]{:S(2)}) collective-permute-start(f32[64,512]{1,0:T(8,128)S(1)} %get-tuple-element.46), channel_id=1, source_target_pairs={{0,2},{1,3},{2,0},{3,1},{4,6},{5,7},{6,4},{7,5},{8,10},{9,11},{10,... | collective-permute-start | bytes 393224 | tf_op jit(solution)/shard_map/ppermute | solution.py:218
  47.0 5.9 %collective-permute-start.14 = (f32[64,512]{1,0:T(8,128)S(1)}, f32[64,512]{1,0:T(8,128)S(1)}, u32[]{:S(2)}, u32[]{:S(2)}) collective-permute-start(f32[64,512]{1,0:T(8,128)S(1)} %get-tuple-element.47), channel_id=1, source_target_pairs={{0,5},{1,4},{2,7},{3,6},{4,1},{5,0},{6,3},{7,2},{8,13},{9,12},{10,... | collective-permute-start | bytes 393224 | tf_op jit(solution)/shard_map/ppermute | solution.py:218
  47.6 5.8 %collective-permute-start.15 = (f32[64,512]{1,0:T(8,128)S(1)}, f32[64,512]{1,0:T(8,128)S(1)}, u32[]{:S(2)}, u32[]{:S(2)}) collective-permute-start(f32[64,512]{1,0:T(8,128)S(1)} %get-tuple-element.48), channel_id=1, source_target_pairs={{0,6},{1,7},{2,4},{3,5},{4,2},{5,3},{6,0},{7,1},{8,14},{9,15},{10,... | collective-permute-start | bytes 393224 | tf_op jit(solution)/shard_map/ppermute | solution.py:218

commit v14 on v11

--- a/solution.py
+++ b/solution.py
@@ -218,7 +218,7 @@
         return lax.ppermute(part, everyone, pairs)
 
     near_order = ranked(half, 2, 1, 3, 0)
-    far_order = ranked(half, 3, 2, 1, 0)[:-1]
+    far_order = ranked(half, 2, 3, 1, 0)[:-1]
     query_order = ranked(half, 3, 2, 1, 0)
     block_bytes = rows * columns * 4
     parts = call(

time: 54.5 us -> 54.5 us (level)
  transfers between devices with their start and end apart: 18 -> 18, of which waited for: 13 -> 12; matrix products, arithmetic and copies ran while one was open for 0% -> 0% of each run, Pallas kernels for 15% -> 15%
where the time goes in v14:
time: 54.5 us; the launch traced here: 54.4 us
  starting transfers between devices  24.2 us (44%)
  waiting for transfers between devices  19.7 us (36%)
  Pallas kernels  10.3 us (19%)
    ppermute x17, starting transfers between devices, swap(): return lax.ppermute(part, everyone, pairs)  20.7 us
    ppermute x17, waiting for transfers between devices, swap(): return lax.ppermute(part, everyone, pairs)  17.5 us
    pallas_call x1, Pallas kernels, body(): call(functools.partial(inside, head_count, docs, rows), 'inside', shape(r...  4.93 us
    ppermute x1, starting transfers between devices, body(): moving = lax.ppermute(total, everyone, up)  3.5 us
    ppermute x1, waiting for transfers between devices, body(): moving = lax.ppermute(total, everyone, up)  2.19 us
    pallas_call x2, Pallas kernels, body(): call(functools.partial(finish, chosen, members, heads, rows), 'finish', s...  1.8 us
    pallas_call x1, Pallas kernels, body(): call(functools.partial(spread, members, width, near_order), 'spread', [sh...  1.48 us
  transfers between devices with their start and end apart: 18, of which 12 were waited for; matrix products, arithmetic and copies ran while one was open for 0% of the time, Pallas kernels for 15%

profile of v14, /device:TPU:0, one launch (start us, length us, event | category | flops | bytes accessed | tf_op | source)
XLA Modules:
  0.0 54.4 jit_solution(18336858361552173697)
XLA Ops:
  0.0 0.0 copy-start
  0.0 0.0 copy-start.2
  0.0 0.0 copy-start.1
  0.0 0.0 copy-start.4
  0.0 1.5 %spread.1 = (f32[2,64,512]{2,1,0:T(8,128)S(1)}, f32[2,64,512]{2,1,0:T(8,128)S(1)}, f32[2,64,512]{2,1,0:T(8,128)S(1)}, f32[2,64,512]{2,1,0:T(8,128)S(1)}, f32[4,3,64,512]{3,2,1,0:T(8,128)S(1)}) custom-call(bf16[64,4096]{1,0:T(8,128)(2,1)} %queries.5, bf16[64,4096]{1,0:T(8,128)(2,1)} %keys.3, bf16[64,4096]{1,0:T(8,128)(2,1)} %values.3), custom_call_target="tpu_custom_call" | custom-call | tf_op jit(solution)/shard_map/spread/pallas_call | solution.py:224
  1.5 0.5 collective-permute-start
  2.0 2.6 %collective-permute-start.1 = (f32[2,64,512]{2,1,0:T(8,128)S(1)}, f32[2,64,512]{2,1,0:T(8,128)S(1)}, u32[]{:S(2)}, u32[]{:S(2)}) collective-permute-start(f32[2,64,512]{2,1,0:T(8,128)S(1)} %get-tuple-element.29), channel_id=1, source_target_pairs={{0,2},{1,3},{2,0},{3,1},{4,6},{5,7},{6,4},{7,5},{8,10},{9,11},{10,... | collective-permute-start | bytes 786440 | tf_op jit(solution)/shard_map/ppermute | solution.py:218
  4.6 1.5 %collective-permute-start.2 = (f32[2,64,512]{2,1,0:T(8,128)S(1)}, f32[2,64,512]{2,1,0:T(8,128)S(1)}, u32[]{:S(2)}, u32[]{:S(2)}) collective-permute-start(f32[2,64,512]{2,1,0:T(8,128)S(1)} %get-tuple-element.30), channel_id=1, source_target_pairs={{0,1},{1,0},{2,3},{3,2},{4,5},{5,4},{6,7},{7,6},{8,9},{9,8},{10,11... | collective-permute-start | bytes 786440 | tf_op jit(solution)/shard_map/ppermute | solution.py:218
  6.1 0.0 collective-permute-start.3
  6.2 0.0 collective-permute-done.swapped.refs_7_
  6.2 0.1 forward.1
  6.2 2.0 %collective-permute-start.4 = (f32[2,64,512]{2,1,0:T(8,128)S(1)}, f32[2,64,512]{2,1,0:T(8,128)S(1)}, u32[]{:S(2)}, u32[]{:S(2)}) collective-permute-start(f32[2,64,512]{2,1,0:T(8,128)S(1)} %get-tuple-element.34), channel_id=1, source_target_pairs={{0,2},{1,3},{2,0},{3,1},{4,6},{5,7},{6,4},{7,5},{8,10},{9,11},{10,... | collective-permute-start | bytes 786440 | tf_op jit(solution)/shard_map/ppermute | solution.py:218
  8.2 1.4 %collective-permute-start.5 = (f32[2,64,512]{2,1,0:T(8,128)S(1)}, f32[2,64,512]{2,1,0:T(8,128)S(1)}, u32[]{:S(2)}, u32[]{:S(2)}) collective-permute-start(f32[2,64,512]{2,1,0:T(8,128)S(1)} %get-tuple-element.35), channel_id=1, source_target_pairs={{0,3},{1,2},{2,1},{3,0},{4,7},{5,6},{6,5},{7,4},{8,11},{9,10},{10,... | collective-permute-start | bytes 786440 | tf_op jit(solution)/shard_map/ppermute | solution.py:218
  9.7 2.1 %collective-permute-done.1.refs_0_ = f32[2,64,512]{2,1,0:T(8,128)S(1)} collective-permute-done((f32[2,64,512]{2,1,0:T(8,128)S(1)}, f32[2,64,512]{2,1,0:T(8,128)S(1)}, u32[]{:S(2)}, u32[]{:S(2)}) %collective-permute-start.1) | collective-permute-done | bytes 262176 | tf_op jit(solution)/shard_map/ppermute | solution.py:218
  11.8 2.0 %collective-permute-start.6 = (f32[2,64,512]{2,1,0:T(8,128)S(1)}, f32[2,64,512]{2,1,0:T(8,128)S(1)}, u32[]{:S(2)}, u32[]{:S(2)}) collective-permute-start(f32[2,64,512]{2,1,0:T(8,128)S(1)} %get-tuple-element.36), channel_id=1, source_target_pairs={{0,1},{1,0},{2,3},{3,2},{4,5},{5,4},{6,7},{7,6},{8,9},{9,8},{10,11... | collective-permute-start | bytes 786440 | tf_op jit(solution)/shard_map/ppermute | solution.py:218
  13.7 0.0 copy-done
  13.7 0.0 copy-done.2
  13.7 0.0 copy-done.1
  13.8 0.0 copy-done.4
  13.8 4.9 %inside.1.refs_8_.own = f32[64,4096]{1,0:T(8,128)S(1)} custom-call(s32[16]{0:T(128)S(1)} %copy-done.4, bf16[64,4096]{1,0:T(8,128)(2,1)S(1)} %copy-done, bf16[64,4096]{1,0:T(8,128)(2,1)S(1)} %copy-done.1, bf16[64,4096]{1,0:T(8,128)(2,1)S(1)} %copy-done.2), custom_call_target="tpu_custom_call" | custom-call | flops 67108864 | bytes 3145728 | tf_op jit(solution)/shard_map/inside/pallas_call | solution.py:258
  18.7 0.0 collective-permute-done.2.refs_1_
  18.7 0.3 collective-permute-done.3.refs_2_
  19.0 0.7 %join_queries.1 = (f32[2,64,512]{2,1,0:T(8,128)S(1)}, f32[2,64,512]{2,1,0:T(8,128)S(1)}, f32[2,64,512]{2,1,0:T(8,128)S(1)}, f32[2,64,512]{2,1,0:T(8,128)S(1)}, s32[10,128]{1,0:T(8,128)S(1)}) custom-call(s32[16]{0:T(128)S(1)} %copy-done.4, bf16[64,4096]{1,0:T(8,128)(2,1)S(1)} %copy-done, f32[4,3,64,512]{3,2,1,0:T(8,128)S(1)} %collective-permute-done.swapped.refs_7_, ...), custom_call_target="tpu_custom_call" | custom-call | bytes 2097152 | tf_op jit(solution)/shard_map/join_queries/pallas_call | solution.py:248
  19.7 3.0 %collective-permute-start.10 = (f32[2,64,512]{2,1,0:T(8,128)S(1)}, f32[2,64,512]{2,1,0:T(8,128)S(1)}, u32[]{:S(2)}, u32[]{:S(2)}) collective-permute-start(f32[2,64,512]{2,1,0:T(8,128)S(1)} %get-tuple-element.42), channel_id=1, source_target_pairs={{0,3},{1,2},{2,1},{3,0},{4,7},{5,6},{6,5},{7,4},{8,11},{9,10},{10,... | collective-permute-start | bytes 786440 | tf_op jit(solution)/shard_map/ppermute | solution.py:218
  22.7 5.7 %collective-permute-done.4.refs_4_ = f32[2,64,512]{2,1,0:T(8,128)S(1)} collective-permute-done((f32[2,64,512]{2,1,0:T(8,128)S(1)}, f32[2,64,512]{2,1,0:T(8,128)S(1)}, u32[]{:S(2)}, u32[]{:S(2)}) %collective-permute-start.4) | collective-permute-done | bytes 262176 | tf_op jit(solution)/shard_map/ppermute | solution.py:218
  28.4 0.0 collective-permute-done.5.refs_5_
  28.4 2.3 %collective-permute-done.6.refs_6_ = f32[2,64,512]{2,1,0:T(8,128)S(1)} collective-permute-done((f32[2,64,512]{2,1,0:T(8,128)S(1)}, f32[2,64,512]{2,1,0:T(8,128)S(1)}, u32[]{:S(2)}, u32[]{:S(2)}) %collective-permute-start.6) | collective-permute-done | bytes 262176 | tf_op jit(solution)/shard_map/ppermute | solution.py:218
  30.7 0.6 %gather_states.1 = (f32[8,4,128,128]{3,2,1,0:T(8,128)S(1)}, f32[4,128,128]{2,1,0:T(8,128)S(1)}) custom-call(s32[10,128]{1,0:T(8,128)S(1)} %get-tuple-element.32.table, f32[2,64,512]{2,1,0:T(8,128)S(1)} %collective-permute-done.1.refs_0_, f32[2,64,512]{2,1,0:T(8,128)S(1)} %collective-permute-done.2.refs_1_, f32[2,64,512]{2,1,0:T(8,128)S(1)} %collective-permute-done.3.refs_2_, ...), custom_call_target="tpu_custom_call" | custom-call | flops 67108864 | bytes 4194304 | tf_op jit(solution)/shard_map/gather_states/pallas_call | solution.py:268
  31.3 3.5 %collective-permute-start.7 = (f32[4,128,128]{2,1,0:T(8,128)S(1)}, f32[4,128,128]{2,1,0:T(8,128)S(1)}, u32[]{:S(2)}, u32[]{:S(2)}) collective-permute-start(f32[4,128,128]{2,1,0:T(8,128)S(1)} %get-tuple-element.38), channel_id=1, source_target_pairs={{0,8},{1,9},{2,10},{3,11},{4,12},{5,13},{6,14},{7,15},{8,16},{9,17... | collective-permute-start | bytes 786440 | tf_op jit(solution)/shard_map/ppermute | solution.py:279
  34.8 0.6 %collective-permute-start.8 = (f32[2,64,512]{2,1,0:T(8,128)S(1)}, f32[2,64,512]{2,1,0:T(8,128)S(1)}, u32[]{:S(2)}, u32[]{:S(2)}) collective-permute-start(f32[2,64,512]{2,1,0:T(8,128)S(1)} %get-tuple-element.39), channel_id=1, source_target_pairs={{0,2},{1,3},{2,0},{3,1},{4,6},{5,7},{6,4},{7,5},{8,10},{9,11},{10,... | collective-permute-start | bytes 786440 | tf_op jit(solution)/shard_map/ppermute | solution.py:218
  35.4 1.5 %collective-permute-start.9 = (f32[2,64,512]{2,1,0:T(8,128)S(1)}, f32[2,64,512]{2,1,0:T(8,128)S(1)}, u32[]{:S(2)}, u32[]{:S(2)}) collective-permute-start(f32[2,64,512]{2,1,0:T(8,128)S(1)} %get-tuple-element.41), channel_id=1, source_target_pairs={{0,1},{1,0},{2,3},{3,2},{4,5},{5,4},{6,7},{7,6},{8,9},{9,8},{10,11... | collective-permute-start | bytes 786440 | tf_op jit(solution)/shard_map/ppermute | solution.py:218
  36.9 0.0 collective-permute-done.10.refs_0_
  36.9 2.2 %collective-permute-done.7.earlier = f32[4,128,128]{2,1,0:T(8,128)S(1)} collective-permute-done((f32[4,128,128]{2,1,0:T(8,128)S(1)}, f32[4,128,128]{2,1,0:T(8,128)S(1)}, u32[]{:S(2)}, u32[]{:S(2)}) %collective-permute-start.7) | collective-permute-done | bytes 262176 | tf_op jit(solution)/shard_map/ppermute | solution.py:279
  39.1 0.2 reach_back.2
  39.3 1.6 %collective-permute-start.17 = (f32[64,512]{1,0:T(8,128)S(1)}, f32[64,512]{1,0:T(8,128)S(1)}, u32[]{:S(2)}, u32[]{:S(2)}) collective-permute-start(f32[64,512]{1,0:T(8,128)S(1)} %get-tuple-element.50), channel_id=1, source_target_pairs={{0,3},{1,2},{2,1},{3,0},{4,7},{5,6},{6,5},{7,4},{8,11},{9,10},{10,... | collective-permute-start | bytes 393224 | tf_op jit(solution)/shard_map/ppermute | solution.py:218
  40.8 0.0 collective-permute-start.16
  40.9 1.4 %collective-permute-done.8.refs_0_ = f32[2,64,512]{2,1,0:T(8,128)S(1)} collective-permute-done((f32[2,64,512]{2,1,0:T(8,128)S(1)}, f32[2,64,512]{2,1,0:T(8,128)S(1)}, u32[]{:S(2)}, u32[]{:S(2)}) %collective-permute-start.8) | collective-permute-done | bytes 262176 | tf_op jit(solution)/shard_map/ppermute | solution.py:218
  42.3 0.9 %collective-permute-done.9.refs_2_ = f32[2,64,512]{2,1,0:T(8,128)S(1)} collective-permute-done((f32[2,64,512]{2,1,0:T(8,128)S(1)}, f32[2,64,512]{2,1,0:T(8,128)S(1)}, u32[]{:S(2)}, u32[]{:S(2)}) %collective-permute-start.9) | collective-permute-done | bytes 262176 | tf_op jit(solution)/shard_map/ppermute | solution.py:218
  43.1 0.0 copy-start.3
  43.2 0.5 reach_back.3
  43.6 0.1 collective-permute-start.11
  43.7 1.6 %collective-permute-start.12 = (f32[64,512]{1,0:T(8,128)S(1)}, f32[64,512]{1,0:T(8,128)S(1)}, u32[]{:S(2)}, u32[]{:S(2)}) collective-permute-start(f32[64,512]{1,0:T(8,128)S(1)} %get-tuple-element.45), channel_id=1, source_target_pairs={{0,1},{1,0},{2,3},{3,2},{4,5},{5,4},{6,7},{7,6},{8,9},{9,8},{10,11... | collective-permute-start | bytes 393224 | tf_op jit(solution)/shard_map/ppermute | solution.py:218
  45.3 1.8 %collective-permute-start.13 = (f32[64,512]{1,0:T(8,128)S(1)}, f32[64,512]{1,0:T(8,128)S(1)}, u32[]{:S(2)}, u32[]{:S(2)}) collective-permute-start(f32[64,512]{1,0:T(8,128)S(1)} %get-tuple-element.46), channel_id=1, source_target_pairs={{0,2},{1,3},{2,0},{3,1},{4,6},{5,7},{6,4},{7,5},{8,10},{9,11},{10,... | collective-permute-start | bytes 393224 | tf_op jit(solution)/shard_map/ppermute | solution.py:218
  47.0 0.0 collective-permute-done.17.refs_2_
  47.0 0.0 collective-permute-start.14
  47.0 0.6 %collective-permute-done.16.refs_1_ = f32[64,512]{1,0:T(8,128)S(1)} collective-permute-done((f32[64,512]{1,0:T(8,128)S(1)}, f32[64,512]{1,0:T(8,128)S(1)}, u32[]{:S(2)}, u32[]{:S(2)}) %collective-permute-start.16) | collective-permute-done | bytes 131104 | tf_op jit(solution)/shard_map/ppermute | solution.py:218
  47.6 0.7 %collective-permute-start.15 = (f32[64,512]{1,0:T(8,128)S(1)}, f32[64,512]{1,0:T(8,128)S(1)}, u32[]{:S(2)}, u32[]{:S(2)}) collective-permute-start(f32[64,512]{1,0:T(8,128)S(1)} %get-tuple-element.48), channel_id=1, source_target_pairs={{0,6},{1,7},{2,4},{3,5},{4,2},{5,3},{6,0},{7,1},{8,14},{9,15},{10,... | collective-permute-start | bytes 393224 | tf_op jit(solution)/shard_map/ppermute | solution.py:218
  48.3 0.0 copy-done.3
  48.3 0.9 %finish.2.refs_5_ = bf16[64,4096]{1,0:T(8,128)(2,1)} custom-call(s32[10,128]{1,0:T(8,128)S(1)} %get-tuple-element.32.table, f32[64,4096]{1,0:T(8,128)S(1)} %inside.1.refs_8_.own, f32[1,4096]{1,0:T(1,128)S(1)} %bitcast.1, f32[64,512]{1,0:T(8,128)S(1)} %get-tuple-element.49.refs_0_, f32[64,512]{1,0:T(8,128)S(1)} %collective-permute-done.16.refs_1_, ...), custom_call_target="tpu_custom_call" | custom-call | bytes 2097152 | tf_op jit(solution)/shard_map/finish/pallas_call | solution.py:316
  49.2 0.0 collective-permute-done.11.refs_0_
  49.2 1.0 %collective-permute-done.12.refs_1_ = f32[64,512]{1,0:T(8,128)S(1)} collective-permute-done((f32[64,512]{1,0:T(8,128)S(1)}, f32[64,512]{1,0:T(8,128)S(1)}, u32[]{:S(2)}, u32[]{:S(2)}) %collective-permute-start.12) | collective-permute-done | bytes 131104 | tf_op jit(solution)/shard_map/ppermute | solution.py:218
  50.2 1.4 %collective-permute-done.13.refs_2_ = f32[64,512]{1,0:T(8,128)S(1)} collective-permute-done((f32[64,512]{1,0:T(8,128)S(1)}, f32[64,512]{1,0:T(8,128)S(1)}, u32[]{:S(2)}, u32[]{:S(2)}) %collective-permute-start.13) | collective-permute-done | bytes 131104 | tf_op jit(solution)/shard_map/ppermute | solution.py:218
  51.6 1.3 %collective-permute-done.14.refs_3_ = f32[64,512]{1,0:T(8,128)S(1)} collective-permute-done((f32[64,512]{1,0:T(8,128)S(1)}, f32[64,512]{1,0:T(8,128)S(1)}, u32[]{:S(2)}, u32[]{:S(2)}) %collective-permute-start.14) | collective-permute-done | bytes 131104 | tf_op jit(solution)/shard_map/ppermute | solution.py:218
  52.9 0.5 collective-permute-done.15.refs_4_
  53.4 0.9 %finish.3 = bf16[64,4096]{1,0:T(8,128)(2,1)} custom-call(s32[10,128]{1,0:T(8,128)S(1)} %get-tuple-element.32.table, f32[64,4096]{1,0:T(8,128)S(1)} %inside.1.refs_8_.own, f32[1,4096]{1,0:T(1,128)S(1)} %bitcast.2, f32[64,512]{1,0:T(8,128)S(1)} %collective-permute-done.11.refs_0_, ...), custom_call_target="tpu_custom_call", output_to_operand_aliasing={{}: (8, {})} | custom-call | bytes 2097152 | tf_op jit(solution)/shard_map/finish/pallas_call | solution.py:316
Async XLA Ops:
  0.0 13.7 %copy-start = (bf16[64,4096]{1,0:T(8,128)(2,1)S(1)}, bf16[64,4096]{1,0:T(8,128)(2,1)}, u32[]{:S(2)}) copy-start(bf16[64,4096]{1,0:T(8,128)(2,1)} %queries.5) | copy-start | bytes 1572868
  0.0 13.7 %copy-start.2 = (bf16[64,4096]{1,0:T(8,128)(2,1)S(1)}, bf16[64,4096]{1,0:T(8,128)(2,1)}, u32[]{:S(2)}) copy-start(bf16[64,4096]{1,0:T(8,128)(2,1)} %values.3) | copy-start | bytes 1572868
  0.0 13.7 %copy-start.1 = (bf16[64,4096]{1,0:T(8,128)(2,1)S(1)}, bf16[64,4096]{1,0:T(8,128)(2,1)}, u32[]{:S(2)}) copy-start(bf16[64,4096]{1,0:T(8,128)(2,1)} %keys.3) | copy-start | bytes 1572868
  0.0 13.7 %copy-start.4 = (s32[16]{0:T(128)S(1)}, s32[16]{0:T(128)}, u32[]{:S(2)}) copy-start(s32[16]{0:T(128)} %lengths.3) | copy-start | bytes 196
  1.5 4.7 %collective-permute-start = (f32[4,3,64,512]{3,2,1,0:T(8,128)S(1)}, f32[4,3,64,512]{3,2,1,0:T(8,128)S(1)}, u32[]{:S(2)}, u32[]{:S(2)}) collective-permute-start(f32[4,3,64,512]{3,2,1,0:T(8,128)S(1)} %get-tuple-element.28), channel_id=1, source_target_pairs={{0,4},{1,5},{2,6},{3,7},{4,0},{5,1},{6,2},{7,3},{8,12},{9,13},{10,... | collective-permute-start | bytes 4718600 | tf_op jit(solution)/shard_map/ppermute | solution.py:218
  2.0 9.8 %collective-permute-start.1 = (f32[2,64,512]{2,1,0:T(8,128)S(1)}, f32[2,64,512]{2,1,0:T(8,128)S(1)}, u32[]{:S(2)}, u32[]{:S(2)}) collective-permute-start(f32[2,64,512]{2,1,0:T(8,128)S(1)} %get-tuple-element.29), channel_id=1, source_target_pairs={{0,2},{1,3},{2,0},{3,1},{4,6},{5,7},{6,4},{7,5},{8,10},{9,11},{10,... | collective-permute-start | bytes 786440 | tf_op jit(solution)/shard_map/ppermute | solution.py:218
  4.6 14.1 %collective-permute-start.2 = (f32[2,64,512]{2,1,0:T(8,128)S(1)}, f32[2,64,512]{2,1,0:T(8,128)S(1)}, u32[]{:S(2)}, u32[]{:S(2)}) collective-permute-start(f32[2,64,512]{2,1,0:T(8,128)S(1)} %get-tuple-element.30), channel_id=1, source_target_pairs={{0,1},{1,0},{2,3},{3,2},{4,5},{5,4},{6,7},{7,6},{8,9},{9,8},{10,11... | collective-permute-start | bytes 786440 | tf_op jit(solution)/shard_map/ppermute | solution.py:218
  6.1 12.9 %collective-permute-start.3 = (f32[2,64,512]{2,1,0:T(8,128)S(1)}, f32[2,64,512]{2,1,0:T(8,128)S(1)}, u32[]{:S(2)}, u32[]{:S(2)}) collective-permute-start(f32[2,64,512]{2,1,0:T(8,128)S(1)} %get-tuple-element.31), channel_id=1, source_target_pairs={{0,3},{1,2},{2,1},{3,0},{4,7},{5,6},{6,5},{7,4},{8,11},{9,10},{10,... | collective-permute-start | bytes 786440 | tf_op jit(solution)/shard_map/ppermute | solution.py:218
  6.2 22.2 %collective-permute-start.4 = (f32[2,64,512]{2,1,0:T(8,128)S(1)}, f32[2,64,512]{2,1,0:T(8,128)S(1)}, u32[]{:S(2)}, u32[]{:S(2)}) collective-permute-start(f32[2,64,512]{2,1,0:T(8,128)S(1)} %get-tuple-element.34), channel_id=1, source_target_pairs={{0,2},{1,3},{2,0},{3,1},{4,6},{5,7},{6,4},{7,5},{8,10},{9,11},{10,... | collective-permute-start | bytes 786440 | tf_op jit(solution)/shard_map/ppermute | solution.py:218
  8.2 20.1 %collective-permute-start.5 = (f32[2,64,512]{2,1,0:T(8,128)S(1)}, f32[2,64,512]{2,1,0:T(8,128)S(1)}, u32[]{:S(2)}, u32[]{:S(2)}) collective-permute-start(f32[2,64,512]{2,1,0:T(8,128)S(1)} %get-tuple-element.35), channel_id=1, source_target_pairs={{0,3},{1,2},{2,1},{3,0},{4,7},{5,6},{6,5},{7,4},{8,11},{9,10},{10,... | collective-permute-start | bytes 786440 | tf_op jit(solution)/shard_map/ppermute | solution.py:218
  11.8 18.9 %collective-permute-start.6 = (f32[2,64,512]{2,1,0:T(8,128)S(1)}, f32[2,64,512]{2,1,0:T(8,128)S(1)}, u32[]{:S(2)}, u32[]{:S(2)}) collective-permute-start(f32[2,64,512]{2,1,0:T(8,128)S(1)} %get-tuple-element.36), channel_id=1, source_target_pairs={{0,1},{1,0},{2,3},{3,2},{4,5},{5,4},{6,7},{7,6},{8,9},{9,8},{10,11... | collective-permute-start | bytes 786440 | tf_op jit(solution)/shard_map/ppermute | solution.py:218
  19.7 17.1 %collective-permute-start.10 = (f32[2,64,512]{2,1,0:T(8,128)S(1)}, f32[2,64,512]{2,1,0:T(8,128)S(1)}, u32[]{:S(2)}, u32[]{:S(2)}) collective-permute-start(f32[2,64,512]{2,1,0:T(8,128)S(1)} %get-tuple-element.42), channel_id=1, source_target_pairs={{0,3},{1,2},{2,1},{3,0},{4,7},{5,6},{6,5},{7,4},{8,11},{9,10},{10,... | collective-permute-start | bytes 786440 | tf_op jit(solution)/shard_map/ppermute | solution.py:218
  31.3 7.8 %collective-permute-start.7 = (f32[4,128,128]{2,1,0:T(8,128)S(1)}, f32[4,128,128]{2,1,0:T(8,128)S(1)}, u32[]{:S(2)}, u32[]{:S(2)}) collective-permute-start(f32[4,128,128]{2,1,0:T(8,128)S(1)} %get-tuple-element.38), channel_id=1, source_target_pairs={{0,8},{1,9},{2,10},{3,11},{4,12},{5,13},{6,14},{7,15},{8,16},{9,17... | collective-permute-start | bytes 786440 | tf_op jit(solution)/shard_map/ppermute | solution.py:279
  34.8 7.5 %collective-permute-start.8 = (f32[2,64,512]{2,1,0:T(8,128)S(1)}, f32[2,64,512]{2,1,0:T(8,128)S(1)}, u32[]{:S(2)}, u32[]{:S(2)}) collective-permute-start(f32[2,64,512]{2,1,0:T(8,128)S(1)} %get-tuple-element.39), channel_id=1, source_target_pairs={{0,2},{1,3},{2,0},{3,1},{4,6},{5,7},{6,4},{7,5},{8,10},{9,11},{10,... | collective-permute-start | bytes 786440 | tf_op jit(solution)/shard_map/ppermute | solution.py:218
  35.4 7.8 %collective-permute-start.9 = (f32[2,64,512]{2,1,0:T(8,128)S(1)}, f32[2,64,512]{2,1,0:T(8,128)S(1)}, u32[]{:S(2)}, u32[]{:S(2)}) collective-permute-start(f32[2,64,512]{2,1,0:T(8,128)S(1)} %get-tuple-element.41), channel_id=1, source_target_pairs={{0,1},{1,0},{2,3},{3,2},{4,5},{5,4},{6,7},{7,6},{8,9},{9,8},{10,11... | collective-permute-start | bytes 786440 | tf_op jit(solution)/shard_map/ppermute | solution.py:218
  39.3 7.8 %collective-permute-start.17 = (f32[64,512]{1,0:T(8,128)S(1)}, f32[64,512]{1,0:T(8,128)S(1)}, u32[]{:S(2)}, u32[]{:S(2)}) collective-permute-start(f32[64,512]{1,0:T(8,128)S(1)} %get-tuple-element.50), channel_id=1, source_target_pairs={{0,3},{1,2},{2,1},{3,0},{4,7},{5,6},{6,5},{7,4},{8,11},{9,10},{10,... | collective-permute-start | bytes 393224 | tf_op jit(solution)/shard_map/ppermute | solution.py:218
  40.8 6.8 %collective-permute-start.16 = (f32[64,512]{1,0:T(8,128)S(1)}, f32[64,512]{1,0:T(8,128)S(1)}, u32[]{:S(2)}, u32[]{:S(2)}) collective-permute-start(f32[64,512]{1,0:T(8,128)S(1)} %get-tuple-element.43.refs_3_), channel_id=1, source_target_pairs={{0,7},{1,6},{2,5},{3,4},{4,3},{5,2},{6,1},{7,0},{8,15},{9,14},{10,... | collective-permute-start | bytes 393224 | tf_op jit(solution)/shard_map/ppermute | solution.py:218
  43.1 5.2 %copy-start.3 = (f32[4096]{0:T(1024)S(1)}, f32[4096]{0:T(1024)}, u32[]{:S(2)}) copy-start(f32[4096]{0:T(1024)} %param.9) | copy-start | bytes 49156
  43.6 5.5 %collective-permute-start.11 = (f32[64,512]{1,0:T(8,128)S(1)}, f32[64,512]{1,0:T(8,128)S(1)}, u32[]{:S(2)}, u32[]{:S(2)}) collective-permute-start(f32[64,512]{1,0:T(8,128)S(1)} %get-tuple-element.44), channel_id=1, source_target_pairs={{0,4},{1,5},{2,6},{3,7},{4,0},{5,1},{6,2},{7,3},{8,12},{9,13},{10,... | collective-permute-start | bytes 393224 | tf_op jit(solution)/shard_map/ppermute | solution.py:218
  43.7 6.5 %collective-permute-start.12 = (f32[64,512]{1,0:T(8,128)S(1)}, f32[64,512]{1,0:T(8,128)S(1)}, u32[]{:S(2)}, u32[]{:S(2)}) collective-permute-start(f32[64,512]{1,0:T(8,128)S(1)} %get-tuple-element.45), channel_id=1, source_target_pairs={{0,1},{1,0},{2,3},{3,2},{4,5},{5,4},{6,7},{7,6},{8,9},{9,8},{10,11... | collective-permute-start | bytes 393224 | tf_op jit(solution)/shard_map/ppermute | solution.py:218
  45.3 6.3 %collective-permute-start.13 = (f32[64,512]{1,0:T(8,128)S(1)}, f32[64,512]{1,0:T(8,128)S(1)}, u32[]{:S(2)}, u32[]{:S(2)}) collective-permute-start(f32[64,512]{1,0:T(8,128)S(1)} %get-tuple-element.46), channel_id=1, source_target_pairs={{0,2},{1,3},{2,0},{3,1},{4,6},{5,7},{6,4},{7,5},{8,10},{9,11},{10,... | collective-permute-start | bytes 393224 | tf_op jit(solution)/shard_map/ppermute | solution.py:218
  47.0 5.9 %collective-permute-start.14 = (f32[64,512]{1,0:T(8,128)S(1)}, f32[64,512]{1,0:T(8,128)S(1)}, u32[]{:S(2)}, u32[]{:S(2)}) collective-permute-start(f32[64,512]{1,0:T(8,128)S(1)} %get-tuple-element.47), channel_id=1, source_target_pairs={{0,5},{1,4},{2,7},{3,6},{4,1},{5,0},{6,3},{7,2},{8,13},{9,12},{10,... | collective-permute-start | bytes 393224 | tf_op jit(solution)/shard_map/ppermute | solution.py:218
  47.6 5.8 %collective-permute-start.15 = (f32[64,512]{1,0:T(8,128)S(1)}, f32[64,512]{1,0:T(8,128)S(1)}, u32[]{:S(2)}, u32[]{:S(2)}) collective-permute-start(f32[64,512]{1,0:T(8,128)S(1)} %get-tuple-element.48), channel_id=1, source_target_pairs={{0,6},{1,7},{2,4},{3,5},{4,2},{5,3},{6,0},{7,1},{8,14},{9,15},{10,... | collective-permute-start | bytes 393224 | tf_op jit(solution)/shard_map/ppermute | solution.py:218

commit v15 on v14

--- a/solution.py
+++ b/solution.py
@@ -244,7 +244,7 @@
         moved=2 * block_bytes,
     )(swapped)
     far_got = [swap(part, e) for e, part in zip(far_order, far_parts)] + [swapped]
-    gates = near_got[:-1]
+    gates = near_got[:1]
     *query_parts, table = call(
         functools.partial(join_queries, members, width, query_order, rows, docs, len(gates)),
         "join_queries",

time: 54.5 us -> 54.5 us (level)
  waiting for transfers between devices: 19.7 us -> 21.1 us
  starting transfers between devices: 24.2 us -> 22.8 us
    ppermute x17, starting transfers between devices: 20.7 us -> 19.3 us  [swap(): return lax.ppermute(part, everyone, pairs)]
    ppermute x17, waiting for transfers between devices: 17.5 us -> 18.9 us  [swap(): return lax.ppermute(part, everyone, pairs)]
  transfers between devices with their start and end apart: 18 -> 18, of which waited for: 12 -> 11; matrix products, arithmetic and copies ran while one was open for 0% -> 0% of each run, Pallas kernels for 15% -> 15%
where the time goes in v15:
time: 54.5 us; the launch traced here: 54.4 us
  starting transfers between devices  22.8 us (42%)
  waiting for transfers between devices  21.1 us (39%)
  Pallas kernels  10.3 us (19%)
    ppermute x17, starting transfers between devices, swap(): return lax.ppermute(part, everyone, pairs)  19.3 us
    ppermute x17, waiting for transfers between devices, swap(): return lax.ppermute(part, everyone, pairs)  18.9 us
    pallas_call x1, Pallas kernels, body(): call(functools.partial(inside, head_count, docs, rows), 'inside', shape(r...  4.93 us
    ppermute x1, starting transfers between devices, body(): moving = lax.ppermute(total, everyone, up)  3.5 us
    ppermute x1, waiting for transfers between devices, body(): moving = lax.ppermute(total, everyone, up)  2.19 us
    pallas_call x2, Pallas kernels, body(): call(functools.partial(finish, chosen, members, heads, rows), 'finish', s...  1.8 us
    pallas_call x1, Pallas kernels, body(): call(functools.partial(spread, members, width, near_order), 'spread', [sh...  1.48 us
  transfers between devices with their start and end apart: 18, of which 11 were waited for; matrix products, arithmetic and copies ran while one was open for 0% of the time, Pallas kernels for 15%

profile of v15, /device:TPU:0, one launch (start us, length us, event | category | flops | bytes accessed | tf_op | source)
XLA Modules:
  0.0 54.4 jit_solution(1504607278157522746)
XLA Ops:
  0.0 0.0 copy-start
  0.0 0.0 copy-start.2
  0.0 0.0 copy-start.1
  0.0 0.0 copy-start.4
  0.0 1.5 %spread.1 = (f32[2,64,512]{2,1,0:T(8,128)S(1)}, f32[2,64,512]{2,1,0:T(8,128)S(1)}, f32[2,64,512]{2,1,0:T(8,128)S(1)}, f32[2,64,512]{2,1,0:T(8,128)S(1)}, f32[4,3,64,512]{3,2,1,0:T(8,128)S(1)}) custom-call(bf16[64,4096]{1,0:T(8,128)(2,1)} %queries.5, bf16[64,4096]{1,0:T(8,128)(2,1)} %keys.3, bf16[64,4096]{1,0:T(8,128)(2,1)} %values.3), custom_call_target="tpu_custom_call" | custom-call | tf_op jit(solution)/shard_map/spread/pallas_call | solution.py:224
  1.5 0.5 collective-permute-start
  2.0 2.6 %collective-permute-start.1 = (f32[2,64,512]{2,1,0:T(8,128)S(1)}, f32[2,64,512]{2,1,0:T(8,128)S(1)}, u32[]{:S(2)}, u32[]{:S(2)}) collective-permute-start(f32[2,64,512]{2,1,0:T(8,128)S(1)} %get-tuple-element.29), channel_id=1, source_target_pairs={{0,2},{1,3},{2,0},{3,1},{4,6},{5,7},{6,4},{7,5},{8,10},{9,11},{10,... | collective-permute-start | bytes 786440 | tf_op jit(solution)/shard_map/ppermute | solution.py:218
  4.6 1.5 %collective-permute-start.2 = (f32[2,64,512]{2,1,0:T(8,128)S(1)}, f32[2,64,512]{2,1,0:T(8,128)S(1)}, u32[]{:S(2)}, u32[]{:S(2)}) collective-permute-start(f32[2,64,512]{2,1,0:T(8,128)S(1)} %get-tuple-element.31), channel_id=1, source_target_pairs={{0,1},{1,0},{2,3},{3,2},{4,5},{5,4},{6,7},{7,6},{8,9},{9,8},{10,11... | collective-permute-start | bytes 786440 | tf_op jit(solution)/shard_map/ppermute | solution.py:218
  6.1 0.0 collective-permute-start.3
  6.2 0.0 collective-permute-done.swapped.refs_7_
  6.2 0.1 forward.1
  6.2 2.0 %collective-permute-start.4 = (f32[2,64,512]{2,1,0:T(8,128)S(1)}, f32[2,64,512]{2,1,0:T(8,128)S(1)}, u32[]{:S(2)}, u32[]{:S(2)}) collective-permute-start(f32[2,64,512]{2,1,0:T(8,128)S(1)} %get-tuple-element.34), channel_id=1, source_target_pairs={{0,2},{1,3},{2,0},{3,1},{4,6},{5,7},{6,4},{7,5},{8,10},{9,11},{10,... | collective-permute-start | bytes 786440 | tf_op jit(solution)/shard_map/ppermute | solution.py:218
  8.2 1.4 %collective-permute-start.5 = (f32[2,64,512]{2,1,0:T(8,128)S(1)}, f32[2,64,512]{2,1,0:T(8,128)S(1)}, u32[]{:S(2)}, u32[]{:S(2)}) collective-permute-start(f32[2,64,512]{2,1,0:T(8,128)S(1)} %get-tuple-element.35), channel_id=1, source_target_pairs={{0,3},{1,2},{2,1},{3,0},{4,7},{5,6},{6,5},{7,4},{8,11},{9,10},{10,... | collective-permute-start | bytes 786440 | tf_op jit(solution)/shard_map/ppermute | solution.py:218
  9.7 2.1 %collective-permute-done.1.refs_0_ = f32[2,64,512]{2,1,0:T(8,128)S(1)} collective-permute-done((f32[2,64,512]{2,1,0:T(8,128)S(1)}, f32[2,64,512]{2,1,0:T(8,128)S(1)}, u32[]{:S(2)}, u32[]{:S(2)}) %collective-permute-start.1) | collective-permute-done | bytes 262176 | tf_op jit(solution)/shard_map/ppermute | solution.py:218
  11.8 2.0 %collective-permute-start.6 = (f32[2,64,512]{2,1,0:T(8,128)S(1)}, f32[2,64,512]{2,1,0:T(8,128)S(1)}, u32[]{:S(2)}, u32[]{:S(2)}) collective-permute-start(f32[2,64,512]{2,1,0:T(8,128)S(1)} %get-tuple-element.36), channel_id=1, source_target_pairs={{0,1},{1,0},{2,3},{3,2},{4,5},{5,4},{6,7},{7,6},{8,9},{9,8},{10,11... | collective-permute-start | bytes 786440 | tf_op jit(solution)/shard_map/ppermute | solution.py:218
  13.7 0.0 copy-done
  13.7 0.0 copy-done.2
  13.7 0.0 copy-done.1
  13.8 0.0 copy-done.4
  13.8 4.9 %inside.1.refs_8_.own = f32[64,4096]{1,0:T(8,128)S(1)} custom-call(s32[16]{0:T(128)S(1)} %copy-done.4, bf16[64,4096]{1,0:T(8,128)(2,1)S(1)} %copy-done, bf16[64,4096]{1,0:T(8,128)(2,1)S(1)} %copy-done.1, bf16[64,4096]{1,0:T(8,128)(2,1)S(1)} %copy-done.2), custom_call_target="tpu_custom_call" | custom-call | flops 67108864 | bytes 3145728 | tf_op jit(solution)/shard_map/inside/pallas_call | solution.py:258
  18.7 0.8 %join_queries.1 = (f32[2,64,512]{2,1,0:T(8,128)S(1)}, f32[2,64,512]{2,1,0:T(8,128)S(1)}, f32[2,64,512]{2,1,0:T(8,128)S(1)}, f32[2,64,512]{2,1,0:T(8,128)S(1)}, s32[10,128]{1,0:T(8,128)S(1)}) custom-call(s32[16]{0:T(128)S(1)} %copy-done.4, bf16[64,4096]{1,0:T(8,128)(2,1)S(1)} %copy-done, f32[4,3,64,512]{3,2,1,0:T(8,128)S(1)} %collective-permute-done.swapped.refs_7_, ...), custom_call_target="tpu_custom_call" | custom-call | bytes 2097152 | tf_op jit(solution)/shard_map/join_queries/pallas_call | solution.py:248
  19.4 0.0 collective-permute-done.2.refs_1_
  19.5 1.6 %collective-permute-start.10 = (f32[2,64,512]{2,1,0:T(8,128)S(1)}, f32[2,64,512]{2,1,0:T(8,128)S(1)}, u32[]{:S(2)}, u32[]{:S(2)}) collective-permute-start(f32[2,64,512]{2,1,0:T(8,128)S(1)} %get-tuple-element.42), channel_id=1, source_target_pairs={{0,3},{1,2},{2,1},{3,0},{4,7},{5,6},{6,5},{7,4},{8,11},{9,10},{10,... | collective-permute-start | bytes 786440 | tf_op jit(solution)/shard_map/ppermute | solution.py:218
  21.0 0.0 collective-permute-done.3.refs_2_
  21.0 7.4 %collective-permute-done.4.refs_4_ = f32[2,64,512]{2,1,0:T(8,128)S(1)} collective-permute-done((f32[2,64,512]{2,1,0:T(8,128)S(1)}, f32[2,64,512]{2,1,0:T(8,128)S(1)}, u32[]{:S(2)}, u32[]{:S(2)}) %collective-permute-start.4) | collective-permute-done | bytes 262176 | tf_op jit(solution)/shard_map/ppermute | solution.py:218
  28.4 0.0 collective-permute-done.5.refs_5_
  28.4 2.3 %collective-permute-done.6.refs_6_ = f32[2,64,512]{2,1,0:T(8,128)S(1)} collective-permute-done((f32[2,64,512]{2,1,0:T(8,128)S(1)}, f32[2,64,512]{2,1,0:T(8,128)S(1)}, u32[]{:S(2)}, u32[]{:S(2)}) %collective-permute-start.6) | collective-permute-done | bytes 262176 | tf_op jit(solution)/shard_map/ppermute | solution.py:218
  30.7 0.6 %gather_states.1 = (f32[8,4,128,128]{3,2,1,0:T(8,128)S(1)}, f32[4,128,128]{2,1,0:T(8,128)S(1)}) custom-call(s32[10,128]{1,0:T(8,128)S(1)} %get-tuple-element.30.table, f32[2,64,512]{2,1,0:T(8,128)S(1)} %collective-permute-done.1.refs_0_, f32[2,64,512]{2,1,0:T(8,128)S(1)} %collective-permute-done.2.refs_1_, f32[2,64,512]{2,1,0:T(8,128)S(1)} %collective-permute-done.3.refs_2_, ...), custom_call_target="tpu_custom_call" | custom-call | flops 67108864 | bytes 4194304 | tf_op jit(solution)/shard_map/gather_states/pallas_call | solution.py:268
  31.3 3.5 %collective-permute-start.7 = (f32[4,128,128]{2,1,0:T(8,128)S(1)}, f32[4,128,128]{2,1,0:T(8,128)S(1)}, u32[]{:S(2)}, u32[]{:S(2)}) collective-permute-start(f32[4,128,128]{2,1,0:T(8,128)S(1)} %get-tuple-element.38), channel_id=1, source_target_pairs={{0,8},{1,9},{2,10},{3,11},{4,12},{5,13},{6,14},{7,15},{8,16},{9,17... | collective-permute-start | bytes 786440 | tf_op jit(solution)/shard_map/ppermute | solution.py:279
  34.8 0.6 %collective-permute-start.8 = (f32[2,64,512]{2,1,0:T(8,128)S(1)}, f32[2,64,512]{2,1,0:T(8,128)S(1)}, u32[]{:S(2)}, u32[]{:S(2)}) collective-permute-start(f32[2,64,512]{2,1,0:T(8,128)S(1)} %get-tuple-element.39), channel_id=1, source_target_pairs={{0,2},{1,3},{2,0},{3,1},{4,6},{5,7},{6,4},{7,5},{8,10},{9,11},{10,... | collective-permute-start | bytes 786440 | tf_op jit(solution)/shard_map/ppermute | solution.py:218
  35.4 1.5 %collective-permute-start.9 = (f32[2,64,512]{2,1,0:T(8,128)S(1)}, f32[2,64,512]{2,1,0:T(8,128)S(1)}, u32[]{:S(2)}, u32[]{:S(2)}) collective-permute-start(f32[2,64,512]{2,1,0:T(8,128)S(1)} %get-tuple-element.41), channel_id=1, source_target_pairs={{0,1},{1,0},{2,3},{3,2},{4,5},{5,4},{6,7},{7,6},{8,9},{9,8},{10,11... | collective-permute-start | bytes 786440 | tf_op jit(solution)/shard_map/ppermute | solution.py:218
  36.9 0.0 collective-permute-done.10.refs_0_
  36.9 2.2 %collective-permute-done.7.earlier = f32[4,128,128]{2,1,0:T(8,128)S(1)} collective-permute-done((f32[4,128,128]{2,1,0:T(8,128)S(1)}, f32[4,128,128]{2,1,0:T(8,128)S(1)}, u32[]{:S(2)}, u32[]{:S(2)}) %collective-permute-start.7) | collective-permute-done | bytes 262176 | tf_op jit(solution)/shard_map/ppermute | solution.py:279
  39.1 0.2 reach_back.2
  39.3 1.6 %collective-permute-start.17 = (f32[64,512]{1,0:T(8,128)S(1)}, f32[64,512]{1,0:T(8,128)S(1)}, u32[]{:S(2)}, u32[]{:S(2)}) collective-permute-start(f32[64,512]{1,0:T(8,128)S(1)} %get-tuple-element.50), channel_id=1, source_target_pairs={{0,3},{1,2},{2,1},{3,0},{4,7},{5,6},{6,5},{7,4},{8,11},{9,10},{10,... | collective-permute-start | bytes 393224 | tf_op jit(solution)/shard_map/ppermute | solution.py:218
  40.8 0.0 collective-permute-start.16
  40.8 1.4 %collective-permute-done.8.refs_0_ = f32[2,64,512]{2,1,0:T(8,128)S(1)} collective-permute-done((f32[2,64,512]{2,1,0:T(8,128)S(1)}, f32[2,64,512]{2,1,0:T(8,128)S(1)}, u32[]{:S(2)}, u32[]{:S(2)}) %collective-permute-start.8) | collective-permute-done | bytes 262176 | tf_op jit(solution)/shard_map/ppermute | solution.py:218
  42.3 0.9 %collective-permute-done.9.refs_2_ = f32[2,64,512]{2,1,0:T(8,128)S(1)} collective-permute-done((f32[2,64,512]{2,1,0:T(8,128)S(1)}, f32[2,64,512]{2,1,0:T(8,128)S(1)}, u32[]{:S(2)}, u32[]{:S(2)}) %collective-permute-start.9) | collective-permute-done | bytes 262176 | tf_op jit(solution)/shard_map/ppermute | solution.py:218
  43.1 0.0 copy-start.3
  43.1 0.5 reach_back.3
  43.6 0.1 collective-permute-start.11
  43.7 1.6 %collective-permute-start.12 = (f32[64,512]{1,0:T(8,128)S(1)}, f32[64,512]{1,0:T(8,128)S(1)}, u32[]{:S(2)}, u32[]{:S(2)}) collective-permute-start(f32[64,512]{1,0:T(8,128)S(1)} %get-tuple-element.45), channel_id=1, source_target_pairs={{0,1},{1,0},{2,3},{3,2},{4,5},{5,4},{6,7},{7,6},{8,9},{9,8},{10,11... | collective-permute-start | bytes 393224 | tf_op jit(solution)/shard_map/ppermute | solution.py:218
  45.3 1.8 %collective-permute-start.13 = (f32[64,512]{1,0:T(8,128)S(1)}, f32[64,512]{1,0:T(8,128)S(1)}, u32[]{:S(2)}, u32[]{:S(2)}) collective-permute-start(f32[64,512]{1,0:T(8,128)S(1)} %get-tuple-element.46), channel_id=1, source_target_pairs={{0,2},{1,3},{2,0},{3,1},{4,6},{5,7},{6,4},{7,5},{8,10},{9,11},{10,... | collective-permute-start | bytes 393224 | tf_op jit(solution)/shard_map/ppermute | solution.py:218
  47.0 0.0 collective-permute-done.17.refs_2_
  47.0 0.0 collective-permute-start.14
  47.0 0.6 %collective-permute-done.16.refs_1_ = f32[64,512]{1,0:T(8,128)S(1)} collective-permute-done((f32[64,512]{1,0:T(8,128)S(1)}, f32[64,512]{1,0:T(8,128)S(1)}, u32[]{:S(2)}, u32[]{:S(2)}) %collective-permute-start.16) | collective-permute-done | bytes 131104 | tf_op jit(solution)/shard_map/ppermute | solution.py:218
  47.6 0.7 %collective-permute-start.15 = (f32[64,512]{1,0:T(8,128)S(1)}, f32[64,512]{1,0:T(8,128)S(1)}, u32[]{:S(2)}, u32[]{:S(2)}) collective-permute-start(f32[64,512]{1,0:T(8,128)S(1)} %get-tuple-element.48), channel_id=1, source_target_pairs={{0,6},{1,7},{2,4},{3,5},{4,2},{5,3},{6,0},{7,1},{8,14},{9,15},{10,... | collective-permute-start | bytes 393224 | tf_op jit(solution)/shard_map/ppermute | solution.py:218
  48.3 0.0 copy-done.3
  48.3 0.9 %finish.2.refs_5_ = bf16[64,4096]{1,0:T(8,128)(2,1)} custom-call(s32[10,128]{1,0:T(8,128)S(1)} %get-tuple-element.30.table, f32[64,4096]{1,0:T(8,128)S(1)} %inside.1.refs_8_.own, f32[1,4096]{1,0:T(1,128)S(1)} %bitcast.1, f32[64,512]{1,0:T(8,128)S(1)} %get-tuple-element.49.refs_0_, f32[64,512]{1,0:T(8,128)S(1)} %collective-permute-done.16.refs_1_, ...), custom_call_target="tpu_custom_call" | custom-call | bytes 2097152 | tf_op jit(solution)/shard_map/finish/pallas_call | solution.py:316
  49.2 0.0 collective-permute-done.11.refs_0_
  49.2 1.0 %collective-permute-done.12.refs_1_ = f32[64,512]{1,0:T(8,128)S(1)} collective-permute-done((f32[64,512]{1,0:T(8,128)S(1)}, f32[64,512]{1,0:T(8,128)S(1)}, u32[]{:S(2)}, u32[]{:S(2)}) %collective-permute-start.12) | collective-permute-done | bytes 131104 | tf_op jit(solution)/shard_map/ppermute | solution.py:218
  50.2 1.4 %collective-permute-done.13.refs_2_ = f32[64,512]{1,0:T(8,128)S(1)} collective-permute-done((f32[64,512]{1,0:T(8,128)S(1)}, f32[64,512]{1,0:T(8,128)S(1)}, u32[]{:S(2)}, u32[]{:S(2)}) %collective-permute-start.13) | collective-permute-done | bytes 131104 | tf_op jit(solution)/shard_map/ppermute | solution.py:218
  51.6 1.3 %collective-permute-done.14.refs_3_ = f32[64,512]{1,0:T(8,128)S(1)} collective-permute-done((f32[64,512]{1,0:T(8,128)S(1)}, f32[64,512]{1,0:T(8,128)S(1)}, u32[]{:S(2)}, u32[]{:S(2)}) %collective-permute-start.14) | collective-permute-done | bytes 131104 | tf_op jit(solution)/shard_map/ppermute | solution.py:218
  52.9 0.5 collective-permute-done.15.refs_4_
  53.4 0.9 %finish.3 = bf16[64,4096]{1,0:T(8,128)(2,1)} custom-call(s32[10,128]{1,0:T(8,128)S(1)} %get-tuple-element.30.table, f32[64,4096]{1,0:T(8,128)S(1)} %inside.1.refs_8_.own, f32[1,4096]{1,0:T(1,128)S(1)} %bitcast.2, f32[64,512]{1,0:T(8,128)S(1)} %collective-permute-done.11.refs_0_, ...), custom_call_target="tpu_custom_call", output_to_operand_aliasing={{}: (8, {})} | custom-call | bytes 2097152 | tf_op jit(solution)/shard_map/finish/pallas_call | solution.py:316
Async XLA Ops:
  0.0 13.7 %copy-start = (bf16[64,4096]{1,0:T(8,128)(2,1)S(1)}, bf16[64,4096]{1,0:T(8,128)(2,1)}, u32[]{:S(2)}) copy-start(bf16[64,4096]{1,0:T(8,128)(2,1)} %queries.5) | copy-start | bytes 1572868
  0.0 13.7 %copy-start.2 = (bf16[64,4096]{1,0:T(8,128)(2,1)S(1)}, bf16[64,4096]{1,0:T(8,128)(2,1)}, u32[]{:S(2)}) copy-start(bf16[64,4096]{1,0:T(8,128)(2,1)} %values.3) | copy-start | bytes 1572868
  0.0 13.7 %copy-start.1 = (bf16[64,4096]{1,0:T(8,128)(2,1)S(1)}, bf16[64,4096]{1,0:T(8,128)(2,1)}, u32[]{:S(2)}) copy-start(bf16[64,4096]{1,0:T(8,128)(2,1)} %keys.3) | copy-start | bytes 1572868
  0.0 13.7 %copy-start.4 = (s32[16]{0:T(128)S(1)}, s32[16]{0:T(128)}, u32[]{:S(2)}) copy-start(s32[16]{0:T(128)} %lengths.3) | copy-start | bytes 196
  1.5 4.7 %collective-permute-start = (f32[4,3,64,512]{3,2,1,0:T(8,128)S(1)}, f32[4,3,64,512]{3,2,1,0:T(8,128)S(1)}, u32[]{:S(2)}, u32[]{:S(2)}) collective-permute-start(f32[4,3,64,512]{3,2,1,0:T(8,128)S(1)} %get-tuple-element.28), channel_id=1, source_target_pairs={{0,4},{1,5},{2,6},{3,7},{4,0},{5,1},{6,2},{7,3},{8,12},{9,13},{10,... | collective-permute-start | bytes 4718600 | tf_op jit(solution)/shard_map/ppermute | solution.py:218
  2.0 9.8 %collective-permute-start.1 = (f32[2,64,512]{2,1,0:T(8,128)S(1)}, f32[2,64,512]{2,1,0:T(8,128)S(1)}, u32[]{:S(2)}, u32[]{:S(2)}) collective-permute-start(f32[2,64,512]{2,1,0:T(8,128)S(1)} %get-tuple-element.29), channel_id=1, source_target_pairs={{0,2},{1,3},{2,0},{3,1},{4,6},{5,7},{6,4},{7,5},{8,10},{9,11},{10,... | collective-permute-start | bytes 786440 | tf_op jit(solution)/shard_map/ppermute | solution.py:218
  4.6 14.8 %collective-permute-start.2 = (f32[2,64,512]{2,1,0:T(8,128)S(1)}, f32[2,64,512]{2,1,0:T(8,128)S(1)}, u32[]{:S(2)}, u32[]{:S(2)}) collective-permute-start(f32[2,64,512]{2,1,0:T(8,128)S(1)} %get-tuple-element.31), channel_id=1, source_target_pairs={{0,1},{1,0},{2,3},{3,2},{4,5},{5,4},{6,7},{7,6},{8,9},{9,8},{10,11... | collective-permute-start | bytes 786440 | tf_op jit(solution)/shard_map/ppermute | solution.py:218
  6.1 14.9 %collective-permute-start.3 = (f32[2,64,512]{2,1,0:T(8,128)S(1)}, f32[2,64,512]{2,1,0:T(8,128)S(1)}, u32[]{:S(2)}, u32[]{:S(2)}) collective-permute-start(f32[2,64,512]{2,1,0:T(8,128)S(1)} %get-tuple-element.32), channel_id=1, source_target_pairs={{0,3},{1,2},{2,1},{3,0},{4,7},{5,6},{6,5},{7,4},{8,11},{9,10},{10,... | collective-permute-start | bytes 786440 | tf_op jit(solution)/shard_map/ppermute | solution.py:218
  6.2 22.2 %collective-permute-start.4 = (f32[2,64,512]{2,1,0:T(8,128)S(1)}, f32[2,64,512]{2,1,0:T(8,128)S(1)}, u32[]{:S(2)}, u32[]{:S(2)}) collective-permute-start(f32[2,64,512]{2,1,0:T(8,128)S(1)} %get-tuple-element.34), channel_id=1, source_target_pairs={{0,2},{1,3},{2,0},{3,1},{4,6},{5,7},{6,4},{7,5},{8,10},{9,11},{10,... | collective-permute-start | bytes 786440 | tf_op jit(solution)/shard_map/ppermute | solution.py:218
  8.2 20.1 %collective-permute-start.5 = (f32[2,64,512]{2,1,0:T(8,128)S(1)}, f32[2,64,512]{2,1,0:T(8,128)S(1)}, u32[]{:S(2)}, u32[]{:S(2)}) collective-permute-start(f32[2,64,512]{2,1,0:T(8,128)S(1)} %get-tuple-element.35), channel_id=1, source_target_pairs={{0,3},{1,2},{2,1},{3,0},{4,7},{5,6},{6,5},{7,4},{8,11},{9,10},{10,... | collective-permute-start | bytes 786440 | tf_op jit(solution)/shard_map/ppermute | solution.py:218
  11.8 18.9 %collective-permute-start.6 = (f32[2,64,512]{2,1,0:T(8,128)S(1)}, f32[2,64,512]{2,1,0:T(8,128)S(1)}, u32[]{:S(2)}, u32[]{:S(2)}) collective-permute-start(f32[2,64,512]{2,1,0:T(8,128)S(1)} %get-tuple-element.36), channel_id=1, source_target_pairs={{0,1},{1,0},{2,3},{3,2},{4,5},{5,4},{6,7},{7,6},{8,9},{9,8},{10,11... | collective-permute-start | bytes 786440 | tf_op jit(solution)/shard_map/ppermute | solution.py:218
  19.5 17.4 %collective-permute-start.10 = (f32[2,64,512]{2,1,0:T(8,128)S(1)}, f32[2,64,512]{2,1,0:T(8,128)S(1)}, u32[]{:S(2)}, u32[]{:S(2)}) collective-permute-start(f32[2,64,512]{2,1,0:T(8,128)S(1)} %get-tuple-element.42), channel_id=1, source_target_pairs={{0,3},{1,2},{2,1},{3,0},{4,7},{5,6},{6,5},{7,4},{8,11},{9,10},{10,... | collective-permute-start | bytes 786440 | tf_op jit(solution)/shard_map/ppermute | solution.py:218
  31.3 7.8 %collective-permute-start.7 = (f32[4,128,128]{2,1,0:T(8,128)S(1)}, f32[4,128,128]{2,1,0:T(8,128)S(1)}, u32[]{:S(2)}, u32[]{:S(2)}) collective-permute-start(f32[4,128,128]{2,1,0:T(8,128)S(1)} %get-tuple-element.38), channel_id=1, source_target_pairs={{0,8},{1,9},{2,10},{3,11},{4,12},{5,13},{6,14},{7,15},{8,16},{9,17... | collective-permute-start | bytes 786440 | tf_op jit(solution)/shard_map/ppermute | solution.py:279
  34.8 7.5 %collective-permute-start.8 = (f32[2,64,512]{2,1,0:T(8,128)S(1)}, f32[2,64,512]{2,1,0:T(8,128)S(1)}, u32[]{:S(2)}, u32[]{:S(2)}) collective-permute-start(f32[2,64,512]{2,1,0:T(8,128)S(1)} %get-tuple-element.39), channel_id=1, source_target_pairs={{0,2},{1,3},{2,0},{3,1},{4,6},{5,7},{6,4},{7,5},{8,10},{9,11},{10,... | collective-permute-start | bytes 786440 | tf_op jit(solution)/shard_map/ppermute | solution.py:218
  35.4 7.8 %collective-permute-start.9 = (f32[2,64,512]{2,1,0:T(8,128)S(1)}, f32[2,64,512]{2,1,0:T(8,128)S(1)}, u32[]{:S(2)}, u32[]{:S(2)}) collective-permute-start(f32[2,64,512]{2,1,0:T(8,128)S(1)} %get-tuple-element.41), channel_id=1, source_target_pairs={{0,1},{1,0},{2,3},{3,2},{4,5},{5,4},{6,7},{7,6},{8,9},{9,8},{10,11... | collective-permute-start | bytes 786440 | tf_op jit(solution)/shard_map/ppermute | solution.py:218
  39.3 7.8 %collective-permute-start.17 = (f32[64,512]{1,0:T(8,128)S(1)}, f32[64,512]{1,0:T(8,128)S(1)}, u32[]{:S(2)}, u32[]{:S(2)}) collective-permute-start(f32[64,512]{1,0:T(8,128)S(1)} %get-tuple-element.50), channel_id=1, source_target_pairs={{0,3},{1,2},{2,1},{3,0},{4,7},{5,6},{6,5},{7,4},{8,11},{9,10},{10,... | collective-permute-start | bytes 393224 | tf_op jit(solution)/shard_map/ppermute | solution.py:218
  40.8 6.8 %collective-permute-start.16 = (f32[64,512]{1,0:T(8,128)S(1)}, f32[64,512]{1,0:T(8,128)S(1)}, u32[]{:S(2)}, u32[]{:S(2)}) collective-permute-start(f32[64,512]{1,0:T(8,128)S(1)} %get-tuple-element.43.refs_3_), channel_id=1, source_target_pairs={{0,7},{1,6},{2,5},{3,4},{4,3},{5,2},{6,1},{7,0},{8,15},{9,14},{10,... | collective-permute-start | bytes 393224 | tf_op jit(solution)/shard_map/ppermute | solution.py:218
  43.1 5.1 %copy-start.3 = (f32[4096]{0:T(1024)S(1)}, f32[4096]{0:T(1024)}, u32[]{:S(2)}) copy-start(f32[4096]{0:T(1024)} %param.9) | copy-start | bytes 49156
  43.6 5.5 %collective-permute-start.11 = (f32[64,512]{1,0:T(8,128)S(1)}, f32[64,512]{1,0:T(8,128)S(1)}, u32[]{:S(2)}, u32[]{:S(2)}) collective-permute-start(f32[64,512]{1,0:T(8,128)S(1)} %get-tuple-element.44), channel_id=1, source_target_pairs={{0,4},{1,5},{2,6},{3,7},{4,0},{5,1},{6,2},{7,3},{8,12},{9,13},{10,... | collective-permute-start | bytes 393224 | tf_op jit(solution)/shard_map/ppermute | solution.py:218
  43.7 6.5 %collective-permute-start.12 = (f32[64,512]{1,0:T(8,128)S(1)}, f32[64,512]{1,0:T(8,128)S(1)}, u32[]{:S(2)}, u32[]{:S(2)}) collective-permute-start(f32[64,512]{1,0:T(8,128)S(1)} %get-tuple-element.45), channel_id=1, source_target_pairs={{0,1},{1,0},{2,3},{3,2},{4,5},{5,4},{6,7},{7,6},{8,9},{9,8},{10,11... | collective-permute-start | bytes 393224 | tf_op jit(solution)/shard_map/ppermute | solution.py:218
  45.3 6.3 %collective-permute-start.13 = (f32[64,512]{1,0:T(8,128)S(1)}, f32[64,512]{1,0:T(8,128)S(1)}, u32[]{:S(2)}, u32[]{:S(2)}) collective-permute-start(f32[64,512]{1,0:T(8,128)S(1)} %get-tuple-element.46), channel_id=1, source_target_pairs={{0,2},{1,3},{2,0},{3,1},{4,6},{5,7},{6,4},{7,5},{8,10},{9,11},{10,... | collective-permute-start | bytes 393224 | tf_op jit(solution)/shard_map/ppermute | solution.py:218
  47.0 5.9 %collective-permute-start.14 = (f32[64,512]{1,0:T(8,128)S(1)}, f32[64,512]{1,0:T(8,128)S(1)}, u32[]{:S(2)}, u32[]{:S(2)}) collective-permute-start(f32[64,512]{1,0:T(8,128)S(1)} %get-tuple-element.47), channel_id=1, source_target_pairs={{0,5},{1,4},{2,7},{3,6},{4,1},{5,0},{6,3},{7,2},{8,13},{9,12},{10,... | collective-permute-start | bytes 393224 | tf_op jit(solution)/shard_map/ppermute | solution.py:218
  47.6 5.8 %collective-permute-start.15 = (f32[64,512]{1,0:T(8,128)S(1)}, f32[64,512]{1,0:T(8,128)S(1)}, u32[]{:S(2)}, u32[]{:S(2)}) collective-permute-start(f32[64,512]{1,0:T(8,128)S(1)} %get-tuple-element.48), channel_id=1, source_target_pairs={{0,6},{1,7},{2,4},{3,5},{4,2},{5,3},{6,0},{7,1},{8,14},{9,15},{10,... | collective-permute-start | bytes 393224 | tf_op jit(solution)/shard_map/ppermute | solution.py:218
